TPU v7x, 256 devices: a whole 4x4x8 slice. The times are simulated.
256 devices in a mesh: shard: 32 (over y, z), blk: 8 (over x, core).
Axes of the slice: x: 4, y: 4, z: 8, core: 2. Of those that a mesh axis runs over, the one named last changes fastest.
Arguments:
- request_embeddings: bfloat16 [65536, 256], P(('shard', 'blk')), may hold values from -0.5 to 0.5
- frequent_entry_matrix: bfloat16 [2048, 256], replicated, may hold values from -0.23925781 to 0.23925781
- rare_entry_matrix: float32 [65536, 256], P('shard'), may hold values from -0.24 to 0.24
- frequent_entry_lines: int32 [65536, 4], P(('shard', 'blk')), may hold values from 0 to 2047
- rare_place_parent: int32 [65536, 4], P(('shard', 'blk')), may hold values from 0 to 31, all different within a row; in each aligned block of 256 rows (0 to 255, 256 to 511, ...) at most 64 rows name the same one
- rare_local_position: int32 [65536, 4], P(('shard', 'blk')), may hold values from 0 to 2047
- rare_place_tally: int32 [65536], P(('shard', 'blk')), may hold values from 1 to 4
- sharpness_factor: float32 [1], replicated, may hold values from 4 to 16
- pairscore_additive: float32 [1], replicated, may hold values from -6 to -2
Outputs:
- request_derivative: float32 [65536, 256], P(('shard', 'blk'))
- hot_grad: float32 [2048, 256], replicated
- cold_grad: float32 [65536, 256], P(('shard', 'blk'))
Inputs may be any that keep to these rules, and one draw needn't show every extreme that they name: `rare_place_parent`: each row names 4 different owners; among the rows of one device no owner is named by more than 64 rows, a bound that some block reaches.
All inputs are finite; a program needn't handle non-finite values.
Results may differ from a plain program's by a relative error of at most 0.007.
Values may be sent and summed in bfloat16 or wider, within the bound.
No kernel may reach another device: no remote copies, remote signals or barrier semaphores. Data moves between devices by JAX's collectives and lax.ppermute only.
A program may use at most 64 MiB of HBM per device.

v0:
```python
import jax
import jax.numpy as jnp
from jax import lax
from jax.sharding import PartitionSpec as P

epsilon = 1e-06


def normalize_rows(vectors):
    radius = jnp.sqrt(jnp.sum(vectors * vectors, axis=1, keepdims=True) + epsilon)
    return (vectors / radius, radius)


def projection_backward(unit_vectors, radius, gradient):
    inner = jnp.sum(unit_vectors * gradient, axis=1, keepdims=True)
    return (gradient - unit_vectors * inner) / radius


def body(
    request_embeddings,
    frequent_entry_matrix,
    rare_entry_matrix,
    frequent_entry_lines,
    rare_place_parent,
    rare_local_position,
    rare_place_tally,
    sharpness_factor,
    pairscore_additive,
):
    pair_count, row_width = request_embeddings.shape
    owner_total = lax.axis_size("shard")
    slots_cold = rare_place_parent.shape[1]
    capacity = 2 * pair_count * slots_cold // owner_total
    sharpness_multiplier = sharpness_factor[0]
    additive_term = pairscore_additive[0]
    live_slot = jnp.arange(slots_cold)[None, :] < rare_place_tally[:, None]
    live_flat = live_slot.reshape(-1)
    owner_flat = rare_place_parent.reshape(-1)
    owner_onehot = (
        (owner_flat[:, None] == jnp.arange(owner_total)[None, :]) & live_flat[:, None]
    ).astype(jnp.int32)
    rank_before = jnp.cumsum(owner_onehot, axis=0) - owner_onehot
    position = jnp.sum(rank_before * owner_onehot, axis=1)
    dump_slot = owner_total * capacity
    bucket = jnp.where(live_flat, owner_flat * capacity + position, dump_slot)
    requests = (
        jnp.zeros((dump_slot + 1,), jnp.int32).at[bucket].set(rare_local_position.reshape(-1))
    )
    requests = requests[:dump_slot].reshape(owner_total, capacity)
    received = lax.all_to_all(requests, "shard", split_axis=0, concat_axis=0, tiled=True)
    looked = jnp.take(rare_entry_matrix, received, axis=0)
    fetched = lax.all_to_all(looked, "shard", split_axis=0, concat_axis=0, tiled=True)
    fetched_flat = fetched.reshape(dump_slot, row_width)
    picked = jnp.take(fetched_flat, jnp.minimum(bucket, dump_slot - 1), axis=0) * live_flat[
        :, None
    ].astype(jnp.float32)
    cold_sum = jnp.sum(picked.reshape(pair_count, slots_cold, row_width), axis=1)
    hot_index = jnp.arange(frequent_entry_matrix.shape[0])
    hot_counts = jnp.sum(
        (frequent_entry_lines[:, :, None] == hot_index[None, None, :]).astype(jnp.bfloat16), axis=1
    )
    hot_sum = jnp.dot(hot_counts, frequent_entry_matrix, preferred_element_type=jnp.float32)
    candidate_normalized, candidate_norm = normalize_rows(hot_sum + cold_sum)
    request_normalized, request_norm = normalize_rows(request_embeddings.astype(jnp.float32))
    candidate_reduced = candidate_normalized.astype(jnp.bfloat16)
    request_reduced = request_normalized.astype(jnp.bfloat16)
    my_base = lax.axis_index("blk") * pair_count
    target = my_base + jnp.arange(pair_count)
    block_rows = lax.all_gather(candidate_reduced, "blk", axis=0, tiled=True)
    pairwise_scores = (
        sharpness_multiplier
        * lax.dot_general(
            request_reduced,
            block_rows,
            (((1,), (1,)), ((), ())),
            preferred_element_type=jnp.float32,
        )
        + additive_term
    )
    column = jnp.arange(block_rows.shape[0])
    positive = (target[:, None] == column[None, :]).astype(jnp.float32)
    pairscore_derivative = (jax.nn.sigmoid(pairwise_scores) - positive).astype(jnp.bfloat16)
    request_running_total = jnp.dot(
        pairscore_derivative, block_rows, preferred_element_type=jnp.float32
    )
    item_acc = lax.dot_general(
        pairscore_derivative,
        request_reduced,
        (((0,), (0,)), ((), ())),
        preferred_element_type=jnp.float32,
    )
    candidate_portion = lax.psum_scatter(item_acc, "blk", scatter_dimension=0, tiled=True)
    request_derivative = projection_backward(
        request_normalized, request_norm, sharpness_multiplier * request_running_total
    )
    candidate_derivative = projection_backward(
        candidate_normalized, candidate_norm, sharpness_multiplier * candidate_portion
    ).astype(jnp.bfloat16)
    hot_local = lax.dot_general(
        hot_counts,
        candidate_derivative,
        (((0,), (0,)), ((), ())),
        preferred_element_type=jnp.float32,
    )
    slot_grads = jnp.repeat(candidate_derivative, slots_cold, axis=0)
    outgoing = jnp.zeros((dump_slot + 1, row_width), jnp.bfloat16).at[bucket].set(slot_grads)
    outgoing = outgoing[:dump_slot].reshape(owner_total, capacity, row_width)
    incoming = lax.all_to_all(outgoing, "shard", split_axis=0, concat_axis=0, tiled=True)
    cold_local = (
        jnp.zeros((rare_entry_matrix.shape[0], row_width), jnp.float32)
        .at[received.reshape(-1)]
        .add(incoming.reshape(dump_slot, row_width).astype(jnp.float32))
    )
    hot_grad = lax.psum(hot_local, ("shard", "blk"))
    cold_grad = lax.psum_scatter(cold_local, "blk", scatter_dimension=0, tiled=True)
    return (request_derivative, hot_grad, cold_grad)


def solution(mesh):
    in_specs = (
        P(("shard", "blk"), None),
        P(),
        P("shard", None),
        P(("shard", "blk"), None),
        P(("shard", "blk"), None),
        P(("shard", "blk"), None),
        P(("shard", "blk")),
        P(),
        P(),
    )
    out_specs = (P(("shard", "blk"), None), P(), P(("shard", "blk"), None))
    return jax.shard_map(body, mesh=mesh, in_specs=in_specs, out_specs=out_specs, check_vma=False)
```

profile of v0, /device:TPU:1, one launch (start us, length us, event | category | flops | bytes accessed | tf_op | source)
XLA Modules:
  0.0 535.2 jit_solution(4409312277664935398)
XLA Ops:
  7.2 0.8 broadcast_multiply_fusion
  8.0 0.8 copy.72
  8.9 0.7 iota_compare_fusion.4
  9.5 0.8 lt.127
  10.3 0.1 eq.55
  10.4 0.1 reshape.263
  10.5 0.2 copy.73
  10.7 0.1 lt.133
  10.9 0.1 lt.124
  11.0 0.1 copy.82
  11.1 0.1 mul.88
  11.3 0.1 lt.126
  11.6 9.0 %reduce-window.6 = s32[32,8,128]{2,1,0:T(8,128)S(1)} reduce-window(s32[32,8,128]{2,1,0:T(8,128)S(1)} %fusion.20, s32[]{:T(128)} %constant.23.clone.1), window={size=1x1x128 pad=0_0x0_0x127_0}, to_apply=%region_2.3 | reduce-window | flops 4161536 | bytes 262148 | tf_op jit(solution)/shard_map/reduce-window
  20.6 0.1 slice.20
  20.7 0.1 copy.77
  20.9 0.1 copy.78
  20.9 0.1 broadcast_add_fusion
  21.1 0.1 copy.83
  21.2 0.1 reshape.291
  21.4 4.3 scatter_custom_fusion
  25.8 0.1 all_to_all.16
  25.9 20.5 %all_to_all.25 = s32[32,1,64]{2,1,0:T(1,128)S(1)} all-to-all(s32[32,1,64]{2,1,0:T(1,128)S(1)} %all_to_all.16), channel_id=1, replica_groups=mesh['shard'=32,'blk'=8] {'shard'}, dimensions={0} | all-to-all | bytes 16384 | tf_op jit(solution)/shard_map/all_to_all | solution.py:50
  46.4 8.6 %gather_fusion = f32[2048,256]{1,0:T(8,128)} fusion(f32[2048,256]{1,0:T(8,128)S(1)} %copy-done, s32[2048]{0:T(1024)S(1)} %broadcast_clamp_fusion), kind=kCustom, calls=%fused_computation | custom fusion | bytes 4202496 | tf_op jit(solution)/shard_map/jit(_take)/gather | solution.py:51
  55.1 3.2 broadcast_select_fusion
  58.3 4.9 all-to-all-start.1
  63.3 0.1 reduce_sum.73
  63.5 0.1 copy.84
  63.7 0.8 copy.80
  64.4 1.2 fusion.1
  65.7 47.0 %all-to-all-done.1 = f32[32,64,256]{2,1,0:T(8,128)} async-done(((f32[32,64,256]{2,1,0:T(8,128)}), f32[32,64,256]{2,1,0:T(8,128)}, u32[]{:S(2)}, u32[]{:S(2)}) %all-to-all-start.1) | async-done | bytes 2097184 | tf_op jit(solution)/shard_map/all_to_all | solution.py:52
  112.6 6.3 %gather_fusion.1 = f32[1024,256]{1,0:T(8,128)} fusion(f32[2048,256]{1,0:T(8,128)} %bitcast.9, s32[1024]{0:T(1024)S(1)} %broadcast_clamp_fusion.1), kind=kCustom, calls=%fused_computation.1 | custom fusion | bytes 2101248 | tf_op jit(solution)/shard_map/jit(_take)/gather | solution.py:54
  118.9 2.5 gather.12
  121.4 2.5 multiply_reduce_fusion
  123.9 0.8 copy.85
  124.8 1.8 multiply_reduce_fusion.3
  126.6 0.7 fusion.28
  127.3 0.2 reduce-scatter.3.cloned.1.call-start
  127.6 1.0 copy.71
  129.9 0.6 iota_add_fusion
  130.5 0.6 add_sqrt_fusion.1
  131.1 21.1 %all-gather.2.cloned.1.call-done = bf16[2048,256]{0,1:T(8,128)(2,1)} async-done(((bf16[256,256]{0,1:T(8,128)(2,1)}), bf16[2048,256]{0,1:T(8,128)(2,1)}) %all-gather.2.cloned.1.call-update) | async-done | bytes 1048592 | tf_op jit(solution)/shard_map/all_gather | solution.py:69
  152.2 2.2 fusion.8
  154.4 1.0 copy-done.2
  155.4 1.8 fusion.25
  157.1 34.7 %reduce-scatter.3.cloned.1.call-done = f32[256,256]{0,1:T(8,128)} async-done(((f32[2048,256]{0,1:T(8,128)}), f32[256,256]{0,1:T(8,128)}) %reduce-scatter.3.cloned.1.call-update) | async-done | bytes 262160 | tf_op jit(solution)/shard_map/reduce_scatter | solution.py:92
  191.8 1.0 multiply_reduce_fusion.1
  192.8 1.7 divide_convert_fusion
  194.5 1.0 copy.87
  195.5 0.9 broadcast_in_dim.61
  196.4 2.0 reshape.299
  198.4 6.4 %scatter_custom_fusion.1 = bf16[2049,256]{1,0:T(8,128)(2,1)} fusion(s32[1024]{0:T(1024)} %bitcast.58, bf16[1024,256]{1,0:T(8,128)(2,1)} %reshape.299, bf16[]{:T(256)} %constant.21.clone.1), kind=kCustom, calls=%fused_computation.24 | custom fusion | bytes 1049600 | tf_op jit(solution)/shard_map/scatter | solution.py:106
  204.8 2.3 slice.23
  207.1 9.4 %all-to-all-start.2 = ((bf16[32,64,256]{2,1,0:T(8,128)(2,1)}), bf16[32,64,256]{2,1,0:T(8,128)(2,1)}, u32[]{:S(2)}, u32[]{:S(2)}) async-start(bf16[32,64,256]{2,1,0:T(8,128)(2,1)} %bitcast.48), calls=%async_computation.3 | async-start | bytes 2097152 | tf_op jit(solution)/shard_map/all_to_all | solution.py:108
  216.6 1.8 fusion.29
  218.5 0.5 broadcast.201
  219.0 0.7 reduce.4
  219.7 0.1 reshape.267
  219.8 18.3 %all-to-all-done.2 = bf16[32,64,256]{2,1,0:T(8,128)(2,1)} async-done(((bf16[32,64,256]{2,1,0:T(8,128)(2,1)}), bf16[32,64,256]{2,1,0:T(8,128)(2,1)}, u32[]{:S(2)}, u32[]{:S(2)}) %all-to-all-start.2) | async-done | bytes 1048608 | tf_op jit(solution)/shard_map/all_to_all | solution.py:108
  238.1 15.3 %scatter_custom_fusion.2 = f32[2048,256]{1,0:T(8,128)} fusion(s32[2048]{0:T(1024)S(1)} %bitcast.56, bf16[2048,256]{1,0:T(8,128)(2,1)} %bitcast.15, f32[]{:T(128)} %constant.19.clone.1), kind=kCustom, calls=%fused_computation.16 | custom fusion | flops 1048576 | bytes 3145732 | tf_op jit(solution)/shard_map/scatter-add | solution.py:112
  253.4 1.7 multiply_reduce_fusion.2
  255.2 0.8 copy.88
  256.0 232.3 %all-reduce.2.cloned.1.call-done = f32[2048,256]{1,0:T(8,128)} async-done(((f32[2048,256]{1,0:T(8,128)}), f32[2048,256]{1,0:T(8,128)}) %all-reduce.2.cloned.1.call-update) | async-done | bytes 2097168 | tf_op jit(solution)/shard_map/psum | solution.py:114
  488.3 37.3 %reduce-scatter.5.cloned.1.call-done = f32[256,256]{1,0:T(8,128)} async-done(((f32[2048,256]{1,0:T(8,128)}), f32[256,256]{1,0:T(8,128)}) %reduce-scatter.5.cloned.1.call-update) | async-done | bytes 262160 | tf_op jit(solution)/shard_map/reduce_scatter | solution.py:115
  525.6 3.0 copy.95
  (52 shorter events, 0.9 us)
Async XLA Ops:
  7.2 39.3 %copy-start = (f32[2048,256]{1,0:T(8,128)S(1)}, f32[2048,256]{1,0:T(8,128)}, u32[]{:S(2)}) copy-start(f32[2048,256]{1,0:T(8,128)} %param.11) | copy-start | bytes 6291460
  7.2 13.9 %copy-start.10 = (s32[256,4]{0,1:T(4,128)S(1)}, s32[256,4]{0,1:T(4,128)}, u32[]{:S(2)}) copy-start(s32[256,4]{0,1:T(4,128)} %param.14) | copy-start | bytes 12292
  21.4 33.6 %copy-start.11 = (s32[1024,1]{0,1:T(1,128)}, s32[1024,1]{0,1:T(1,128)S(1)}, u32[]{:S(2)}) copy-start(s32[1024,1]{0,1:T(1,128)S(1)} %get-tuple-element.22) | copy-start | bytes 12292
  58.3 5.2 copy-start.4
  58.3 5.2 copy-start.8
  58.3 6.1 %copy-start.9 = (s32[256,4]{0,1:T(4,128)S(1)}, s32[256,4]{0,1:T(4,128)}, u32[]{:S(2)}) copy-start(s32[256,4]{0,1:T(4,128)} %param.12) | copy-start | bytes 12292
  58.3 54.3 %all-to-all-start.1 = ((f32[32,64,256]{2,1,0:T(8,128)}), f32[32,64,256]{2,1,0:T(8,128)}, u32[]{:S(2)}, u32[]{:S(2)}) async-start(f32[32,64,256]{2,1,0:T(8,128)} %broadcast_select_fusion), calls=%async_computation.1 | async-start | bytes 4194304 | tf_op jit(solution)/shard_map/all_to_all | solution.py:52
  63.2 89.0 %all-gather.2.cloned.1.call-start = ((), (), s32[]{:S(2)}) async-start(), calls=%async_computation.5 | async-start | bytes 1179648 | tf_op jit(solution)/shard_map/all_gather | solution.py:69
  126.6 0.9 copy-start.5
  127.3 64.5 %reduce-scatter.3.cloned.1.call-start = ((), (), s32[]{:S(2)}) async-start(), calls=%async_computation.6 | async-start | bytes 2359296 | tf_op jit(solution)/shard_map/reduce_scatter | solution.py:92
  152.2 3.2 copy-start.6
  154.3 1.0 copy-start.2
  204.8 11.8 %copy-start.1 = (bf16[256,256]{0,1:T(8,128)(2,1)S(1)}, bf16[256,256]{0,1:T(8,128)(2,1)}, u32[]{:S(2)}) copy-start(bf16[256,256]{0,1:T(8,128)(2,1)} %divide_convert_fusion) | copy-start | bytes 393220
  207.1 31.0 %all-to-all-start.2 = ((bf16[32,64,256]{2,1,0:T(8,128)(2,1)}), bf16[32,64,256]{2,1,0:T(8,128)(2,1)}, u32[]{:S(2)}, u32[]{:S(2)}) async-start(bf16[32,64,256]{2,1,0:T(8,128)(2,1)} %bitcast.48), calls=%async_computation.3 | async-start | bytes 2097152 | tf_op jit(solution)/shard_map/all_to_all | solution.py:108
  216.6 271.7 %all-reduce.2.cloned.1.call-start = ((), (), s32[]{:S(2)}) async-start(), calls=%async_computation.7 | async-start | bytes 4194304 | tf_op jit(solution)/shard_map/psum | solution.py:114
  218.5 307.1 %reduce-scatter.5.cloned.1.call-start = ((), (), s32[]{:S(2)}) async-start(), calls=%async_computation.8 | async-start | bytes 2359296 | tf_op jit(solution)/shard_map/reduce_scatter | solution.py:115
  238.1 15.3 %copy-start.3 = (bf16[256,2048]{1,0:T(8,128)(2,1)S(1)}, bf16[256,2048]{1,0:T(8,128)(2,1)}, u32[]{:S(2)}) copy-start(bf16[256,2048]{1,0:T(8,128)(2,1)} %copy-done.2) | copy-start | bytes 3145732
  238.1 15.3 %copy-start.7 = (f32[256]{0:T(256)S(1)}, f32[256]{0:T(256)}, u32[]{:S(2)}) copy-start(f32[256]{0:T(256)} %add_sqrt_fusion.1) | copy-start | bytes 3076
Sparse Core Ops, SparseCore 0:
  127.4 24.6 all-gather.1
  157.3 34.5 reduce-scatter.2
  223.3 264.9 all-reduce.1
  491.3 34.2 reduce-scatter.4
where the time goes:
time: 538 us; the launch traced here: 535 us
  waiting for transfers between devices  391 us (73%)
  local copies, waits for them, and re-layouts  46.3 us (9%)
  other arithmetic  38.4 us (7%)
  blocking collectives  20.5 us (4%)
  between operations  15.4 us (3%)
  starting transfers between devices  14.7 us (3%)
  matrix products  9.25 us (2%)
    psum x1, waiting for transfers between devices, body(): hot_grad = lax.psum(hot_local, ('shard', 'blk'))  232 us
    all_to_all x1, waiting for transfers between devices, body(): lax.all_to_all(looked, 'shard', split_axis=0, concat_axis=0, tiled=True)  47 us
    reduce_scatter x1, waiting for transfers between devices, body(): lax.psum_scatter(cold_local, 'blk', scatter_dimension=0, tiled=True)  37.3 us
    reduce_scatter x1, waiting for transfers between devices, body(): lax.psum_scatter(item_acc, 'blk', scatter_dimension=0, tiled=True)  34.7 us
    all_gather x1, waiting for transfers between devices, body(): block_rows = lax.all_gather(candidate_reduced, 'blk', axis=0, tiled=True)  21.1 us
    all_to_all x1, blocking collectives, body(): lax.all_to_all(requests, 'shard', split_axis=0, concat_axis=0, tiled=True)  20.5 us
    all_to_all x1, waiting for transfers between devices, body(): lax.all_to_all(outgoing, 'shard', split_axis=0, concat_axis=0, tiled=True)  18.3 us
    scatter-add x1, other arithmetic, body(): cold_local = jnp.zeros((rare_entry_matrix.shape[0], row_width), jnp.float...  15.3 us
  transfers between devices with their start and end apart: 6, of which 6 were waited for; matrix products, arithmetic and copies ran while one was open for 5% of the time, Pallas kernels for 0%

commit v1 on v0

v1 whole, which is shorter than its diff:
```python
import jax
import jax.numpy as jnp
from jax import lax
from jax.experimental import pallas as pl
from jax.experimental.pallas import tpu as pltpu
from jax.sharding import PartitionSpec as P

epsilon = 1e-06
F32 = jnp.float32
BF16 = jnp.bfloat16
NN = (((1,), (0,)), ((), ()))
NT = (((1,), (1,)), ((), ()))


def mm(a, b, dims=NN):
    return lax.dot_general(a, b, dims, preferred_element_type=F32)


def iota(shape, dim):
    return lax.broadcasted_iota(jnp.int32, shape, dim)


def call(kernel, outs, *args, smem=0, scratch=(), flops=0, grid=None, in_specs=None, out_specs=None):
    moved = sum(a.size * a.dtype.itemsize for a in args) + sum(o.size * o.dtype.itemsize for o in outs)
    extra = {}
    if grid is not None:
        extra = dict(grid=grid, in_specs=in_specs, out_specs=out_specs)
    else:
        spaces = [pltpu.SMEM] * smem + [pltpu.VMEM] * (len(args) - smem)
        extra = dict(
            in_specs=[pl.BlockSpec(memory_space=s) for s in spaces],
            out_specs=[pl.BlockSpec(memory_space=pltpu.VMEM) for _ in outs],
        )
    return pl.pallas_call(
        kernel,
        out_shape=list(outs),
        scratch_shapes=list(scratch),
        cost_estimate=pl.CostEstimate(flops=flops, bytes_accessed=moved, transcendentals=0),
        **extra,
    )(*args)


def shape(dims, dtype):
    return jax.ShapeDtypeStruct(dims, dtype)


def expander(owners, cap, base, width):
    return ((iota((owners, width), 1) + base) // cap == iota((owners, width), 0)).astype(F32).astype(BF16)


def make_requests(owners, cap):
    def kernel(parent_ref, place_ref, tally_ref, rank_ref, ask_ref, row_ref):
        pairs, slots = parent_ref.shape
        lane = iota((pairs, owners), 1)
        tally = tally_ref[...]
        named = jnp.zeros((pairs, owners), F32)
        high = jnp.zeros((pairs, owners), F32)
        low = jnp.zeros((pairs, owners), F32)
        for c in range(slots):
            hit = jnp.logical_and(parent_ref[:, c : c + 1] == lane, tally > c)
            place = place_ref[:, c : c + 1]
            named = jnp.where(hit, 1.0, named)
            high = jnp.where(hit, (place // 64).astype(F32), high)
            low = jnp.where(hit, (place % 64).astype(F32), low)
        before = (iota((pairs, pairs), 0) > iota((pairs, pairs), 1)).astype(F32).astype(BF16)
        rank = jnp.where(named > 0, mm(before, named.astype(BF16)), -1.0)
        rank_ref[...] = rank
        rank, high, low = rank.astype(BF16), high.astype(BF16), low.astype(BF16)
        total = owners * cap
        width = 512
        for base in range(0, total, width):
            spread = expander(owners, cap, base, width)
            want = (iota((pairs, width), 1) % cap).astype(F32)
            place = mm(high, spread) * 64.0 + mm(low, spread)
            row_ref[:, base : base + width] = jnp.sum(
                jnp.where(mm(rank, spread) == want, place, 0.0), axis=0, keepdims=True
            )
        for o in range(owners):
            ask_ref[o : o + 1, :] = row_ref[:, o * cap : (o + 1) * cap].astype(jnp.int32)

    return kernel


def prepare(owners, cap):
    def kernel(rank_ref, rank_t_ref, lines_ref, hot_ref, query_ref,
               pick_ref, place_ref, hot_sum_ref, unit_ref, radius_ref, low_ref):
        pairs = rank_ref.shape[0]
        total = owners * cap
        width = 256
        rank = rank_ref[...].astype(BF16)
        rank_t = rank_t_ref[...].astype(BF16)
        hot_sum_ref[...] = jnp.zeros_like(hot_sum_ref)

        def step(i, _):
            base = pl.multiple_of(i * width, width)
            spread = expander(owners, cap, base, width)
            want = (iota((pairs, width), 1) % cap).astype(F32)
            pick_ref[:, pl.ds(base, width)] = (mm(rank, spread) == want).astype(F32).astype(BF16)
            spread_t = ((iota((width, owners), 0) + base) // cap == iota((width, owners), 1))
            want_t = (iota((width, pairs), 0) % cap).astype(F32)
            hit = mm(spread_t.astype(F32).astype(BF16), rank_t) == want_t
            place_ref[pl.ds(base, width), :] = hit.astype(F32).astype(BF16)
            column = iota((pairs, width), 1) + base
            counts = jnp.zeros((pairs, width), F32)
            for h in range(lines_ref.shape[1]):
                counts += (lines_ref[:, h : h + 1] == column).astype(F32)
            hot_sum_ref[...] += mm(counts.astype(BF16), hot_ref[pl.ds(base, width), :])
            return 0

        lax.fori_loop(0, total // width, step, 0)
        query = query_ref[...].astype(F32)
        radius = jnp.sqrt(jnp.sum(query * query, axis=1, keepdims=True) + epsilon)
        unit = query / radius
        unit_ref[...] = unit
        radius_ref[...] = radius
        low_ref[...] = unit.astype(BF16)

    return kernel


def fetch(ask_ref, table_ref, out_ref, low_ref):
    rows = table_ref.shape[0]
    width = ask_ref.shape[1]

    @pl.when(pl.program_id(0) == 0)
    def _():
        low_ref[...] = table_ref[...].astype(BF16)

    ask = ask_ref[pl.ds(pl.program_id(0), 1), :]
    diagonal = iota((width, width), 0) == iota((width, width), 1)
    column = jnp.sum(jnp.where(diagonal, ask, 0).astype(F32), axis=1, keepdims=True).astype(jnp.int32)
    hit = (column == iota((width, rows), 1)).astype(F32).astype(BF16)
    out_ref[...] = mm(hit, low_ref[...]).astype(BF16)


def loss_side(own_low, others_ref, total_ref, own_block, sharpness, additive):
    rows = own_low.shape[0]
    width = 256
    total_ref[...] = jnp.zeros_like(total_ref)

    def step(i, _):
        base = pl.multiple_of(i * width, width)
        other = others_ref[pl.ds(base, width), :]
        logits = sharpness * mm(own_low, other, NT) + additive
        same = iota((rows, width), 0) + own_block * rows == iota((rows, width), 1) + base
        grad = (jax.nn.sigmoid(logits) - same.astype(F32)).astype(BF16)
        total_ref[...] += mm(grad, other)
        return 0

    lax.fori_loop(0, others_ref.shape[0] // width, step, 0)
    return sharpness * total_ref[...]


def project(unit, radius, direction):
    inner = jnp.sum(unit * direction, axis=1, keepdims=True)
    return (direction - unit * inner) / radius


def item_side(block_ref, sharp_ref, add_ref, fetched_ref, pick_ref, place_ref, hot_sum_ref, queries_ref,
              low_ref, grad_ref, out_ref, total_ref):
    item = hot_sum_ref[...] + mm(pick_ref[...], fetched_ref[...])
    radius = jnp.sqrt(jnp.sum(item * item, axis=1, keepdims=True) + epsilon)
    unit = item / radius
    low = unit.astype(BF16)
    low_ref[...] = low
    direction = loss_side(low, queries_ref, total_ref, block_ref[0], sharp_ref[0], add_ref[0])
    grad = project(unit, radius, direction).astype(BF16)
    grad_ref[...] = grad
    width = 256

    def step(i, _):
        base = pl.multiple_of(i * width, width)
        out_ref[pl.ds(base, width), :] = mm(place_ref[pl.ds(base, width), :], grad).astype(BF16)
        return 0

    lax.fori_loop(0, out_ref.shape[0] // width, step, 0)


def query_side(block_ref, sharp_ref, add_ref, unit_ref, radius_ref, items_ref, out_ref, total_ref):
    unit = unit_ref[...]
    direction = loss_side(unit.astype(BF16), items_ref, total_ref, block_ref[0], sharp_ref[0], add_ref[0])
    out_ref[...] = project(unit, radius_ref[...], direction)


def hot_terms(lines_t_ref, grad_ref, out_ref):
    width, pairs = out_ref.shape[0], grad_ref.shape[0]
    row = iota((width, pairs), 0) + pl.program_id(0) * width
    counts = jnp.zeros((width, pairs), F32)
    for h in range(lines_t_ref.shape[0]):
        counts += (lines_t_ref[h : h + 1, :] == row).astype(F32)
    out_ref[...] = mm(counts.astype(BF16), grad_ref[...]).astype(BF16)


def cold_terms(ask_ref, grad_ref, out_ref):
    width, total = out_ref.shape[0], grad_ref.shape[0]
    row = iota((width, total), 0) + pl.program_id(0) * width
    hit = (ask_ref[...] == row).astype(F32).astype(BF16)
    out_ref[...] = mm(hit, grad_ref[...]).astype(BF16)


def whole(array):
    return pl.BlockSpec(array.shape, lambda i: (0,) * array.ndim)


def swap(array, axis):
    return lax.all_to_all(array, axis, split_axis=0, concat_axis=0, tiled=True)


def spread(array, axis):
    return swap(jnp.broadcast_to(array[None], (lax.axis_size(axis),) + array.shape), axis)


def body(queries, hot_table, cold_table, lines, parent, place, tally, sharpness, additive):
    pairs, width = queries.shape
    owners, blocks = lax.axis_size("shard"), lax.axis_size("blk")
    slots = parent.shape[1]
    cap = 2 * pairs * slots // owners
    total = owners * cap
    rows = cold_table.shape[0]
    hot_rows = hot_table.shape[0]
    block = lax.axis_index("blk").astype(jnp.int32).reshape(1)
    step = 256

    rank, ask = call(
        make_requests(owners, cap),
        [shape((pairs, owners), F32), shape((owners, cap), jnp.int32)],
        parent, place, tally.reshape(pairs, 1),
        scratch=[pltpu.VMEM((1, total), F32)],
        flops=2 * pairs * total * owners * 3,
    )
    asked = swap(ask.reshape(owners, 1, cap), "shard").reshape(total // step, step)

    pick, placed, hot_sum, unit, radius, query_low = call(
        prepare(owners, cap),
        [
            shape((pairs, total), BF16),
            shape((total, pairs), BF16),
            shape((pairs, width), F32),
            shape((pairs, width), F32),
            shape((pairs, 1), F32),
            shape((pairs, width), BF16),
        ],
        rank, rank.T, lines, hot_table, queries,
        flops=2 * pairs * total * (width + 2 * owners),
    )
    all_queries = spread(query_low, "blk").reshape(blocks * pairs, width)

    (looked,) = call(
        fetch,
        [shape((total, width), BF16)],
        asked, cold_table,
        grid=(total // step,),
        in_specs=[whole(asked), whole(cold_table)],
        out_specs=[pl.BlockSpec((step, width), lambda i: (i, 0))],
        scratch=[pltpu.VMEM((rows, width), BF16)],
        flops=2 * total * rows * width,
    )
    fetched = swap(looked.reshape(owners, cap, width), "shard").reshape(total, width)

    item_low, item_grad, outgoing = call(
        item_side,
        [shape((pairs, width), BF16), shape((pairs, width), BF16), shape((total, width), BF16)],
        block, sharpness, additive, fetched, pick, placed, hot_sum, all_queries,
        smem=3,
        scratch=[pltpu.VMEM((pairs, width), F32)],
        flops=2 * pairs * width * (2 * total + 2 * blocks * pairs),
    )
    incoming = swap(outgoing.reshape(owners, cap, width), "shard").reshape(total, width)

    (hot_local,) = call(
        hot_terms,
        [shape((hot_rows, width), BF16)],
        lines.T, item_grad,
        grid=(hot_rows // step,),
        in_specs=[pl.BlockSpec((slots, pairs), lambda i: (0, 0)), whole(item_grad)],
        out_specs=[pl.BlockSpec((step, width), lambda i: (i, 0))],
        flops=2 * pairs * hot_rows * width,
    )
    hot_parts = swap(hot_local.reshape(blocks, hot_rows // blocks, width), "blk")
    hot_block = jnp.sum(hot_parts.astype(F32), axis=0).astype(BF16)
    hot_parts = swap(hot_block.reshape(owners, hot_rows // blocks // owners, width), "shard")
    hot_piece = jnp.sum(hot_parts.astype(F32), axis=0).astype(BF16)
    hot_block = spread(hot_piece, "shard").reshape(hot_rows // blocks, width)
    hot_grad = spread(hot_block, "blk").reshape(hot_rows, width).astype(F32)

    all_items = spread(item_low, "blk").reshape(blocks * pairs, width)
    (query_grad,) = call(
        query_side,
        [shape((pairs, width), F32)],
        block, sharpness, additive, unit, radius, all_items,
        smem=3,
        scratch=[pltpu.VMEM((pairs, width), F32)],
        flops=4 * pairs * width * blocks * pairs,
    )

    (cold_local,) = call(
        cold_terms,
        [shape((rows, width), BF16)],
        asked.reshape(1, total), incoming,
        grid=(rows // step,),
        in_specs=[pl.BlockSpec((1, total), lambda i: (0, 0)), whole(incoming)],
        out_specs=[pl.BlockSpec((step, width), lambda i: (i, 0))],
        flops=2 * total * rows * width,
    )
    cold_parts = swap(cold_local.reshape(blocks, rows // blocks, width), "blk")
    cold_grad = jnp.sum(cold_parts.astype(F32), axis=0)
    return (query_grad, hot_grad, cold_grad)


def solution(mesh):
    pair = P(("shard", "blk"), None)
    in_specs = (pair, P(), P("shard", None), pair, pair, pair, P(("shard", "blk")), P(), P())
    return jax.shard_map(body, mesh=mesh, in_specs=in_specs, out_specs=(pair, P(), pair), check_vma=False)
```

time: 538 us -> 246 us (0.46)
  waiting for transfers between devices: 391 us -> 61.5 us
  blocking collectives: 20.5 us -> 77 us
  Pallas kernels: 0 us -> 40.9 us
  other arithmetic: 38.4 us -> 3.26 us
  local copies, waits for them, and re-layouts: 46.3 us -> 14.5 us
  starting transfers between devices: 14.7 us -> 45.9 us
  between operations: 15.4 us -> 1.99 us
  matrix products: 9.25 us -> 0 us
    psum x1 -> x0, waiting for transfers between devices: 232 us -> none  [body(): hot_grad = lax.psum(hot_local, ('shard', 'blk'))]
    reduce_scatter x2 -> x0, waiting for transfers between devices: 72 us -> none  [the longest x1 37.3 us: body(): lax.psum_scatter(cold_local, 'blk', scatter_dimension=0, tiled=True)]
    all_to_all x1 -> x4, blocking collectives: 20.5 us -> 77 us  [swap(): return lax.all_to_all(array, axis, split_axis=0, concat_axis=0, tiled=True)]
    pallas_call x0 -> x7, Pallas kernels: none -> 40.9 us  [call(): pl.pallas_call(kernel, out_shape=list(outs), scratch_shapes=list(scratch)...]
    all_to_all x2 -> x6, starting transfers between devices: 14.3 us -> 45.9 us  [swap(): return lax.all_to_all(array, axis, split_axis=0, concat_axis=0, tiled=True)]
    all_gather x1 -> x0, waiting for transfers between devices: 21.1 us -> none  [body(): block_rows = lax.all_gather(candidate_reduced, 'blk', axis=0, tiled=True)]
    gather x3 -> x0, local copies, waits for them, and re-layouts: 17.4 us -> none  [the longest x2 8.78 us: body(): jnp.take(fetched_flat, jnp.minimum(bucket, dump_slot - 1), axis=0)]
    scatter-add x1 -> x0, other arithmetic: 15.3 us -> none  [body(): cold_local = jnp.zeros((rare_entry_matrix.shape[0], row_width), jnp.float...]
  transfers between devices with their start and end apart: 6 -> 6, of which waited for: 6 -> 5; matrix products, arithmetic and copies ran while one was open for 5% -> 3% of each run, Pallas kernels for 0% -> 10%
where the time goes in v1:
time: 246 us; the launch traced here: 245 us
  blocking collectives  77 us (31%)
  waiting for transfers between devices  61.5 us (25%)
  starting transfers between devices  45.9 us (19%)
  Pallas kernels  40.9 us (17%)
  local copies, waits for them, and re-layouts  14.5 us (6%)
  other arithmetic  3.26 us (1%)
    all_to_all x4, blocking collectives, swap(): return lax.all_to_all(array, axis, split_axis=0, concat_axis=0, tiled=True)  77 us
    all_to_all x6, waiting for transfers between devices, swap(): return lax.all_to_all(array, axis, split_axis=0, concat_axis=0, tiled=True)  61.5 us
    all_to_all x6, starting transfers between devices, swap(): return lax.all_to_all(array, axis, split_axis=0, concat_axis=0, tiled=True)  45.9 us
    pallas_call x7, Pallas kernels, call(): pl.pallas_call(kernel, out_shape=list(outs), scratch_shapes=list(scratch)...  40.9 us
    unnamed x13, local copies, waits for them, and re-layouts  5.44 us
  transfers between devices with their start and end apart: 6, of which 5 were waited for; matrix products, arithmetic and copies ran while one was open for 3% of the time, Pallas kernels for 10%

profile of v1, /device:TPU:1, one launch (start us, length us, event | category | flops | bytes accessed | tf_op | source)
XLA Modules:
  0.0 245.1 jit_solution(7052434179210992858)
XLA Ops:
  0.6 1.5 copy.27.parent_ref
  2.1 1.5 copy.28.place_ref
  3.6 1.5 copy.29.tally_ref
  5.1 3.2 %shard_map.112 = (f32[256,32]{1,0:T(8,128)}, s32[32,64]{1,0:T(8,128)}) custom-call(s32[256,4]{1,0:T(8,128)} %copy.27.parent_ref, s32[256,4]{1,0:T(8,128)} %copy.28.place_ref, s32[256,1]{1,0:T(8,128)} %copy.29.tally_ref), custom_call_target="tpu_custom_call" | custom-call | flops 100663296 | bytes 50176 | tf_op jit(solution)/shard_map/pallas_call | solution.py:34
  8.3 12.0 %all-to-all-start = ((s32[32,1,64]{2,1,0:T(1,128)}), s32[32,1,64]{2,1,0:T(1,128)S(1)}, u32[]{:S(2)}, u32[]{:S(2)}) async-start(s32[32,1,64]{2,1,0:T(1,128)} %bitcast.34), calls=%async_computation | async-start | bytes 32768 | tf_op jit(solution)/shard_map/all_to_all | solution.py:206
  20.3 1.6 copy.30
  21.9 1.5 copy.31.lines_ref
  23.4 6.3 %shard_map.113 = (bf16[256,2048]{1,0:T(8,128)(2,1)}, bf16[2048,256]{1,0:T(8,128)(2,1)}, f32[256,256]{1,0:T(8,128)}, f32[256,256]{1,0:T(8,128)}, f32[256,1]{1,0:T(8,128)}, /*index=5*/bf16[256,256]{1,0:T(8,128)(2,1)}) custom-call(f32[256,32]{1,0:T(8,128)} %get-tuple-element.14.rank_ref, f32[32,256]{1,0:T(8,128)} %bitcast.32, s32[256,4]{1,0:T(8,128)} %copy.31.lines_ref, ...), custom_call_target="tpu_custom_call" | custom-call | flops 335544320 | bytes 4002816 | tf_op jit(solution)/shard_map/pallas_call | solution.py:34
  29.7 0.0 all-to-all-done
  29.7 2.0 broadcast_in_dim.10
  31.7 5.7 %all-to-all-start.2 = ((bf16[8,256,256]{2,1,0:T(8,128)(2,1)}), bf16[8,256,256]{2,1,0:T(8,128)(2,1)S(1)}, u32[]{:S(2)}, u32[]{:S(2)}) async-start(bf16[8,256,256]{2,1,0:T(8,128)(2,1)} %broadcast_in_dim.10), calls=%async_computation.2 | async-start | bytes 2097152 | tf_op jit(solution)/shard_map/all_to_all | solution.py:206
  37.4 0.5 broadcast.8
  37.9 0.7 reduce.7
  38.6 0.7 reshape.55.ask_ref
  39.3 6.8 %shard_map.114 = bf16[2048,256]{1,0:T(8,128)(2,1)} custom-call(s32[8,256]{1,0:T(8,128)} %reshape.55.ask_ref, f32[2048,256]{1,0:T(8,128)} %table_ref.1), custom_call_target="tpu_custom_call" | custom-call | flops 2147483648 | bytes 3153920 | tf_op jit(solution)/shard_map/pallas_call | solution.py:34
  46.0 6.3 %all-to-all-done.2 = bf16[8,256,256]{2,1,0:T(8,128)(2,1)S(1)} async-done(((bf16[8,256,256]{2,1,0:T(8,128)(2,1)}), bf16[8,256,256]{2,1,0:T(8,128)(2,1)S(1)}, u32[]{:S(2)}, u32[]{:S(2)}) %all-to-all-start.2) | async-done | bytes 1048608 | tf_op jit(solution)/shard_map/all_to_all | solution.py:206
  52.3 0.0 copy-start
  52.3 9.1 %all-to-all-start.1 = ((bf16[32,64,256]{2,1,0:T(8,128)(2,1)}), bf16[32,64,256]{2,1,0:T(8,128)(2,1)S(1)}, u32[]{:S(2)}, u32[]{:S(2)}) async-start(bf16[32,64,256]{2,1,0:T(8,128)(2,1)} %bitcast.27), calls=%async_computation.1 | async-start | bytes 2097152 | tf_op jit(solution)/shard_map/all_to_all | solution.py:206
  62.7 23.8 %all-to-all-done.1 = bf16[32,64,256]{2,1,0:T(8,128)(2,1)S(1)} async-done(((bf16[32,64,256]{2,1,0:T(8,128)(2,1)}), bf16[32,64,256]{2,1,0:T(8,128)(2,1)S(1)}, u32[]{:S(2)}, u32[]{:S(2)}) %all-to-all-start.1) | async-done | bytes 1048608 | tf_op jit(solution)/shard_map/all_to_all | solution.py:206
  86.5 0.0 copy-start.1
  86.5 0.0 copy-done
  86.5 1.0 copy-done.1
  87.5 8.4 %shard_map.115 = (bf16[256,256]{1,0:T(8,128)(2,1)}, bf16[256,256]{1,0:T(8,128)(2,1)}, bf16[2048,256]{1,0:T(8,128)(2,1)}) custom-call(s32[1]{0:T(128)} %bitcast.block_ref, f32[1]{0:T(128)S(6)} %copy.33.sharp_ref, f32[1]{0:T(128)S(6)} %copy.34.add_ref, bf16[2048,256]{1,0:T(8,128)(2,1)} %bitcast.23, bf16[256,2048]{1,0:T(8,128)(2,1)} %get-tuple-element.18.pick_ref, ...), custom_call_target="tpu_custom_call" | custom-call | flops 1073741824 | bytes 5767180 | tf_op jit(solution)/shard_map/pallas_call | solution.py:34
  95.9 0.0 copy-start.4
  95.9 4.8 %shard_map.117 = bf16[2048,256]{1,0:T(8,128)(2,1)} custom-call(s32[4,256]{1,0:T(4,128)} %bitcast.33, bf16[256,256]{1,0:T(8,128)(2,1)} %get-tuple-element.23.grad_ref), custom_call_target="tpu_custom_call" | custom-call | flops 268435456 | bytes 1183744 | tf_op jit(solution)/shard_map/pallas_call | solution.py:34
  100.7 23.0 %all_to_all.50 = bf16[8,256,256]{2,1,0:T(8,128)(2,1)S(1)} all-to-all(bf16[8,256,256]{2,1,0:T(8,128)(2,1)} %bitcast.21), channel_id=1, replica_groups=mesh['shard'=32,'blk'=8] {'blk'}, dimensions={0} | all-to-all | bytes 2097152 | tf_op jit(solution)/shard_map/all_to_all | solution.py:206
  123.7 0.1 reduce_sum.33
  123.9 0.0 copy-start.3
  123.9 13.7 %all_to_all.51 = bf16[32,8,256]{2,1,0:T(8,128)(2,1)S(1)} all-to-all(bf16[32,8,256]{2,1,0:T(8,128)(2,1)S(1)} %bitcast.30), channel_id=1, replica_groups=mesh['shard'=32,'blk'=8] {'shard'}, dimensions={0} | all-to-all | bytes 262144 | tf_op jit(solution)/shard_map/all_to_all | solution.py:206
  137.6 0.0 copy-done.4
  137.7 1.0 broadcast_in_dim.11
  138.7 6.0 %all-to-all-start.3 = ((bf16[8,256,256]{2,1,0:T(8,128)(2,1)}), bf16[8,256,256]{2,1,0:T(8,128)(2,1)S(1)}, u32[]{:S(2)}, u32[]{:S(2)}) async-start(bf16[8,256,256]{2,1,0:T(8,128)(2,1)} %broadcast_in_dim.11), calls=%async_computation.3 | async-start | bytes 2097152 | tf_op jit(solution)/shard_map/all_to_all | solution.py:206
  144.7 15.0 %all-to-all-done.3 = bf16[8,256,256]{2,1,0:T(8,128)(2,1)S(1)} async-done(((bf16[8,256,256]{2,1,0:T(8,128)(2,1)}), bf16[8,256,256]{2,1,0:T(8,128)(2,1)S(1)}, u32[]{:S(2)}, u32[]{:S(2)}) %all-to-all-start.3) | async-done | bytes 1048608 | tf_op jit(solution)/shard_map/all_to_all | solution.py:206
  159.7 0.0 copy-start.2
  159.7 12.4 %all_to_all.52 = bf16[32,8,256]{2,1,0:T(8,128)(2,1)S(1)} all-to-all(bf16[32,8,256]{2,1,0:T(8,128)(2,1)S(1)} %broadcast_in_dim.12), channel_id=1, replica_groups=mesh['shard'=32,'blk'=8] {'shard'}, dimensions={0} | all-to-all | bytes 262144 | tf_op jit(solution)/shard_map/all_to_all | solution.py:206
  172.1 0.0 copy-done.3
  172.1 27.9 %all_to_all.53 = bf16[32,64,256]{2,1,0:T(8,128)(2,1)} all-to-all(bf16[32,64,256]{2,1,0:T(8,128)(2,1)S(1)} %bitcast.25), channel_id=1, replica_groups=mesh['shard'=32,'blk'=8] {'shard'}, dimensions={0} | all-to-all | bytes 2097152 | tf_op jit(solution)/shard_map/all_to_all | solution.py:206
  200.0 1.1 broadcast_in_dim.14
  201.1 0.0 copy-done.2
  201.1 8.7 %all-to-all-start.7 = ((bf16[8,256,256]{2,1,0:T(8,128)(2,1)}), bf16[8,256,256]{2,1,0:T(8,128)(2,1)S(1)}, u32[]{:S(2)}, u32[]{:S(2)}) async-start(bf16[8,256,256]{2,1,0:T(8,128)(2,1)} %broadcast_in_dim.14), calls=%async_computation.7 | async-start | bytes 2097152 | tf_op jit(solution)/shard_map/all_to_all | solution.py:206
  209.8 0.7 reshape_reshape.3.ask_ref
  210.5 6.1 %shard_map.118 = bf16[2048,256]{1,0:T(8,128)(2,1)} custom-call(s32[1,2048]{1,0:T(1,128)} %reshape_reshape.3.ask_ref, bf16[2048,256]{1,0:T(8,128)(2,1)} %bitcast.28), custom_call_target="tpu_custom_call" | custom-call | flops 2147483648 | bytes 2105344 | tf_op jit(solution)/shard_map/pallas_call | solution.py:34
  216.6 8.2 %all-to-all-done.7 = bf16[8,256,256]{2,1,0:T(8,128)(2,1)S(1)} async-done(((bf16[8,256,256]{2,1,0:T(8,128)(2,1)}), bf16[8,256,256]{2,1,0:T(8,128)(2,1)S(1)}, u32[]{:S(2)}, u32[]{:S(2)}) %all-to-all-start.7) | async-done | bytes 1048608 | tf_op jit(solution)/shard_map/all_to_all | solution.py:206
  224.8 4.4 %all-to-all-start.9 = ((bf16[8,256,256]{2,1,0:T(8,128)(2,1)}), bf16[8,256,256]{2,1,0:T(8,128)(2,1)S(1)}, u32[]{:S(2)}, u32[]{:S(2)}) async-start(bf16[8,256,256]{2,1,0:T(8,128)(2,1)} %bitcast.26), calls=%async_computation.9 | async-start | bytes 2097152 | tf_op jit(solution)/shard_map/all_to_all | solution.py:206
  229.2 5.3 %shard_map.116 = f32[256,256]{1,0:T(8,128)} custom-call(s32[1]{0:T(128)} %bitcast.block_ref, f32[1]{0:T(128)S(6)} %copy.33.sharp_ref, f32[1]{0:T(128)S(6)} %copy.34.add_ref, f32[256,256]{1,0:T(8,128)} %get-tuple-element.15.unit_ref, f32[256,1]{1,0:T(8,128)} %get-tuple-element.16.radius_ref, bf16[2048,256]{1,0:T(8,128)(2,1)} %bitcast.24), custom_call_target="tpu_custom_call" | custom-call | flops 536870912 | bytes 1573900 | tf_op jit(solution)/shard_map/pallas_call | solution.py:34
  234.5 1.5 bitcast_convert_fusion
  236.1 8.1 %all-to-all-done.9 = bf16[8,256,256]{2,1,0:T(8,128)(2,1)S(1)} async-done(((bf16[8,256,256]{2,1,0:T(8,128)(2,1)}), bf16[8,256,256]{2,1,0:T(8,128)(2,1)S(1)}, u32[]{:S(2)}, u32[]{:S(2)}) %all-to-all-start.9) | async-done | bytes 1048608 | tf_op jit(solution)/shard_map/all_to_all | solution.py:206
  244.2 0.8 convert_reduce_fusion
  (2 shorter events, 0.0 us)
Async XLA Ops:
  8.3 21.4 %all-to-all-start = ((s32[32,1,64]{2,1,0:T(1,128)}), s32[32,1,64]{2,1,0:T(1,128)S(1)}, u32[]{:S(2)}, u32[]{:S(2)}) async-start(s32[32,1,64]{2,1,0:T(1,128)} %bitcast.34), calls=%async_computation | async-start | bytes 32768 | tf_op jit(solution)/shard_map/all_to_all | solution.py:206
  31.7 20.6 %all-to-all-start.2 = ((bf16[8,256,256]{2,1,0:T(8,128)(2,1)}), bf16[8,256,256]{2,1,0:T(8,128)(2,1)S(1)}, u32[]{:S(2)}, u32[]{:S(2)}) async-start(bf16[8,256,256]{2,1,0:T(8,128)(2,1)} %broadcast_in_dim.10), calls=%async_computation.2 | async-start | bytes 2097152 | tf_op jit(solution)/shard_map/all_to_all | solution.py:206
  52.3 34.2 %copy-start = (bf16[8,256,256]{2,1,0:T(8,128)(2,1)}, bf16[8,256,256]{2,1,0:T(8,128)(2,1)S(1)}, u32[]{:S(2)}) copy-start(bf16[8,256,256]{2,1,0:T(8,128)(2,1)S(1)} %all-to-all-done.2) | copy-start | bytes 3145732
  52.3 34.2 %all-to-all-start.1 = ((bf16[32,64,256]{2,1,0:T(8,128)(2,1)}), bf16[32,64,256]{2,1,0:T(8,128)(2,1)S(1)}, u32[]{:S(2)}, u32[]{:S(2)}) async-start(bf16[32,64,256]{2,1,0:T(8,128)(2,1)} %bitcast.27), calls=%async_computation.1 | async-start | bytes 2097152 | tf_op jit(solution)/shard_map/all_to_all | solution.py:206
  86.5 1.0 copy-start.1
  95.9 41.7 %copy-start.4 = (bf16[256,256]{1,0:T(8,128)(2,1)S(1)}, bf16[256,256]{1,0:T(8,128)(2,1)}, u32[]{:S(2)}) copy-start(bf16[256,256]{1,0:T(8,128)(2,1)} %get-tuple-element.22) | copy-start | bytes 393220
  123.9 48.2 %copy-start.3 = (bf16[2048,256]{1,0:T(8,128)(2,1)S(1)}, bf16[2048,256]{1,0:T(8,128)(2,1)}, u32[]{:S(2)}) copy-start(bf16[2048,256]{1,0:T(8,128)(2,1)} %get-tuple-element.24) | copy-start | bytes 3145732
  138.7 21.0 %all-to-all-start.3 = ((bf16[8,256,256]{2,1,0:T(8,128)(2,1)}), bf16[8,256,256]{2,1,0:T(8,128)(2,1)S(1)}, u32[]{:S(2)}, u32[]{:S(2)}) async-start(bf16[8,256,256]{2,1,0:T(8,128)(2,1)} %broadcast_in_dim.11), calls=%async_computation.3 | async-start | bytes 2097152 | tf_op jit(solution)/shard_map/all_to_all | solution.py:206
  159.7 41.4 %copy-start.2 = (bf16[8,256,256]{2,1,0:T(8,128)(2,1)}, bf16[8,256,256]{2,1,0:T(8,128)(2,1)S(1)}, u32[]{:S(2)}) copy-start(bf16[8,256,256]{2,1,0:T(8,128)(2,1)S(1)} %all-to-all-done.3) | copy-start | bytes 3145732
  201.1 23.7 %all-to-all-start.7 = ((bf16[8,256,256]{2,1,0:T(8,128)(2,1)}), bf16[8,256,256]{2,1,0:T(8,128)(2,1)S(1)}, u32[]{:S(2)}, u32[]{:S(2)}) async-start(bf16[8,256,256]{2,1,0:T(8,128)(2,1)} %broadcast_in_dim.14), calls=%async_computation.7 | async-start | bytes 2097152 | tf_op jit(solution)/shard_map/all_to_all | solution.py:206
  224.8 19.4 %all-to-all-start.9 = ((bf16[8,256,256]{2,1,0:T(8,128)(2,1)}), bf16[8,256,256]{2,1,0:T(8,128)(2,1)S(1)}, u32[]{:S(2)}, u32[]{:S(2)}) async-start(bf16[8,256,256]{2,1,0:T(8,128)(2,1)} %bitcast.26), calls=%async_computation.9 | async-start | bytes 2097152 | tf_op jit(solution)/shard_map/all_to_all | solution.py:206

commit v2 on v1

v2 whole, which is shorter than its diff:
```python
import jax
import jax.numpy as jnp
from jax import lax
from jax.experimental import pallas as pl
from jax.experimental.pallas import tpu as pltpu
from jax.sharding import PartitionSpec as P

epsilon = 1e-06
F32 = jnp.float32
BF16 = jnp.bfloat16
NN = (((1,), (0,)), ((), ()))
NT = (((1,), (1,)), ((), ()))


def mm(a, b, dims=NN):
    return lax.dot_general(a, b, dims, preferred_element_type=F32)


def iota(shape, dim):
    return lax.broadcasted_iota(jnp.int32, shape, dim)


def call(kernel, outs, *args, smem=0, scratch=(), flops=0, grid=None, in_specs=None, out_specs=None):
    moved = sum(a.size * a.dtype.itemsize for a in args) + sum(o.size * o.dtype.itemsize for o in outs)
    extra = {}
    if grid is not None:
        extra = dict(grid=grid, in_specs=in_specs, out_specs=out_specs)
    else:
        spaces = [pltpu.SMEM] * smem + [pltpu.VMEM] * (len(args) - smem)
        extra = dict(
            in_specs=[pl.BlockSpec(memory_space=s) for s in spaces],
            out_specs=[pl.BlockSpec(memory_space=pltpu.VMEM) for _ in outs],
        )
    return pl.pallas_call(
        kernel,
        out_shape=list(outs),
        scratch_shapes=list(scratch),
        compiler_params=pltpu.CompilerParams(vmem_limit_bytes=24 << 20),
        cost_estimate=pl.CostEstimate(flops=flops, bytes_accessed=moved, transcendentals=0),
        **extra,
    )(*args)


def shape(dims, dtype):
    return jax.ShapeDtypeStruct(dims, dtype)


def expander(owners, cap, base, width):
    return ((iota((owners, width), 1) + base) // cap == iota((owners, width), 0)).astype(F32).astype(BF16)


LANES = 128


def make_requests(owners, cap):
    def kernel(parent_ref, place_ref, tally_ref, rank_ref, rank_t_ref, ask_ref, row_ref):
        slots, pairs = parent_ref.shape
        line = iota((LANES, pairs), 0)
        tally = tally_ref[...]
        named = jnp.zeros((LANES, pairs), F32)
        where = jnp.zeros((LANES, pairs), F32)
        for c in range(slots):
            hit = jnp.logical_and(parent_ref[c : c + 1, :] == line, tally > c)
            named = jnp.where(hit, 1.0, named)
            where = jnp.where(hit, place_ref[c : c + 1, :].astype(F32), where)
        before = (iota((pairs, pairs), 0) < iota((pairs, pairs), 1)).astype(F32).astype(BF16)
        rank_t = jnp.where(named > 0, mm(named.astype(BF16), before), -1.0)
        rank = rank_t.T
        rank_t_ref[...] = rank_t.astype(BF16)
        rank_ref[...] = rank.astype(BF16)
        where = where.T.astype(jnp.int32)
        high = (where // 64).astype(F32).astype(BF16)
        low = (where % 64).astype(F32).astype(BF16)
        rank = rank.astype(BF16)
        total = owners * cap
        width = 512
        for base in range(0, total, width):
            spread = expander(LANES, cap, base, width)
            want = (iota((pairs, width), 1) % cap).astype(F32)
            place = mm(high, spread) * 64.0 + mm(low, spread)
            row_ref[:, base : base + width] = jnp.sum(
                jnp.where(mm(rank, spread) == want, place, 0.0), axis=0, keepdims=True
            )
        for o in range(owners):
            ask = row_ref[:, o * cap : (o + 1) * cap].astype(jnp.int32)
            ask_ref[o, :, 0:cap] = jnp.broadcast_to(ask, (ask_ref.shape[1], cap))

    return kernel


def unit_queries(query_ref, lines_ref, unit_ref, radius_ref, send_ref):
    pairs = query_ref.shape[0]
    slots = lines_ref.shape[0]
    query = query_ref[...].astype(F32)
    radius = jnp.sqrt(jnp.sum(query * query, axis=1, keepdims=True) + epsilon)
    unit = query / radius
    unit_ref[...] = unit
    radius_ref[...] = radius
    send_ref[0:pairs, :] = unit.astype(BF16)
    tail = send_ref.shape[0] - pairs
    line = iota((tail, pairs), 0)
    extra = jnp.zeros((tail, pairs), F32)
    for h in range(slots):
        row = lines_ref[h : h + 1, :]
        extra = jnp.where(line == h, (row // 64).astype(F32), extra)
        extra = jnp.where(line == h + slots, (row % 64).astype(F32), extra)
    send_ref[pairs:, :] = extra.astype(BF16)


def prepare(owners, cap):
    def kernel(rank_ref, rank_t_ref, lines_ref, hot_ref, table_ref, table_low_ref,
               pick_ref, place_ref, hot_sum_ref):
        pairs = rank_ref.shape[0]
        slots = lines_ref.shape[0]
        total = owners * cap
        width = 256
        rank = rank_ref[...]
        rank_t = rank_t_ref[...]
        hot_sum_ref[...] = jnp.zeros_like(hot_sum_ref)
        line = iota((LANES, pairs), 0)
        lines = jnp.zeros((LANES, pairs), F32)
        for h in range(slots):
            lines = jnp.where(line == h, lines_ref[h : h + 1, :].astype(F32), lines)
        lines = lines.T.astype(jnp.int32)

        def step(i, _):
            base = pl.multiple_of(i * width, width)
            table_low_ref[pl.ds(base, width), :] = table_ref[pl.ds(base, width), :].astype(BF16)
            spread = expander(LANES, cap, base, width)
            want = (iota((pairs, width), 1) % cap).astype(F32)
            pick_ref[:, pl.ds(base, width)] = (mm(rank, spread) == want).astype(F32).astype(BF16)
            spread_t = ((iota((width, LANES), 0) + base) // cap == iota((width, LANES), 1))
            want_t = (iota((width, pairs), 0) % cap).astype(F32)
            hit = mm(spread_t.astype(F32).astype(BF16), rank_t) == want_t
            place_ref[pl.ds(base, width), :] = hit.astype(F32).astype(BF16)
            column = iota((pairs, width), 1) + base
            counts = jnp.zeros((pairs, width), F32)
            for h in range(slots):
                counts += (lines[:, h : h + 1] == column).astype(F32)
            hot_sum_ref[...] += mm(counts.astype(BF16), hot_ref[pl.ds(base, width), :])
            return 0

        lax.fori_loop(0, total // width, step, 0)

    return kernel


def fetch(ask_ref, table_ref, out_ref):
    rows = table_ref.shape[0]
    group, cap = out_ref.shape[0], out_ref.shape[1]
    diagonal = iota((cap, cap), 0) == iota((cap, cap), 1)
    columns = []
    for g in range(group):
        ask = ask_ref[pl.program_id(0) * group + g, 0:1, 0:cap]
        columns.append(jnp.sum(jnp.where(diagonal, ask, 0).astype(F32), axis=1, keepdims=True))
    column = jnp.concatenate(columns, axis=0).astype(jnp.int32)
    hit = (column == iota((group * cap, rows), 1)).astype(F32).astype(BF16)
    out_ref[...] = mm(hit, table_ref[...]).astype(BF16).reshape(out_ref.shape)


def loss_side(own_low, other_refs, total_ref, sharpness, additive):
    rows = own_low.shape[0]
    for i, ref in enumerate(other_refs):
        other = ref[0:rows, :]
        grad = jax.nn.sigmoid(sharpness * mm(own_low, other, NT) + additive)
        if i == 0:
            grad = grad - (iota((rows, rows), 0) == iota((rows, rows), 1)).astype(F32)
            total_ref[...] = mm(grad.astype(BF16), other)
        else:
            total_ref[...] += mm(grad.astype(BF16), other)
    return sharpness * total_ref[...]


def project(unit, radius, direction):
    inner = jnp.sum(unit * direction, axis=1, keepdims=True)
    return (direction - unit * inner) / radius


def item_side(blocks):
    def kernel(sharp_ref, add_ref, fetched_ref, pick_ref, place_ref, hot_sum_ref, *refs):
        query_refs, (low_ref, grad_ref, out_ref, total_ref) = refs[:blocks], refs[blocks:]
        item = hot_sum_ref[...] + mm(pick_ref[...], fetched_ref[...])
        radius = jnp.sqrt(jnp.sum(item * item, axis=1, keepdims=True) + epsilon)
        unit = item / radius
        low = unit.astype(BF16)
        low_ref[...] = low
        direction = loss_side(low, query_refs, total_ref, sharp_ref[0], add_ref[0])
        grad = project(unit, radius, direction).astype(BF16)
        grad_ref[...] = grad
        width = 256

        def step(i, _):
            base = pl.multiple_of(i * width, width)
            out_ref[pl.ds(base, width), :] = mm(place_ref[pl.ds(base, width), :], grad).astype(BF16)
            return 0

        lax.fori_loop(0, out_ref.shape[0] // width, step, 0)

    return kernel


def query_side(sharp_ref, add_ref, unit_ref, radius_ref, *refs):
    item_refs, (out_ref, total_ref) = refs[:-2], refs[-2:]
    unit = unit_ref[...]
    direction = loss_side(unit.astype(BF16), item_refs, total_ref, sharp_ref[0], add_ref[0])
    out_ref[...] = project(unit, radius_ref[...], direction)


def hot_terms(blocks, slots):
    def kernel(block_ref, *refs):
        grad_refs, line_refs, (out_ref, total_ref) = refs[:blocks], refs[blocks : 2 * blocks], refs[2 * blocks :]
        width, pairs = out_ref.shape[0], grad_refs[0].shape[0]
        row = (iota((width, pairs), 0) + block_ref[0] * width).astype(F32)
        total_ref[...] = jnp.zeros_like(total_ref)
        for grad_ref, line_ref in zip(grad_refs, line_refs):
            lines = line_ref[pairs:, :].astype(F32)
            counts = jnp.zeros((width, pairs), F32)
            for h in range(slots):
                counts += (lines[h : h + 1, :] * 64.0 + lines[h + slots : h + slots + 1, :] == row).astype(F32)
            total_ref[...] += mm(counts.astype(BF16), grad_ref[...])
        out_ref[...] = total_ref[...].astype(BF16)

    return kernel


def hot_sum_spread(parts_ref, out_ref):
    piece = jnp.sum(parts_ref[...].astype(F32), axis=0, keepdims=True)
    out_ref[...] = jnp.broadcast_to(piece, out_ref.shape).astype(BF16)


def widen(blocks):
    def kernel(block_ref, *refs):
        part_refs, out_ref = refs[:blocks], refs[blocks]
        chips = blocks // 2
        width = part_refs[0].shape[0]
        mine, core = block_ref[0] // 2, block_ref[0] % 2
        for i, ref in enumerate(part_refs):
            chip = (mine + chips - i % chips) % chips
            index = chip * 2 + (core if i < chips else 1 - core)
            out_ref[pl.ds(pl.multiple_of(index * width, width), width), :] = ref[...].astype(F32)

    return kernel


def cold_terms(same_core):
    def kernel(block_ref, ask_ref, grad_ref, out_ref, row_ref):
        width, total = out_ref.shape[1], grad_ref.shape[0]
        owners, chips = ask_ref.shape[0], pl.num_programs(0)
        cap = total // owners

        @pl.when(pl.program_id(0) == 0)
        def _():
            for o in range(owners):
                row_ref[:, o * cap : (o + 1) * cap] = ask_ref[o, 0:1, 0:cap]

        core = block_ref[0] % 2
        core = core if same_core else 1 - core
        chip = (block_ref[0] // 2 + pl.program_id(0)) % chips
        row = iota((width, total), 0) + (chip * 2 + core) * width
        hit = (row_ref[...] == row).astype(F32).astype(BF16)
        out_ref[0] = mm(hit, grad_ref[...]).astype(out_ref.dtype)

    return kernel


def cold_join(mine_ref, theirs_ref, keep_ref, *send_refs):
    keep_ref[...] = mine_ref[0] + theirs_ref[0].astype(F32)
    for d, ref in enumerate(send_refs):
        ref[...] = (mine_ref[d + 1] + theirs_ref[d + 1].astype(F32)).astype(BF16)


def add_parts(keep_ref, *refs):
    part_refs, out_ref = refs[:-1], refs[-1]
    total = keep_ref[...]
    for ref in part_refs:
        total += ref[...].astype(F32)
    out_ref[...] = total


def whole(array):
    return pl.BlockSpec(array.shape, lambda i: (0,) * array.ndim)


def swap(array, axis):
    return lax.all_to_all(array, axis, split_axis=0, concat_axis=0, tiled=True)


def cross(array, blocks):
    return lax.ppermute(array, "blk", [(i, i ^ 1) for i in range(blocks)])


def shift(array, blocks, d):
    return lax.ppermute(array, "blk", [(i, (i + 2 * d) % blocks) for i in range(blocks)])


def gather_blocks(array, blocks):
    first = cross(array, blocks)
    mine = [shift(array, blocks, d) for d in range(1, blocks // 2)]
    return [array] + mine + [first] + [cross(m, blocks) for m in mine]


def body(queries, hot_table, cold_table, lines, parent, place, tally, sharpness, additive):
    pairs, width = queries.shape
    owners, blocks = lax.axis_size("shard"), lax.axis_size("blk")
    chips = blocks // 2
    slots = parent.shape[1]
    cap = 2 * pairs * slots // owners
    total = owners * cap
    rows = cold_table.shape[0]
    hot_rows = hot_table.shape[0]
    block = lax.axis_index("blk").astype(jnp.int32).reshape(1)

    rank, rank_t, ask = call(
        make_requests(owners, cap),
        [shape((pairs, LANES), BF16), shape((LANES, pairs), BF16), shape((owners, 8, LANES), jnp.int32)],
        parent.T, place.T, tally.reshape(1, pairs),
        scratch=[pltpu.VMEM((1, total), F32)],
        flops=2 * pairs * total * LANES * 3,
    )
    with jax.named_scope("ask"):
        asked = swap(ask, "shard")

    unit, radius, query_block = call(
        unit_queries,
        [shape((pairs, width), F32), shape((pairs, 1), F32), shape((pairs + 16, width), BF16)],
        queries, lines.T,
    )
    with jax.named_scope("queries"):
        query_blocks = gather_blocks(query_block, blocks)

    table_low, pick, placed, hot_sum = call(
        prepare(owners, cap),
        [
            shape((rows, width), BF16),
            shape((pairs, total), BF16),
            shape((total, pairs), BF16),
            shape((pairs, width), F32),
        ],
        rank, rank_t, lines.T, hot_table, cold_table,
        flops=2 * pairs * total * (width + 2 * LANES),
    )

    group = 4
    (looked,) = call(
        fetch,
        [shape((owners, cap, width), BF16)],
        asked, table_low,
        grid=(owners // group,),
        in_specs=[whole(asked), whole(table_low)],
        out_specs=[pl.BlockSpec((group, cap, width), lambda i: (i, 0, 0))],
        flops=2 * total * rows * width,
    )
    with jax.named_scope("rows"):
        fetched = swap(looked, "shard").reshape(total, width)

    item_low, item_grad, outgoing = call(
        item_side(blocks),
        [shape((pairs, width), BF16), shape((pairs, width), BF16), shape((total, width), BF16)],
        sharpness, additive, fetched, pick, placed, hot_sum, *query_blocks,
        smem=2,
        scratch=[pltpu.VMEM((pairs, width), F32)],
        flops=2 * pairs * width * (2 * total + 2 * blocks * pairs),
    )
    with jax.named_scope("cold"):
        incoming = swap(outgoing.reshape(owners, cap, width), "shard").reshape(total, width)

    with jax.named_scope("grads"):
        grad_blocks = gather_blocks(item_grad, blocks)
    (hot_block,) = call(
        hot_terms(blocks, slots),
        [shape((hot_rows // blocks, width), BF16)],
        block, *grad_blocks, *query_blocks,
        smem=1,
        scratch=[pltpu.VMEM((hot_rows // blocks, width), F32)],
        flops=2 * blocks * pairs * width * hot_rows // blocks,
    )
    with jax.named_scope("hot_parts"):
        hot_parts = swap(hot_block.reshape(owners, hot_rows // blocks // owners, width), "shard")
    (hot_piece,) = call(hot_sum_spread, [shape(hot_parts.shape, BF16)], hot_parts)
    with jax.named_scope("hot_whole"):
        hot_block = swap(hot_piece, "shard").reshape(hot_rows // blocks, width)
    with jax.named_scope("hot_blocks"):
        hot_blocks = gather_blocks(hot_block, blocks)
    (hot_grad,) = call(widen(blocks), [shape((hot_rows, width), F32)], block, *hot_blocks, smem=1)

    with jax.named_scope("items"):
        item_blocks = gather_blocks(item_low, blocks)
    (query_grad,) = call(
        query_side,
        [shape((pairs, width), F32)],
        sharpness, additive, unit, radius, *item_blocks,
        smem=2,
        scratch=[pltpu.VMEM((pairs, width), F32)],
        flops=4 * pairs * width * blocks * pairs,
    )

    def cold_half(same_core, dtype):
        return call(
            cold_terms(same_core),
            [shape((chips, rows // blocks, width), dtype)],
            block, asked, incoming,
            grid=(chips,),
            in_specs=[pl.BlockSpec(memory_space=pltpu.SMEM), whole(asked), whole(incoming)],
            out_specs=[pl.BlockSpec((1, rows // blocks, width), lambda i: (i, 0, 0))],
            scratch=[pltpu.VMEM((1, total), jnp.int32)],
            flops=total * rows * width,
        )[0]

    theirs = cold_half(False, BF16)
    with jax.named_scope("cold_cross"):
        theirs = cross(theirs, blocks)
    mine = cold_half(True, F32)
    keep, *sends = call(
        cold_join,
        [shape((rows // blocks, width), F32)] + [shape((rows // blocks, width), BF16)] * (chips - 1),
        mine, theirs,
    )
    with jax.named_scope("cold_shift"):
        parts = [shift(part, blocks, d + 1) for d, part in enumerate(sends)]
    (cold_grad,) = call(add_parts, [shape((rows // blocks, width), F32)], keep, *parts)
    return (query_grad, hot_grad, cold_grad)


def solution(mesh):
    pair = P(("shard", "blk"), None)
    in_specs = (pair, P(), P("shard", None), pair, pair, pair, P(("shard", "blk")), P(), P())
    return jax.shard_map(body, mesh=mesh, in_specs=in_specs, out_specs=(pair, P(), pair), check_vma=False)
```

time: 246 us -> 168 us (0.68)
  blocking collectives: 77 us -> 0 us
  starting transfers between devices: 45.9 us -> 86.9 us
  waiting for transfers between devices: 61.5 us -> 30 us
  Pallas kernels: 40.9 us -> 24.4 us
  local copies, waits for them, and re-layouts: 14.5 us -> 23.6 us
  other arithmetic: 3.26 us -> 0 us
    all_to_all x4 -> x0, blocking collectives: 77 us -> none  [swap(): return lax.all_to_all(array, axis, split_axis=0, concat_axis=0, tiled=True)]
    ppermute x0 -> x32, starting transfers between devices: none -> 47 us  [the longest x17 25.1 us: cross(): return lax.ppermute(array, 'blk', [(i, i ^ 1) for i in range(blocks)])]
    all_to_all x6 -> x5, waiting for transfers between devices: 61.5 us -> 25.5 us  [swap(): return lax.all_to_all(array, axis, split_axis=0, concat_axis=0, tiled=True)]
    unnamed x13 -> x92, local copies, waits for them, and re-layouts: 5.44 us -> 23.6 us
    pallas_call x7 -> x13, Pallas kernels: 40.9 us -> 24.4 us  [call(): pl.pallas_call(kernel, out_shape=list(outs), scratch_shapes=list(scratch)...]
    all_to_all x6 -> x5, starting transfers between devices: 45.9 us -> 39.9 us  [swap(): return lax.all_to_all(array, axis, split_axis=0, concat_axis=0, tiled=True)]
    ppermute x0 -> x32, waiting for transfers between devices: none -> 4.46 us  [the longest x15 3.14 us: shift(): lax.ppermute(array, 'blk', [(i, (i + 2 * d) % blocks) for i in range(bloc...]
    broadcast_in_dim x4 -> x0, local copies, waits for them, and re-layouts: 4.14 us -> none  [spread(): jnp.broadcast_to(array[None], (lax.axis_size(axis),) + array.shape)]
  transfers between devices with their start and end apart: 6 -> 37, of which waited for: 5 -> 7; matrix products, arithmetic and copies ran while one was open for 3% -> 0% of each run, Pallas kernels for 10% -> 8%
where the time goes in v2:
time: 168 us; the launch traced here: 167 us
  starting transfers between devices  86.9 us (52%)
  waiting for transfers between devices  30 us (18%)
  Pallas kernels  24.4 us (15%)
  local copies, waits for them, and re-layouts  23.6 us (14%)
  between operations  2.33 us (1%)
    all_to_all x5, starting transfers between devices, swap(): return lax.all_to_all(array, axis, split_axis=0, concat_axis=0, tiled=True)  39.9 us
    all_to_all x5, waiting for transfers between devices, swap(): return lax.all_to_all(array, axis, split_axis=0, concat_axis=0, tiled=True)  25.5 us
    ppermute x17, starting transfers between devices, cross(): return lax.ppermute(array, 'blk', [(i, i ^ 1) for i in range(blocks)])  25.1 us
    pallas_call x13, Pallas kernels, call(): pl.pallas_call(kernel, out_shape=list(outs), scratch_shapes=list(scratch)...  24.4 us
    unnamed x92, local copies, waits for them, and re-layouts  23.6 us
    ppermute x15, starting transfers between devices, shift(): lax.ppermute(array, 'blk', [(i, (i + 2 * d) % blocks) for i in range(bloc...  21.9 us
  transfers between devices with their start and end apart: 37, of which 7 were waited for; matrix products, arithmetic and copies ran while one was open for 0% of the time, Pallas kernels for 8%

profile of v2, /device:TPU:1, one launch (start us, length us, event | category | flops | bytes accessed | tf_op | source)
XLA Modules:
  0.0 167.2 jit_solution(3264840071109286743)
XLA Ops:
  0.7 0.8 copy-done.43
  1.4 0.7 copy-done.44
  2.1 0.7 copy-done.45
  2.8 1.9 %shard_map.113 = (bf16[256,128]{1,0:T(8,128)(2,1)S(1)}, bf16[128,256]{1,0:T(8,128)(2,1)S(1)}, s32[32,8,128]{2,1,0:T(8,128)}) custom-call(s32[4,256]{1,0:T(4,128)S(1)} %bitcast.21, s32[4,256]{1,0:T(4,128)S(1)} %bitcast.22, s32[1,256]{1,0:T(1,128)S(1)} %bitcast.23), custom_call_target="tpu_custom_call" | custom-call | flops 402653184 | bytes 271360 | tf_op jit(solution)/shard_map/pallas_call | solution.py:34
  4.7 12.0 %all-to-all-start = ((s32[32,8,128]{2,1,0:T(8,128)}), s32[32,8,128]{2,1,0:T(8,128)S(1)}, u32[]{:S(2)}, u32[]{:S(2)}) async-start(s32[32,8,128]{2,1,0:T(8,128)} %get-tuple-element.22), calls=%async_computation | async-start | bytes 262144 | tf_op jit(solution)/shard_map/ask/all_to_all | solution.py:285
  16.7 1.6 copy-done
  18.3 0.7 copy-done.27
  19.0 3.5 %shard_map.114 = (bf16[2048,256]{1,0:T(8,128)(2,1)S(1)}, bf16[256,2048]{1,0:T(8,128)(2,1)S(1)}, bf16[2048,256]{1,0:T(8,128)(2,1)S(1)}, f32[256,256]{1,0:T(8,128)S(1)}) custom-call(bf16[256,128]{1,0:T(8,128)(2,1)S(1)} %get-tuple-element.23.rank_ref, bf16[128,256]{1,0:T(8,128)(2,1)S(1)} %get-tuple-element.24.rank_t_ref, s32[4,256]{1,0:T(4,128)S(1)} %bitcast.19, ...), custom_call_target="tpu_custom_call" | custom-call | flops 536870912 | bytes 6688768 | tf_op jit(solution)/shard_map/pallas_call | solution.py:34
  22.5 0.7 copy-done.22
  23.2 1.0 copy-done.29
  24.2 1.6 all-to-all-done.ask_ref
  25.8 1.3 copy-done.30
  27.1 5.1 %shard_map.115 = bf16[32,64,256]{2,1,0:T(8,128)(2,1)S(1)} custom-call(s32[32,8,128]{2,1,0:T(8,128)S(1)} %all-to-all-done.ask_ref, bf16[2048,256]{1,0:T(8,128)(2,1)S(1)} %copy-done.30), custom_call_target="tpu_custom_call" | custom-call | flops 2147483648 | bytes 2228224 | tf_op jit(solution)/shard_map/pallas_call | solution.py:34
  32.2 1.0 copy-done.3
  33.2 7.7 %all-to-all-start.1 = ((bf16[32,64,256]{2,1,0:T(8,128)(2,1)}), bf16[32,64,256]{2,1,0:T(8,128)(2,1)S(1)}, u32[]{:S(2)}, u32[]{:S(2)}) async-start(bf16[32,64,256]{2,1,0:T(8,128)(2,1)} %copy-done.3), calls=%async_computation.1 | async-start | bytes 2097152 | tf_op jit(solution)/shard_map/rows/all_to_all | solution.py:285
  41.1 0.7 copy-done.31
  42.5 1.2 collective-permute-start
  43.7 2.4 %collective-permute-start.1 = (bf16[272,256]{1,0:T(8,128)(2,1)S(1)}, bf16[272,256]{1,0:T(8,128)(2,1)S(1)}, u32[]{:S(2)}, u32[]{:S(2)}) collective-permute-start(bf16[272,256]{1,0:T(8,128)(2,1)S(1)} %get-tuple-element.29.refs_0_.refs_8_), channel_id=1, source_target_pairs={{0,4},{1,5},{2,6},{3,7},{4,0},{5,1},{6,2},{7,3},{8,12},{9,13},{10,... | collective-permute-start | bytes 417800 | tf_op jit(solution)/shard_map/queries/ppermute | solution.py:293
  46.1 1.2 collective-permute-start.2
  47.3 2.4 %collective-permute-start.3 = (bf16[272,256]{1,0:T(8,128)(2,1)S(1)}, bf16[272,256]{1,0:T(8,128)(2,1)S(1)}, u32[]{:S(2)}, u32[]{:S(2)}) collective-permute-start(bf16[272,256]{1,0:T(8,128)(2,1)S(1)} %get-tuple-element.29.refs_0_.refs_8_), channel_id=1, source_target_pairs={{0,1},{1,0},{2,3},{3,2},{4,5},{5,4},{6,7},{7,6},{8,9},{9,8},{10,11... | collective-permute-start | bytes 417800 | tf_op jit(solution)/shard_map/queries/ppermute | solution.py:289
  49.6 2.1 %collective-permute-start.4 = (bf16[272,256]{1,0:T(8,128)(2,1)S(1)}, bf16[272,256]{1,0:T(8,128)(2,1)S(1)}, u32[]{:S(2)}, u32[]{:S(2)}) collective-permute-start(bf16[272,256]{1,0:T(8,128)(2,1)S(1)} %collective-permute-done.refs_1_.refs_9_), channel_id=1, source_target_pairs={{0,1},{1,0},{2,3},{3,2},{4,5},{5,4},{6,7},{7,6},{8,9},{9,8},{10,11... | collective-permute-start | bytes 417800 | tf_op jit(solution)/shard_map/queries/ppermute | solution.py:289
  51.7 2.0 %collective-permute-start.5 = (bf16[272,256]{1,0:T(8,128)(2,1)S(1)}, bf16[272,256]{1,0:T(8,128)(2,1)S(1)}, u32[]{:S(2)}, u32[]{:S(2)}) collective-permute-start(bf16[272,256]{1,0:T(8,128)(2,1)S(1)} %collective-permute-done.1.refs_2_.refs_10_), channel_id=1, source_target_pairs={{0,1},{1,0},{2,3},{3,2},{4,5},{5,4},{6,7},{7,6},{8,9},{9,8},{10,11... | collective-permute-start | bytes 417800 | tf_op jit(solution)/shard_map/queries/ppermute | solution.py:289
  59.0 7.1 %all-to-all-done.1 = bf16[32,64,256]{2,1,0:T(8,128)(2,1)S(1)} async-done(((bf16[32,64,256]{2,1,0:T(8,128)(2,1)}), bf16[32,64,256]{2,1,0:T(8,128)(2,1)S(1)}, u32[]{:S(2)}, u32[]{:S(2)}) %all-to-all-start.1) | async-done | bytes 1048608 | tf_op jit(solution)/shard_map/rows/all_to_all | solution.py:285
  66.1 0.9 copy-done.5
  67.0 0.9 copy-done.8
  67.9 0.9 copy-done.11
  68.8 0.9 copy-done.14
  69.8 0.9 copy-done.17
  70.7 0.9 copy-done.20
  71.6 0.9 copy-done.23
  72.5 3.5 %shard_map.116 = (bf16[256,256]{1,0:T(8,128)(2,1)S(1)}, bf16[256,256]{1,0:T(8,128)(2,1)S(1)}, bf16[2048,256]{1,0:T(8,128)(2,1)S(1)}) custom-call(f32[1]{0:T(128)S(6)} %copy.12.sharp_ref, f32[1]{0:T(128)S(6)} %copy.13.add_ref, bf16[2048,256]{1,0:T(8,128)(2,1)S(1)} %bitcast.10, bf16[256,2048]{1,0:T(8,128)(2,1)S(1)} %get-tuple-element.26.pick_ref, ...), custom_call_target="tpu_custom_call" | custom-call | flops 1073741824 | bytes 5832712 | tf_op jit(solution)/shard_map/pallas_call | solution.py:34
  76.1 1.0 copy-done.2
  77.7 8.2 %all-to-all-start.4 = ((bf16[32,64,256]{2,1,0:T(8,128)(2,1)}), bf16[32,64,256]{2,1,0:T(8,128)(2,1)S(1)}, u32[]{:S(2)}, u32[]{:S(2)}) async-start(bf16[32,64,256]{2,1,0:T(8,128)(2,1)} %bitcast.13), calls=%async_computation.4 | async-start | bytes 2097152 | tf_op jit(solution)/shard_map/cold/all_to_all | solution.py:285
  85.9 1.3 collective-permute-start.14
  87.2 2.4 %collective-permute-start.15 = (bf16[256,256]{1,0:T(8,128)(2,1)S(1)}, bf16[256,256]{1,0:T(8,128)(2,1)S(1)}, u32[]{:S(2)}, u32[]{:S(2)}) collective-permute-start(bf16[256,256]{1,0:T(8,128)(2,1)S(1)} %get-tuple-element.31.refs_0_), channel_id=1, source_target_pairs={{0,4},{1,5},{2,6},{3,7},{4,0},{5,1},{6,2},{7,3},{8,12},{9,13},{10,... | collective-permute-start | bytes 393224 | tf_op jit(solution)/shard_map/grads/ppermute | solution.py:293
  89.7 1.2 collective-permute-start.16
  90.8 2.3 %collective-permute-start.17 = (bf16[256,256]{1,0:T(8,128)(2,1)S(1)}, bf16[256,256]{1,0:T(8,128)(2,1)S(1)}, u32[]{:S(2)}, u32[]{:S(2)}) collective-permute-start(bf16[256,256]{1,0:T(8,128)(2,1)S(1)} %get-tuple-element.31.refs_0_), channel_id=1, source_target_pairs={{0,1},{1,0},{2,3},{3,2},{4,5},{5,4},{6,7},{7,6},{8,9},{9,8},{10,11... | collective-permute-start | bytes 393224 | tf_op jit(solution)/shard_map/grads/ppermute | solution.py:289
  93.1 1.9 %collective-permute-start.18 = (bf16[256,256]{1,0:T(8,128)(2,1)S(1)}, bf16[256,256]{1,0:T(8,128)(2,1)S(1)}, u32[]{:S(2)}, u32[]{:S(2)}) collective-permute-start(bf16[256,256]{1,0:T(8,128)(2,1)S(1)} %collective-permute-done.14.refs_1_), channel_id=1, source_target_pairs={{0,1},{1,0},{2,3},{3,2},{4,5},{5,4},{6,7},{7,6},{8,9},{9,8},{10,11... | collective-permute-start | bytes 393224 | tf_op jit(solution)/shard_map/grads/ppermute | solution.py:289
  95.0 1.9 %collective-permute-start.19 = (bf16[256,256]{1,0:T(8,128)(2,1)S(1)}, bf16[256,256]{1,0:T(8,128)(2,1)S(1)}, u32[]{:S(2)}, u32[]{:S(2)}) collective-permute-start(bf16[256,256]{1,0:T(8,128)(2,1)S(1)} %collective-permute-done.15.refs_2_), channel_id=1, source_target_pairs={{0,1},{1,0},{2,3},{3,2},{4,5},{5,4},{6,7},{7,6},{8,9},{9,8},{10,11... | collective-permute-start | bytes 393224 | tf_op jit(solution)/shard_map/grads/ppermute | solution.py:289
  97.0 0.9 collective-permute-done.19.refs_6_
  98.3 1.6 shard_map.118
  99.9 11.1 %all-to-all-done.4 = bf16[32,64,256]{2,1,0:T(8,128)(2,1)S(1)} async-done(((bf16[32,64,256]{2,1,0:T(8,128)(2,1)}), bf16[32,64,256]{2,1,0:T(8,128)(2,1)S(1)}, u32[]{:S(2)}, u32[]{:S(2)}) %all-to-all-start.4) | async-done | bytes 1048608 | tf_op jit(solution)/shard_map/cold/all_to_all | solution.py:285
  111.0 8.1 %all-to-all-start.2 = ((bf16[32,8,256]{2,1,0:T(8,128)(2,1)}), bf16[32,8,256]{2,1,0:T(8,128)(2,1)S(1)}, u32[]{:S(2)}, u32[]{:S(2)}) async-start(bf16[32,8,256]{2,1,0:T(8,128)(2,1)} %bitcast.6), calls=%async_computation.2 | async-start | bytes 262144 | tf_op jit(solution)/shard_map/hot_parts/all_to_all | solution.py:285
  119.2 1.9 %shard_map.122 = bf16[4,256,256]{2,1,0:T(8,128)(2,1)S(1)} custom-call(s32[1]{0:T(128)} %bitcast.5.block_ref, s32[32,8,128]{2,1,0:T(8,128)S(1)} %copy-done.26, bf16[2048,256]{1,0:T(8,128)(2,1)S(1)} %bitcast.11), custom_call_target="tpu_custom_call" | custom-call | flops 1073741824 | bytes 1703940 | tf_op jit(solution)/shard_map/pallas_call | solution.py:34
  121.1 1.5 collective-permute-start.28
  122.6 5.7 %all-to-all-done.2.parts_ref = bf16[32,8,256]{2,1,0:T(8,128)(2,1)S(1)} async-done(((bf16[32,8,256]{2,1,0:T(8,128)(2,1)}), bf16[32,8,256]{2,1,0:T(8,128)(2,1)S(1)}, u32[]{:S(2)}, u32[]{:S(2)}) %all-to-all-start.2) | async-done | bytes 131104 | tf_op jit(solution)/shard_map/hot_parts/all_to_all | solution.py:285
  128.3 0.7 shard_map.119
  129.0 3.9 %all-to-all-start.3 = ((bf16[32,8,256]{2,1,0:T(8,128)(2,1)}), bf16[32,8,256]{2,1,0:T(8,128)(2,1)S(1)}, u32[]{:S(2)}, u32[]{:S(2)}) async-start(bf16[32,8,256]{2,1,0:T(8,128)(2,1)} %shard_map.119), calls=%async_computation.3 | async-start | bytes 262144 | tf_op jit(solution)/shard_map/hot_whole/all_to_all | solution.py:285
  132.9 1.3 collective-permute-start.7
  134.2 2.4 %collective-permute-start.8 = (bf16[256,256]{1,0:T(8,128)(2,1)S(1)}, bf16[256,256]{1,0:T(8,128)(2,1)S(1)}, u32[]{:S(2)}, u32[]{:S(2)}) collective-permute-start(bf16[256,256]{1,0:T(8,128)(2,1)S(1)} %copy-done.36), channel_id=1, source_target_pairs={{0,4},{1,5},{2,6},{3,7},{4,0},{5,1},{6,2},{7,3},{8,12},{9,13},{10,... | collective-permute-start | bytes 393224 | tf_op jit(solution)/shard_map/items/ppermute | solution.py:293
  136.6 1.2 collective-permute-start.9
  137.8 3.5 %collective-permute-start.10 = (bf16[256,256]{1,0:T(8,128)(2,1)S(1)}, bf16[256,256]{1,0:T(8,128)(2,1)S(1)}, u32[]{:S(2)}, u32[]{:S(2)}) collective-permute-start(bf16[256,256]{1,0:T(8,128)(2,1)S(1)} %copy-done.36), channel_id=1, source_target_pairs={{0,1},{1,0},{2,3},{3,2},{4,5},{5,4},{6,7},{7,6},{8,9},{9,8},{10,11... | collective-permute-start | bytes 393224 | tf_op jit(solution)/shard_map/items/ppermute | solution.py:289
  141.3 1.1 collective-permute-start.11
  142.5 1.8 %collective-permute-start.12 = (bf16[256,256]{1,0:T(8,128)(2,1)S(1)}, bf16[256,256]{1,0:T(8,128)(2,1)S(1)}, u32[]{:S(2)}, u32[]{:S(2)}) collective-permute-start(bf16[256,256]{1,0:T(8,128)(2,1)S(1)} %collective-permute-done.8.refs_2_), channel_id=1, source_target_pairs={{0,1},{1,0},{2,3},{3,2},{4,5},{5,4},{6,7},{7,6},{8,9},{9,8},{10,11... | collective-permute-start | bytes 393224 | tf_op jit(solution)/shard_map/items/ppermute | solution.py:289
  144.2 0.8 collective-permute-start.21
  145.7 1.3 collective-permute-start.22
  147.7 1.9 %collective-permute-start.23 = (bf16[256,256]{1,0:T(8,128)(2,1)S(1)}, bf16[256,256]{1,0:T(8,128)(2,1)S(1)}, u32[]{:S(2)}, u32[]{:S(2)}) collective-permute-start(bf16[256,256]{1,0:T(8,128)(2,1)S(1)} %bitcast.16), channel_id=1, source_target_pairs={{0,6},{1,7},{2,0},{3,1},{4,2},{5,3},{6,4},{7,5},{8,14},{9,15},{10,... | collective-permute-start | bytes 393224 | tf_op jit(solution)/shard_map/hot_blocks/ppermute | solution.py:293
  150.2 3.4 %collective-permute-start.13 = (bf16[256,256]{1,0:T(8,128)(2,1)S(1)}, bf16[256,256]{1,0:T(8,128)(2,1)S(1)}, u32[]{:S(2)}, u32[]{:S(2)}) collective-permute-start(bf16[256,256]{1,0:T(8,128)(2,1)S(1)} %collective-permute-done.9.refs_3_), channel_id=1, source_target_pairs={{0,1},{1,0},{2,3},{3,2},{4,5},{5,4},{6,7},{7,6},{8,9},{9,8},{10,11... | collective-permute-start | bytes 393224 | tf_op jit(solution)/shard_map/items/ppermute | solution.py:289
  154.1 1.9 %shard_map.121.mine_ref = f32[4,256,256]{2,1,0:T(8,128)S(1)} custom-call(s32[1]{0:T(128)} %bitcast.5.block_ref, s32[32,8,128]{2,1,0:T(8,128)S(1)} %copy-done.26, bf16[2048,256]{1,0:T(8,128)(2,1)S(1)} %bitcast.12), custom_call_target="tpu_custom_call" | custom-call | flops 1073741824 | bytes 2228228 | tf_op jit(solution)/shard_map/pallas_call | solution.py:34
  157.2 2.8 %collective-permute-start.30 = (bf16[256,256]{1,0:T(8,128)(2,1)S(1)}, bf16[256,256]{1,0:T(8,128)(2,1)S(1)}, u32[]{:S(2)}, u32[]{:S(2)}) collective-permute-start(bf16[256,256]{1,0:T(8,128)(2,1)S(1)} %get-tuple-element.35), channel_id=1, source_target_pairs={{0,4},{1,5},{2,6},{3,7},{4,0},{5,1},{6,2},{7,3},{8,12},{9,13},{10,... | collective-permute-start | bytes 393224 | tf_op jit(solution)/shard_map/cold_shift/ppermute | solution.py:293
  160.1 1.8 %shard_map.117 = f32[256,256]{1,0:T(8,128)} custom-call(f32[1]{0:T(128)S(6)} %copy.12.sharp_ref, f32[1]{0:T(128)S(6)} %copy.13.add_ref, f32[256,256]{1,0:T(8,128)S(1)} %copy-done.32, f32[256,1]{1,0:T(8,128)S(1)} %copy-done.34, bf16[256,256]{1,0:T(8,128)(2,1)S(1)} %copy-done.36, bf16[256,256]{1,0:T(8,128)(2,1)S(1)} %collective-permute-done.7.refs_1_, ...), custom_call_target="tpu_custom_call" | custom-call | flops 536870912 | bytes 1573896 | tf_op jit(solution)/shard_map/pallas_call | solution.py:34
  161.9 1.5 shard_map.120
  163.3 3.1 %collective-permute-done.30.refs_1_ = bf16[256,256]{1,0:T(8,128)(2,1)S(1)} collective-permute-done((bf16[256,256]{1,0:T(8,128)(2,1)S(1)}, bf16[256,256]{1,0:T(8,128)(2,1)S(1)}, u32[]{:S(2)}, u32[]{:S(2)}) %collective-permute-start.30) | collective-permute-done | bytes 131104 | tf_op jit(solution)/shard_map/cold_shift/ppermute | solution.py:293
  166.4 0.8 shard_map.124
  (115 shorter events, 9.6 us)
Async XLA Ops:
  0.6 16.1 %copy-start.1 = (bf16[2048,256]{1,0:T(8,128)(2,1)S(1)}, bf16[2048,256]{1,0:T(8,128)(2,1)}, u32[]{:S(2)}) copy-start(bf16[2048,256]{1,0:T(8,128)(2,1)} %hot_ref.1) | copy-start | bytes 3145732
  4.7 21.2 %all-to-all-start = ((s32[32,8,128]{2,1,0:T(8,128)}), s32[32,8,128]{2,1,0:T(8,128)S(1)}, u32[]{:S(2)}, u32[]{:S(2)}) async-start(s32[32,8,128]{2,1,0:T(8,128)} %get-tuple-element.22), calls=%async_computation | async-start | bytes 262144 | tf_op jit(solution)/shard_map/ask/all_to_all | solution.py:285
  16.7 1.6 copy-start
  23.2 1.0 copy-start.29
  25.8 6.4 %copy-start.25 = (s32[32,8,128]{2,1,0:T(8,128)}, s32[32,8,128]{2,1,0:T(8,128)S(1)}, u32[]{:S(2)}) copy-start(s32[32,8,128]{2,1,0:T(8,128)S(1)} %all-to-all-done.ask_ref) | copy-start | bytes 393220
  25.8 1.3 copy-start.30
  32.2 1.0 copy-start.3
  33.2 7.7 %copy-start.24 = (bf16[256,256]{1,0:T(8,128)(2,1)S(1)}, bf16[256,256]{1,0:T(8,128)(2,1)}, u32[]{:S(2)}) copy-start(bf16[256,256]{1,0:T(8,128)(2,1)} %query_ref.1) | copy-start | bytes 393220
  33.2 7.8 %copy-start.28 = (s32[256,4]{0,1:T(4,128)S(1)}, s32[256,4]{0,1:T(4,128)}, u32[]{:S(2)}) copy-start(s32[256,4]{0,1:T(4,128)} %param.12) | copy-start | bytes 12292
  33.2 32.9 %all-to-all-start.1 = ((bf16[32,64,256]{2,1,0:T(8,128)(2,1)}), bf16[32,64,256]{2,1,0:T(8,128)(2,1)S(1)}, u32[]{:S(2)}, u32[]{:S(2)}) async-start(bf16[32,64,256]{2,1,0:T(8,128)(2,1)} %copy-done.3), calls=%async_computation.1 | async-start | bytes 2097152 | tf_op jit(solution)/shard_map/rows/all_to_all | solution.py:285
  42.5 7.2 %collective-permute-start = (bf16[272,256]{1,0:T(8,128)(2,1)S(1)}, bf16[272,256]{1,0:T(8,128)(2,1)S(1)}, u32[]{:S(2)}, u32[]{:S(2)}) collective-permute-start(bf16[272,256]{1,0:T(8,128)(2,1)S(1)} %get-tuple-element.29.refs_0_.refs_8_), channel_id=1, source_target_pairs={{0,2},{1,3},{2,4},{3,5},{4,6},{5,7},{6,0},{7,1},{8,10},{9,11},{10,... | collective-permute-start | bytes 417800 | tf_op jit(solution)/shard_map/queries/ppermute | solution.py:293
  43.7 8.0 %collective-permute-start.1 = (bf16[272,256]{1,0:T(8,128)(2,1)S(1)}, bf16[272,256]{1,0:T(8,128)(2,1)S(1)}, u32[]{:S(2)}, u32[]{:S(2)}) collective-permute-start(bf16[272,256]{1,0:T(8,128)(2,1)S(1)} %get-tuple-element.29.refs_0_.refs_8_), channel_id=1, source_target_pairs={{0,4},{1,5},{2,6},{3,7},{4,0},{5,1},{6,2},{7,3},{8,12},{9,13},{10,... | collective-permute-start | bytes 417800 | tf_op jit(solution)/shard_map/queries/ppermute | solution.py:293
  46.1 8.3 %collective-permute-start.2 = (bf16[272,256]{1,0:T(8,128)(2,1)S(1)}, bf16[272,256]{1,0:T(8,128)(2,1)S(1)}, u32[]{:S(2)}, u32[]{:S(2)}) collective-permute-start(bf16[272,256]{1,0:T(8,128)(2,1)S(1)} %get-tuple-element.29.refs_0_.refs_8_), channel_id=1, source_target_pairs={{0,6},{1,7},{2,0},{3,1},{4,2},{5,3},{6,4},{7,5},{8,14},{9,15},{10,... | collective-permute-start | bytes 417800 | tf_op jit(solution)/shard_map/queries/ppermute | solution.py:293
  47.3 9.1 %collective-permute-start.3 = (bf16[272,256]{1,0:T(8,128)(2,1)S(1)}, bf16[272,256]{1,0:T(8,128)(2,1)S(1)}, u32[]{:S(2)}, u32[]{:S(2)}) collective-permute-start(bf16[272,256]{1,0:T(8,128)(2,1)S(1)} %get-tuple-element.29.refs_0_.refs_8_), channel_id=1, source_target_pairs={{0,1},{1,0},{2,3},{3,2},{4,5},{5,4},{6,7},{7,6},{8,9},{9,8},{10,11... | collective-permute-start | bytes 417800 | tf_op jit(solution)/shard_map/queries/ppermute | solution.py:289
  49.6 7.4 %collective-permute-start.4 = (bf16[272,256]{1,0:T(8,128)(2,1)S(1)}, bf16[272,256]{1,0:T(8,128)(2,1)S(1)}, u32[]{:S(2)}, u32[]{:S(2)}) collective-permute-start(bf16[272,256]{1,0:T(8,128)(2,1)S(1)} %collective-permute-done.refs_1_.refs_9_), channel_id=1, source_target_pairs={{0,1},{1,0},{2,3},{3,2},{4,5},{5,4},{6,7},{7,6},{8,9},{9,8},{10,11... | collective-permute-start | bytes 417800 | tf_op jit(solution)/shard_map/queries/ppermute | solution.py:289
  51.7 5.9 %collective-permute-start.5 = (bf16[272,256]{1,0:T(8,128)(2,1)S(1)}, bf16[272,256]{1,0:T(8,128)(2,1)S(1)}, u32[]{:S(2)}, u32[]{:S(2)}) collective-permute-start(bf16[272,256]{1,0:T(8,128)(2,1)S(1)} %collective-permute-done.1.refs_2_.refs_10_), channel_id=1, source_target_pairs={{0,1},{1,0},{2,3},{3,2},{4,5},{5,4},{6,7},{7,6},{8,9},{9,8},{10,11... | collective-permute-start | bytes 417800 | tf_op jit(solution)/shard_map/queries/ppermute | solution.py:289
  54.4 4.0 %collective-permute-start.6 = (bf16[272,256]{1,0:T(8,128)(2,1)S(1)}, bf16[272,256]{1,0:T(8,128)(2,1)S(1)}, u32[]{:S(2)}, u32[]{:S(2)}) collective-permute-start(bf16[272,256]{1,0:T(8,128)(2,1)S(1)} %collective-permute-done.2.refs_3_.refs_11_), channel_id=1, source_target_pairs={{0,1},{1,0},{2,3},{3,2},{4,5},{5,4},{6,7},{7,6},{8,9},{9,8},{10,11... | collective-permute-start | bytes 417800 | tf_op jit(solution)/shard_map/queries/ppermute | solution.py:289
  66.1 0.9 copy-start.5
  67.0 0.9 copy-start.8
  67.9 0.9 copy-start.11
  68.8 0.9 copy-start.14
  71.6 0.9 copy-start.23
  76.1 1.0 copy-start.2
  77.7 20.6 %copy-start.6 = (bf16[272,256]{1,0:T(8,128)(2,1)S(1)}, bf16[272,256]{1,0:T(8,128)(2,1)}, u32[]{:S(2)}) copy-start(bf16[272,256]{1,0:T(8,128)(2,1)} %copy-done.4) | copy-start | bytes 417796
  77.7 20.6 %copy-start.9 = (bf16[272,256]{1,0:T(8,128)(2,1)S(1)}, bf16[272,256]{1,0:T(8,128)(2,1)}, u32[]{:S(2)}) copy-start(bf16[272,256]{1,0:T(8,128)(2,1)} %copy-done.7) | copy-start | bytes 417796
  77.7 20.6 %copy-start.12 = (bf16[272,256]{1,0:T(8,128)(2,1)S(1)}, bf16[272,256]{1,0:T(8,128)(2,1)}, u32[]{:S(2)}) copy-start(bf16[272,256]{1,0:T(8,128)(2,1)} %copy-done.10) | copy-start | bytes 417796
  77.7 20.6 %copy-start.15 = (bf16[272,256]{1,0:T(8,128)(2,1)S(1)}, bf16[272,256]{1,0:T(8,128)(2,1)}, u32[]{:S(2)}) copy-start(bf16[272,256]{1,0:T(8,128)(2,1)} %copy-done.13) | copy-start | bytes 417796
  77.7 20.6 %copy-start.18 = (bf16[272,256]{1,0:T(8,128)(2,1)S(1)}, bf16[272,256]{1,0:T(8,128)(2,1)}, u32[]{:S(2)}) copy-start(bf16[272,256]{1,0:T(8,128)(2,1)} %copy-done.16) | copy-start | bytes 417796
  77.7 20.6 %copy-start.21 = (bf16[272,256]{1,0:T(8,128)(2,1)S(1)}, bf16[272,256]{1,0:T(8,128)(2,1)}, u32[]{:S(2)}) copy-start(bf16[272,256]{1,0:T(8,128)(2,1)} %copy-done.19) | copy-start | bytes 417796
  77.7 41.4 %copy-start.26 = (s32[32,8,128]{2,1,0:T(8,128)S(1)}, s32[32,8,128]{2,1,0:T(8,128)}, u32[]{:S(2)}) copy-start(s32[32,8,128]{2,1,0:T(8,128)} %copy-done.25) | copy-start | bytes 393220
  77.7 33.2 %all-to-all-start.4 = ((bf16[32,64,256]{2,1,0:T(8,128)(2,1)}), bf16[32,64,256]{2,1,0:T(8,128)(2,1)S(1)}, u32[]{:S(2)}, u32[]{:S(2)}) async-start(bf16[32,64,256]{2,1,0:T(8,128)(2,1)} %bitcast.13), calls=%async_computation.4 | async-start | bytes 2097152 | tf_op jit(solution)/shard_map/cold/all_to_all | solution.py:285
  85.9 7.2 %collective-permute-start.14 = (bf16[256,256]{1,0:T(8,128)(2,1)S(1)}, bf16[256,256]{1,0:T(8,128)(2,1)S(1)}, u32[]{:S(2)}, u32[]{:S(2)}) collective-permute-start(bf16[256,256]{1,0:T(8,128)(2,1)S(1)} %get-tuple-element.31.refs_0_), channel_id=1, source_target_pairs={{0,2},{1,3},{2,4},{3,5},{4,6},{5,7},{6,0},{7,1},{8,10},{9,11},{10,... | collective-permute-start | bytes 393224 | tf_op jit(solution)/shard_map/grads/ppermute | solution.py:293
  87.2 7.8 %collective-permute-start.15 = (bf16[256,256]{1,0:T(8,128)(2,1)S(1)}, bf16[256,256]{1,0:T(8,128)(2,1)S(1)}, u32[]{:S(2)}, u32[]{:S(2)}) collective-permute-start(bf16[256,256]{1,0:T(8,128)(2,1)S(1)} %get-tuple-element.31.refs_0_), channel_id=1, source_target_pairs={{0,4},{1,5},{2,6},{3,7},{4,0},{5,1},{6,2},{7,3},{8,12},{9,13},{10,... | collective-permute-start | bytes 393224 | tf_op jit(solution)/shard_map/grads/ppermute | solution.py:293
  89.7 7.3 %collective-permute-start.16 = (bf16[256,256]{1,0:T(8,128)(2,1)S(1)}, bf16[256,256]{1,0:T(8,128)(2,1)S(1)}, u32[]{:S(2)}, u32[]{:S(2)}) collective-permute-start(bf16[256,256]{1,0:T(8,128)(2,1)S(1)} %get-tuple-element.31.refs_0_), channel_id=1, source_target_pairs={{0,6},{1,7},{2,0},{3,1},{4,2},{5,3},{6,4},{7,5},{8,14},{9,15},{10,... | collective-permute-start | bytes 393224 | tf_op jit(solution)/shard_map/grads/ppermute | solution.py:293
  90.8 6.2 %collective-permute-start.17 = (bf16[256,256]{1,0:T(8,128)(2,1)S(1)}, bf16[256,256]{1,0:T(8,128)(2,1)S(1)}, u32[]{:S(2)}, u32[]{:S(2)}) collective-permute-start(bf16[256,256]{1,0:T(8,128)(2,1)S(1)} %get-tuple-element.31.refs_0_), channel_id=1, source_target_pairs={{0,1},{1,0},{2,3},{3,2},{4,5},{5,4},{6,7},{7,6},{8,9},{9,8},{10,11... | collective-permute-start | bytes 393224 | tf_op jit(solution)/shard_map/grads/ppermute | solution.py:289
  93.1 3.9 %collective-permute-start.18 = (bf16[256,256]{1,0:T(8,128)(2,1)S(1)}, bf16[256,256]{1,0:T(8,128)(2,1)S(1)}, u32[]{:S(2)}, u32[]{:S(2)}) collective-permute-start(bf16[256,256]{1,0:T(8,128)(2,1)S(1)} %collective-permute-done.14.refs_1_), channel_id=1, source_target_pairs={{0,1},{1,0},{2,3},{3,2},{4,5},{5,4},{6,7},{7,6},{8,9},{9,8},{10,11... | collective-permute-start | bytes 393224 | tf_op jit(solution)/shard_map/grads/ppermute | solution.py:289
  95.0 2.9 %collective-permute-start.19 = (bf16[256,256]{1,0:T(8,128)(2,1)S(1)}, bf16[256,256]{1,0:T(8,128)(2,1)S(1)}, u32[]{:S(2)}, u32[]{:S(2)}) collective-permute-start(bf16[256,256]{1,0:T(8,128)(2,1)S(1)} %collective-permute-done.15.refs_2_), channel_id=1, source_target_pairs={{0,1},{1,0},{2,3},{3,2},{4,5},{5,4},{6,7},{7,6},{8,9},{9,8},{10,11... | collective-permute-start | bytes 393224 | tf_op jit(solution)/shard_map/grads/ppermute | solution.py:289
  96.9 1.3 collective-permute-start.20
  111.0 17.3 %all-to-all-start.2 = ((bf16[32,8,256]{2,1,0:T(8,128)(2,1)}), bf16[32,8,256]{2,1,0:T(8,128)(2,1)S(1)}, u32[]{:S(2)}, u32[]{:S(2)}) async-start(bf16[32,8,256]{2,1,0:T(8,128)(2,1)} %bitcast.6), calls=%async_computation.2 | async-start | bytes 262144 | tf_op jit(solution)/shard_map/hot_parts/all_to_all | solution.py:285
  119.1 13.7 %copy-start.36 = (bf16[256,256]{1,0:T(8,128)(2,1)S(1)}, bf16[256,256]{1,0:T(8,128)(2,1)}, u32[]{:S(2)}) copy-start(bf16[256,256]{1,0:T(8,128)(2,1)} %copy-done.35) | copy-start | bytes 393220
  121.1 32.6 %collective-permute-start.28 = (bf16[4,256,256]{2,1,0:T(8,128)(2,1)S(1)}, bf16[4,256,256]{2,1,0:T(8,128)(2,1)S(1)}, u32[]{:S(2)}, u32[]{:S(2)}) collective-permute-start(bf16[4,256,256]{2,1,0:T(8,128)(2,1)S(1)} %shard_map.122), channel_id=1, source_target_pairs={{0,1},{1,0},{2,3},{3,2},{4,5},{5,4},{6,7},{7,6},{8,9},{9,8},{10,11... | collective-permute-start | bytes 1572872 | tf_op jit(solution)/shard_map/cold_cross/ppermute | solution.py:289
  129.0 15.2 %all-to-all-start.3 = ((bf16[32,8,256]{2,1,0:T(8,128)(2,1)}), bf16[32,8,256]{2,1,0:T(8,128)(2,1)S(1)}, u32[]{:S(2)}, u32[]{:S(2)}) async-start(bf16[32,8,256]{2,1,0:T(8,128)(2,1)} %shard_map.119), calls=%async_computation.3 | async-start | bytes 262144 | tf_op jit(solution)/shard_map/hot_whole/all_to_all | solution.py:285
  132.9 8.5 %collective-permute-start.7 = (bf16[256,256]{1,0:T(8,128)(2,1)S(1)}, bf16[256,256]{1,0:T(8,128)(2,1)S(1)}, u32[]{:S(2)}, u32[]{:S(2)}) collective-permute-start(bf16[256,256]{1,0:T(8,128)(2,1)S(1)} %copy-done.36), channel_id=1, source_target_pairs={{0,2},{1,3},{2,4},{3,5},{4,6},{5,7},{6,0},{7,1},{8,10},{9,11},{10,... | collective-permute-start | bytes 393224 | tf_op jit(solution)/shard_map/items/ppermute | solution.py:293
  134.2 8.3 %collective-permute-start.8 = (bf16[256,256]{1,0:T(8,128)(2,1)S(1)}, bf16[256,256]{1,0:T(8,128)(2,1)S(1)}, u32[]{:S(2)}, u32[]{:S(2)}) collective-permute-start(bf16[256,256]{1,0:T(8,128)(2,1)S(1)} %copy-done.36), channel_id=1, source_target_pairs={{0,4},{1,5},{2,6},{3,7},{4,0},{5,1},{6,2},{7,3},{8,12},{9,13},{10,... | collective-permute-start | bytes 393224 | tf_op jit(solution)/shard_map/items/ppermute | solution.py:293
  136.6 7.6 %collective-permute-start.9 = (bf16[256,256]{1,0:T(8,128)(2,1)S(1)}, bf16[256,256]{1,0:T(8,128)(2,1)S(1)}, u32[]{:S(2)}, u32[]{:S(2)}) collective-permute-start(bf16[256,256]{1,0:T(8,128)(2,1)S(1)} %copy-done.36), channel_id=1, source_target_pairs={{0,6},{1,7},{2,0},{3,1},{4,2},{5,3},{6,4},{7,5},{8,14},{9,15},{10,... | collective-permute-start | bytes 393224 | tf_op jit(solution)/shard_map/items/ppermute | solution.py:293
  137.8 7.3 %collective-permute-start.10 = (bf16[256,256]{1,0:T(8,128)(2,1)S(1)}, bf16[256,256]{1,0:T(8,128)(2,1)S(1)}, u32[]{:S(2)}, u32[]{:S(2)}) collective-permute-start(bf16[256,256]{1,0:T(8,128)(2,1)S(1)} %copy-done.36), channel_id=1, source_target_pairs={{0,1},{1,0},{2,3},{3,2},{4,5},{5,4},{6,7},{7,6},{8,9},{9,8},{10,11... | collective-permute-start | bytes 393224 | tf_op jit(solution)/shard_map/items/ppermute | solution.py:289
  141.3 5.7 %collective-permute-start.11 = (bf16[256,256]{1,0:T(8,128)(2,1)S(1)}, bf16[256,256]{1,0:T(8,128)(2,1)S(1)}, u32[]{:S(2)}, u32[]{:S(2)}) collective-permute-start(bf16[256,256]{1,0:T(8,128)(2,1)S(1)} %collective-permute-done.7.refs_1_), channel_id=1, source_target_pairs={{0,1},{1,0},{2,3},{3,2},{4,5},{5,4},{6,7},{7,6},{8,9},{9,8},{10,11... | collective-permute-start | bytes 393224 | tf_op jit(solution)/shard_map/items/ppermute | solution.py:289
  142.5 7.1 %collective-permute-start.12 = (bf16[256,256]{1,0:T(8,128)(2,1)S(1)}, bf16[256,256]{1,0:T(8,128)(2,1)S(1)}, u32[]{:S(2)}, u32[]{:S(2)}) collective-permute-start(bf16[256,256]{1,0:T(8,128)(2,1)S(1)} %collective-permute-done.8.refs_2_), channel_id=1, source_target_pairs={{0,1},{1,0},{2,3},{3,2},{4,5},{5,4},{6,7},{7,6},{8,9},{9,8},{10,11... | collective-permute-start | bytes 393224 | tf_op jit(solution)/shard_map/items/ppermute | solution.py:289
  144.2 15.8 %copy-start.32 = (f32[256,256]{1,0:T(8,128)S(1)}, f32[256,256]{1,0:T(8,128)}, u32[]{:S(2)}) copy-start(f32[256,256]{1,0:T(8,128)} %copy-done.31) | copy-start | bytes 786436
  144.2 15.8 %copy-start.34 = (f32[256,1]{1,0:T(8,128)S(1)}, f32[256,1]{1,0:T(8,128)}, u32[]{:S(2)}) copy-start(f32[256,1]{1,0:T(8,128)} %copy-done.33) | copy-start | bytes 3076
  144.2 9.4 %collective-permute-start.21 = (bf16[256,256]{1,0:T(8,128)(2,1)S(1)}, bf16[256,256]{1,0:T(8,128)(2,1)S(1)}, u32[]{:S(2)}, u32[]{:S(2)}) collective-permute-start(bf16[256,256]{1,0:T(8,128)(2,1)S(1)} %bitcast.14), channel_id=1, source_target_pairs={{0,2},{1,3},{2,4},{3,5},{4,6},{5,7},{6,0},{7,1},{8,10},{9,11},{10,... | collective-permute-start | bytes 393224 | tf_op jit(solution)/shard_map/hot_blocks/ppermute | solution.py:293
  145.7 10.4 %collective-permute-start.22 = (bf16[256,256]{1,0:T(8,128)(2,1)S(1)}, bf16[256,256]{1,0:T(8,128)(2,1)S(1)}, u32[]{:S(2)}, u32[]{:S(2)}) collective-permute-start(bf16[256,256]{1,0:T(8,128)(2,1)S(1)} %bitcast.15), channel_id=1, source_target_pairs={{0,4},{1,5},{2,6},{3,7},{4,0},{5,1},{6,2},{7,3},{8,12},{9,13},{10,... | collective-permute-start | bytes 393224 | tf_op jit(solution)/shard_map/hot_blocks/ppermute | solution.py:293
  147.0 13.1 %copy-start.38 = (bf16[256,256]{1,0:T(8,128)(2,1)S(1)}, bf16[256,256]{1,0:T(8,128)(2,1)}, u32[]{:S(2)}) copy-start(bf16[256,256]{1,0:T(8,128)(2,1)} %copy-done.37) | copy-start | bytes 393220
  147.7 8.9 %collective-permute-start.23 = (bf16[256,256]{1,0:T(8,128)(2,1)S(1)}, bf16[256,256]{1,0:T(8,128)(2,1)S(1)}, u32[]{:S(2)}, u32[]{:S(2)}) collective-permute-start(bf16[256,256]{1,0:T(8,128)(2,1)S(1)} %bitcast.16), channel_id=1, source_target_pairs={{0,6},{1,7},{2,0},{3,1},{4,2},{5,3},{6,4},{7,5},{8,14},{9,15},{10,... | collective-permute-start | bytes 393224 | tf_op jit(solution)/shard_map/hot_blocks/ppermute | solution.py:293
  149.6 10.5 %copy-start.40 = (bf16[256,256]{1,0:T(8,128)(2,1)S(1)}, bf16[256,256]{1,0:T(8,128)(2,1)}, u32[]{:S(2)}) copy-start(bf16[256,256]{1,0:T(8,128)(2,1)} %copy-done.39) | copy-start | bytes 393220
  150.2 6.5 %collective-permute-start.13 = (bf16[256,256]{1,0:T(8,128)(2,1)S(1)}, bf16[256,256]{1,0:T(8,128)(2,1)S(1)}, u32[]{:S(2)}, u32[]{:S(2)}) collective-permute-start(bf16[256,256]{1,0:T(8,128)(2,1)S(1)} %collective-permute-done.9.refs_3_), channel_id=1, source_target_pairs={{0,1},{1,0},{2,3},{3,2},{4,5},{5,4},{6,7},{7,6},{8,9},{9,8},{10,11... | collective-permute-start | bytes 393224 | tf_op jit(solution)/shard_map/items/ppermute | solution.py:289
  153.6 6.5 %copy-start.42 = (bf16[256,256]{1,0:T(8,128)(2,1)S(1)}, bf16[256,256]{1,0:T(8,128)(2,1)}, u32[]{:S(2)}) copy-start(bf16[256,256]{1,0:T(8,128)(2,1)} %copy-done.41) | copy-start | bytes 393220
  153.6 3.6 %collective-permute-start.24 = (bf16[256,256]{1,0:T(8,128)(2,1)S(1)}, bf16[256,256]{1,0:T(8,128)(2,1)S(1)}, u32[]{:S(2)}, u32[]{:S(2)}) collective-permute-start(bf16[256,256]{1,0:T(8,128)(2,1)S(1)} %bitcast.17), channel_id=1, source_target_pairs={{0,1},{1,0},{2,3},{3,2},{4,5},{5,4},{6,7},{7,6},{8,9},{9,8},{10,11... | collective-permute-start | bytes 393224 | tf_op jit(solution)/shard_map/hot_blocks/ppermute | solution.py:289
  153.7 6.3 %collective-permute-start.25 = (bf16[256,256]{1,0:T(8,128)(2,1)S(1)}, bf16[256,256]{1,0:T(8,128)(2,1)S(1)}, u32[]{:S(2)}, u32[]{:S(2)}) collective-permute-start(bf16[256,256]{1,0:T(8,128)(2,1)S(1)} %collective-permute-done.21.refs_1_), channel_id=1, source_target_pairs={{0,1},{1,0},{2,3},{3,2},{4,5},{5,4},{6,7},{7,6},{8,9},{9,8},{10,11... | collective-permute-start | bytes 393224 | tf_op jit(solution)/shard_map/hot_blocks/ppermute | solution.py:289
  156.1 5.7 %collective-permute-start.26 = (bf16[256,256]{1,0:T(8,128)(2,1)S(1)}, bf16[256,256]{1,0:T(8,128)(2,1)S(1)}, u32[]{:S(2)}, u32[]{:S(2)}) collective-permute-start(bf16[256,256]{1,0:T(8,128)(2,1)S(1)} %collective-permute-done.22.refs_2_), channel_id=1, source_target_pairs={{0,1},{1,0},{2,3},{3,2},{4,5},{5,4},{6,7},{7,6},{8,9},{9,8},{10,11... | collective-permute-start | bytes 393224 | tf_op jit(solution)/shard_map/hot_blocks/ppermute | solution.py:289
  156.6 5.3 %collective-permute-start.27 = (bf16[256,256]{1,0:T(8,128)(2,1)S(1)}, bf16[256,256]{1,0:T(8,128)(2,1)S(1)}, u32[]{:S(2)}, u32[]{:S(2)}) collective-permute-start(bf16[256,256]{1,0:T(8,128)(2,1)S(1)} %collective-permute-done.23.refs_3_), channel_id=1, source_target_pairs={{0,1},{1,0},{2,3},{3,2},{4,5},{5,4},{6,7},{7,6},{8,9},{9,8},{10,11... | collective-permute-start | bytes 393224 | tf_op jit(solution)/shard_map/hot_blocks/ppermute | solution.py:289
  156.8 6.6 %collective-permute-start.29 = (bf16[256,256]{1,0:T(8,128)(2,1)S(1)}, bf16[256,256]{1,0:T(8,128)(2,1)S(1)}, u32[]{:S(2)}, u32[]{:S(2)}) collective-permute-start(bf16[256,256]{1,0:T(8,128)(2,1)S(1)} %get-tuple-element.34), channel_id=1, source_target_pairs={{0,2},{1,3},{2,4},{3,5},{4,6},{5,7},{6,0},{7,1},{8,10},{9,11},{10,... | collective-permute-start | bytes 393224 | tf_op jit(solution)/shard_map/cold_shift/ppermute | solution.py:293
  157.2 9.2 %collective-permute-start.30 = (bf16[256,256]{1,0:T(8,128)(2,1)S(1)}, bf16[256,256]{1,0:T(8,128)(2,1)S(1)}, u32[]{:S(2)}, u32[]{:S(2)}) collective-permute-start(bf16[256,256]{1,0:T(8,128)(2,1)S(1)} %get-tuple-element.35), channel_id=1, source_target_pairs={{0,4},{1,5},{2,6},{3,7},{4,0},{5,1},{6,2},{7,3},{8,12},{9,13},{10,... | collective-permute-start | bytes 393224 | tf_op jit(solution)/shard_map/cold_shift/ppermute | solution.py:293
  160.1 6.4 %collective-permute-start.31 = (bf16[256,256]{1,0:T(8,128)(2,1)S(1)}, bf16[256,256]{1,0:T(8,128)(2,1)S(1)}, u32[]{:S(2)}, u32[]{:S(2)}) collective-permute-start(bf16[256,256]{1,0:T(8,128)(2,1)S(1)} %get-tuple-element.36), channel_id=1, source_target_pairs={{0,6},{1,7},{2,0},{3,1},{4,2},{5,3},{6,4},{7,5},{8,14},{9,15},{10,... | collective-permute-start | bytes 393224 | tf_op jit(solution)/shard_map/cold_shift/ppermute | solution.py:293
  (19 other events, 13.2 us)

commit v3 on v2

v3 whole, which is shorter than its diff:
```python
import jax
import jax.numpy as jnp
from jax import lax
from jax.experimental import pallas as pl
from jax.experimental.pallas import tpu as pltpu
from jax.sharding import PartitionSpec as P


epsilon = 1e-06
F32 = jnp.float32
BF16 = jnp.bfloat16
NN = (((1,), (0,)), ((), ()))
NT = (((1,), (1,)), ((), ()))


def mm(a, b, dims=NN):
    return lax.dot_general(a, b, dims, preferred_element_type=F32)


def iota(shape, dim):
    return lax.broadcasted_iota(jnp.int32, shape, dim)


HBM = pltpu.HBM


class Late:
    def __init__(self, source, buffer, sem):
        self.copy = pltpu.make_async_copy(source, buffer, sem)
        self.buffer = buffer
        self.copy.start()
        self.waits = True

    def get(self):
        if self.waits:
            self.copy.wait()
            self.waits = False
        return self.buffer


def call(kernel, outs, *args, kinds=None, scratch=(), flops=0, grid=(1,), in_specs=None, out_specs=None):
    kinds = kinds or ["v"] * len(args)
    late = [k for k, kind in enumerate(kinds) if isinstance(kind, slice)]
    specs, operands = [], []
    for k, (kind, arg) in enumerate(zip(kinds, args)):
        if kind == "s":
            specs.append(pl.BlockSpec(memory_space=pltpu.SMEM))
        elif k in late:
            specs.append(pl.BlockSpec(memory_space=HBM))
            arg = pltpu.with_memory_space_constraint(arg, HBM)
        else:
            specs.append(in_specs[k] if in_specs else whole(arg))
            if kind == "h":
                arg = pltpu.with_memory_space_constraint(arg, HBM)
        operands.append(arg)
    buffers = []
    for k in late:
        rows = kinds[k].stop - kinds[k].start
        buffers.append(pltpu.VMEM((rows,) + args[k].shape[1:], args[k].dtype))

    def run(*refs):
        refs, extra = list(refs[: len(refs) - len(late) - 1]), refs[len(refs) - len(late) - 1 :]
        for n, k in enumerate(late):
            refs[k] = Late(refs[k].at[kinds[k]], extra[n], extra[-1].at[n])
        kernel(*refs)

    moved = sum(a.size * a.dtype.itemsize for a in args)
    return pl.pallas_call(
        run if late else kernel,
        out_shape=list(outs),
        grid=grid,
        in_specs=specs,
        out_specs=out_specs or [whole(o) for o in outs],
        scratch_shapes=list(scratch) + (buffers + [pltpu.SemaphoreType.DMA((len(late),))] if late else []),
        compiler_params=pltpu.CompilerParams(vmem_limit_bytes=24 << 20),
        cost_estimate=pl.CostEstimate(flops=flops, bytes_accessed=moved, transcendentals=0),
    )(*operands)


def shape(dims, dtype):
    return jax.ShapeDtypeStruct(dims, dtype)


def expander(owners, cap, base, width):
    return ((iota((owners, width), 1) + base) // cap == iota((owners, width), 0)).astype(F32).astype(BF16)


LANES = 128


def make_requests(owners, cap):
    def kernel(parent_ref, place_ref, tally_ref, table, rank_ref, rank_t_ref, ask_ref, table_low_ref, row_ref):
        slots, pairs = parent_ref.shape
        line = iota((LANES, pairs), 0)
        tally = tally_ref[...]
        named = jnp.zeros((LANES, pairs), F32)
        where = jnp.zeros((LANES, pairs), F32)
        for c in range(slots):
            hit = jnp.logical_and(parent_ref[c : c + 1, :] == line, tally > c)
            named = jnp.where(hit, 1.0, named)
            where = jnp.where(hit, place_ref[c : c + 1, :].astype(F32), where)
        before = (iota((pairs, pairs), 0) < iota((pairs, pairs), 1)).astype(F32).astype(BF16)
        rank_t = jnp.where(named > 0, mm(named.astype(BF16), before), -1.0)
        rank = rank_t.T
        rank_t_ref[...] = rank_t.astype(BF16)
        rank_ref[...] = rank.astype(BF16)
        where = where.T.astype(jnp.int32)
        high = (where // 64).astype(F32).astype(BF16)
        low = (where % 64).astype(F32).astype(BF16)
        rank = rank.astype(BF16)
        total = owners * cap
        width = 512
        for base in range(0, total, width):
            spread = expander(LANES, cap, base, width)
            want = (iota((pairs, width), 1) % cap).astype(F32)
            place = mm(high, spread) * 64.0 + mm(low, spread)
            row_ref[:, base : base + width] = jnp.sum(
                jnp.where(mm(rank, spread) == want, place, 0.0), axis=0, keepdims=True
            )
        for o in range(owners):
            ask = row_ref[:, o * cap : (o + 1) * cap].astype(jnp.int32)
            ask_ref[o, :, 0:cap] = jnp.broadcast_to(ask, (ask_ref.shape[1], cap))
        table_low_ref[...] = table.get()[...].astype(BF16)

    return kernel


def normalize(rows):
    radius = jnp.sqrt(jnp.sum(rows * rows, axis=1, keepdims=True) + epsilon)
    return rows / radius, radius


def unit_queries(query_ref, lines_ref, send_ref):
    pairs = query_ref.shape[0]
    slots = lines_ref.shape[0]
    unit, _ = normalize(query_ref[...].astype(F32))
    send_ref[0:pairs, :] = unit.astype(BF16)
    tail = send_ref.shape[0] - pairs
    line = iota((tail, pairs), 0)
    extra = jnp.zeros((tail, pairs), F32)
    for h in range(slots):
        row = lines_ref[h : h + 1, :]
        extra = jnp.where(line == h, (row // 64).astype(F32), extra)
        extra = jnp.where(line == h + slots, (row % 64).astype(F32), extra)
    send_ref[pairs:, :] = extra.astype(BF16)


def prepare(cap):
    def kernel(rank_ref, rank_t_ref, lines_ref, hot_ref, pick_ref, place_ref, hot_sum_ref, lines_t_ref):
        pairs = rank_ref.shape[0]
        slots = lines_ref.shape[0]
        width = pick_ref.shape[1]
        base = pl.program_id(0) * width

        @pl.when(pl.program_id(0) == 0)
        def _():
            hot_sum_ref[...] = jnp.zeros_like(hot_sum_ref)
            line = iota((LANES, pairs), 0)
            lines = jnp.zeros((LANES, pairs), F32)
            for h in range(slots):
                lines = jnp.where(line == h, lines_ref[h : h + 1, :].astype(F32), lines)
            lines_t_ref[...] = lines.T.astype(jnp.int32)

        spread = expander(LANES, cap, base, width)
        want = (iota((pairs, width), 1) % cap).astype(F32)
        pick_ref[...] = (mm(rank_ref[...], spread) == want).astype(F32).astype(BF16)
        spread_t = ((iota((width, LANES), 0) + base) // cap == iota((width, LANES), 1))
        want_t = (iota((width, pairs), 0) % cap).astype(F32)
        hit = mm(spread_t.astype(F32).astype(BF16), rank_t_ref[...]) == want_t
        place_ref[...] = hit.astype(F32).astype(BF16)
        column = iota((pairs, width), 1) + base
        counts = jnp.zeros((pairs, width), F32)
        for h in range(slots):
            counts += (lines_t_ref[:, h : h + 1] == column).astype(F32)
        hot_sum_ref[...] += mm(counts.astype(BF16), hot_ref[...])

    return kernel


def fetch(ask_ref, table_ref, out_ref):
    rows = table_ref.shape[0]
    group, cap = out_ref.shape[0], out_ref.shape[1]
    diagonal = iota((cap, cap), 0) == iota((cap, cap), 1)
    columns = []
    for g in range(group):
        ask = ask_ref[pl.program_id(0) * group + g, 0:1, 0:cap]
        columns.append(jnp.sum(jnp.where(diagonal, ask, 0).astype(F32), axis=1, keepdims=True))
    column = jnp.concatenate(columns, axis=0).astype(jnp.int32)
    hit = (column == iota((group * cap, rows), 1)).astype(F32).astype(BF16)
    out_ref[...] = mm(hit, table_ref[...]).astype(BF16).reshape(out_ref.shape)


def loss_side(own_low, others, total_ref, sharpness, additive):
    rows = own_low.shape[0]
    for i, late in enumerate(others):
        other = late.get()[...]
        grad = jax.nn.sigmoid(sharpness * mm(own_low, other, NT) + additive)
        if i == 0:
            grad = grad - (iota((rows, rows), 0) == iota((rows, rows), 1)).astype(F32)
            total_ref[...] = mm(grad.astype(BF16), other)
        else:
            total_ref[...] += mm(grad.astype(BF16), other)
    return sharpness * total_ref[...]


def project(unit, radius, direction):
    inner = jnp.sum(unit * direction, axis=1, keepdims=True)
    return (direction - unit * inner) / radius


def item_side(blocks):
    def kernel(sharp_ref, add_ref, fetched_ref, pick_ref, place, hot_sum, *refs):
        queries, (sides_ref, out_ref, total_ref, stage_ref, sem) = refs[:blocks], refs[blocks:]
        pairs = total_ref.shape[0]
        unit, radius = normalize(mm(pick_ref[...], fetched_ref[...]) + hot_sum.get()[...])
        low = unit.astype(BF16)
        sides_ref[0:pairs, :] = low
        direction = loss_side(low, queries, total_ref, sharp_ref[0], add_ref[0])
        grad = project(unit, radius, direction).astype(BF16)
        sides_ref[pairs:, :] = grad
        place_ref = place.get()
        steps = sem.shape[0]
        width = place_ref.shape[0] // steps

        def leave(i):
            part = pl.ds(pl.multiple_of(i * width, width), width)
            return pltpu.make_async_copy(stage_ref.at[part], out_ref.at[part], sem.at[i])

        def step(i, _):
            part = pl.ds(pl.multiple_of(i * width, width), width)
            stage_ref[part, :] = mm(place_ref[part, :], grad).astype(BF16)
            leave(i).start()
            return 0

        def finish(i, _):
            leave(i).wait()
            return 0

        lax.fori_loop(0, steps, step, 0)
        lax.fori_loop(0, steps, finish, 0)

    return kernel


def query_side(sharp_ref, add_ref, query_ref, *refs):
    items, (out_ref, total_ref) = refs[:-2], refs[-2:]
    unit, radius = normalize(query_ref[...].astype(F32))
    direction = loss_side(unit.astype(BF16), items, total_ref, sharp_ref[0], add_ref[0])
    out_ref[...] = project(unit, radius, direction)


def hot_terms(blocks, slots):
    def kernel(block_ref, *refs):
        grads, lines, (out_ref, total_ref) = refs[:blocks], refs[blocks : 2 * blocks], refs[2 * blocks :]
        width, pairs = out_ref.shape
        row = (iota((width, pairs), 0) + block_ref[0] * width).astype(F32)
        for i, (grad, line) in enumerate(zip(grads, lines)):
            line = line.get()[...].astype(F32)
            counts = jnp.zeros((width, pairs), F32)
            for h in range(slots):
                counts += (line[h : h + 1, :] * 64.0 + line[h + slots : h + slots + 1, :] == row).astype(F32)
            term = mm(counts.astype(BF16), grad.get()[...])
            total_ref[...] = term if i == 0 else total_ref[...] + term
        out_ref[...] = total_ref[...].astype(BF16)

    return kernel


def hot_sum_spread(parts_ref, out_ref):
    piece = jnp.sum(parts_ref[...].astype(F32), axis=0, keepdims=True)
    out_ref[...] = jnp.broadcast_to(piece, out_ref.shape).astype(BF16)


def widen(blocks):
    def kernel(block_ref, *refs):
        part_refs, out_ref = refs[:blocks], refs[blocks]
        chips = blocks // 2
        width = part_refs[0].shape[0]
        mine, core = block_ref[0] // 2, block_ref[0] % 2
        for i, ref in enumerate(part_refs):
            chip = (mine + chips - i % chips) % chips
            index = chip * 2 + (core if i < chips else 1 - core)
            out_ref[pl.ds(pl.multiple_of(index * width, width), width), :] = ref[...].astype(F32)

    return kernel


def cold_terms(same_core):
    def kernel(block_ref, ask_ref, grad_ref, out_ref, row_ref):
        width, total = out_ref.shape[1], grad_ref.shape[0]
        owners, chips = ask_ref.shape[0], pl.num_programs(0)
        cap = total // owners

        @pl.when(pl.program_id(0) == 0)
        def _():
            for o in range(owners):
                row_ref[:, o * cap : (o + 1) * cap] = ask_ref[o, 0:1, 0:cap]

        core = block_ref[0] % 2
        core = core if same_core else 1 - core
        chip = (block_ref[0] // 2 + pl.program_id(0)) % chips
        row = iota((width, total), 0) + (chip * 2 + core) * width
        hit = (row_ref[...] == row).astype(F32).astype(BF16)
        out_ref[0] = mm(hit, grad_ref[...]).astype(out_ref.dtype)

    return kernel


def cold_join(mine_ref, theirs_ref, keep_ref, *send_refs):
    keep_ref[...] = mine_ref[0] + theirs_ref[0].astype(F32)
    for d, ref in enumerate(send_refs):
        ref[...] = (mine_ref[d + 1] + theirs_ref[d + 1].astype(F32)).astype(BF16)


def add_parts(keep_ref, *refs):
    part_refs, out_ref = refs[:-1], refs[-1]
    total = keep_ref[...]
    for ref in part_refs:
        total += ref[...].astype(F32)
    out_ref[...] = total


def whole(array):
    rank = len(array.shape)
    return pl.BlockSpec(array.shape, lambda i: (0,) * rank)


def swap(array, axis):
    return lax.all_to_all(array, axis, split_axis=0, concat_axis=0, tiled=True)


def cross(array, blocks):
    return lax.ppermute(array, "blk", [(i, i ^ 1) for i in range(blocks)])


def shift(array, blocks, d):
    return lax.ppermute(array, "blk", [(i, (i + 2 * d) % blocks) for i in range(blocks)])


def gather_blocks(array, blocks):
    first = cross(array, blocks)
    mine = [shift(array, blocks, d) for d in range(1, blocks // 2)]
    return [array] + mine + [first] + [cross(m, blocks) for m in mine]


def step_of(queries, hot_table, cold_table, lines, parent, place, tally, sharpness, additive):
    pairs, width = queries.shape
    owners, blocks = lax.axis_size("shard"), lax.axis_size("blk")
    chips = blocks // 2
    slots = parent.shape[1]
    cap = 2 * pairs * slots // owners
    total = owners * cap
    rows = cold_table.shape[0]
    hot_rows = hot_table.shape[0]
    block = lax.axis_index("blk").astype(jnp.int32).reshape(1)

    rank, rank_t, ask, table_low = call(
        make_requests(owners, cap),
        [shape((pairs, LANES), BF16), shape((LANES, pairs), BF16), HBM((owners, 8, LANES), jnp.int32), shape((rows, width), BF16)],
        parent.T, place.T, tally.reshape(1, pairs), cold_table,
        kinds=["h", "h", "h", slice(0, rows)],
        scratch=[pltpu.VMEM((1, total), F32)],
        flops=2 * pairs * total * LANES * 3,
    )
    asked = swap(ask, "shard")

    group = 4
    (looked,) = call(
        fetch,
        [HBM((owners, cap, width), BF16)],
        asked, table_low,
        grid=(owners // group,),
        out_specs=[pl.BlockSpec((group, cap, width), lambda i: (i, 0, 0))],
        flops=2 * total * rows * width,
    )
    looked, queries, rank, rank_t = lax.optimization_barrier((looked, queries, rank, rank_t))
    fetched = swap(looked, "shard").reshape(total, width)

    lines_t = lines.T
    (query_block,) = call(unit_queries, [HBM((pairs + 16, width), BF16)], queries, lines_t, kinds=["h", "h"])
    query_blocks = gather_blocks(query_block, blocks)

    step = 256
    pick, placed, hot_sum = call(
        prepare(cap),
        [shape((pairs, total), BF16), HBM((total, pairs), BF16), HBM((pairs, width), F32)],
        rank, rank_t, lines_t, hot_table,
        kinds=["v", "v", "h", "h"],
        grid=(total // step,),
        in_specs=[whole(rank), whole(rank_t), whole(lines_t), pl.BlockSpec((hot_rows * step // total, width), lambda i: (i, 0))],
        out_specs=[
            pl.BlockSpec((pairs, step), lambda i: (0, i)),
            pl.BlockSpec((step, pairs), lambda i: (i, 0)),
            pl.BlockSpec((pairs, width), lambda i: (0, 0)),
        ],
        scratch=[pltpu.VMEM((pairs, LANES), jnp.int32)],
        flops=2 * pairs * total * (width + 2 * LANES),
    )

    mine, after, tail = slice(0, pairs), slice(pairs, 2 * pairs), slice(pairs, pairs + 16)
    steps = 8
    sides, outgoing = call(
        item_side(blocks),
        [HBM((2 * pairs, width), BF16), HBM((total, width), BF16)],
        sharpness, additive, fetched, pick, placed, hot_sum, *query_blocks,
        kinds=["s", "s", "v", "v", slice(0, total), mine] + [mine] * blocks,
        out_specs=[pl.BlockSpec((2 * pairs, width), lambda i: (0, 0)), pl.BlockSpec(memory_space=HBM)],
        scratch=[
            pltpu.VMEM((pairs, width), F32),
            pltpu.VMEM((total, width), BF16),
            pltpu.SemaphoreType.DMA((steps,)),
        ],
        flops=2 * pairs * width * (2 * total + 2 * blocks * pairs),
    )
    incoming = swap(outgoing.reshape(owners, cap, width), "shard").reshape(total, width)

    side_blocks = gather_blocks(sides, blocks)
    (hot_block,) = call(
        hot_terms(blocks, slots),
        [HBM((hot_rows // blocks, width), BF16)],
        block, *side_blocks, *query_blocks,
        kinds=["s"] + [after] * blocks + [tail] * blocks,
        scratch=[pltpu.VMEM((hot_rows // blocks, width), F32)],
        flops=2 * blocks * pairs * width * hot_rows // blocks,
    )
    (query_grad,) = call(
        query_side,
        [HBM((pairs, width), F32)],
        sharpness, additive, queries, *side_blocks,
        kinds=["s", "s", "h"] + [mine] * blocks,
        scratch=[pltpu.VMEM((pairs, width), F32)],
        flops=4 * pairs * width * blocks * pairs,
    )
    hot_parts = swap(hot_block.reshape(owners, hot_rows // blocks // owners, width), "shard")
    (hot_piece,) = call(hot_sum_spread, [HBM(hot_parts.shape, BF16)], hot_parts)

    def cold_half(same_core, dtype, incoming):
        return call(
            cold_terms(same_core),
            [shape((chips, rows // blocks, width), dtype)],
            block, asked, incoming,
            kinds=["s", "v", "v"],
            grid=(chips,),
            out_specs=[pl.BlockSpec((1, rows // blocks, width), lambda i: (i, 0, 0))],
            scratch=[pltpu.VMEM((1, total), jnp.int32)],
            flops=total * rows * width,
        )[0]

    theirs = cold_half(False, BF16, incoming)
    theirs = cross(theirs, blocks)
    mine = cold_half(True, F32, incoming)
    keep, *sends = call(
        cold_join,
        [shape((rows // blocks, width), F32)] + [shape((rows // blocks, width), BF16)] * (chips - 1),
        mine, theirs,
    )
    hot_block = swap(hot_piece, "shard").reshape(hot_rows // blocks, width)
    parts = [shift(part, blocks, d + 1) for d, part in enumerate(sends)]
    (cold_grad,) = call(add_parts, [HBM((rows // blocks, width), F32)], keep, *parts)
    hot_blocks = gather_blocks(hot_block, blocks)
    (hot_grad,) = call(widen(blocks), [HBM((hot_rows, width), F32)], block, *hot_blocks, kinds=["s"] + ["v"] * blocks)
    return (query_grad, hot_grad, cold_grad)


def solution(mesh):
    pair = P(("shard", "blk"), None)
    in_specs = (pair, P(), P("shard", None), pair, pair, pair, P(("shard", "blk")), P(), P())
    return jax.shard_map(step_of, mesh=mesh, in_specs=in_specs, out_specs=(pair, P(), pair), check_vma=False)
```

time: 168 us -> 159 us (0.946)
  blocking collectives: 0 us -> 34.9 us
  local copies, waits for them, and re-layouts: 23.6 us -> 0.73 us
  starting transfers between devices: 86.9 us -> 65.7 us
  Pallas kernels: 24.4 us -> 41.7 us
  waiting for transfers between devices: 30 us -> 13.2 us
    all_to_all x0 -> x2, blocking collectives: none -> 34.9 us  [swap(): return lax.all_to_all(array, axis, split_axis=0, concat_axis=0, tiled=True)]
    unnamed x92 -> x30, local copies, waits for them, and re-layouts: 23.6 us -> 0.73 us
    all_to_all x5 -> x3, starting transfers between devices: 39.9 us -> 20.2 us  [swap(): return lax.all_to_all(array, axis, split_axis=0, concat_axis=0, tiled=True)]
    pallas_call x13, Pallas kernels: 24.4 us -> 41.7 us  [call(): pl.pallas_call(run if late else kernel, out_shape=list(outs), grid=grid,...]
    all_to_all x5 -> x3, waiting for transfers between devices: 25.5 us -> 9.56 us  [swap(): return lax.all_to_all(array, axis, split_axis=0, concat_axis=0, tiled=True)]
    ppermute x15 -> x12, starting transfers between devices: 21.9 us -> 18.7 us  [shift(): lax.ppermute(array, 'blk', [(i, (i + 2 * d) % blocks) for i in range(bloc...]
    ppermute x17 -> x13, starting transfers between devices: 25.1 us -> 26.8 us  [cross(): return lax.ppermute(array, 'blk', [(i, i ^ 1) for i in range(blocks)])]
  transfers between devices with their start and end apart: 37 -> 28, of which waited for: 7 -> 6; matrix products, arithmetic and copies ran while one was open for 0% -> 0% of each run, Pallas kernels for 8% -> 15%
where the time goes in v3:
time: 159 us; the launch traced here: 158 us
  starting transfers between devices  65.7 us (41%)
  Pallas kernels  41.7 us (26%)
  blocking collectives  34.9 us (22%)
  waiting for transfers between devices  13.2 us (8%)
  between operations  2.2 us (1%)
    pallas_call x13, Pallas kernels, call(): pl.pallas_call(run if late else kernel, out_shape=list(outs), grid=grid,...  41.7 us
    all_to_all x2, blocking collectives, swap(): return lax.all_to_all(array, axis, split_axis=0, concat_axis=0, tiled=True)  34.9 us
    ppermute x13, starting transfers between devices, cross(): return lax.ppermute(array, 'blk', [(i, i ^ 1) for i in range(blocks)])  26.8 us
    all_to_all x3, starting transfers between devices, swap(): return lax.all_to_all(array, axis, split_axis=0, concat_axis=0, tiled=True)  20.2 us
    ppermute x12, starting transfers between devices, shift(): lax.ppermute(array, 'blk', [(i, (i + 2 * d) % blocks) for i in range(bloc...  18.7 us
    all_to_all x3, waiting for transfers between devices, swap(): return lax.all_to_all(array, axis, split_axis=0, concat_axis=0, tiled=True)  9.56 us
  transfers between devices with their start and end apart: 28, of which 6 were waited for; matrix products, arithmetic and copies ran while one was open for 0% of the time, Pallas kernels for 15%

profile of v3, /device:TPU:1, one launch (start us, length us, event | category | flops | bytes accessed | tf_op | source)
XLA Modules:
  0.0 158.4 jit_solution(10442773331446450032)
XLA Ops:
  0.6 3.9 %shard_map.112 = (bf16[256,128]{1,0:T(8,128)(2,1)S(1)}, bf16[128,256]{1,0:T(8,128)(2,1)S(1)}, s32[32,8,128]{2,1,0:T(8,128)}, bf16[2048,256]{1,0:T(8,128)(2,1)S(1)}) custom-call(s32[4,256]{1,0:T(4,128)} %bitcast.20, s32[4,256]{1,0:T(4,128)} %bitcast.21, s32[1,256]{1,0:T(1,128)} %bitcast.24, f32[2048,256]{1,0:T(8,128)} %refs_3_.1), custom_call_target="tpu_custom_call" | custom-call | flops 402653184 | bytes 2106368 | tf_op jit(solution)/shard_map/pallas_call | solution.py:68
  4.6 21.2 %all_to_all.25.ask_ref = s32[32,8,128]{2,1,0:T(8,128)S(1)} all-to-all(s32[32,8,128]{2,1,0:T(8,128)} %get-tuple-element.20), channel_id=1, replica_groups=mesh['shard'=32,'blk'=8] {'shard'}, dimensions={0} | all-to-all | bytes 262144 | tf_op jit(solution)/shard_map/all_to_all | solution.py:329
  25.8 5.8 %shard_map.113 = bf16[32,64,256]{2,1,0:T(8,128)(2,1)} custom-call(s32[32,8,128]{2,1,0:T(8,128)S(1)} %all_to_all.25.ask_ref, bf16[2048,256]{1,0:T(8,128)(2,1)S(1)} %get-tuple-element.21.table_ref), custom_call_target="tpu_custom_call" | custom-call | flops 2147483648 | bytes 1179648 | tf_op jit(solution)/shard_map/pallas_call | solution.py:68
  31.6 3.9 %all-to-all-start.1 = ((bf16[32,64,256]{2,1,0:T(8,128)(2,1)}), bf16[32,64,256]{2,1,0:T(8,128)(2,1)S(1)}, u32[]{:S(2)}, u32[]{:S(2)}) async-start(bf16[32,64,256]{2,1,0:T(8,128)(2,1)} %shard_map.113), calls=%async_computation.1 | async-start | bytes 2097152 | tf_op jit(solution)/shard_map/all_to_all | solution.py:329
  35.5 1.7 %shard_map.115.refs_6_.refs_9_ = bf16[272,256]{1,0:T(8,128)(2,1)} custom-call(bf16[256,256]{1,0:T(8,128)(2,1)} %refs_2_, s32[4,256]{1,0:T(4,128)} %bitcast.22), custom_call_target="tpu_custom_call" | custom-call | bytes 135168 | tf_op jit(solution)/shard_map/pallas_call | solution.py:68
  37.2 1.2 collective-permute-start
  38.4 2.5 %collective-permute-start.1 = (bf16[272,256]{1,0:T(8,128)(2,1)}, bf16[272,256]{1,0:T(8,128)(2,1)S(1)}, u32[]{:S(2)}, u32[]{:S(2)}) collective-permute-start(bf16[272,256]{1,0:T(8,128)(2,1)} %shard_map.115.refs_6_.refs_9_), channel_id=1, source_target_pairs={{0,4},{1,5},{2,6},{3,7},{4,0},{5,1},{6,2},{7,3},{8,12},{9,13},{10,... | collective-permute-start | bytes 417800 | tf_op jit(solution)/shard_map/ppermute | solution.py:337
  40.9 1.2 collective-permute-start.2
  42.0 2.9 %collective-permute-start.3 = (bf16[272,256]{1,0:T(8,128)(2,1)}, bf16[272,256]{1,0:T(8,128)(2,1)S(1)}, u32[]{:S(2)}, u32[]{:S(2)}) collective-permute-start(bf16[272,256]{1,0:T(8,128)(2,1)} %shard_map.115.refs_6_.refs_9_), channel_id=1, source_target_pairs={{0,1},{1,0},{2,3},{3,2},{4,5},{5,4},{6,7},{7,6},{8,9},{9,8},{10,11... | collective-permute-start | bytes 417800 | tf_op jit(solution)/shard_map/ppermute | solution.py:333
  44.9 0.0 collective-permute-done.refs_7_.refs_10_
  44.9 2.3 %collective-permute-start.4 = (bf16[272,256]{1,0:T(8,128)(2,1)S(1)}, bf16[272,256]{1,0:T(8,128)(2,1)S(1)}, u32[]{:S(2)}, u32[]{:S(2)}) collective-permute-start(bf16[272,256]{1,0:T(8,128)(2,1)S(1)} %collective-permute-done.refs_7_.refs_10_), channel_id=1, source_target_pairs={{0,1},{1,0},{2,3},{3,2},{4,5},{5,4},{6,7},{7,6},{8,9},{9,8},{10,11... | collective-permute-start | bytes 417800 | tf_op jit(solution)/shard_map/ppermute | solution.py:333
  47.2 0.0 collective-permute-done.1.refs_8_.refs_11_
  47.2 1.5 collective-permute-start.5
  48.7 0.0 collective-permute-done.2.refs_9_.refs_12_
  48.7 0.1 collective-permute-start.6
  50.1 7.1 %shard_map.114 = (bf16[256,2048]{1,0:T(8,128)(2,1)S(1)}, bf16[2048,256]{1,0:T(8,128)(2,1)}, f32[256,256]{1,0:T(8,128)}) custom-call(bf16[256,128]{1,0:T(8,128)(2,1)S(1)} %get-tuple-element.26.rank_ref, bf16[128,256]{1,0:T(8,128)(2,1)S(1)} %get-tuple-element.27.rank_t_ref, s32[4,256]{1,0:T(4,128)} %bitcast.23, bf16[2048,256]{1,0:T(8,128)(2,1)} %hot_ref.1), custom_call_target="tpu_custom_call" | custom-call | flops 536870912 | bytes 1183744 | tf_op jit(solution)/shard_map/pallas_call | solution.py:68
  57.2 0.0 collective-permute-done.5.refs_12_.refs_15_
  57.2 2.8 %all-to-all-done.1 = bf16[32,64,256]{2,1,0:T(8,128)(2,1)S(1)} async-done(((bf16[32,64,256]{2,1,0:T(8,128)(2,1)}), bf16[32,64,256]{2,1,0:T(8,128)(2,1)S(1)}, u32[]{:S(2)}, u32[]{:S(2)}) %all-to-all-start.1) | async-done | bytes 1048608 | tf_op jit(solution)/shard_map/all_to_all | solution.py:329
  60.1 7.4 %shard_map.116 = (bf16[512,256]{1,0:T(8,128)(2,1)}, bf16[2048,256]{1,0:T(8,128)(2,1)}) custom-call(f32[1]{0:T(128)S(6)} %copy.12.refs_0_, f32[1]{0:T(128)S(6)} %copy.13.refs_1_, bf16[2048,256]{1,0:T(8,128)(2,1)S(1)} %bitcast.10, bf16[256,2048]{1,0:T(8,128)(2,1)S(1)} %get-tuple-element.28.refs_3_, bf16[2048,256]{1,0:T(8,128)(2,1)} %get-tuple-element.29.refs_4_, ...), custom_call_target="tpu_custom_call" | custom-call | flops 1073741824 | bytes 4521992 | tf_op jit(solution)/shard_map/pallas_call | solution.py:68
  67.5 8.2 %all-to-all-start.4 = ((bf16[32,64,256]{2,1,0:T(8,128)(2,1)}), bf16[32,64,256]{2,1,0:T(8,128)(2,1)S(1)}, u32[]{:S(2)}, u32[]{:S(2)}) async-start(bf16[32,64,256]{2,1,0:T(8,128)(2,1)} %bitcast.18), calls=%async_computation.4 | async-start | bytes 2097152 | tf_op jit(solution)/shard_map/all_to_all | solution.py:329
  75.8 1.3 collective-permute-start.7
  77.1 2.5 %collective-permute-start.8 = (bf16[512,256]{1,0:T(8,128)(2,1)S(1)}, bf16[512,256]{1,0:T(8,128)(2,1)S(1)}, u32[]{:S(2)}, u32[]{:S(2)}) collective-permute-start(bf16[512,256]{1,0:T(8,128)(2,1)S(1)} %copy-done), channel_id=1, source_target_pairs={{0,4},{1,5},{2,6},{3,7},{4,0},{5,1},{6,2},{7,3},{8,12},{9,13},{10,... | collective-permute-start | bytes 786440 | tf_op jit(solution)/shard_map/ppermute | solution.py:337
  79.5 1.1 collective-permute-start.9
  80.7 2.9 %collective-permute-start.10 = (bf16[512,256]{1,0:T(8,128)(2,1)S(1)}, bf16[512,256]{1,0:T(8,128)(2,1)S(1)}, u32[]{:S(2)}, u32[]{:S(2)}) collective-permute-start(bf16[512,256]{1,0:T(8,128)(2,1)S(1)} %copy-done), channel_id=1, source_target_pairs={{0,1},{1,0},{2,3},{3,2},{4,5},{5,4},{6,7},{7,6},{8,9},{9,8},{10,11... | collective-permute-start | bytes 786440 | tf_op jit(solution)/shard_map/ppermute | solution.py:333
  83.6 0.0 collective-permute-done.7.refs_4_.refs_2_
  83.6 3.7 %collective-permute-start.11 = (bf16[512,256]{1,0:T(8,128)(2,1)S(1)}, bf16[512,256]{1,0:T(8,128)(2,1)S(1)}, u32[]{:S(2)}, u32[]{:S(2)}) collective-permute-start(bf16[512,256]{1,0:T(8,128)(2,1)S(1)} %collective-permute-done.7.refs_4_.refs_2_), channel_id=1, source_target_pairs={{0,1},{1,0},{2,3},{3,2},{4,5},{5,4},{6,7},{7,6},{8,9},{9,8},{10,11... | collective-permute-start | bytes 786440 | tf_op jit(solution)/shard_map/ppermute | solution.py:333
  87.3 2.2 %collective-permute-done.8.refs_5_.refs_3_ = bf16[512,256]{1,0:T(8,128)(2,1)S(1)} collective-permute-done((bf16[512,256]{1,0:T(8,128)(2,1)S(1)}, bf16[512,256]{1,0:T(8,128)(2,1)S(1)}, u32[]{:S(2)}, u32[]{:S(2)}) %collective-permute-start.8) | collective-permute-done | bytes 262176 | tf_op jit(solution)/shard_map/ppermute | solution.py:337
  89.5 2.9 %collective-permute-start.12 = (bf16[512,256]{1,0:T(8,128)(2,1)S(1)}, bf16[512,256]{1,0:T(8,128)(2,1)S(1)}, u32[]{:S(2)}, u32[]{:S(2)}) collective-permute-start(bf16[512,256]{1,0:T(8,128)(2,1)S(1)} %collective-permute-done.8.refs_5_.refs_3_), channel_id=1, source_target_pairs={{0,1},{1,0},{2,3},{3,2},{4,5},{5,4},{6,7},{7,6},{8,9},{9,8},{10,11... | collective-permute-start | bytes 786440 | tf_op jit(solution)/shard_map/ppermute | solution.py:333
  92.4 0.0 collective-permute-done.9.refs_6_.refs_4_
  92.4 0.1 collective-permute-start.13
  92.5 0.0 collective-permute-done.10.refs_7_.refs_5_
  92.5 0.0 collective-permute-done.11.refs_8_.refs_6_
  92.5 1.0 collective-permute-done.12.refs_9_.refs_7_
  93.6 0.4 collective-permute-done.13.refs_10_.refs_8_
  94.0 0.3 copy-done.6
  94.3 0.4 copy-done.7
  94.6 4.0 %shard_map.118 = bf16[256,256]{1,0:T(8,128)(2,1)} custom-call(s32[1]{0:T(128)} %bitcast.5.refs_0_.block_ref, bf16[512,256]{1,0:T(8,128)(2,1)} %get-tuple-element.31.refs_3_.refs_1_, bf16[512,256]{1,0:T(8,128)(2,1)} %copy-done.1, bf16[512,256]{1,0:T(8,128)(2,1)} %copy-done.2, bf16[512,256]{1,0:T(8,128)(2,1)} %copy-done.3, bf16[512,256]{1,0:T(8,128)(2,1)} %copy-done.4, ...), custom_call_target="tpu_custom_call" | custom-call | flops 268435456 | bytes 3211268 | tf_op jit(solution)/shard_map/pallas_call | solution.py:68
  98.6 1.7 %all-to-all-done.4 = bf16[32,64,256]{2,1,0:T(8,128)(2,1)S(1)} async-done(((bf16[32,64,256]{2,1,0:T(8,128)(2,1)}), bf16[32,64,256]{2,1,0:T(8,128)(2,1)S(1)}, u32[]{:S(2)}, u32[]{:S(2)}) %all-to-all-start.4) | async-done | bytes 1048608 | tf_op jit(solution)/shard_map/all_to_all | solution.py:329
  100.3 8.1 %all-to-all-start.2 = ((bf16[32,8,256]{2,1,0:T(8,128)(2,1)}), bf16[32,8,256]{2,1,0:T(8,128)(2,1)S(1)}, u32[]{:S(2)}, u32[]{:S(2)}) async-start(bf16[32,8,256]{2,1,0:T(8,128)(2,1)} %bitcast.19), calls=%async_computation.2 | async-start | bytes 262144 | tf_op jit(solution)/shard_map/all_to_all | solution.py:329
  108.4 1.9 %shard_map.122 = bf16[4,256,256]{2,1,0:T(8,128)(2,1)S(1)} custom-call(s32[1]{0:T(128)} %bitcast.5.refs_0_.block_ref, s32[32,8,128]{2,1,0:T(8,128)S(1)} %all_to_all.25.ask_ref, bf16[2048,256]{1,0:T(8,128)(2,1)S(1)} %bitcast.11), custom_call_target="tpu_custom_call" | custom-call | flops 1073741824 | bytes 1179652 | tf_op jit(solution)/shard_map/pallas_call | solution.py:68
  110.3 2.1 %collective-permute-start.21 = (bf16[4,256,256]{2,1,0:T(8,128)(2,1)S(1)}, bf16[4,256,256]{2,1,0:T(8,128)(2,1)S(1)}, u32[]{:S(2)}, u32[]{:S(2)}) collective-permute-start(bf16[4,256,256]{2,1,0:T(8,128)(2,1)S(1)} %shard_map.122), channel_id=1, source_target_pairs={{0,1},{1,0},{2,3},{3,2},{4,5},{5,4},{6,7},{7,6},{8,9},{9,8},{10,11... | collective-permute-start | bytes 1572872 | tf_op jit(solution)/shard_map/ppermute | solution.py:333
  112.5 5.1 %all-to-all-done.2.parts_ref = bf16[32,8,256]{2,1,0:T(8,128)(2,1)S(1)} async-done(((bf16[32,8,256]{2,1,0:T(8,128)(2,1)}), bf16[32,8,256]{2,1,0:T(8,128)(2,1)S(1)}, u32[]{:S(2)}, u32[]{:S(2)}) %all-to-all-start.2) | async-done | bytes 131104 | tf_op jit(solution)/shard_map/all_to_all | solution.py:329
  117.5 0.7 shard_map.119
  118.2 13.7 %all_to_all.26 = bf16[32,8,256]{2,1,0:T(8,128)(2,1)S(1)} all-to-all(bf16[32,8,256]{2,1,0:T(8,128)(2,1)} %shard_map.119), channel_id=1, replica_groups=mesh['shard'=32,'blk'=8] {'shard'}, dimensions={0} | all-to-all | bytes 262144 | tf_op jit(solution)/shard_map/all_to_all | solution.py:329
  131.9 1.2 collective-permute-start.14
  133.1 2.5 %collective-permute-start.15 = (bf16[256,256]{1,0:T(8,128)(2,1)S(1)}, bf16[256,256]{1,0:T(8,128)(2,1)S(1)}, u32[]{:S(2)}, u32[]{:S(2)}) collective-permute-start(bf16[256,256]{1,0:T(8,128)(2,1)S(1)} %bitcast.14), channel_id=1, source_target_pairs={{0,4},{1,5},{2,6},{3,7},{4,0},{5,1},{6,2},{7,3},{8,12},{9,13},{10,... | collective-permute-start | bytes 393224 | tf_op jit(solution)/shard_map/ppermute | solution.py:337
  135.6 1.1 collective-permute-start.16
  136.7 4.7 %collective-permute-start.17 = (bf16[256,256]{1,0:T(8,128)(2,1)S(1)}, bf16[256,256]{1,0:T(8,128)(2,1)S(1)}, u32[]{:S(2)}, u32[]{:S(2)}) collective-permute-start(bf16[256,256]{1,0:T(8,128)(2,1)S(1)} %bitcast.16), channel_id=1, source_target_pairs={{0,1},{1,0},{2,3},{3,2},{4,5},{5,4},{6,7},{7,6},{8,9},{9,8},{10,11... | collective-permute-start | bytes 393224 | tf_op jit(solution)/shard_map/ppermute | solution.py:333
  141.4 0.0 collective-permute-done.14.refs_1_
  141.4 0.5 collective-permute-start.18
  141.9 0.0 collective-permute-done.15.refs_2_
  142.0 2.4 %collective-permute-start.19 = (bf16[256,256]{1,0:T(8,128)(2,1)S(1)}, bf16[256,256]{1,0:T(8,128)(2,1)S(1)}, u32[]{:S(2)}, u32[]{:S(2)}) collective-permute-start(bf16[256,256]{1,0:T(8,128)(2,1)S(1)} %collective-permute-done.15.refs_2_), channel_id=1, source_target_pairs={{0,1},{1,0},{2,3},{3,2},{4,5},{5,4},{6,7},{7,6},{8,9},{9,8},{10,11... | collective-permute-start | bytes 393224 | tf_op jit(solution)/shard_map/ppermute | solution.py:333
  144.3 0.0 collective-permute-done.16.refs_3_
  144.3 0.6 collective-permute-start.20
  145.0 1.9 %shard_map.121.mine_ref = f32[4,256,256]{2,1,0:T(8,128)S(1)} custom-call(s32[1]{0:T(128)} %bitcast.5.refs_0_.block_ref, s32[32,8,128]{2,1,0:T(8,128)S(1)} %all_to_all.25.ask_ref, bf16[2048,256]{1,0:T(8,128)(2,1)S(1)} %bitcast.12), custom_call_target="tpu_custom_call" | custom-call | flops 1073741824 | bytes 1179652 | tf_op jit(solution)/shard_map/pallas_call | solution.py:68
  146.9 0.0 collective-permute-done.21.theirs_ref
  146.9 0.1 shard_map.123
  147.0 1.1 collective-permute-start.22
  148.0 0.0 collective-permute-done.17.refs_4_
  148.0 2.5 %collective-permute-start.23 = (bf16[256,256]{1,0:T(8,128)(2,1)S(1)}, bf16[256,256]{1,0:T(8,128)(2,1)S(1)}, u32[]{:S(2)}, u32[]{:S(2)}) collective-permute-start(bf16[256,256]{1,0:T(8,128)(2,1)S(1)} %get-tuple-element.35), channel_id=1, source_target_pairs={{0,4},{1,5},{2,6},{3,7},{4,0},{5,1},{6,2},{7,3},{8,12},{9,13},{10,... | collective-permute-start | bytes 393224 | tf_op jit(solution)/shard_map/ppermute | solution.py:337
  150.6 0.6 collective-permute-start.24
  151.2 5.0 %shard_map.117 = f32[256,256]{1,0:T(8,128)} custom-call(f32[1]{0:T(128)S(6)} %copy.12.refs_0_, f32[1]{0:T(128)S(6)} %copy.13.refs_1_, bf16[256,256]{1,0:T(8,128)(2,1)} %refs_2_, bf16[512,256]{1,0:T(8,128)(2,1)} %get-tuple-element.31.refs_3_.refs_1_, bf16[512,256]{1,0:T(8,128)(2,1)} %copy-done.1, bf16[512,256]{1,0:T(8,128)(2,1)} %copy-done.2, ...), custom_call_target="tpu_custom_call" | custom-call | flops 536870912 | bytes 2228232 | tf_op jit(solution)/shard_map/pallas_call | solution.py:68
  156.2 1.5 shard_map.120
  157.6 0.8 shard_map.124
  (37 shorter events, 0.1 us)
Async XLA Ops:
  31.6 28.5 %all-to-all-start.1 = ((bf16[32,64,256]{2,1,0:T(8,128)(2,1)}), bf16[32,64,256]{2,1,0:T(8,128)(2,1)S(1)}, u32[]{:S(2)}, u32[]{:S(2)}) async-start(bf16[32,64,256]{2,1,0:T(8,128)(2,1)} %shard_map.113), calls=%async_computation.1 | async-start | bytes 2097152 | tf_op jit(solution)/shard_map/all_to_all | solution.py:329
  37.2 7.7 %collective-permute-start = (bf16[272,256]{1,0:T(8,128)(2,1)}, bf16[272,256]{1,0:T(8,128)(2,1)S(1)}, u32[]{:S(2)}, u32[]{:S(2)}) collective-permute-start(bf16[272,256]{1,0:T(8,128)(2,1)} %shard_map.115.refs_6_.refs_9_), channel_id=1, source_target_pairs={{0,2},{1,3},{2,4},{3,5},{4,6},{5,7},{6,0},{7,1},{8,10},{9,11},{10,... | collective-permute-start | bytes 417800 | tf_op jit(solution)/shard_map/ppermute | solution.py:337
  38.4 8.8 %collective-permute-start.1 = (bf16[272,256]{1,0:T(8,128)(2,1)}, bf16[272,256]{1,0:T(8,128)(2,1)S(1)}, u32[]{:S(2)}, u32[]{:S(2)}) collective-permute-start(bf16[272,256]{1,0:T(8,128)(2,1)} %shard_map.115.refs_6_.refs_9_), channel_id=1, source_target_pairs={{0,4},{1,5},{2,6},{3,7},{4,0},{5,1},{6,2},{7,3},{8,12},{9,13},{10,... | collective-permute-start | bytes 417800 | tf_op jit(solution)/shard_map/ppermute | solution.py:337
  40.9 7.8 %collective-permute-start.2 = (bf16[272,256]{1,0:T(8,128)(2,1)}, bf16[272,256]{1,0:T(8,128)(2,1)S(1)}, u32[]{:S(2)}, u32[]{:S(2)}) collective-permute-start(bf16[272,256]{1,0:T(8,128)(2,1)} %shard_map.115.refs_6_.refs_9_), channel_id=1, source_target_pairs={{0,6},{1,7},{2,0},{3,1},{4,2},{5,3},{6,4},{7,5},{8,14},{9,15},{10,... | collective-permute-start | bytes 417800 | tf_op jit(solution)/shard_map/ppermute | solution.py:337
  42.0 15.1 %collective-permute-start.3 = (bf16[272,256]{1,0:T(8,128)(2,1)}, bf16[272,256]{1,0:T(8,128)(2,1)S(1)}, u32[]{:S(2)}, u32[]{:S(2)}) collective-permute-start(bf16[272,256]{1,0:T(8,128)(2,1)} %shard_map.115.refs_6_.refs_9_), channel_id=1, source_target_pairs={{0,1},{1,0},{2,3},{3,2},{4,5},{5,4},{6,7},{7,6},{8,9},{9,8},{10,11... | collective-permute-start | bytes 417800 | tf_op jit(solution)/shard_map/ppermute | solution.py:333
  44.9 15.1 %copy-start.8 = (bf16[272,256]{1,0:T(8,128)(2,1)}, bf16[272,256]{1,0:T(8,128)(2,1)S(1)}, u32[]{:S(2)}) copy-start(bf16[272,256]{1,0:T(8,128)(2,1)S(1)} %collective-permute-done.refs_7_.refs_10_) | copy-start | bytes 417796
  44.9 12.2 %collective-permute-start.4 = (bf16[272,256]{1,0:T(8,128)(2,1)S(1)}, bf16[272,256]{1,0:T(8,128)(2,1)S(1)}, u32[]{:S(2)}, u32[]{:S(2)}) collective-permute-start(bf16[272,256]{1,0:T(8,128)(2,1)S(1)} %collective-permute-done.refs_7_.refs_10_), channel_id=1, source_target_pairs={{0,1},{1,0},{2,3},{3,2},{4,5},{5,4},{6,7},{7,6},{8,9},{9,8},{10,11... | collective-permute-start | bytes 417800 | tf_op jit(solution)/shard_map/ppermute | solution.py:333
  47.2 12.8 %copy-start.9 = (bf16[272,256]{1,0:T(8,128)(2,1)}, bf16[272,256]{1,0:T(8,128)(2,1)S(1)}, u32[]{:S(2)}) copy-start(bf16[272,256]{1,0:T(8,128)(2,1)S(1)} %collective-permute-done.1.refs_8_.refs_11_) | copy-start | bytes 417796
  47.2 10.0 %collective-permute-start.5 = (bf16[272,256]{1,0:T(8,128)(2,1)S(1)}, bf16[272,256]{1,0:T(8,128)(2,1)S(1)}, u32[]{:S(2)}, u32[]{:S(2)}) collective-permute-start(bf16[272,256]{1,0:T(8,128)(2,1)S(1)} %collective-permute-done.1.refs_8_.refs_11_), channel_id=1, source_target_pairs={{0,1},{1,0},{2,3},{3,2},{4,5},{5,4},{6,7},{7,6},{8,9},{9,8},{10,11... | collective-permute-start | bytes 417800 | tf_op jit(solution)/shard_map/ppermute | solution.py:333
  48.7 11.3 %copy-start.10 = (bf16[272,256]{1,0:T(8,128)(2,1)}, bf16[272,256]{1,0:T(8,128)(2,1)S(1)}, u32[]{:S(2)}) copy-start(bf16[272,256]{1,0:T(8,128)(2,1)S(1)} %collective-permute-done.2.refs_9_.refs_12_) | copy-start | bytes 417796
  48.7 8.5 %collective-permute-start.6 = (bf16[272,256]{1,0:T(8,128)(2,1)S(1)}, bf16[272,256]{1,0:T(8,128)(2,1)S(1)}, u32[]{:S(2)}, u32[]{:S(2)}) collective-permute-start(bf16[272,256]{1,0:T(8,128)(2,1)S(1)} %collective-permute-done.2.refs_9_.refs_12_), channel_id=1, source_target_pairs={{0,1},{1,0},{2,3},{3,2},{4,5},{5,4},{6,7},{7,6},{8,9},{9,8},{10,11... | collective-permute-start | bytes 417800 | tf_op jit(solution)/shard_map/ppermute | solution.py:333
  57.2 2.9 %copy-start.11 = (bf16[272,256]{1,0:T(8,128)(2,1)}, bf16[272,256]{1,0:T(8,128)(2,1)S(1)}, u32[]{:S(2)}) copy-start(bf16[272,256]{1,0:T(8,128)(2,1)S(1)} %collective-permute-done.3.refs_10_.refs_13_) | copy-start | bytes 417796
  57.2 2.9 %copy-start.12 = (bf16[272,256]{1,0:T(8,128)(2,1)}, bf16[272,256]{1,0:T(8,128)(2,1)S(1)}, u32[]{:S(2)}) copy-start(bf16[272,256]{1,0:T(8,128)(2,1)S(1)} %collective-permute-done.4.refs_11_.refs_14_) | copy-start | bytes 417796
  57.2 2.9 %copy-start.13 = (bf16[272,256]{1,0:T(8,128)(2,1)}, bf16[272,256]{1,0:T(8,128)(2,1)S(1)}, u32[]{:S(2)}) copy-start(bf16[272,256]{1,0:T(8,128)(2,1)S(1)} %collective-permute-done.5.refs_12_.refs_15_) | copy-start | bytes 417796
  57.2 2.8 %copy-start.14 = (bf16[272,256]{1,0:T(8,128)(2,1)}, bf16[272,256]{1,0:T(8,128)(2,1)S(1)}, u32[]{:S(2)}) copy-start(bf16[272,256]{1,0:T(8,128)(2,1)S(1)} %collective-permute-done.6.refs_13_.refs_16_) | copy-start | bytes 417796
  67.5 8.3 %copy-start = (bf16[512,256]{1,0:T(8,128)(2,1)S(1)}, bf16[512,256]{1,0:T(8,128)(2,1)}, u32[]{:S(2)}) copy-start(bf16[512,256]{1,0:T(8,128)(2,1)} %get-tuple-element.31.refs_3_.refs_1_) | copy-start | bytes 786436
  67.5 32.8 %all-to-all-start.4 = ((bf16[32,64,256]{2,1,0:T(8,128)(2,1)}), bf16[32,64,256]{2,1,0:T(8,128)(2,1)S(1)}, u32[]{:S(2)}, u32[]{:S(2)}) async-start(bf16[32,64,256]{2,1,0:T(8,128)(2,1)} %bitcast.18), calls=%async_computation.4 | async-start | bytes 2097152 | tf_op jit(solution)/shard_map/all_to_all | solution.py:329
  75.8 7.8 %collective-permute-start.7 = (bf16[512,256]{1,0:T(8,128)(2,1)S(1)}, bf16[512,256]{1,0:T(8,128)(2,1)S(1)}, u32[]{:S(2)}, u32[]{:S(2)}) collective-permute-start(bf16[512,256]{1,0:T(8,128)(2,1)S(1)} %copy-done), channel_id=1, source_target_pairs={{0,2},{1,3},{2,4},{3,5},{4,6},{5,7},{6,0},{7,1},{8,10},{9,11},{10,... | collective-permute-start | bytes 786440 | tf_op jit(solution)/shard_map/ppermute | solution.py:337
  77.1 12.4 %collective-permute-start.8 = (bf16[512,256]{1,0:T(8,128)(2,1)S(1)}, bf16[512,256]{1,0:T(8,128)(2,1)S(1)}, u32[]{:S(2)}, u32[]{:S(2)}) collective-permute-start(bf16[512,256]{1,0:T(8,128)(2,1)S(1)} %copy-done), channel_id=1, source_target_pairs={{0,4},{1,5},{2,6},{3,7},{4,0},{5,1},{6,2},{7,3},{8,12},{9,13},{10,... | collective-permute-start | bytes 786440 | tf_op jit(solution)/shard_map/ppermute | solution.py:337
  79.5 12.9 %collective-permute-start.9 = (bf16[512,256]{1,0:T(8,128)(2,1)S(1)}, bf16[512,256]{1,0:T(8,128)(2,1)S(1)}, u32[]{:S(2)}, u32[]{:S(2)}) collective-permute-start(bf16[512,256]{1,0:T(8,128)(2,1)S(1)} %copy-done), channel_id=1, source_target_pairs={{0,6},{1,7},{2,0},{3,1},{4,2},{5,3},{6,4},{7,5},{8,14},{9,15},{10,... | collective-permute-start | bytes 786440 | tf_op jit(solution)/shard_map/ppermute | solution.py:337
  80.7 11.8 %collective-permute-start.10 = (bf16[512,256]{1,0:T(8,128)(2,1)S(1)}, bf16[512,256]{1,0:T(8,128)(2,1)S(1)}, u32[]{:S(2)}, u32[]{:S(2)}) collective-permute-start(bf16[512,256]{1,0:T(8,128)(2,1)S(1)} %copy-done), channel_id=1, source_target_pairs={{0,1},{1,0},{2,3},{3,2},{4,5},{5,4},{6,7},{7,6},{8,9},{9,8},{10,11... | collective-permute-start | bytes 786440 | tf_op jit(solution)/shard_map/ppermute | solution.py:333
  83.6 10.4 %copy-start.1 = (bf16[512,256]{1,0:T(8,128)(2,1)}, bf16[512,256]{1,0:T(8,128)(2,1)S(1)}, u32[]{:S(2)}) copy-start(bf16[512,256]{1,0:T(8,128)(2,1)S(1)} %collective-permute-done.7.refs_4_.refs_2_) | copy-start | bytes 786436
  83.6 8.9 %collective-permute-start.11 = (bf16[512,256]{1,0:T(8,128)(2,1)S(1)}, bf16[512,256]{1,0:T(8,128)(2,1)S(1)}, u32[]{:S(2)}, u32[]{:S(2)}) collective-permute-start(bf16[512,256]{1,0:T(8,128)(2,1)S(1)} %collective-permute-done.7.refs_4_.refs_2_), channel_id=1, source_target_pairs={{0,1},{1,0},{2,3},{3,2},{4,5},{5,4},{6,7},{7,6},{8,9},{9,8},{10,11... | collective-permute-start | bytes 786440 | tf_op jit(solution)/shard_map/ppermute | solution.py:333
  89.5 4.5 %copy-start.2 = (bf16[512,256]{1,0:T(8,128)(2,1)}, bf16[512,256]{1,0:T(8,128)(2,1)S(1)}, u32[]{:S(2)}) copy-start(bf16[512,256]{1,0:T(8,128)(2,1)S(1)} %collective-permute-done.8.refs_5_.refs_3_) | copy-start | bytes 786436
  89.5 4.1 %collective-permute-start.12 = (bf16[512,256]{1,0:T(8,128)(2,1)S(1)}, bf16[512,256]{1,0:T(8,128)(2,1)S(1)}, u32[]{:S(2)}, u32[]{:S(2)}) collective-permute-start(bf16[512,256]{1,0:T(8,128)(2,1)S(1)} %collective-permute-done.8.refs_5_.refs_3_), channel_id=1, source_target_pairs={{0,1},{1,0},{2,3},{3,2},{4,5},{5,4},{6,7},{7,6},{8,9},{9,8},{10,11... | collective-permute-start | bytes 786440 | tf_op jit(solution)/shard_map/ppermute | solution.py:333
  92.4 1.5 copy-start.3
  92.4 1.5 collective-permute-start.13
  92.5 1.4 copy-start.4
  92.5 1.5 copy-start.5
  93.6 0.7 copy-start.6
  93.9 0.7 copy-start.7
  100.3 17.2 %all-to-all-start.2 = ((bf16[32,8,256]{2,1,0:T(8,128)(2,1)}), bf16[32,8,256]{2,1,0:T(8,128)(2,1)S(1)}, u32[]{:S(2)}, u32[]{:S(2)}) async-start(bf16[32,8,256]{2,1,0:T(8,128)(2,1)} %bitcast.19), calls=%async_computation.2 | async-start | bytes 262144 | tf_op jit(solution)/shard_map/all_to_all | solution.py:329
  110.3 36.6 %collective-permute-start.21 = (bf16[4,256,256]{2,1,0:T(8,128)(2,1)S(1)}, bf16[4,256,256]{2,1,0:T(8,128)(2,1)S(1)}, u32[]{:S(2)}, u32[]{:S(2)}) collective-permute-start(bf16[4,256,256]{2,1,0:T(8,128)(2,1)S(1)} %shard_map.122), channel_id=1, source_target_pairs={{0,1},{1,0},{2,3},{3,2},{4,5},{5,4},{6,7},{7,6},{8,9},{9,8},{10,11... | collective-permute-start | bytes 1572872 | tf_op jit(solution)/shard_map/ppermute | solution.py:333
  131.9 9.5 %collective-permute-start.14 = (bf16[256,256]{1,0:T(8,128)(2,1)S(1)}, bf16[256,256]{1,0:T(8,128)(2,1)S(1)}, u32[]{:S(2)}, u32[]{:S(2)}) collective-permute-start(bf16[256,256]{1,0:T(8,128)(2,1)S(1)} %bitcast.13), channel_id=1, source_target_pairs={{0,2},{1,3},{2,4},{3,5},{4,6},{5,7},{6,0},{7,1},{8,10},{9,11},{10,... | collective-permute-start | bytes 393224 | tf_op jit(solution)/shard_map/ppermute | solution.py:337
  133.1 8.8 %collective-permute-start.15 = (bf16[256,256]{1,0:T(8,128)(2,1)S(1)}, bf16[256,256]{1,0:T(8,128)(2,1)S(1)}, u32[]{:S(2)}, u32[]{:S(2)}) collective-permute-start(bf16[256,256]{1,0:T(8,128)(2,1)S(1)} %bitcast.14), channel_id=1, source_target_pairs={{0,4},{1,5},{2,6},{3,7},{4,0},{5,1},{6,2},{7,3},{8,12},{9,13},{10,... | collective-permute-start | bytes 393224 | tf_op jit(solution)/shard_map/ppermute | solution.py:337
  135.6 8.8 %collective-permute-start.16 = (bf16[256,256]{1,0:T(8,128)(2,1)S(1)}, bf16[256,256]{1,0:T(8,128)(2,1)S(1)}, u32[]{:S(2)}, u32[]{:S(2)}) collective-permute-start(bf16[256,256]{1,0:T(8,128)(2,1)S(1)} %bitcast.15), channel_id=1, source_target_pairs={{0,6},{1,7},{2,0},{3,1},{4,2},{5,3},{6,4},{7,5},{8,14},{9,15},{10,... | collective-permute-start | bytes 393224 | tf_op jit(solution)/shard_map/ppermute | solution.py:337
  136.7 11.3 %collective-permute-start.17 = (bf16[256,256]{1,0:T(8,128)(2,1)S(1)}, bf16[256,256]{1,0:T(8,128)(2,1)S(1)}, u32[]{:S(2)}, u32[]{:S(2)}) collective-permute-start(bf16[256,256]{1,0:T(8,128)(2,1)S(1)} %bitcast.16), channel_id=1, source_target_pairs={{0,1},{1,0},{2,3},{3,2},{4,5},{5,4},{6,7},{7,6},{8,9},{9,8},{10,11... | collective-permute-start | bytes 393224 | tf_op jit(solution)/shard_map/ppermute | solution.py:333
  141.4 9.2 %collective-permute-start.18 = (bf16[256,256]{1,0:T(8,128)(2,1)S(1)}, bf16[256,256]{1,0:T(8,128)(2,1)S(1)}, u32[]{:S(2)}, u32[]{:S(2)}) collective-permute-start(bf16[256,256]{1,0:T(8,128)(2,1)S(1)} %collective-permute-done.14.refs_1_), channel_id=1, source_target_pairs={{0,1},{1,0},{2,3},{3,2},{4,5},{5,4},{6,7},{7,6},{8,9},{9,8},{10,11... | collective-permute-start | bytes 393224 | tf_op jit(solution)/shard_map/ppermute | solution.py:333
  142.0 14.2 %collective-permute-start.19 = (bf16[256,256]{1,0:T(8,128)(2,1)S(1)}, bf16[256,256]{1,0:T(8,128)(2,1)S(1)}, u32[]{:S(2)}, u32[]{:S(2)}) collective-permute-start(bf16[256,256]{1,0:T(8,128)(2,1)S(1)} %collective-permute-done.15.refs_2_), channel_id=1, source_target_pairs={{0,1},{1,0},{2,3},{3,2},{4,5},{5,4},{6,7},{7,6},{8,9},{9,8},{10,11... | collective-permute-start | bytes 393224 | tf_op jit(solution)/shard_map/ppermute | solution.py:333
  144.3 11.8 %collective-permute-start.20 = (bf16[256,256]{1,0:T(8,128)(2,1)S(1)}, bf16[256,256]{1,0:T(8,128)(2,1)S(1)}, u32[]{:S(2)}, u32[]{:S(2)}) collective-permute-start(bf16[256,256]{1,0:T(8,128)(2,1)S(1)} %collective-permute-done.16.refs_3_), channel_id=1, source_target_pairs={{0,1},{1,0},{2,3},{3,2},{4,5},{5,4},{6,7},{7,6},{8,9},{9,8},{10,11... | collective-permute-start | bytes 393224 | tf_op jit(solution)/shard_map/ppermute | solution.py:333
  147.0 10.7 %collective-permute-start.22 = (bf16[256,256]{1,0:T(8,128)(2,1)S(1)}, bf16[256,256]{1,0:T(8,128)(2,1)S(1)}, u32[]{:S(2)}, u32[]{:S(2)}) collective-permute-start(bf16[256,256]{1,0:T(8,128)(2,1)S(1)} %get-tuple-element.34), channel_id=1, source_target_pairs={{0,2},{1,3},{2,4},{3,5},{4,6},{5,7},{6,0},{7,1},{8,10},{9,11},{10,... | collective-permute-start | bytes 393224 | tf_op jit(solution)/shard_map/ppermute | solution.py:337
  148.0 9.6 %collective-permute-start.23 = (bf16[256,256]{1,0:T(8,128)(2,1)S(1)}, bf16[256,256]{1,0:T(8,128)(2,1)S(1)}, u32[]{:S(2)}, u32[]{:S(2)}) collective-permute-start(bf16[256,256]{1,0:T(8,128)(2,1)S(1)} %get-tuple-element.35), channel_id=1, source_target_pairs={{0,4},{1,5},{2,6},{3,7},{4,0},{5,1},{6,2},{7,3},{8,12},{9,13},{10,... | collective-permute-start | bytes 393224 | tf_op jit(solution)/shard_map/ppermute | solution.py:337
  150.6 7.0 %collective-permute-start.24 = (bf16[256,256]{1,0:T(8,128)(2,1)S(1)}, bf16[256,256]{1,0:T(8,128)(2,1)S(1)}, u32[]{:S(2)}, u32[]{:S(2)}) collective-permute-start(bf16[256,256]{1,0:T(8,128)(2,1)S(1)} %get-tuple-element.36), channel_id=1, source_target_pairs={{0,6},{1,7},{2,0},{3,1},{4,2},{5,3},{6,4},{7,5},{8,14},{9,15},{10,... | collective-permute-start | bytes 393224 | tf_op jit(solution)/shard_map/ppermute | solution.py:337

commit v4 on v3

--- a/solution.py
+++ b/solution.py
@@ -38,16 +38,43 @@
         return self.buffer
 
 
+class Leave:
+    def __init__(self, out_ref, stage_ref, sem):
+        self.out, self.stage, self.sem = out_ref, stage_ref, sem
+        self.steps = sem.shape[0]
+        self.width = stage_ref.shape[0] // self.steps
+
+    def copy(self, i):
+        part = pl.ds(i * self.width, self.width)
+        return pltpu.make_async_copy(self.stage.at[part], self.out.at[part], self.sem.at[i])
+
+    def run(self, compute):
+        def step(i, _):
+            self.stage[pl.ds(i * self.width, self.width)] = compute(i)
+            self.copy(i).start()
+            return 0
+
+        def finish(i, _):
+            self.copy(i).wait()
+            return 0
+
+        lax.fori_loop(0, self.steps, step, 0)
+        lax.fori_loop(0, self.steps, finish, 0)
+
+
 def call(kernel, outs, *args, kinds=None, scratch=(), flops=0, grid=(1,), in_specs=None, out_specs=None):
     kinds = kinds or ["v"] * len(args)
+    near = [isinstance(kind, tuple) for kind in kinds]
+    kinds = [kind[0] if isinstance(kind, tuple) else kind for kind in kinds]
     late = [k for k, kind in enumerate(kinds) if isinstance(kind, slice)]
     specs, operands = [], []
     for k, (kind, arg) in enumerate(zip(kinds, args)):
         if kind == "s":
             specs.append(pl.BlockSpec(memory_space=pltpu.SMEM))
         elif k in late:
-            specs.append(pl.BlockSpec(memory_space=HBM))
-            arg = pltpu.with_memory_space_constraint(arg, HBM)
+            specs.append(pl.BlockSpec(memory_space=pl.ANY if near[k] else HBM))
+            if not near[k]:
+                arg = pltpu.with_memory_space_constraint(arg, HBM)
         else:
             specs.append(in_specs[k] if in_specs else whole(arg))
             if kind == "h":
@@ -146,54 +173,64 @@
 
 
 def prepare(cap):
-    def kernel(rank_ref, rank_t_ref, lines_ref, hot_ref, pick_ref, place_ref, hot_sum_ref, lines_t_ref):
+    def kernel(rank_ref, rank_t_ref, lines_ref, hot, pick_ref, out_ref, hot_sum_ref, stage_ref, sem):
         pairs = rank_ref.shape[0]
         slots = lines_ref.shape[0]
-        width = pick_ref.shape[1]
-        base = pl.program_id(0) * width
-
-        @pl.when(pl.program_id(0) == 0)
-        def _():
-            hot_sum_ref[...] = jnp.zeros_like(hot_sum_ref)
-            line = iota((LANES, pairs), 0)
-            lines = jnp.zeros((LANES, pairs), F32)
+        rank, rank_t = rank_ref[...], rank_t_ref[...]
+        line = iota((LANES, pairs), 0)
+        lines = jnp.zeros((LANES, pairs), F32)
+        for h in range(slots):
+            lines = jnp.where(line == h, lines_ref[h : h + 1, :].astype(F32), lines)
+        lines = lines.T.astype(jnp.int32)
+        leave = Leave(out_ref, stage_ref, sem)
+        width = leave.width
+        want = (iota((pairs, width), 1) % cap).astype(F32)
+        want_t = (iota((width, pairs), 0) % cap).astype(F32)
+        hot_ref = hot.get()
+        hot_sum_ref[...] = jnp.zeros_like(hot_sum_ref)
+
+        def compute(i):
+            base = pl.multiple_of(i * width, width)
+            spread = expander(LANES, cap, base, width)
+            pick_ref[:, pl.ds(base, width)] = (mm(rank, spread) == want).astype(F32).astype(BF16)
+            column = iota((pairs, width), 1) + base
+            counts = jnp.zeros((pairs, width), F32)
             for h in range(slots):
-                lines = jnp.where(line == h, lines_ref[h : h + 1, :].astype(F32), lines)
-            lines_t_ref[...] = lines.T.astype(jnp.int32)
-
-        spread = expander(LANES, cap, base, width)
-        want = (iota((pairs, width), 1) % cap).astype(F32)
-        pick_ref[...] = (mm(rank_ref[...], spread) == want).astype(F32).astype(BF16)
-        spread_t = ((iota((width, LANES), 0) + base) // cap == iota((width, LANES), 1))
-        want_t = (iota((width, pairs), 0) % cap).astype(F32)
-        hit = mm(spread_t.astype(F32).astype(BF16), rank_t_ref[...]) == want_t
-        place_ref[...] = hit.astype(F32).astype(BF16)
-        column = iota((pairs, width), 1) + base
-        counts = jnp.zeros((pairs, width), F32)
-        for h in range(slots):
-            counts += (lines_t_ref[:, h : h + 1] == column).astype(F32)
-        hot_sum_ref[...] += mm(counts.astype(BF16), hot_ref[...])
-
-    return kernel
-
-
-def fetch(ask_ref, table_ref, out_ref):
+                counts += (lines[:, h : h + 1] == column).astype(F32)
+            hot_sum_ref[...] += mm(counts.astype(BF16), hot_ref[pl.ds(base, width), :])
+            spread_t = ((iota((width, LANES), 0) + base) // cap == iota((width, LANES), 1))
+            hit = mm(spread_t.astype(F32).astype(BF16), rank_t) == want_t
+            return hit.astype(F32).astype(BF16)
+
+        leave.run(compute)
+
+    return kernel
+
+
+def fetch(ask_ref, table_ref, out_ref, stage_ref, sem):
     rows = table_ref.shape[0]
-    group, cap = out_ref.shape[0], out_ref.shape[1]
+    cap = stage_ref.shape[1]
+    leave = Leave(out_ref, stage_ref, sem)
+    group = leave.width
     diagonal = iota((cap, cap), 0) == iota((cap, cap), 1)
-    columns = []
-    for g in range(group):
-        ask = ask_ref[pl.program_id(0) * group + g, 0:1, 0:cap]
-        columns.append(jnp.sum(jnp.where(diagonal, ask, 0).astype(F32), axis=1, keepdims=True))
-    column = jnp.concatenate(columns, axis=0).astype(jnp.int32)
-    hit = (column == iota((group * cap, rows), 1)).astype(F32).astype(BF16)
-    out_ref[...] = mm(hit, table_ref[...]).astype(BF16).reshape(out_ref.shape)
+    lane = iota((group * cap, rows), 1)
+
+    def compute(i):
+        columns = []
+        for g in range(group):
+            ask = ask_ref[i * group + g, 0:1, 0:cap]
+            columns.append(jnp.sum(jnp.where(diagonal, ask, 0).astype(F32), axis=1, keepdims=True))
+        column = jnp.concatenate(columns, axis=0).astype(jnp.int32)
+        hit = (column == lane).astype(F32).astype(BF16)
+        return mm(hit, table_ref[...]).astype(BF16).reshape(group, cap, table_ref.shape[1])
+
+    leave.run(compute)
 
 
 def loss_side(own_low, others, total_ref, sharpness, additive):
     rows = own_low.shape[0]
     for i, late in enumerate(others):
-        other = late.get()[...]
+        other = late.get()[0:rows, :]
         grad = jax.nn.sigmoid(sharpness * mm(own_low, other, NT) + additive)
         if i == 0:
             grad = grad - (iota((rows, rows), 0) == iota((rows, rows), 1)).astype(F32)
@@ -209,35 +246,21 @@
 
 
 def item_side(blocks):
-    def kernel(sharp_ref, add_ref, fetched_ref, pick_ref, place, hot_sum, *refs):
-        queries, (sides_ref, out_ref, total_ref, stage_ref, sem) = refs[:blocks], refs[blocks:]
+    def kernel(sharp_ref, add_ref, fetched_ref, pick_ref, hot_sum, *refs):
+        queries, place = refs[:blocks], refs[blocks]
+        sides_ref, tails_ref, out_ref, total_ref, stage_ref, sem = refs[blocks + 1 :]
         pairs = total_ref.shape[0]
         unit, radius = normalize(mm(pick_ref[...], fetched_ref[...]) + hot_sum.get()[...])
         low = unit.astype(BF16)
         sides_ref[0:pairs, :] = low
         direction = loss_side(low, queries, total_ref, sharp_ref[0], add_ref[0])
+        for i, query in enumerate(queries):
+            tails_ref[i] = query.get()[pairs:, :]
         grad = project(unit, radius, direction).astype(BF16)
         sides_ref[pairs:, :] = grad
         place_ref = place.get()
-        steps = sem.shape[0]
-        width = place_ref.shape[0] // steps
-
-        def leave(i):
-            part = pl.ds(pl.multiple_of(i * width, width), width)
-            return pltpu.make_async_copy(stage_ref.at[part], out_ref.at[part], sem.at[i])
-
-        def step(i, _):
-            part = pl.ds(pl.multiple_of(i * width, width), width)
-            stage_ref[part, :] = mm(place_ref[part, :], grad).astype(BF16)
-            leave(i).start()
-            return 0
-
-        def finish(i, _):
-            leave(i).wait()
-            return 0
-
-        lax.fori_loop(0, steps, step, 0)
-        lax.fori_loop(0, steps, finish, 0)
+        leave = Leave(out_ref, stage_ref, sem)
+        leave.run(lambda i: mm(place_ref[pl.ds(i * leave.width, leave.width), :], grad).astype(BF16))
 
     return kernel
 
@@ -250,12 +273,12 @@
 
 
 def hot_terms(blocks, slots):
-    def kernel(block_ref, *refs):
-        grads, lines, (out_ref, total_ref) = refs[:blocks], refs[blocks : 2 * blocks], refs[2 * blocks :]
+    def kernel(block_ref, lines_ref, *refs):
+        grads, (out_ref, total_ref) = refs[:blocks], refs[blocks:]
         width, pairs = out_ref.shape
         row = (iota((width, pairs), 0) + block_ref[0] * width).astype(F32)
-        for i, (grad, line) in enumerate(zip(grads, lines)):
-            line = line.get()[...].astype(F32)
+        for i, grad in enumerate(grads):
+            line = lines_ref[i].astype(F32)
             counts = jnp.zeros((width, pairs), F32)
             for h in range(slots):
                 counts += (line[h : h + 1, :] * 64.0 + line[h + slots : h + slots + 1, :] == row).astype(F32)
@@ -364,13 +387,13 @@
     )
     asked = swap(ask, "shard")
 
-    group = 4
+    steps = 8
     (looked,) = call(
         fetch,
         [HBM((owners, cap, width), BF16)],
         asked, table_low,
-        grid=(owners // group,),
-        out_specs=[pl.BlockSpec((group, cap, width), lambda i: (i, 0, 0))],
+        out_specs=[pl.BlockSpec(memory_space=HBM)],
+        scratch=[pltpu.VMEM((owners, cap, width), BF16), pltpu.SemaphoreType.DMA((steps,))],
         flops=2 * total * rows * width,
     )
     looked, queries, rank, rank_t = lax.optimization_barrier((looked, queries, rank, rank_t))
@@ -380,31 +403,31 @@
     (query_block,) = call(unit_queries, [HBM((pairs + 16, width), BF16)], queries, lines_t, kinds=["h", "h"])
     query_blocks = gather_blocks(query_block, blocks)
 
-    step = 256
     pick, placed, hot_sum = call(
         prepare(cap),
         [shape((pairs, total), BF16), HBM((total, pairs), BF16), HBM((pairs, width), F32)],
         rank, rank_t, lines_t, hot_table,
-        kinds=["v", "v", "h", "h"],
-        grid=(total // step,),
-        in_specs=[whole(rank), whole(rank_t), whole(lines_t), pl.BlockSpec((hot_rows * step // total, width), lambda i: (i, 0))],
+        kinds=["v", "v", "h", slice(0, hot_rows)],
         out_specs=[
-            pl.BlockSpec((pairs, step), lambda i: (0, i)),
-            pl.BlockSpec((step, pairs), lambda i: (i, 0)),
+            pl.BlockSpec((pairs, total), lambda i: (0, 0)),
+            pl.BlockSpec(memory_space=HBM),
             pl.BlockSpec((pairs, width), lambda i: (0, 0)),
         ],
-        scratch=[pltpu.VMEM((pairs, LANES), jnp.int32)],
+        scratch=[pltpu.VMEM((total, pairs), BF16), pltpu.SemaphoreType.DMA((steps,))],
         flops=2 * pairs * total * (width + 2 * LANES),
     )
 
-    mine, after, tail = slice(0, pairs), slice(pairs, 2 * pairs), slice(pairs, pairs + 16)
-    steps = 8
-    sides, outgoing = call(
+    mine, after, block_rows = slice(0, pairs), slice(pairs, 2 * pairs), slice(0, pairs + 16)
+    sides, tails, outgoing = call(
         item_side(blocks),
-        [HBM((2 * pairs, width), BF16), HBM((total, width), BF16)],
-        sharpness, additive, fetched, pick, placed, hot_sum, *query_blocks,
-        kinds=["s", "s", "v", "v", slice(0, total), mine] + [mine] * blocks,
-        out_specs=[pl.BlockSpec((2 * pairs, width), lambda i: (0, 0)), pl.BlockSpec(memory_space=HBM)],
+        [HBM((2 * pairs, width), BF16), shape((blocks, 16, width), BF16), HBM((total, width), BF16)],
+        sharpness, additive, fetched, pick, hot_sum, *query_blocks, placed,
+        kinds=["s", "s", "v", "v", mine, block_rows] + [(block_rows,)] * (blocks - 1) + [slice(0, total)],
+        out_specs=[
+            pl.BlockSpec((2 * pairs, width), lambda i: (0, 0)),
+            pl.BlockSpec((blocks, 16, width), lambda i: (0, 0, 0)),
+            pl.BlockSpec(memory_space=HBM),
+        ],
         scratch=[
             pltpu.VMEM((pairs, width), F32),
             pltpu.VMEM((total, width), BF16),
@@ -418,8 +441,8 @@
     (hot_block,) = call(
         hot_terms(blocks, slots),
         [HBM((hot_rows // blocks, width), BF16)],
-        block, *side_blocks, *query_blocks,
-        kinds=["s"] + [after] * blocks + [tail] * blocks,
+        block, tails, *side_blocks,
+        kinds=["s", "v", after] + [(after,)] * (blocks - 1),
         scratch=[pltpu.VMEM((hot_rows // blocks, width), F32)],
         flops=2 * blocks * pairs * width * hot_rows // blocks,
     )
@@ -427,7 +450,7 @@
         query_side,
         [HBM((pairs, width), F32)],
         sharpness, additive, queries, *side_blocks,
-        kinds=["s", "s", "h"] + [mine] * blocks,
+        kinds=["s", "s", "h", mine] + [(mine,)] * (blocks - 1),
         scratch=[pltpu.VMEM((pairs, width), F32)],
         flops=4 * pairs * width * blocks * pairs,
     )

time: 159 us -> 160 us (level)
  no operation moved by 1% of the time
where the time goes in v4:
time: 160 us
  starting transfers between devices  64.8 us (40%)
  Pallas kernels  42.2 us (26%)
  blocking collectives  35.5 us (22%)
  waiting for transfers between devices  14.2 us (9%)
  between operations  2.14 us (1%)
    pallas_call x13, Pallas kernels, call(): pl.pallas_call(run if late else kernel, out_shape=list(outs), grid=grid,...  42.2 us
    all_to_all x2, blocking collectives, swap(): return lax.all_to_all(array, axis, split_axis=0, concat_axis=0, tiled=True)  35.5 us
    ppermute x13, starting transfers between devices, cross(): return lax.ppermute(array, 'blk', [(i, i ^ 1) for i in range(blocks)])  25.9 us
    all_to_all x3, starting transfers between devices, swap(): return lax.all_to_all(array, axis, split_axis=0, concat_axis=0, tiled=True)  20.2 us
    ppermute x12, starting transfers between devices, shift(): lax.ppermute(array, 'blk', [(i, (i + 2 * d) % blocks) for i in range(bloc...  18.7 us
    all_to_all x3, waiting for transfers between devices, swap(): return lax.all_to_all(array, axis, split_axis=0, concat_axis=0, tiled=True)  10.4 us
  transfers between devices with their start and end apart: 28, of which 6 were waited for; matrix products, arithmetic and copies ran while one was open for 0% of the time, Pallas kernels for 15%

profile of v4, /device:TPU:1, one launch (start us, length us, event | category | flops | bytes accessed | tf_op | source)
XLA Modules:
  0.0 159.7 jit_solution(10043765940847058994)
XLA Ops:
  0.6 3.9 %shard_map.112 = (bf16[256,128]{1,0:T(8,128)(2,1)S(1)}, bf16[128,256]{1,0:T(8,128)(2,1)S(1)}, s32[32,8,128]{2,1,0:T(8,128)}, bf16[2048,256]{1,0:T(8,128)(2,1)S(1)}) custom-call(s32[4,256]{1,0:T(4,128)} %bitcast.20, s32[4,256]{1,0:T(4,128)} %bitcast.21, s32[1,256]{1,0:T(1,128)} %bitcast.24, f32[2048,256]{1,0:T(8,128)} %refs_3_.2), custom_call_target="tpu_custom_call" | custom-call | flops 402653184 | bytes 2106368 | tf_op jit(solution)/shard_map/pallas_call | solution.py:95
  4.6 21.2 %all_to_all.25.ask_ref = s32[32,8,128]{2,1,0:T(8,128)S(1)} all-to-all(s32[32,8,128]{2,1,0:T(8,128)} %get-tuple-element.21), channel_id=1, replica_groups=mesh['shard'=32,'blk'=8] {'shard'}, dimensions={0} | all-to-all | bytes 262144 | tf_op jit(solution)/shard_map/all_to_all | solution.py:352
  25.8 5.8 %shard_map.113 = bf16[32,64,256]{2,1,0:T(8,128)(2,1)} custom-call(s32[32,8,128]{2,1,0:T(8,128)S(1)} %all_to_all.25.ask_ref, bf16[2048,256]{1,0:T(8,128)(2,1)S(1)} %get-tuple-element.22.table_ref), custom_call_target="tpu_custom_call" | custom-call | flops 2147483648 | bytes 1179648 | tf_op jit(solution)/shard_map/pallas_call | solution.py:95
  31.6 3.9 %all-to-all-start.1 = ((bf16[32,64,256]{2,1,0:T(8,128)(2,1)}), bf16[32,64,256]{2,1,0:T(8,128)(2,1)S(1)}, u32[]{:S(2)}, u32[]{:S(2)}) async-start(bf16[32,64,256]{2,1,0:T(8,128)(2,1)} %shard_map.113), calls=%async_computation.1 | async-start | bytes 2097152 | tf_op jit(solution)/shard_map/all_to_all | solution.py:352
  35.5 1.7 %shard_map.115.refs_5_ = bf16[272,256]{1,0:T(8,128)(2,1)} custom-call(bf16[256,256]{1,0:T(8,128)(2,1)} %refs_2_, s32[4,256]{1,0:T(4,128)} %bitcast.22), custom_call_target="tpu_custom_call" | custom-call | bytes 135168 | tf_op jit(solution)/shard_map/pallas_call | solution.py:95
  37.3 1.2 collective-permute-start
  38.5 2.5 %collective-permute-start.1 = (bf16[272,256]{1,0:T(8,128)(2,1)}, bf16[272,256]{1,0:T(8,128)(2,1)S(1)}, u32[]{:S(2)}, u32[]{:S(2)}) collective-permute-start(bf16[272,256]{1,0:T(8,128)(2,1)} %shard_map.115.refs_5_), channel_id=1, source_target_pairs={{0,4},{1,5},{2,6},{3,7},{4,0},{5,1},{6,2},{7,3},{8,12},{9,13},{10,... | collective-permute-start | bytes 417800 | tf_op jit(solution)/shard_map/ppermute | solution.py:360
  40.9 1.2 collective-permute-start.2
  42.1 2.9 %collective-permute-start.3 = (bf16[272,256]{1,0:T(8,128)(2,1)}, bf16[272,256]{1,0:T(8,128)(2,1)S(1)}, u32[]{:S(2)}, u32[]{:S(2)}) collective-permute-start(bf16[272,256]{1,0:T(8,128)(2,1)} %shard_map.115.refs_5_), channel_id=1, source_target_pairs={{0,1},{1,0},{2,3},{3,2},{4,5},{5,4},{6,7},{7,6},{8,9},{9,8},{10,11... | collective-permute-start | bytes 417800 | tf_op jit(solution)/shard_map/ppermute | solution.py:356
  45.0 0.0 collective-permute-done.refs_6_
  45.0 2.3 %collective-permute-start.4 = (bf16[272,256]{1,0:T(8,128)(2,1)S(1)}, bf16[272,256]{1,0:T(8,128)(2,1)S(1)}, u32[]{:S(2)}, u32[]{:S(2)}) collective-permute-start(bf16[272,256]{1,0:T(8,128)(2,1)S(1)} %collective-permute-done.refs_6_), channel_id=1, source_target_pairs={{0,1},{1,0},{2,3},{3,2},{4,5},{5,4},{6,7},{7,6},{8,9},{9,8},{10,11... | collective-permute-start | bytes 417800 | tf_op jit(solution)/shard_map/ppermute | solution.py:356
  47.2 1.5 collective-permute-start.5
  48.7 0.0 collective-permute-done.2.refs_8_
  48.7 0.1 collective-permute-start.6
  50.1 6.8 %shard_map.114 = (bf16[256,2048]{1,0:T(8,128)(2,1)S(1)}, bf16[2048,256]{1,0:T(8,128)(2,1)}, f32[256,256]{1,0:T(8,128)}) custom-call(bf16[256,128]{1,0:T(8,128)(2,1)S(1)} %get-tuple-element.27.refs_0_, bf16[128,256]{1,0:T(8,128)(2,1)S(1)} %get-tuple-element.28.refs_1_, s32[4,256]{1,0:T(4,128)} %bitcast.23, bf16[2048,256]{1,0:T(8,128)(2,1)} %refs_3_.3), custom_call_target="tpu_custom_call" | custom-call | flops 536870912 | bytes 1183744 | tf_op jit(solution)/shard_map/pallas_call | solution.py:95
  56.9 0.0 collective-permute-done.3.refs_9_
  56.9 0.0 collective-permute-done.5.refs_11_
  56.9 0.0 collective-permute-done.6.refs_12_
  56.9 3.1 %all-to-all-done.1 = bf16[32,64,256]{2,1,0:T(8,128)(2,1)S(1)} async-done(((bf16[32,64,256]{2,1,0:T(8,128)(2,1)}), bf16[32,64,256]{2,1,0:T(8,128)(2,1)S(1)}, u32[]{:S(2)}, u32[]{:S(2)}) %all-to-all-start.1) | async-done | bytes 1048608 | tf_op jit(solution)/shard_map/all_to_all | solution.py:352
  60.1 7.5 %shard_map.116 = (bf16[512,256]{1,0:T(8,128)(2,1)}, bf16[8,16,256]{2,1,0:T(8,128)(2,1)S(1)}, bf16[2048,256]{1,0:T(8,128)(2,1)}) custom-call(f32[1]{0:T(128)S(6)} %copy.12.refs_0_, f32[1]{0:T(128)S(6)} %copy.13.refs_1_, bf16[2048,256]{1,0:T(8,128)(2,1)S(1)} %bitcast.10, bf16[256,2048]{1,0:T(8,128)(2,1)S(1)} %get-tuple-element.29.refs_3_, ...), custom_call_target="tpu_custom_call" | custom-call | flops 1073741824 | bytes 4521992 | tf_op jit(solution)/shard_map/pallas_call | solution.py:95
  67.6 8.2 %all-to-all-start.4 = ((bf16[32,64,256]{2,1,0:T(8,128)(2,1)}), bf16[32,64,256]{2,1,0:T(8,128)(2,1)S(1)}, u32[]{:S(2)}, u32[]{:S(2)}) async-start(bf16[32,64,256]{2,1,0:T(8,128)(2,1)} %bitcast.18), calls=%async_computation.4 | async-start | bytes 2097152 | tf_op jit(solution)/shard_map/all_to_all | solution.py:352
  75.9 1.3 collective-permute-start.7
  77.1 2.5 %collective-permute-start.8 = (bf16[512,256]{1,0:T(8,128)(2,1)S(1)}, bf16[512,256]{1,0:T(8,128)(2,1)S(1)}, u32[]{:S(2)}, u32[]{:S(2)}) collective-permute-start(bf16[512,256]{1,0:T(8,128)(2,1)S(1)} %copy-done.2), channel_id=1, source_target_pairs={{0,4},{1,5},{2,6},{3,7},{4,0},{5,1},{6,2},{7,3},{8,12},{9,13},{10,... | collective-permute-start | bytes 786440 | tf_op jit(solution)/shard_map/ppermute | solution.py:360
  79.6 1.1 collective-permute-start.9
  80.7 2.9 %collective-permute-start.10 = (bf16[512,256]{1,0:T(8,128)(2,1)S(1)}, bf16[512,256]{1,0:T(8,128)(2,1)S(1)}, u32[]{:S(2)}, u32[]{:S(2)}) collective-permute-start(bf16[512,256]{1,0:T(8,128)(2,1)S(1)} %copy-done.2), channel_id=1, source_target_pairs={{0,1},{1,0},{2,3},{3,2},{4,5},{5,4},{6,7},{7,6},{8,9},{9,8},{10,11... | collective-permute-start | bytes 786440 | tf_op jit(solution)/shard_map/ppermute | solution.py:356
  83.6 0.0 collective-permute-done.7.refs_4_.refs_3_
  83.6 3.7 %collective-permute-start.11 = (bf16[512,256]{1,0:T(8,128)(2,1)S(1)}, bf16[512,256]{1,0:T(8,128)(2,1)S(1)}, u32[]{:S(2)}, u32[]{:S(2)}) collective-permute-start(bf16[512,256]{1,0:T(8,128)(2,1)S(1)} %collective-permute-done.7.refs_4_.refs_3_), channel_id=1, source_target_pairs={{0,1},{1,0},{2,3},{3,2},{4,5},{5,4},{6,7},{7,6},{8,9},{9,8},{10,11... | collective-permute-start | bytes 786440 | tf_op jit(solution)/shard_map/ppermute | solution.py:356
  87.4 2.2 %collective-permute-done.8.refs_5_.refs_4_ = bf16[512,256]{1,0:T(8,128)(2,1)S(1)} collective-permute-done((bf16[512,256]{1,0:T(8,128)(2,1)S(1)}, bf16[512,256]{1,0:T(8,128)(2,1)S(1)}, u32[]{:S(2)}, u32[]{:S(2)}) %collective-permute-start.8) | collective-permute-done | bytes 262176 | tf_op jit(solution)/shard_map/ppermute | solution.py:360
  89.6 2.9 %collective-permute-start.12 = (bf16[512,256]{1,0:T(8,128)(2,1)S(1)}, bf16[512,256]{1,0:T(8,128)(2,1)S(1)}, u32[]{:S(2)}, u32[]{:S(2)}) collective-permute-start(bf16[512,256]{1,0:T(8,128)(2,1)S(1)} %collective-permute-done.8.refs_5_.refs_4_), channel_id=1, source_target_pairs={{0,1},{1,0},{2,3},{3,2},{4,5},{5,4},{6,7},{7,6},{8,9},{9,8},{10,11... | collective-permute-start | bytes 786440 | tf_op jit(solution)/shard_map/ppermute | solution.py:356
  92.5 0.0 collective-permute-done.9.refs_6_.refs_5_
  92.5 0.0 collective-permute-start.13
  92.5 0.0 collective-permute-done.10.refs_7_.refs_6_
  92.5 1.1 collective-permute-done.12.refs_9_.refs_8_
  93.6 0.4 collective-permute-done.13.refs_10_.refs_9_
  94.0 3.4 %shard_map.118 = bf16[256,256]{1,0:T(8,128)(2,1)} custom-call(s32[1]{0:T(128)} %bitcast.5.refs_0_.block_ref, bf16[8,16,256]{2,1,0:T(8,128)(2,1)S(1)} %get-tuple-element.33.refs_1_, bf16[512,256]{1,0:T(8,128)(2,1)} %get-tuple-element.32.refs_3_.refs_2_, bf16[512,256]{1,0:T(8,128)(2,1)S(1)} %collective-permute-done.7.refs_4_.refs_3_, ...), custom_call_target="tpu_custom_call" | custom-call | flops 268435456 | bytes 2162692 | tf_op jit(solution)/shard_map/pallas_call | solution.py:95
  97.4 3.0 %all-to-all-done.4 = bf16[32,64,256]{2,1,0:T(8,128)(2,1)S(1)} async-done(((bf16[32,64,256]{2,1,0:T(8,128)(2,1)}), bf16[32,64,256]{2,1,0:T(8,128)(2,1)S(1)}, u32[]{:S(2)}, u32[]{:S(2)}) %all-to-all-start.4) | async-done | bytes 1048608 | tf_op jit(solution)/shard_map/all_to_all | solution.py:352
  100.4 8.1 %all-to-all-start.2 = ((bf16[32,8,256]{2,1,0:T(8,128)(2,1)}), bf16[32,8,256]{2,1,0:T(8,128)(2,1)S(1)}, u32[]{:S(2)}, u32[]{:S(2)}) async-start(bf16[32,8,256]{2,1,0:T(8,128)(2,1)} %bitcast.19), calls=%async_computation.2 | async-start | bytes 262144 | tf_op jit(solution)/shard_map/all_to_all | solution.py:352
  108.5 2.8 %shard_map.122 = bf16[4,256,256]{2,1,0:T(8,128)(2,1)} custom-call(s32[1]{0:T(128)} %bitcast.5.refs_0_.block_ref, s32[32,8,128]{2,1,0:T(8,128)S(1)} %all_to_all.25.ask_ref, bf16[2048,256]{1,0:T(8,128)(2,1)S(1)} %bitcast.11), custom_call_target="tpu_custom_call" | custom-call | flops 1073741824 | bytes 1179652 | tf_op jit(solution)/shard_map/pallas_call | solution.py:95
  111.2 2.1 %collective-permute-start.21 = (bf16[4,256,256]{2,1,0:T(8,128)(2,1)}, bf16[4,256,256]{2,1,0:T(8,128)(2,1)S(1)}, u32[]{:S(2)}, u32[]{:S(2)}) collective-permute-start(bf16[4,256,256]{2,1,0:T(8,128)(2,1)} %shard_map.122), channel_id=1, source_target_pairs={{0,1},{1,0},{2,3},{3,2},{4,5},{5,4},{6,7},{7,6},{8,9},{9,8},{10,11... | collective-permute-start | bytes 1572872 | tf_op jit(solution)/shard_map/ppermute | solution.py:356
  113.3 4.3 %all-to-all-done.2.parts_ref = bf16[32,8,256]{2,1,0:T(8,128)(2,1)S(1)} async-done(((bf16[32,8,256]{2,1,0:T(8,128)(2,1)}), bf16[32,8,256]{2,1,0:T(8,128)(2,1)S(1)}, u32[]{:S(2)}, u32[]{:S(2)}) %all-to-all-start.2) | async-done | bytes 131104 | tf_op jit(solution)/shard_map/all_to_all | solution.py:352
  117.6 0.7 shard_map.119
  118.3 14.3 %all_to_all.26 = bf16[32,8,256]{2,1,0:T(8,128)(2,1)S(1)} all-to-all(bf16[32,8,256]{2,1,0:T(8,128)(2,1)} %shard_map.119), channel_id=1, replica_groups=mesh['shard'=32,'blk'=8] {'shard'}, dimensions={0} | all-to-all | bytes 262144 | tf_op jit(solution)/shard_map/all_to_all | solution.py:352
  132.7 1.2 collective-permute-start.14
  133.9 2.5 %collective-permute-start.15 = (bf16[256,256]{1,0:T(8,128)(2,1)S(1)}, bf16[256,256]{1,0:T(8,128)(2,1)S(1)}, u32[]{:S(2)}, u32[]{:S(2)}) collective-permute-start(bf16[256,256]{1,0:T(8,128)(2,1)S(1)} %bitcast.14), channel_id=1, source_target_pairs={{0,4},{1,5},{2,6},{3,7},{4,0},{5,1},{6,2},{7,3},{8,12},{9,13},{10,... | collective-permute-start | bytes 393224 | tf_op jit(solution)/shard_map/ppermute | solution.py:360
  136.3 1.1 collective-permute-start.16
  137.5 4.0 %collective-permute-start.17 = (bf16[256,256]{1,0:T(8,128)(2,1)S(1)}, bf16[256,256]{1,0:T(8,128)(2,1)S(1)}, u32[]{:S(2)}, u32[]{:S(2)}) collective-permute-start(bf16[256,256]{1,0:T(8,128)(2,1)S(1)} %bitcast.16), channel_id=1, source_target_pairs={{0,1},{1,0},{2,3},{3,2},{4,5},{5,4},{6,7},{7,6},{8,9},{9,8},{10,11... | collective-permute-start | bytes 393224 | tf_op jit(solution)/shard_map/ppermute | solution.py:356
  141.4 0.0 collective-permute-done.14.refs_1_
  141.4 0.7 collective-permute-start.18
  142.2 2.2 %collective-permute-start.19 = (bf16[256,256]{1,0:T(8,128)(2,1)S(1)}, bf16[256,256]{1,0:T(8,128)(2,1)S(1)}, u32[]{:S(2)}, u32[]{:S(2)}) collective-permute-start(bf16[256,256]{1,0:T(8,128)(2,1)S(1)} %collective-permute-done.15.refs_2_), channel_id=1, source_target_pairs={{0,1},{1,0},{2,3},{3,2},{4,5},{5,4},{6,7},{7,6},{8,9},{9,8},{10,11... | collective-permute-start | bytes 393224 | tf_op jit(solution)/shard_map/ppermute | solution.py:356
  144.4 0.6 collective-permute-start.20
  145.0 0.9 copy-done.1
  145.9 1.9 %shard_map.121.mine_ref = f32[4,256,256]{2,1,0:T(8,128)S(1)} custom-call(s32[1]{0:T(128)} %bitcast.5.refs_0_.block_ref, s32[32,8,128]{2,1,0:T(8,128)S(1)} %copy-done.1, bf16[2048,256]{1,0:T(8,128)(2,1)S(1)} %bitcast.12), custom_call_target="tpu_custom_call" | custom-call | flops 1073741824 | bytes 1179652 | tf_op jit(solution)/shard_map/pallas_call | solution.py:95
  147.8 0.1 shard_map.123
  147.9 1.1 collective-permute-start.22
  149.0 0.0 collective-permute-done.17.refs_4_
  149.0 2.5 %collective-permute-start.23 = (bf16[256,256]{1,0:T(8,128)(2,1)S(1)}, bf16[256,256]{1,0:T(8,128)(2,1)S(1)}, u32[]{:S(2)}, u32[]{:S(2)}) collective-permute-start(bf16[256,256]{1,0:T(8,128)(2,1)S(1)} %get-tuple-element.37), channel_id=1, source_target_pairs={{0,4},{1,5},{2,6},{3,7},{4,0},{5,1},{6,2},{7,3},{8,12},{9,13},{10,... | collective-permute-start | bytes 393224 | tf_op jit(solution)/shard_map/ppermute | solution.py:360
  151.5 0.0 collective-permute-done.18.refs_5_
  151.5 0.6 collective-permute-start.24
  152.1 5.4 %shard_map.117 = f32[256,256]{1,0:T(8,128)} custom-call(f32[1]{0:T(128)S(6)} %copy.12.refs_0_, f32[1]{0:T(128)S(6)} %copy.13.refs_1_, bf16[256,256]{1,0:T(8,128)(2,1)} %refs_2_, bf16[512,256]{1,0:T(8,128)(2,1)} %get-tuple-element.32.refs_3_.refs_2_, bf16[512,256]{1,0:T(8,128)(2,1)S(1)} %collective-permute-done.7.refs_4_.refs_3_, ...), custom_call_target="tpu_custom_call" | custom-call | flops 536870912 | bytes 2228232 | tf_op jit(solution)/shard_map/pallas_call | solution.py:95
  157.5 0.0 collective-permute-done.20.refs_7_
  157.5 1.5 shard_map.120
  159.0 0.0 collective-permute-done.22.refs_0_
  159.0 0.0 collective-permute-done.23.refs_1_
  159.0 0.8 shard_map.124
  (13 shorter events, 0.0 us)
Async XLA Ops:
  25.8 82.7 %copy-start = (s32[32,8,128]{2,1,0:T(8,128)}, s32[32,8,128]{2,1,0:T(8,128)S(1)}, u32[]{:S(2)}) copy-start(s32[32,8,128]{2,1,0:T(8,128)S(1)} %all_to_all.25.ask_ref) | copy-start | bytes 393220
  31.6 28.5 %all-to-all-start.1 = ((bf16[32,64,256]{2,1,0:T(8,128)(2,1)}), bf16[32,64,256]{2,1,0:T(8,128)(2,1)S(1)}, u32[]{:S(2)}, u32[]{:S(2)}) async-start(bf16[32,64,256]{2,1,0:T(8,128)(2,1)} %shard_map.113), calls=%async_computation.1 | async-start | bytes 2097152 | tf_op jit(solution)/shard_map/all_to_all | solution.py:352
  37.3 7.7 %collective-permute-start = (bf16[272,256]{1,0:T(8,128)(2,1)}, bf16[272,256]{1,0:T(8,128)(2,1)S(1)}, u32[]{:S(2)}, u32[]{:S(2)}) collective-permute-start(bf16[272,256]{1,0:T(8,128)(2,1)} %shard_map.115.refs_5_), channel_id=1, source_target_pairs={{0,2},{1,3},{2,4},{3,5},{4,6},{5,7},{6,0},{7,1},{8,10},{9,11},{10,... | collective-permute-start | bytes 417800 | tf_op jit(solution)/shard_map/ppermute | solution.py:360
  38.5 8.8 %collective-permute-start.1 = (bf16[272,256]{1,0:T(8,128)(2,1)}, bf16[272,256]{1,0:T(8,128)(2,1)S(1)}, u32[]{:S(2)}, u32[]{:S(2)}) collective-permute-start(bf16[272,256]{1,0:T(8,128)(2,1)} %shard_map.115.refs_5_), channel_id=1, source_target_pairs={{0,4},{1,5},{2,6},{3,7},{4,0},{5,1},{6,2},{7,3},{8,12},{9,13},{10,... | collective-permute-start | bytes 417800 | tf_op jit(solution)/shard_map/ppermute | solution.py:360
  40.9 7.8 %collective-permute-start.2 = (bf16[272,256]{1,0:T(8,128)(2,1)}, bf16[272,256]{1,0:T(8,128)(2,1)S(1)}, u32[]{:S(2)}, u32[]{:S(2)}) collective-permute-start(bf16[272,256]{1,0:T(8,128)(2,1)} %shard_map.115.refs_5_), channel_id=1, source_target_pairs={{0,6},{1,7},{2,0},{3,1},{4,2},{5,3},{6,4},{7,5},{8,14},{9,15},{10,... | collective-permute-start | bytes 417800 | tf_op jit(solution)/shard_map/ppermute | solution.py:360
  42.1 14.8 %collective-permute-start.3 = (bf16[272,256]{1,0:T(8,128)(2,1)}, bf16[272,256]{1,0:T(8,128)(2,1)S(1)}, u32[]{:S(2)}, u32[]{:S(2)}) collective-permute-start(bf16[272,256]{1,0:T(8,128)(2,1)} %shard_map.115.refs_5_), channel_id=1, source_target_pairs={{0,1},{1,0},{2,3},{3,2},{4,5},{5,4},{6,7},{7,6},{8,9},{9,8},{10,11... | collective-permute-start | bytes 417800 | tf_op jit(solution)/shard_map/ppermute | solution.py:356
  45.0 11.9 %collective-permute-start.4 = (bf16[272,256]{1,0:T(8,128)(2,1)S(1)}, bf16[272,256]{1,0:T(8,128)(2,1)S(1)}, u32[]{:S(2)}, u32[]{:S(2)}) collective-permute-start(bf16[272,256]{1,0:T(8,128)(2,1)S(1)} %collective-permute-done.refs_6_), channel_id=1, source_target_pairs={{0,1},{1,0},{2,3},{3,2},{4,5},{5,4},{6,7},{7,6},{8,9},{9,8},{10,11... | collective-permute-start | bytes 417800 | tf_op jit(solution)/shard_map/ppermute | solution.py:356
  47.2 9.7 %collective-permute-start.5 = (bf16[272,256]{1,0:T(8,128)(2,1)S(1)}, bf16[272,256]{1,0:T(8,128)(2,1)S(1)}, u32[]{:S(2)}, u32[]{:S(2)}) collective-permute-start(bf16[272,256]{1,0:T(8,128)(2,1)S(1)} %collective-permute-done.1.refs_7_), channel_id=1, source_target_pairs={{0,1},{1,0},{2,3},{3,2},{4,5},{5,4},{6,7},{7,6},{8,9},{9,8},{10,11... | collective-permute-start | bytes 417800 | tf_op jit(solution)/shard_map/ppermute | solution.py:356
  48.7 8.2 %collective-permute-start.6 = (bf16[272,256]{1,0:T(8,128)(2,1)S(1)}, bf16[272,256]{1,0:T(8,128)(2,1)S(1)}, u32[]{:S(2)}, u32[]{:S(2)}) collective-permute-start(bf16[272,256]{1,0:T(8,128)(2,1)S(1)} %collective-permute-done.2.refs_8_), channel_id=1, source_target_pairs={{0,1},{1,0},{2,3},{3,2},{4,5},{5,4},{6,7},{7,6},{8,9},{9,8},{10,11... | collective-permute-start | bytes 417800 | tf_op jit(solution)/shard_map/ppermute | solution.py:356
  67.6 8.3 %copy-start.2 = (bf16[512,256]{1,0:T(8,128)(2,1)S(1)}, bf16[512,256]{1,0:T(8,128)(2,1)}, u32[]{:S(2)}) copy-start(bf16[512,256]{1,0:T(8,128)(2,1)} %get-tuple-element.32.refs_3_.refs_2_) | copy-start | bytes 786436
  67.6 32.8 %all-to-all-start.4 = ((bf16[32,64,256]{2,1,0:T(8,128)(2,1)}), bf16[32,64,256]{2,1,0:T(8,128)(2,1)S(1)}, u32[]{:S(2)}, u32[]{:S(2)}) async-start(bf16[32,64,256]{2,1,0:T(8,128)(2,1)} %bitcast.18), calls=%async_computation.4 | async-start | bytes 2097152 | tf_op jit(solution)/shard_map/all_to_all | solution.py:352
  75.9 7.8 %collective-permute-start.7 = (bf16[512,256]{1,0:T(8,128)(2,1)S(1)}, bf16[512,256]{1,0:T(8,128)(2,1)S(1)}, u32[]{:S(2)}, u32[]{:S(2)}) collective-permute-start(bf16[512,256]{1,0:T(8,128)(2,1)S(1)} %copy-done.2), channel_id=1, source_target_pairs={{0,2},{1,3},{2,4},{3,5},{4,6},{5,7},{6,0},{7,1},{8,10},{9,11},{10,... | collective-permute-start | bytes 786440 | tf_op jit(solution)/shard_map/ppermute | solution.py:360
  77.1 12.4 %collective-permute-start.8 = (bf16[512,256]{1,0:T(8,128)(2,1)S(1)}, bf16[512,256]{1,0:T(8,128)(2,1)S(1)}, u32[]{:S(2)}, u32[]{:S(2)}) collective-permute-start(bf16[512,256]{1,0:T(8,128)(2,1)S(1)} %copy-done.2), channel_id=1, source_target_pairs={{0,4},{1,5},{2,6},{3,7},{4,0},{5,1},{6,2},{7,3},{8,12},{9,13},{10,... | collective-permute-start | bytes 786440 | tf_op jit(solution)/shard_map/ppermute | solution.py:360
  79.6 12.9 %collective-permute-start.9 = (bf16[512,256]{1,0:T(8,128)(2,1)S(1)}, bf16[512,256]{1,0:T(8,128)(2,1)S(1)}, u32[]{:S(2)}, u32[]{:S(2)}) collective-permute-start(bf16[512,256]{1,0:T(8,128)(2,1)S(1)} %copy-done.2), channel_id=1, source_target_pairs={{0,6},{1,7},{2,0},{3,1},{4,2},{5,3},{6,4},{7,5},{8,14},{9,15},{10,... | collective-permute-start | bytes 786440 | tf_op jit(solution)/shard_map/ppermute | solution.py:360
  80.7 11.7 %collective-permute-start.10 = (bf16[512,256]{1,0:T(8,128)(2,1)S(1)}, bf16[512,256]{1,0:T(8,128)(2,1)S(1)}, u32[]{:S(2)}, u32[]{:S(2)}) collective-permute-start(bf16[512,256]{1,0:T(8,128)(2,1)S(1)} %copy-done.2), channel_id=1, source_target_pairs={{0,1},{1,0},{2,3},{3,2},{4,5},{5,4},{6,7},{7,6},{8,9},{9,8},{10,11... | collective-permute-start | bytes 786440 | tf_op jit(solution)/shard_map/ppermute | solution.py:356
  83.6 8.8 %collective-permute-start.11 = (bf16[512,256]{1,0:T(8,128)(2,1)S(1)}, bf16[512,256]{1,0:T(8,128)(2,1)S(1)}, u32[]{:S(2)}, u32[]{:S(2)}) collective-permute-start(bf16[512,256]{1,0:T(8,128)(2,1)S(1)} %collective-permute-done.7.refs_4_.refs_3_), channel_id=1, source_target_pairs={{0,1},{1,0},{2,3},{3,2},{4,5},{5,4},{6,7},{7,6},{8,9},{9,8},{10,11... | collective-permute-start | bytes 786440 | tf_op jit(solution)/shard_map/ppermute | solution.py:356
  89.6 4.1 %collective-permute-start.12 = (bf16[512,256]{1,0:T(8,128)(2,1)S(1)}, bf16[512,256]{1,0:T(8,128)(2,1)S(1)}, u32[]{:S(2)}, u32[]{:S(2)}) collective-permute-start(bf16[512,256]{1,0:T(8,128)(2,1)S(1)} %collective-permute-done.8.refs_5_.refs_4_), channel_id=1, source_target_pairs={{0,1},{1,0},{2,3},{3,2},{4,5},{5,4},{6,7},{7,6},{8,9},{9,8},{10,11... | collective-permute-start | bytes 786440 | tf_op jit(solution)/shard_map/ppermute | solution.py:356
  92.5 1.5 collective-permute-start.13
  100.4 17.2 %all-to-all-start.2 = ((bf16[32,8,256]{2,1,0:T(8,128)(2,1)}), bf16[32,8,256]{2,1,0:T(8,128)(2,1)S(1)}, u32[]{:S(2)}, u32[]{:S(2)}) async-start(bf16[32,8,256]{2,1,0:T(8,128)(2,1)} %bitcast.19), calls=%async_computation.2 | async-start | bytes 262144 | tf_op jit(solution)/shard_map/all_to_all | solution.py:352
  111.2 36.6 %collective-permute-start.21 = (bf16[4,256,256]{2,1,0:T(8,128)(2,1)}, bf16[4,256,256]{2,1,0:T(8,128)(2,1)S(1)}, u32[]{:S(2)}, u32[]{:S(2)}) collective-permute-start(bf16[4,256,256]{2,1,0:T(8,128)(2,1)} %shard_map.122), channel_id=1, source_target_pairs={{0,1},{1,0},{2,3},{3,2},{4,5},{5,4},{6,7},{7,6},{8,9},{9,8},{10,11... | collective-permute-start | bytes 1572872 | tf_op jit(solution)/shard_map/ppermute | solution.py:356
  132.7 8.8 %collective-permute-start.14 = (bf16[256,256]{1,0:T(8,128)(2,1)S(1)}, bf16[256,256]{1,0:T(8,128)(2,1)S(1)}, u32[]{:S(2)}, u32[]{:S(2)}) collective-permute-start(bf16[256,256]{1,0:T(8,128)(2,1)S(1)} %bitcast.13), channel_id=1, source_target_pairs={{0,2},{1,3},{2,4},{3,5},{4,6},{5,7},{6,0},{7,1},{8,10},{9,11},{10,... | collective-permute-start | bytes 393224 | tf_op jit(solution)/shard_map/ppermute | solution.py:360
  133.9 8.3 %collective-permute-start.15 = (bf16[256,256]{1,0:T(8,128)(2,1)S(1)}, bf16[256,256]{1,0:T(8,128)(2,1)S(1)}, u32[]{:S(2)}, u32[]{:S(2)}) collective-permute-start(bf16[256,256]{1,0:T(8,128)(2,1)S(1)} %bitcast.14), channel_id=1, source_target_pairs={{0,4},{1,5},{2,6},{3,7},{4,0},{5,1},{6,2},{7,3},{8,12},{9,13},{10,... | collective-permute-start | bytes 393224 | tf_op jit(solution)/shard_map/ppermute | solution.py:360
  136.3 8.1 %collective-permute-start.16 = (bf16[256,256]{1,0:T(8,128)(2,1)S(1)}, bf16[256,256]{1,0:T(8,128)(2,1)S(1)}, u32[]{:S(2)}, u32[]{:S(2)}) collective-permute-start(bf16[256,256]{1,0:T(8,128)(2,1)S(1)} %bitcast.15), channel_id=1, source_target_pairs={{0,6},{1,7},{2,0},{3,1},{4,2},{5,3},{6,4},{7,5},{8,14},{9,15},{10,... | collective-permute-start | bytes 393224 | tf_op jit(solution)/shard_map/ppermute | solution.py:360
  137.5 11.5 %collective-permute-start.17 = (bf16[256,256]{1,0:T(8,128)(2,1)S(1)}, bf16[256,256]{1,0:T(8,128)(2,1)S(1)}, u32[]{:S(2)}, u32[]{:S(2)}) collective-permute-start(bf16[256,256]{1,0:T(8,128)(2,1)S(1)} %bitcast.16), channel_id=1, source_target_pairs={{0,1},{1,0},{2,3},{3,2},{4,5},{5,4},{6,7},{7,6},{8,9},{9,8},{10,11... | collective-permute-start | bytes 393224 | tf_op jit(solution)/shard_map/ppermute | solution.py:356
  141.4 10.1 %collective-permute-start.18 = (bf16[256,256]{1,0:T(8,128)(2,1)S(1)}, bf16[256,256]{1,0:T(8,128)(2,1)S(1)}, u32[]{:S(2)}, u32[]{:S(2)}) collective-permute-start(bf16[256,256]{1,0:T(8,128)(2,1)S(1)} %collective-permute-done.14.refs_1_), channel_id=1, source_target_pairs={{0,1},{1,0},{2,3},{3,2},{4,5},{5,4},{6,7},{7,6},{8,9},{9,8},{10,11... | collective-permute-start | bytes 393224 | tf_op jit(solution)/shard_map/ppermute | solution.py:356
  142.2 15.3 %collective-permute-start.19 = (bf16[256,256]{1,0:T(8,128)(2,1)S(1)}, bf16[256,256]{1,0:T(8,128)(2,1)S(1)}, u32[]{:S(2)}, u32[]{:S(2)}) collective-permute-start(bf16[256,256]{1,0:T(8,128)(2,1)S(1)} %collective-permute-done.15.refs_2_), channel_id=1, source_target_pairs={{0,1},{1,0},{2,3},{3,2},{4,5},{5,4},{6,7},{7,6},{8,9},{9,8},{10,11... | collective-permute-start | bytes 393224 | tf_op jit(solution)/shard_map/ppermute | solution.py:356
  144.4 13.1 %collective-permute-start.20 = (bf16[256,256]{1,0:T(8,128)(2,1)S(1)}, bf16[256,256]{1,0:T(8,128)(2,1)S(1)}, u32[]{:S(2)}, u32[]{:S(2)}) collective-permute-start(bf16[256,256]{1,0:T(8,128)(2,1)S(1)} %collective-permute-done.16.refs_3_), channel_id=1, source_target_pairs={{0,1},{1,0},{2,3},{3,2},{4,5},{5,4},{6,7},{7,6},{8,9},{9,8},{10,11... | collective-permute-start | bytes 393224 | tf_op jit(solution)/shard_map/ppermute | solution.py:356
  145.0 0.9 copy-start.1
  147.9 11.1 %collective-permute-start.22 = (bf16[256,256]{1,0:T(8,128)(2,1)S(1)}, bf16[256,256]{1,0:T(8,128)(2,1)S(1)}, u32[]{:S(2)}, u32[]{:S(2)}) collective-permute-start(bf16[256,256]{1,0:T(8,128)(2,1)S(1)} %get-tuple-element.36), channel_id=1, source_target_pairs={{0,2},{1,3},{2,4},{3,5},{4,6},{5,7},{6,0},{7,1},{8,10},{9,11},{10,... | collective-permute-start | bytes 393224 | tf_op jit(solution)/shard_map/ppermute | solution.py:360
  149.0 10.0 %collective-permute-start.23 = (bf16[256,256]{1,0:T(8,128)(2,1)S(1)}, bf16[256,256]{1,0:T(8,128)(2,1)S(1)}, u32[]{:S(2)}, u32[]{:S(2)}) collective-permute-start(bf16[256,256]{1,0:T(8,128)(2,1)S(1)} %get-tuple-element.37), channel_id=1, source_target_pairs={{0,4},{1,5},{2,6},{3,7},{4,0},{5,1},{6,2},{7,3},{8,12},{9,13},{10,... | collective-permute-start | bytes 393224 | tf_op jit(solution)/shard_map/ppermute | solution.py:360
  151.5 7.4 %collective-permute-start.24 = (bf16[256,256]{1,0:T(8,128)(2,1)S(1)}, bf16[256,256]{1,0:T(8,128)(2,1)S(1)}, u32[]{:S(2)}, u32[]{:S(2)}) collective-permute-start(bf16[256,256]{1,0:T(8,128)(2,1)S(1)} %get-tuple-element.38), channel_id=1, source_target_pairs={{0,6},{1,7},{2,0},{3,1},{4,2},{5,3},{6,4},{7,5},{8,14},{9,15},{10,... | collective-permute-start | bytes 393224 | tf_op jit(solution)/shard_map/ppermute | solution.py:360

commit v5 on v4

v5 whole, which is shorter than its diff:
```python
import jax
import jax.numpy as jnp
from jax import lax
from jax.experimental import pallas as pl
from jax.experimental.pallas import tpu as pltpu
from jax.sharding import PartitionSpec as P


epsilon = 1e-06
F32 = jnp.float32
BF16 = jnp.bfloat16
NN = (((1,), (0,)), ((), ()))
NT = (((1,), (1,)), ((), ()))


def mm(a, b, dims=NN):
    return lax.dot_general(a, b, dims, preferred_element_type=F32)


def iota(shape, dim):
    return lax.broadcasted_iota(jnp.int32, shape, dim)


HBM = pltpu.HBM


class Late:
    def __init__(self, source, buffer, sem):
        self.copy = pltpu.make_async_copy(source, buffer, sem)
        self.buffer = buffer
        self.copy.start()
        self.waits = True

    def get(self):
        if self.waits:
            self.copy.wait()
            self.waits = False
        return self.buffer


class Leave:
    def __init__(self, out_ref, stage_ref, sem):
        self.out, self.stage, self.sem = out_ref, stage_ref, sem
        self.steps = sem.shape[0]
        self.width = stage_ref.shape[0] // self.steps

    def copy(self, i):
        part = pl.ds(i * self.width, self.width)
        return pltpu.make_async_copy(self.stage.at[part], self.out.at[part], self.sem.at[i])

    def write(self, value):
        self.stage[...] = value
        self.start()

    def start(self):
        for i in range(self.steps):
            self.copy(i).start()

    def finish(self):
        for i in range(self.steps):
            self.copy(i).wait()

    def run(self, compute):
        def step(i, _):
            self.stage[pl.ds(i * self.width, self.width)] = compute(i)
            self.copy(i).start()
            return 0

        def finish(i, _):
            self.copy(i).wait()
            return 0

        lax.fori_loop(0, self.steps, step, 0)
        lax.fori_loop(0, self.steps, finish, 0)


def call(kernel, outs, *args, kinds=None, scratch=(), flops=0, steps=1):
    kinds = kinds or ["v"] * len(args)
    late = [k for k, kind in enumerate(kinds) if kind == "h" or isinstance(kind, slice)]
    leaves = [k for k, out in enumerate(outs) if not isinstance(out, jax.ShapeDtypeStruct)]
    operands = [pltpu.with_memory_space_constraint(a, HBM) if k in late else a for k, a in enumerate(args)]
    spaces = [pltpu.SMEM if kind == "s" else HBM if k in late else pltpu.VMEM for k, kind in enumerate(kinds)]
    buffers = []
    for k in late:
        rows = args[k].shape[0] if kinds[k] == "h" else kinds[k].stop - kinds[k].start
        buffers += [pltpu.VMEM((rows,) + args[k].shape[1:], args[k].dtype), pltpu.SemaphoreType.DMA]
    for k in leaves:
        buffers += [pltpu.VMEM(outs[k].shape, outs[k].dtype), pltpu.SemaphoreType.DMA((steps,))]

    def run(*refs):
        refs, extra = list(refs[: len(refs) - len(buffers)]), list(refs[len(refs) - len(buffers) :])
        for k in late:
            source = refs[k] if kinds[k] == "h" else refs[k].at[kinds[k]]
            refs[k] = Late(source, extra.pop(0), extra.pop(0))
        for k in leaves:
            refs[len(args) + k] = Leave(refs[len(args) + k], extra.pop(0), extra.pop(0))
        kernel(*refs)

    moved = sum(a.size * a.dtype.itemsize for a in args)
    return pl.pallas_call(
        run,
        out_shape=list(outs),
        in_specs=[pl.BlockSpec(memory_space=space) for space in spaces],
        out_specs=[pl.BlockSpec(memory_space=HBM if k in leaves else pltpu.VMEM) for k in range(len(outs))],
        scratch_shapes=list(scratch) + buffers,
        compiler_params=pltpu.CompilerParams(vmem_limit_bytes=24 << 20),
        cost_estimate=pl.CostEstimate(flops=flops, bytes_accessed=moved, transcendentals=0),
    )(*operands)


def shape(dims, dtype):
    return jax.ShapeDtypeStruct(dims, dtype)


def expander(owners, cap, base, width):
    return ((iota((owners, width), 1) + base) // cap == iota((owners, width), 0)).astype(F32).astype(BF16)


LANES = 128


def make_requests(owners, cap):
    def kernel(parent, place, tally, table, rank_ref, rank_t_ref, ask, table_low_ref, row_ref):
        parent_ref, place_ref = parent.get(), place.get()
        slots, pairs = parent_ref.shape
        line = iota((LANES, pairs), 0)
        tally = tally.get()[...]
        named = jnp.zeros((LANES, pairs), F32)
        where = jnp.zeros((LANES, pairs), F32)
        for c in range(slots):
            hit = jnp.logical_and(parent_ref[c : c + 1, :] == line, tally > c)
            named = jnp.where(hit, 1.0, named)
            where = jnp.where(hit, place_ref[c : c + 1, :].astype(F32), where)
        before = (iota((pairs, pairs), 0) < iota((pairs, pairs), 1)).astype(F32).astype(BF16)
        rank_t = jnp.where(named > 0, mm(named.astype(BF16), before), -1.0)
        rank = rank_t.T
        rank_t_ref[...] = rank_t.astype(BF16)
        rank_ref[...] = rank.astype(BF16)
        where = where.T.astype(jnp.int32)
        high = (where // 64).astype(F32).astype(BF16)
        low = (where % 64).astype(F32).astype(BF16)
        rank = rank.astype(BF16)
        total = owners * cap
        width = 512
        for base in range(0, total, width):
            spread = expander(LANES, cap, base, width)
            want = (iota((pairs, width), 1) % cap).astype(F32)
            place = mm(high, spread) * 64.0 + mm(low, spread)
            row_ref[:, base : base + width] = jnp.sum(
                jnp.where(mm(rank, spread) == want, place, 0.0), axis=0, keepdims=True
            )
        for o in range(owners):
            row = row_ref[:, o * cap : (o + 1) * cap].astype(jnp.int32)
            ask.stage[o, :, 0:cap] = jnp.broadcast_to(row, (ask.stage.shape[1], cap))
        ask.start()
        table_low_ref[...] = table.get()[...].astype(BF16)
        ask.finish()

    return kernel


def normalize(rows):
    radius = jnp.sqrt(jnp.sum(rows * rows, axis=1, keepdims=True) + epsilon)
    return rows / radius, radius


def unit_queries(query, lines, send_ref):
    query_ref, lines_ref = query.get(), lines.get()
    pairs = query_ref.shape[0]
    slots = lines_ref.shape[0]
    unit, _ = normalize(query_ref[...].astype(F32))
    send_ref[0:pairs, :] = unit.astype(BF16)
    tail = send_ref.shape[0] - pairs
    line = iota((tail, pairs), 0)
    extra = jnp.zeros((tail, pairs), F32)
    for h in range(slots):
        row = lines_ref[h : h + 1, :]
        extra = jnp.where(line == h, (row // 64).astype(F32), extra)
        extra = jnp.where(line == h + slots, (row % 64).astype(F32), extra)
    send_ref[pairs:, :] = extra.astype(BF16)


def prepare(cap):
    def kernel(rank_ref, rank_t_ref, lines, hot, pick_ref, placed, hot_sum):
        lines_ref = lines.get()
        pairs = rank_ref.shape[0]
        slots = lines_ref.shape[0]
        rank, rank_t = rank_ref[...], rank_t_ref[...]
        line = iota((LANES, pairs), 0)
        lines = jnp.zeros((LANES, pairs), F32)
        for h in range(slots):
            lines = jnp.where(line == h, lines_ref[h : h + 1, :].astype(F32), lines)
        lines = lines.T.astype(jnp.int32)
        width = placed.width
        want = (iota((pairs, width), 1) % cap).astype(F32)
        want_t = (iota((width, pairs), 0) % cap).astype(F32)
        hot_ref = hot.get()
        hot_sum_ref = hot_sum.stage
        hot_sum_ref[...] = jnp.zeros_like(hot_sum_ref)

        def compute(i):
            base = pl.multiple_of(i * width, width)
            spread = expander(LANES, cap, base, width)
            pick_ref[:, pl.ds(base, width)] = (mm(rank, spread) == want).astype(F32).astype(BF16)
            column = iota((pairs, width), 1) + base
            counts = jnp.zeros((pairs, width), F32)
            for h in range(slots):
                counts += (lines[:, h : h + 1] == column).astype(F32)
            hot_sum_ref[...] += mm(counts.astype(BF16), hot_ref[pl.ds(base, width), :])
            spread_t = ((iota((width, LANES), 0) + base) // cap == iota((width, LANES), 1))
            hit = mm(spread_t.astype(F32).astype(BF16), rank_t) == want_t
            return hit.astype(F32).astype(BF16)

        placed.run(compute)
        hot_sum.start()
        hot_sum.finish()

    return kernel


def fetch(ask_ref, table_ref, out):
    rows = table_ref.shape[0]
    cap = out.stage.shape[1]
    group = out.width
    diagonal = iota((cap, cap), 0) == iota((cap, cap), 1)
    lane = iota((group * cap, rows), 1)

    def compute(i):
        columns = []
        for g in range(group):
            ask = ask_ref[i * group + g, 0:1, 0:cap]
            columns.append(jnp.sum(jnp.where(diagonal, ask, 0).astype(F32), axis=1, keepdims=True))
        column = jnp.concatenate(columns, axis=0).astype(jnp.int32)
        hit = (column == lane).astype(F32).astype(BF16)
        return mm(hit, table_ref[...]).astype(BF16).reshape(group, cap, table_ref.shape[1])

    out.run(compute)


def loss_side(own_low, other_refs, total_ref, sharpness, additive):
    rows = own_low.shape[0]
    for i, ref in enumerate(other_refs):
        other = ref[0:rows, :]
        grad = jax.nn.sigmoid(sharpness * mm(own_low, other, NT) + additive)
        if i == 0:
            grad = grad - (iota((rows, rows), 0) == iota((rows, rows), 1)).astype(F32)
            total_ref[...] = mm(grad.astype(BF16), other)
        else:
            total_ref[...] += mm(grad.astype(BF16), other)
    return sharpness * total_ref[...]


def project(unit, radius, direction):
    inner = jnp.sum(unit * direction, axis=1, keepdims=True)
    return (direction - unit * inner) / radius


def item_side(blocks):
    def kernel(sharp_ref, add_ref, fetched_ref, pick_ref, hot_sum, place, own, *refs):
        query_refs, refs = refs[: blocks - 1], refs[blocks - 1 :]
        (sides_ref, tails_ref, outgoing, total_ref) = refs
        pairs = total_ref.shape[0]
        unit, radius = normalize(mm(pick_ref[...], fetched_ref[...]) + hot_sum.get()[...])
        low = unit.astype(BF16)
        sides_ref[0:pairs, :] = low
        query_refs = [own.get()] + list(query_refs)
        direction = loss_side(low, query_refs, total_ref, sharp_ref[0], add_ref[0])
        for i, ref in enumerate(query_refs):
            tails_ref[i] = ref[pairs:, :]
        grad = project(unit, radius, direction).astype(BF16)
        sides_ref[pairs:, :] = grad
        place_ref = place.get()
        width = outgoing.width
        outgoing.run(lambda i: mm(place_ref[pl.ds(i * width, width), :], grad).astype(BF16))

    return kernel


def query_side(sharp_ref, add_ref, query, *refs):
    item_refs, (out, total_ref) = refs[:-2], refs[-2:]
    unit, radius = normalize(query.get()[...].astype(F32))
    direction = loss_side(unit.astype(BF16), item_refs, total_ref, sharp_ref[0], add_ref[0])
    out.write(project(unit, radius, direction))
    out.finish()


def hot_terms(blocks, slots):
    def kernel(block_ref, lines_ref, *refs):
        side_refs, (out, total_ref) = refs[:blocks], refs[blocks:]
        width, pairs = total_ref.shape
        row = (iota((width, pairs), 0) + block_ref[0] * width).astype(F32)
        for i, ref in enumerate(side_refs):
            line = lines_ref[i].astype(F32)
            counts = jnp.zeros((width, pairs), F32)
            for h in range(slots):
                counts += (line[h : h + 1, :] * 64.0 + line[h + slots : h + slots + 1, :] == row).astype(F32)
            term = mm(counts.astype(BF16), ref[pairs:, :])
            total_ref[...] = term if i == 0 else total_ref[...] + term
        out.write(total_ref[...].astype(BF16))
        out.finish()

    return kernel


def hot_sum_spread(parts_ref, out):
    piece = jnp.sum(parts_ref[...].astype(F32), axis=0, keepdims=True)
    out.write(jnp.broadcast_to(piece, parts_ref.shape).astype(BF16))
    out.finish()


def widen(blocks):
    def kernel(block_ref, *refs):
        part_refs, out = refs[:blocks], refs[blocks]
        chips = blocks // 2
        width = part_refs[0].shape[0]
        mine, core = block_ref[0] // 2, block_ref[0] % 2
        copies = []
        for i, ref in enumerate(part_refs):
            chip = (mine + chips - i % chips) % chips
            index = chip * 2 + (core if i < chips else 1 - core)
            part = pl.ds(i * width, width)
            out.stage[part, :] = ref[...].astype(F32)
            place = pl.ds(pl.multiple_of(index * width, width), width)
            copies.append(pltpu.make_async_copy(out.stage.at[part], out.out.at[place], out.sem.at[i]))
            copies[-1].start()
        for copy in copies:
            copy.wait()

    return kernel


def cold_terms(same_core):
    def kernel(block_ref, ask_ref, grad_ref, out_ref, row_ref):
        chips, width, _ = out_ref.shape
        total = grad_ref.shape[0]
        owners = ask_ref.shape[0]
        cap = total // owners
        for o in range(owners):
            row_ref[:, o * cap : (o + 1) * cap] = ask_ref[o, 0:1, 0:cap]
        core = block_ref[0] % 2
        core = core if same_core else 1 - core

        def step(i, _):
            chip = (block_ref[0] // 2 + i) % chips
            row = iota((width, total), 0) + (chip * 2 + core) * width
            hit = (row_ref[...] == row).astype(F32).astype(BF16)
            out_ref[i] = mm(hit, grad_ref[...]).astype(out_ref.dtype)
            return 0

        lax.fori_loop(0, chips, step, 0)

    return kernel


def cold_join(mine_ref, theirs_ref, keep_ref, *send_refs):
    keep_ref[...] = mine_ref[0] + theirs_ref[0].astype(F32)
    for d, ref in enumerate(send_refs):
        ref[...] = (mine_ref[d + 1] + theirs_ref[d + 1].astype(F32)).astype(BF16)


def add_parts(keep_ref, *refs):
    part_refs, out = refs[:-1], refs[-1]
    total = keep_ref[...]
    for ref in part_refs:
        total += ref[...].astype(F32)
    out.write(total)
    out.finish()


def swap(array, axis):
    return lax.all_to_all(array, axis, split_axis=0, concat_axis=0, tiled=True)


def cross(array, blocks):
    return lax.ppermute(array, "blk", [(i, i ^ 1) for i in range(blocks)])


def shift(array, blocks, d):
    return lax.ppermute(array, "blk", [(i, (i + 2 * d) % blocks) for i in range(blocks)])


def gather_blocks(array, blocks):
    first = cross(array, blocks)
    mine = [shift(array, blocks, d) for d in range(1, blocks // 2)]
    return [array] + mine + [first] + [cross(m, blocks) for m in mine]


def step_of(queries, hot_table, cold_table, lines, parent, place, tally, sharpness, additive):
    pairs, width = queries.shape
    owners, blocks = lax.axis_size("shard"), lax.axis_size("blk")
    chips = blocks // 2
    slots = parent.shape[1]
    cap = 2 * pairs * slots // owners
    total = owners * cap
    rows = cold_table.shape[0]
    hot_rows = hot_table.shape[0]
    block = lax.axis_index("blk").astype(jnp.int32).reshape(1)

    rank, rank_t, ask, table_low = call(
        make_requests(owners, cap),
        [shape((pairs, LANES), BF16), shape((LANES, pairs), BF16), HBM((owners, 8, LANES), jnp.int32), shape((rows, width), BF16)],
        parent.T, place.T, tally.reshape(1, pairs), cold_table,
        kinds=["h"] * 4,
        scratch=[pltpu.VMEM((1, total), F32)],
        flops=2 * pairs * total * LANES * 3,
    )
    asked = swap(ask, "shard")

    steps = 8
    (looked,) = call(
        fetch,
        [HBM((owners, cap, width), BF16)],
        asked, table_low,
        steps=steps,
        flops=2 * total * rows * width,
    )
    looked, queries, rank, rank_t = lax.optimization_barrier((looked, queries, rank, rank_t))
    fetched = swap(looked, "shard").reshape(total, width)

    lines_t = lines.T
    (query_block,) = call(unit_queries, [shape((pairs + 16, width), BF16)], queries, lines_t, kinds=["h", "h"])
    query_blocks = gather_blocks(query_block, blocks)

    pick, placed, hot_sum = call(
        prepare(cap),
        [shape((pairs, total), BF16), HBM((total, pairs), BF16), HBM((pairs, width), F32)],
        rank, rank_t, lines_t, hot_table,
        kinds=["v", "v", "h", "h"],
        steps=steps,
        flops=2 * pairs * total * (width + 2 * LANES),
    )

    sides, tails, outgoing = call(
        item_side(blocks),
        [shape((2 * pairs, width), BF16), shape((blocks, 16, width), BF16), HBM((total, width), BF16)],
        sharpness, additive, fetched, pick, hot_sum, placed, *query_blocks,
        kinds=["s", "s", "v", "v", "h", "h", "h"] + ["v"] * (blocks - 1),
        scratch=[pltpu.VMEM((pairs, width), F32)],
        steps=steps,
        flops=2 * pairs * width * (2 * total + 2 * blocks * pairs),
    )
    incoming = swap(outgoing.reshape(owners, cap, width), "shard").reshape(total, width)

    side_blocks = gather_blocks(sides, blocks)
    (hot_block,) = call(
        hot_terms(blocks, slots),
        [HBM((hot_rows // blocks, width), BF16)],
        block, tails, *side_blocks,
        kinds=["s"] + ["v"] * (blocks + 1),
        scratch=[pltpu.VMEM((hot_rows // blocks, width), F32)],
        flops=2 * blocks * pairs * width * hot_rows // blocks,
    )
    (query_grad,) = call(
        query_side,
        [HBM((pairs, width), F32)],
        sharpness, additive, queries, *side_blocks,
        kinds=["s", "s", "h"] + ["v"] * blocks,
        scratch=[pltpu.VMEM((pairs, width), F32)],
        flops=4 * pairs * width * blocks * pairs,
    )
    hot_parts = swap(hot_block.reshape(owners, hot_rows // blocks // owners, width), "shard")
    (hot_piece,) = call(hot_sum_spread, [HBM(hot_parts.shape, BF16)], hot_parts)

    def cold_half(same_core, dtype, incoming):
        return call(
            cold_terms(same_core),
            [shape((chips, rows // blocks, width), dtype)],
            block, asked, incoming,
            kinds=["s", "v", "v"],
            scratch=[pltpu.VMEM((1, total), jnp.int32)],
            flops=total * rows * width,
        )[0]

    theirs = cold_half(False, BF16, incoming)
    theirs = cross(theirs, blocks)
    mine = cold_half(True, F32, incoming)
    keep, *sends = call(
        cold_join,
        [shape((rows // blocks, width), F32)] + [shape((rows // blocks, width), BF16)] * (chips - 1),
        mine, theirs,
    )
    hot_block = swap(hot_piece, "shard").reshape(hot_rows // blocks, width)
    parts = [shift(part, blocks, d + 1) for d, part in enumerate(sends)]
    (cold_grad,) = call(add_parts, [HBM((rows // blocks, width), F32)], keep, *parts)
    hot_blocks = gather_blocks(hot_block, blocks)
    (hot_grad,) = call(
        widen(blocks),
        [HBM((hot_rows, width), F32)],
        block, *hot_blocks,
        kinds=["s"] + ["v"] * blocks,
        steps=blocks,
    )
    return (query_grad, hot_grad, cold_grad)


def solution(mesh):
    pair = P(("shard", "blk"), None)
    in_specs = (pair, P(), P("shard", None), pair, pair, pair, P(("shard", "blk")), P(), P())
    return jax.shard_map(step_of, mesh=mesh, in_specs=in_specs, out_specs=(pair, P(), pair), check_vma=False)
```

time: 160 us -> 156 us (0.975)
  Pallas kernels: 42.2 us -> 33.8 us
  waiting for transfers between devices: 14.2 us -> 19.1 us
    pallas_call x13, Pallas kernels: 42.2 us -> 33.8 us  [call(): pl.pallas_call(run, out_shape=list(outs), in_specs=[pl.BlockSpec(memory_s...]
    all_to_all x3, waiting for transfers between devices: 10.4 us -> 13.7 us  [swap(): return lax.all_to_all(array, axis, split_axis=0, concat_axis=0, tiled=True)]
    ppermute x12, waiting for transfers between devices: 2.19 us -> 3.9 us  [shift(): lax.ppermute(array, 'blk', [(i, (i + 2 * d) % blocks) for i in range(bloc...]
  transfers between devices with their start and end apart: 28 -> 28, of which waited for: 6 -> 7; matrix products, arithmetic and copies ran while one was open for 0% -> 0% of each run, Pallas kernels for 15% -> 12%
where the time goes in v5:
time: 156 us; the launch traced here: 155 us
  starting transfers between devices  64.8 us (42%)
  blocking collectives  35.4 us (23%)
  Pallas kernels  33.8 us (22%)
  waiting for transfers between devices  19.1 us (12%)
  between operations  2.33 us (1%)
    all_to_all x2, blocking collectives, swap(): return lax.all_to_all(array, axis, split_axis=0, concat_axis=0, tiled=True)  35.4 us
    pallas_call x13, Pallas kernels, call(): pl.pallas_call(run, out_shape=list(outs), in_specs=[pl.BlockSpec(memory_s...  33.8 us
    ppermute x13, starting transfers between devices, cross(): return lax.ppermute(array, 'blk', [(i, i ^ 1) for i in range(blocks)])  25.8 us
    all_to_all x3, starting transfers between devices, swap(): return lax.all_to_all(array, axis, split_axis=0, concat_axis=0, tiled=True)  20.3 us
    ppermute x12, starting transfers between devices, shift(): lax.ppermute(array, 'blk', [(i, (i + 2 * d) % blocks) for i in range(bloc...  18.8 us
    all_to_all x3, waiting for transfers between devices, swap(): return lax.all_to_all(array, axis, split_axis=0, concat_axis=0, tiled=True)  13.7 us
    ppermute x12, waiting for transfers between devices, shift(): lax.ppermute(array, 'blk', [(i, (i + 2 * d) % blocks) for i in range(bloc...  3.9 us
  transfers between devices with their start and end apart: 28, of which 7 were waited for; matrix products, arithmetic and copies ran while one was open for 0% of the time, Pallas kernels for 12%

profile of v5, /device:TPU:1, one launch (start us, length us, event | category | flops | bytes accessed | tf_op | source)
XLA Modules:
  0.0 155.5 jit_solution(17947817634407399619)
XLA Ops:
  0.6 2.6 %shard_map.112 = (bf16[256,128]{1,0:T(8,128)(2,1)S(1)}, bf16[128,256]{1,0:T(8,128)(2,1)S(1)}, s32[32,8,128]{2,1,0:T(8,128)}, bf16[2048,256]{1,0:T(8,128)(2,1)S(1)}) custom-call(s32[4,256]{1,0:T(4,128)} %bitcast.20, s32[4,256]{1,0:T(4,128)} %bitcast.21, s32[1,256]{1,0:T(1,128)} %bitcast.24, f32[2048,256]{1,0:T(8,128)} %refs_3_.2), custom_call_target="tpu_custom_call" | custom-call | flops 402653184 | bytes 2106368 | tf_op jit(solution)/shard_map/pallas_call | solution.py:100
  3.3 21.2 %all_to_all.25.refs_0_.refs_1_ = s32[32,8,128]{2,1,0:T(8,128)S(1)} all-to-all(s32[32,8,128]{2,1,0:T(8,128)} %get-tuple-element.21), channel_id=1, replica_groups=mesh['shard'=32,'blk'=8] {'shard'}, dimensions={0} | all-to-all | bytes 262144 | tf_op jit(solution)/shard_map/all_to_all | solution.py:371
  24.5 5.8 %shard_map.113 = bf16[32,64,256]{2,1,0:T(8,128)(2,1)} custom-call(s32[32,8,128]{2,1,0:T(8,128)S(1)} %all_to_all.25.refs_0_.refs_1_, bf16[2048,256]{1,0:T(8,128)(2,1)S(1)} %get-tuple-element.22.refs_1_), custom_call_target="tpu_custom_call" | custom-call | flops 2147483648 | bytes 1179648 | tf_op jit(solution)/shard_map/pallas_call | solution.py:100
  30.3 3.9 %all-to-all-start.1 = ((bf16[32,64,256]{2,1,0:T(8,128)(2,1)}), bf16[32,64,256]{2,1,0:T(8,128)(2,1)S(1)}, u32[]{:S(2)}, u32[]{:S(2)}) async-start(bf16[32,64,256]{2,1,0:T(8,128)(2,1)} %shard_map.113), calls=%async_computation.1 | async-start | bytes 2097152 | tf_op jit(solution)/shard_map/all_to_all | solution.py:371
  34.2 1.1 shard_map.115.refs_6_
  35.3 0.0 copy-start
  35.4 1.3 collective-permute-start
  36.6 2.5 %collective-permute-start.1 = (bf16[272,256]{1,0:T(8,128)(2,1)S(1)}, bf16[272,256]{1,0:T(8,128)(2,1)S(1)}, u32[]{:S(2)}, u32[]{:S(2)}) collective-permute-start(bf16[272,256]{1,0:T(8,128)(2,1)S(1)} %shard_map.115.refs_6_), channel_id=1, source_target_pairs={{0,4},{1,5},{2,6},{3,7},{4,0},{5,1},{6,2},{7,3},{8,12},{9,13},{10,... | collective-permute-start | bytes 417800 | tf_op jit(solution)/shard_map/ppermute | solution.py:379
  39.1 1.2 collective-permute-start.2
  40.2 2.9 %collective-permute-start.3 = (bf16[272,256]{1,0:T(8,128)(2,1)S(1)}, bf16[272,256]{1,0:T(8,128)(2,1)S(1)}, u32[]{:S(2)}, u32[]{:S(2)}) collective-permute-start(bf16[272,256]{1,0:T(8,128)(2,1)S(1)} %shard_map.115.refs_6_), channel_id=1, source_target_pairs={{0,1},{1,0},{2,3},{3,2},{4,5},{5,4},{6,7},{7,6},{8,9},{9,8},{10,11... | collective-permute-start | bytes 417800 | tf_op jit(solution)/shard_map/ppermute | solution.py:375
  43.2 0.0 collective-permute-done.refs_7_
  43.2 2.0 %collective-permute-start.4 = (bf16[272,256]{1,0:T(8,128)(2,1)S(1)}, bf16[272,256]{1,0:T(8,128)(2,1)S(1)}, u32[]{:S(2)}, u32[]{:S(2)}) collective-permute-start(bf16[272,256]{1,0:T(8,128)(2,1)S(1)} %collective-permute-done.refs_7_), channel_id=1, source_target_pairs={{0,1},{1,0},{2,3},{3,2},{4,5},{5,4},{6,7},{7,6},{8,9},{9,8},{10,11... | collective-permute-start | bytes 417800 | tf_op jit(solution)/shard_map/ppermute | solution.py:375
  45.2 0.0 collective-permute-done.1.refs_8_
  45.2 1.5 collective-permute-start.5
  46.7 0.0 collective-permute-done.2.refs_9_
  46.7 0.1 collective-permute-start.6
  48.1 6.1 %shard_map.114 = (bf16[256,2048]{1,0:T(8,128)(2,1)S(1)}, bf16[2048,256]{1,0:T(8,128)(2,1)}, f32[256,256]{1,0:T(8,128)}) custom-call(bf16[256,128]{1,0:T(8,128)(2,1)S(1)} %get-tuple-element.27.refs_0_, bf16[128,256]{1,0:T(8,128)(2,1)S(1)} %get-tuple-element.28.refs_1_, s32[4,256]{1,0:T(4,128)} %bitcast.23, bf16[2048,256]{1,0:T(8,128)(2,1)} %refs_3_.3), custom_call_target="tpu_custom_call" | custom-call | flops 536870912 | bytes 1183744 | tf_op jit(solution)/shard_map/pallas_call | solution.py:100
  54.2 0.0 collective-permute-done.3.refs_10_
  54.2 0.0 collective-permute-done.4.refs_11_
  54.3 0.0 collective-permute-done.6.refs_13_
  54.3 4.5 %all-to-all-done.1 = bf16[32,64,256]{2,1,0:T(8,128)(2,1)S(1)} async-done(((bf16[32,64,256]{2,1,0:T(8,128)(2,1)}), bf16[32,64,256]{2,1,0:T(8,128)(2,1)S(1)}, u32[]{:S(2)}, u32[]{:S(2)}) %all-to-all-start.1) | async-done | bytes 1048608 | tf_op jit(solution)/shard_map/all_to_all | solution.py:371
  58.8 5.3 %shard_map.116 = (bf16[512,256]{1,0:T(8,128)(2,1)S(1)}, bf16[8,16,256]{2,1,0:T(8,128)(2,1)S(1)}, bf16[2048,256]{1,0:T(8,128)(2,1)}) custom-call(f32[1]{0:T(128)S(6)} %copy.12.refs_0_, f32[1]{0:T(128)S(6)} %copy.13.refs_1_, bf16[2048,256]{1,0:T(8,128)(2,1)S(1)} %bitcast.10, bf16[256,2048]{1,0:T(8,128)(2,1)S(1)} %get-tuple-element.29.refs_3_, ...), custom_call_target="tpu_custom_call" | custom-call | flops 1073741824 | bytes 4521992 | tf_op jit(solution)/shard_map/pallas_call | solution.py:100
  64.1 8.2 %all-to-all-start.4 = ((bf16[32,64,256]{2,1,0:T(8,128)(2,1)}), bf16[32,64,256]{2,1,0:T(8,128)(2,1)S(1)}, u32[]{:S(2)}, u32[]{:S(2)}) async-start(bf16[32,64,256]{2,1,0:T(8,128)(2,1)} %bitcast.18), calls=%async_computation.4 | async-start | bytes 2097152 | tf_op jit(solution)/shard_map/all_to_all | solution.py:371
  72.4 1.3 collective-permute-start.7
  73.6 2.5 %collective-permute-start.8 = (bf16[512,256]{1,0:T(8,128)(2,1)S(1)}, bf16[512,256]{1,0:T(8,128)(2,1)S(1)}, u32[]{:S(2)}, u32[]{:S(2)}) collective-permute-start(bf16[512,256]{1,0:T(8,128)(2,1)S(1)} %get-tuple-element.32.refs_3_.refs_2_), channel_id=1, source_target_pairs={{0,4},{1,5},{2,6},{3,7},{4,0},{5,1},{6,2},{7,3},{8,12},{9,13},{10,... | collective-permute-start | bytes 786440 | tf_op jit(solution)/shard_map/ppermute | solution.py:379
  76.1 1.1 collective-permute-start.9
  77.2 2.9 %collective-permute-start.10 = (bf16[512,256]{1,0:T(8,128)(2,1)S(1)}, bf16[512,256]{1,0:T(8,128)(2,1)S(1)}, u32[]{:S(2)}, u32[]{:S(2)}) collective-permute-start(bf16[512,256]{1,0:T(8,128)(2,1)S(1)} %get-tuple-element.32.refs_3_.refs_2_), channel_id=1, source_target_pairs={{0,1},{1,0},{2,3},{3,2},{4,5},{5,4},{6,7},{7,6},{8,9},{9,8},{10,11... | collective-permute-start | bytes 786440 | tf_op jit(solution)/shard_map/ppermute | solution.py:375
  80.1 0.0 collective-permute-done.7.refs_4_.refs_3_
  80.2 3.7 %collective-permute-start.11 = (bf16[512,256]{1,0:T(8,128)(2,1)S(1)}, bf16[512,256]{1,0:T(8,128)(2,1)S(1)}, u32[]{:S(2)}, u32[]{:S(2)}) collective-permute-start(bf16[512,256]{1,0:T(8,128)(2,1)S(1)} %collective-permute-done.7.refs_4_.refs_3_), channel_id=1, source_target_pairs={{0,1},{1,0},{2,3},{3,2},{4,5},{5,4},{6,7},{7,6},{8,9},{9,8},{10,11... | collective-permute-start | bytes 786440 | tf_op jit(solution)/shard_map/ppermute | solution.py:375
  83.9 2.2 %collective-permute-done.8.refs_5_.refs_4_ = bf16[512,256]{1,0:T(8,128)(2,1)S(1)} collective-permute-done((bf16[512,256]{1,0:T(8,128)(2,1)S(1)}, bf16[512,256]{1,0:T(8,128)(2,1)S(1)}, u32[]{:S(2)}, u32[]{:S(2)}) %collective-permute-start.8) | collective-permute-done | bytes 262176 | tf_op jit(solution)/shard_map/ppermute | solution.py:379
  86.1 2.9 %collective-permute-start.12 = (bf16[512,256]{1,0:T(8,128)(2,1)S(1)}, bf16[512,256]{1,0:T(8,128)(2,1)S(1)}, u32[]{:S(2)}, u32[]{:S(2)}) collective-permute-start(bf16[512,256]{1,0:T(8,128)(2,1)S(1)} %collective-permute-done.8.refs_5_.refs_4_), channel_id=1, source_target_pairs={{0,1},{1,0},{2,3},{3,2},{4,5},{5,4},{6,7},{7,6},{8,9},{9,8},{10,11... | collective-permute-start | bytes 786440 | tf_op jit(solution)/shard_map/ppermute | solution.py:375
  89.0 0.0 collective-permute-done.9.refs_6_.refs_5_
  89.0 0.0 collective-permute-start.13
  89.0 0.0 collective-permute-done.11.refs_8_.refs_7_
  89.0 1.1 collective-permute-done.12.refs_9_.refs_8_
  90.1 0.4 collective-permute-done.13.refs_10_.refs_9_
  90.5 1.6 %shard_map.118 = bf16[256,256]{1,0:T(8,128)(2,1)} custom-call(s32[1]{0:T(128)} %bitcast.5.refs_0_, bf16[8,16,256]{2,1,0:T(8,128)(2,1)S(1)} %get-tuple-element.33.refs_1_, bf16[512,256]{1,0:T(8,128)(2,1)S(1)} %get-tuple-element.32.refs_3_.refs_2_, bf16[512,256]{1,0:T(8,128)(2,1)S(1)} %collective-permute-done.7.refs_4_.refs_3_, ...), custom_call_target="tpu_custom_call" | custom-call | flops 268435456 | bytes 2162692 | tf_op jit(solution)/shard_map/pallas_call | solution.py:100
  92.1 4.8 %all-to-all-done.4 = bf16[32,64,256]{2,1,0:T(8,128)(2,1)S(1)} async-done(((bf16[32,64,256]{2,1,0:T(8,128)(2,1)}), bf16[32,64,256]{2,1,0:T(8,128)(2,1)S(1)}, u32[]{:S(2)}, u32[]{:S(2)}) %all-to-all-start.4) | async-done | bytes 1048608 | tf_op jit(solution)/shard_map/all_to_all | solution.py:371
  96.9 8.1 %all-to-all-start.2 = ((bf16[32,8,256]{2,1,0:T(8,128)(2,1)}), bf16[32,8,256]{2,1,0:T(8,128)(2,1)S(1)}, u32[]{:S(2)}, u32[]{:S(2)}) async-start(bf16[32,8,256]{2,1,0:T(8,128)(2,1)} %bitcast.19), calls=%async_computation.2 | async-start | bytes 262144 | tf_op jit(solution)/shard_map/all_to_all | solution.py:371
  105.0 2.7 %shard_map.122 = bf16[4,256,256]{2,1,0:T(8,128)(2,1)} custom-call(s32[1]{0:T(128)} %bitcast.5.refs_0_, s32[32,8,128]{2,1,0:T(8,128)S(1)} %copy-done.2, bf16[2048,256]{1,0:T(8,128)(2,1)S(1)} %bitcast.11), custom_call_target="tpu_custom_call" | custom-call | flops 1073741824 | bytes 1179652 | tf_op jit(solution)/shard_map/pallas_call | solution.py:100
  107.6 2.1 %collective-permute-start.21 = (bf16[4,256,256]{2,1,0:T(8,128)(2,1)}, bf16[4,256,256]{2,1,0:T(8,128)(2,1)}, u32[]{:S(2)}, u32[]{:S(2)}) collective-permute-start(bf16[4,256,256]{2,1,0:T(8,128)(2,1)} %shard_map.122), channel_id=1, source_target_pairs={{0,1},{1,0},{2,3},{3,2},{4,5},{5,4},{6,7},{7,6},{8,9},{9,8},{10,11... | collective-permute-start | bytes 1572872 | tf_op jit(solution)/shard_map/ppermute | solution.py:375
  109.7 4.4 %all-to-all-done.2.refs_0_ = bf16[32,8,256]{2,1,0:T(8,128)(2,1)S(1)} async-done(((bf16[32,8,256]{2,1,0:T(8,128)(2,1)}), bf16[32,8,256]{2,1,0:T(8,128)(2,1)S(1)}, u32[]{:S(2)}, u32[]{:S(2)}) %all-to-all-start.2) | async-done | bytes 131104 | tf_op jit(solution)/shard_map/all_to_all | solution.py:371
  114.1 0.7 shard_map.119
  114.8 14.2 %all_to_all.26 = bf16[32,8,256]{2,1,0:T(8,128)(2,1)S(1)} all-to-all(bf16[32,8,256]{2,1,0:T(8,128)(2,1)} %shard_map.119), channel_id=1, replica_groups=mesh['shard'=32,'blk'=8] {'shard'}, dimensions={0} | all-to-all | bytes 262144 | tf_op jit(solution)/shard_map/all_to_all | solution.py:371
  129.1 1.2 collective-permute-start.14
  130.3 2.5 %collective-permute-start.15 = (bf16[256,256]{1,0:T(8,128)(2,1)S(1)}, bf16[256,256]{1,0:T(8,128)(2,1)S(1)}, u32[]{:S(2)}, u32[]{:S(2)}) collective-permute-start(bf16[256,256]{1,0:T(8,128)(2,1)S(1)} %bitcast.14), channel_id=1, source_target_pairs={{0,4},{1,5},{2,6},{3,7},{4,0},{5,1},{6,2},{7,3},{8,12},{9,13},{10,... | collective-permute-start | bytes 393224 | tf_op jit(solution)/shard_map/ppermute | solution.py:379
  132.8 1.1 collective-permute-start.16
  133.9 4.1 %collective-permute-start.17 = (bf16[256,256]{1,0:T(8,128)(2,1)S(1)}, bf16[256,256]{1,0:T(8,128)(2,1)S(1)}, u32[]{:S(2)}, u32[]{:S(2)}) collective-permute-start(bf16[256,256]{1,0:T(8,128)(2,1)S(1)} %bitcast.16), channel_id=1, source_target_pairs={{0,1},{1,0},{2,3},{3,2},{4,5},{5,4},{6,7},{7,6},{8,9},{9,8},{10,11... | collective-permute-start | bytes 393224 | tf_op jit(solution)/shard_map/ppermute | solution.py:375
  138.0 0.0 collective-permute-done.14.refs_2_
  138.0 0.6 collective-permute-start.18
  138.6 0.0 collective-permute-done.15.refs_3_
  138.6 2.3 %collective-permute-start.19 = (bf16[256,256]{1,0:T(8,128)(2,1)S(1)}, bf16[256,256]{1,0:T(8,128)(2,1)S(1)}, u32[]{:S(2)}, u32[]{:S(2)}) collective-permute-start(bf16[256,256]{1,0:T(8,128)(2,1)S(1)} %collective-permute-done.15.refs_3_), channel_id=1, source_target_pairs={{0,1},{1,0},{2,3},{3,2},{4,5},{5,4},{6,7},{7,6},{8,9},{9,8},{10,11... | collective-permute-start | bytes 393224 | tf_op jit(solution)/shard_map/ppermute | solution.py:375
  140.9 0.0 collective-permute-done.16.refs_4_
  140.9 0.6 collective-permute-start.20
  141.5 1.9 %shard_map.121.refs_0_ = f32[4,256,256]{2,1,0:T(8,128)S(1)} custom-call(s32[1]{0:T(128)} %bitcast.5.refs_0_, s32[32,8,128]{2,1,0:T(8,128)S(1)} %copy-done.2, bf16[2048,256]{1,0:T(8,128)(2,1)S(1)} %bitcast.12), custom_call_target="tpu_custom_call" | custom-call | flops 1073741824 | bytes 1179652 | tf_op jit(solution)/shard_map/pallas_call | solution.py:100
  143.4 0.0 collective-permute-done.21.refs_1_
  143.4 1.1 shard_map.123
  144.5 1.1 collective-permute-start.22
  145.6 2.5 %collective-permute-start.23 = (bf16[256,256]{1,0:T(8,128)(2,1)S(1)}, bf16[256,256]{1,0:T(8,128)(2,1)S(1)}, u32[]{:S(2)}, u32[]{:S(2)}) collective-permute-start(bf16[256,256]{1,0:T(8,128)(2,1)S(1)} %get-tuple-element.37), channel_id=1, source_target_pairs={{0,4},{1,5},{2,6},{3,7},{4,0},{5,1},{6,2},{7,3},{8,12},{9,13},{10,... | collective-permute-start | bytes 393224 | tf_op jit(solution)/shard_map/ppermute | solution.py:379
  148.2 0.6 collective-permute-start.24
  148.7 2.7 %shard_map.117 = f32[256,256]{1,0:T(8,128)} custom-call(f32[1]{0:T(128)S(6)} %copy.12.refs_0_, f32[1]{0:T(128)S(6)} %copy.13.refs_1_, bf16[256,256]{1,0:T(8,128)(2,1)} %refs_2_, bf16[512,256]{1,0:T(8,128)(2,1)S(1)} %get-tuple-element.32.refs_3_.refs_2_, bf16[512,256]{1,0:T(8,128)(2,1)S(1)} %collective-permute-done.7.refs_4_.refs_3_, ...), custom_call_target="tpu_custom_call" | custom-call | flops 536870912 | bytes 2228232 | tf_op jit(solution)/shard_map/pallas_call | solution.py:100
  151.4 1.4 shard_map.120
  152.8 1.7 %collective-permute-done.23.refs_2_ = bf16[256,256]{1,0:T(8,128)(2,1)S(1)} collective-permute-done((bf16[256,256]{1,0:T(8,128)(2,1)S(1)}, bf16[256,256]{1,0:T(8,128)(2,1)S(1)}, u32[]{:S(2)}, u32[]{:S(2)}) %collective-permute-start.23) | collective-permute-done | bytes 131104 | tf_op jit(solution)/shard_map/ppermute | solution.py:379
  154.6 0.8 shard_map.124
  (13 shorter events, 0.0 us)
Async XLA Ops:
  24.5 5.8 %copy-start.1 = (s32[32,8,128]{2,1,0:T(8,128)}, s32[32,8,128]{2,1,0:T(8,128)S(1)}, u32[]{:S(2)}) copy-start(s32[32,8,128]{2,1,0:T(8,128)S(1)} %all_to_all.25.refs_0_.refs_1_) | copy-start | bytes 393220
  30.3 28.5 %all-to-all-start.1 = ((bf16[32,64,256]{2,1,0:T(8,128)(2,1)}), bf16[32,64,256]{2,1,0:T(8,128)(2,1)S(1)}, u32[]{:S(2)}, u32[]{:S(2)}) async-start(bf16[32,64,256]{2,1,0:T(8,128)(2,1)} %shard_map.113), calls=%async_computation.1 | async-start | bytes 2097152 | tf_op jit(solution)/shard_map/all_to_all | solution.py:371
  35.3 23.4 %copy-start = (bf16[272,256]{1,0:T(8,128)(2,1)}, bf16[272,256]{1,0:T(8,128)(2,1)S(1)}, u32[]{:S(2)}) copy-start(bf16[272,256]{1,0:T(8,128)(2,1)S(1)} %shard_map.115.refs_6_) | copy-start | bytes 417796
  35.4 7.8 %collective-permute-start = (bf16[272,256]{1,0:T(8,128)(2,1)S(1)}, bf16[272,256]{1,0:T(8,128)(2,1)S(1)}, u32[]{:S(2)}, u32[]{:S(2)}) collective-permute-start(bf16[272,256]{1,0:T(8,128)(2,1)S(1)} %shard_map.115.refs_6_), channel_id=1, source_target_pairs={{0,2},{1,3},{2,4},{3,5},{4,6},{5,7},{6,0},{7,1},{8,10},{9,11},{10,... | collective-permute-start | bytes 417800 | tf_op jit(solution)/shard_map/ppermute | solution.py:379
  36.6 8.6 %collective-permute-start.1 = (bf16[272,256]{1,0:T(8,128)(2,1)S(1)}, bf16[272,256]{1,0:T(8,128)(2,1)S(1)}, u32[]{:S(2)}, u32[]{:S(2)}) collective-permute-start(bf16[272,256]{1,0:T(8,128)(2,1)S(1)} %shard_map.115.refs_6_), channel_id=1, source_target_pairs={{0,4},{1,5},{2,6},{3,7},{4,0},{5,1},{6,2},{7,3},{8,12},{9,13},{10,... | collective-permute-start | bytes 417800 | tf_op jit(solution)/shard_map/ppermute | solution.py:379
  39.1 7.6 %collective-permute-start.2 = (bf16[272,256]{1,0:T(8,128)(2,1)S(1)}, bf16[272,256]{1,0:T(8,128)(2,1)S(1)}, u32[]{:S(2)}, u32[]{:S(2)}) collective-permute-start(bf16[272,256]{1,0:T(8,128)(2,1)S(1)} %shard_map.115.refs_6_), channel_id=1, source_target_pairs={{0,6},{1,7},{2,0},{3,1},{4,2},{5,3},{6,4},{7,5},{8,14},{9,15},{10,... | collective-permute-start | bytes 417800 | tf_op jit(solution)/shard_map/ppermute | solution.py:379
  40.2 14.0 %collective-permute-start.3 = (bf16[272,256]{1,0:T(8,128)(2,1)S(1)}, bf16[272,256]{1,0:T(8,128)(2,1)S(1)}, u32[]{:S(2)}, u32[]{:S(2)}) collective-permute-start(bf16[272,256]{1,0:T(8,128)(2,1)S(1)} %shard_map.115.refs_6_), channel_id=1, source_target_pairs={{0,1},{1,0},{2,3},{3,2},{4,5},{5,4},{6,7},{7,6},{8,9},{9,8},{10,11... | collective-permute-start | bytes 417800 | tf_op jit(solution)/shard_map/ppermute | solution.py:375
  43.2 11.1 %collective-permute-start.4 = (bf16[272,256]{1,0:T(8,128)(2,1)S(1)}, bf16[272,256]{1,0:T(8,128)(2,1)S(1)}, u32[]{:S(2)}, u32[]{:S(2)}) collective-permute-start(bf16[272,256]{1,0:T(8,128)(2,1)S(1)} %collective-permute-done.refs_7_), channel_id=1, source_target_pairs={{0,1},{1,0},{2,3},{3,2},{4,5},{5,4},{6,7},{7,6},{8,9},{9,8},{10,11... | collective-permute-start | bytes 417800 | tf_op jit(solution)/shard_map/ppermute | solution.py:375
  45.2 9.0 %collective-permute-start.5 = (bf16[272,256]{1,0:T(8,128)(2,1)S(1)}, bf16[272,256]{1,0:T(8,128)(2,1)S(1)}, u32[]{:S(2)}, u32[]{:S(2)}) collective-permute-start(bf16[272,256]{1,0:T(8,128)(2,1)S(1)} %collective-permute-done.1.refs_8_), channel_id=1, source_target_pairs={{0,1},{1,0},{2,3},{3,2},{4,5},{5,4},{6,7},{7,6},{8,9},{9,8},{10,11... | collective-permute-start | bytes 417800 | tf_op jit(solution)/shard_map/ppermute | solution.py:375
  46.7 7.6 %collective-permute-start.6 = (bf16[272,256]{1,0:T(8,128)(2,1)S(1)}, bf16[272,256]{1,0:T(8,128)(2,1)S(1)}, u32[]{:S(2)}, u32[]{:S(2)}) collective-permute-start(bf16[272,256]{1,0:T(8,128)(2,1)S(1)} %collective-permute-done.2.refs_9_), channel_id=1, source_target_pairs={{0,1},{1,0},{2,3},{3,2},{4,5},{5,4},{6,7},{7,6},{8,9},{9,8},{10,11... | collective-permute-start | bytes 417800 | tf_op jit(solution)/shard_map/ppermute | solution.py:375
  64.1 40.9 %copy-start.2 = (s32[32,8,128]{2,1,0:T(8,128)S(1)}, s32[32,8,128]{2,1,0:T(8,128)}, u32[]{:S(2)}) copy-start(s32[32,8,128]{2,1,0:T(8,128)} %copy-done.1) | copy-start | bytes 393220
  64.1 32.8 %all-to-all-start.4 = ((bf16[32,64,256]{2,1,0:T(8,128)(2,1)}), bf16[32,64,256]{2,1,0:T(8,128)(2,1)S(1)}, u32[]{:S(2)}, u32[]{:S(2)}) async-start(bf16[32,64,256]{2,1,0:T(8,128)(2,1)} %bitcast.18), calls=%async_computation.4 | async-start | bytes 2097152 | tf_op jit(solution)/shard_map/all_to_all | solution.py:371
  72.4 7.8 %collective-permute-start.7 = (bf16[512,256]{1,0:T(8,128)(2,1)S(1)}, bf16[512,256]{1,0:T(8,128)(2,1)S(1)}, u32[]{:S(2)}, u32[]{:S(2)}) collective-permute-start(bf16[512,256]{1,0:T(8,128)(2,1)S(1)} %get-tuple-element.32.refs_3_.refs_2_), channel_id=1, source_target_pairs={{0,2},{1,3},{2,4},{3,5},{4,6},{5,7},{6,0},{7,1},{8,10},{9,11},{10,... | collective-permute-start | bytes 786440 | tf_op jit(solution)/shard_map/ppermute | solution.py:379
  73.6 12.4 %collective-permute-start.8 = (bf16[512,256]{1,0:T(8,128)(2,1)S(1)}, bf16[512,256]{1,0:T(8,128)(2,1)S(1)}, u32[]{:S(2)}, u32[]{:S(2)}) collective-permute-start(bf16[512,256]{1,0:T(8,128)(2,1)S(1)} %get-tuple-element.32.refs_3_.refs_2_), channel_id=1, source_target_pairs={{0,4},{1,5},{2,6},{3,7},{4,0},{5,1},{6,2},{7,3},{8,12},{9,13},{10,... | collective-permute-start | bytes 786440 | tf_op jit(solution)/shard_map/ppermute | solution.py:379
  76.1 12.9 %collective-permute-start.9 = (bf16[512,256]{1,0:T(8,128)(2,1)S(1)}, bf16[512,256]{1,0:T(8,128)(2,1)S(1)}, u32[]{:S(2)}, u32[]{:S(2)}) collective-permute-start(bf16[512,256]{1,0:T(8,128)(2,1)S(1)} %get-tuple-element.32.refs_3_.refs_2_), channel_id=1, source_target_pairs={{0,6},{1,7},{2,0},{3,1},{4,2},{5,3},{6,4},{7,5},{8,14},{9,15},{10,... | collective-permute-start | bytes 786440 | tf_op jit(solution)/shard_map/ppermute | solution.py:379
  77.2 11.7 %collective-permute-start.10 = (bf16[512,256]{1,0:T(8,128)(2,1)S(1)}, bf16[512,256]{1,0:T(8,128)(2,1)S(1)}, u32[]{:S(2)}, u32[]{:S(2)}) collective-permute-start(bf16[512,256]{1,0:T(8,128)(2,1)S(1)} %get-tuple-element.32.refs_3_.refs_2_), channel_id=1, source_target_pairs={{0,1},{1,0},{2,3},{3,2},{4,5},{5,4},{6,7},{7,6},{8,9},{9,8},{10,11... | collective-permute-start | bytes 786440 | tf_op jit(solution)/shard_map/ppermute | solution.py:375
  80.2 8.8 %collective-permute-start.11 = (bf16[512,256]{1,0:T(8,128)(2,1)S(1)}, bf16[512,256]{1,0:T(8,128)(2,1)S(1)}, u32[]{:S(2)}, u32[]{:S(2)}) collective-permute-start(bf16[512,256]{1,0:T(8,128)(2,1)S(1)} %collective-permute-done.7.refs_4_.refs_3_), channel_id=1, source_target_pairs={{0,1},{1,0},{2,3},{3,2},{4,5},{5,4},{6,7},{7,6},{8,9},{9,8},{10,11... | collective-permute-start | bytes 786440 | tf_op jit(solution)/shard_map/ppermute | solution.py:375
  86.1 4.1 %collective-permute-start.12 = (bf16[512,256]{1,0:T(8,128)(2,1)S(1)}, bf16[512,256]{1,0:T(8,128)(2,1)S(1)}, u32[]{:S(2)}, u32[]{:S(2)}) collective-permute-start(bf16[512,256]{1,0:T(8,128)(2,1)S(1)} %collective-permute-done.8.refs_5_.refs_4_), channel_id=1, source_target_pairs={{0,1},{1,0},{2,3},{3,2},{4,5},{5,4},{6,7},{7,6},{8,9},{9,8},{10,11... | collective-permute-start | bytes 786440 | tf_op jit(solution)/shard_map/ppermute | solution.py:375
  89.0 1.5 collective-permute-start.13
  96.9 17.2 %all-to-all-start.2 = ((bf16[32,8,256]{2,1,0:T(8,128)(2,1)}), bf16[32,8,256]{2,1,0:T(8,128)(2,1)S(1)}, u32[]{:S(2)}, u32[]{:S(2)}) async-start(bf16[32,8,256]{2,1,0:T(8,128)(2,1)} %bitcast.19), calls=%async_computation.2 | async-start | bytes 262144 | tf_op jit(solution)/shard_map/all_to_all | solution.py:371
  107.6 35.8 %collective-permute-start.21 = (bf16[4,256,256]{2,1,0:T(8,128)(2,1)}, bf16[4,256,256]{2,1,0:T(8,128)(2,1)}, u32[]{:S(2)}, u32[]{:S(2)}) collective-permute-start(bf16[4,256,256]{2,1,0:T(8,128)(2,1)} %shard_map.122), channel_id=1, source_target_pairs={{0,1},{1,0},{2,3},{3,2},{4,5},{5,4},{6,7},{7,6},{8,9},{9,8},{10,11... | collective-permute-start | bytes 1572872 | tf_op jit(solution)/shard_map/ppermute | solution.py:375
  129.1 8.9 %collective-permute-start.14 = (bf16[256,256]{1,0:T(8,128)(2,1)S(1)}, bf16[256,256]{1,0:T(8,128)(2,1)S(1)}, u32[]{:S(2)}, u32[]{:S(2)}) collective-permute-start(bf16[256,256]{1,0:T(8,128)(2,1)S(1)} %bitcast.13), channel_id=1, source_target_pairs={{0,2},{1,3},{2,4},{3,5},{4,6},{5,7},{6,0},{7,1},{8,10},{9,11},{10,... | collective-permute-start | bytes 393224 | tf_op jit(solution)/shard_map/ppermute | solution.py:379
  130.3 8.3 %collective-permute-start.15 = (bf16[256,256]{1,0:T(8,128)(2,1)S(1)}, bf16[256,256]{1,0:T(8,128)(2,1)S(1)}, u32[]{:S(2)}, u32[]{:S(2)}) collective-permute-start(bf16[256,256]{1,0:T(8,128)(2,1)S(1)} %bitcast.14), channel_id=1, source_target_pairs={{0,4},{1,5},{2,6},{3,7},{4,0},{5,1},{6,2},{7,3},{8,12},{9,13},{10,... | collective-permute-start | bytes 393224 | tf_op jit(solution)/shard_map/ppermute | solution.py:379
  132.8 8.2 %collective-permute-start.16 = (bf16[256,256]{1,0:T(8,128)(2,1)S(1)}, bf16[256,256]{1,0:T(8,128)(2,1)S(1)}, u32[]{:S(2)}, u32[]{:S(2)}) collective-permute-start(bf16[256,256]{1,0:T(8,128)(2,1)S(1)} %bitcast.15), channel_id=1, source_target_pairs={{0,6},{1,7},{2,0},{3,1},{4,2},{5,3},{6,4},{7,5},{8,14},{9,15},{10,... | collective-permute-start | bytes 393224 | tf_op jit(solution)/shard_map/ppermute | solution.py:379
  133.9 11.7 %collective-permute-start.17 = (bf16[256,256]{1,0:T(8,128)(2,1)S(1)}, bf16[256,256]{1,0:T(8,128)(2,1)S(1)}, u32[]{:S(2)}, u32[]{:S(2)}) collective-permute-start(bf16[256,256]{1,0:T(8,128)(2,1)S(1)} %bitcast.16), channel_id=1, source_target_pairs={{0,1},{1,0},{2,3},{3,2},{4,5},{5,4},{6,7},{7,6},{8,9},{9,8},{10,11... | collective-permute-start | bytes 393224 | tf_op jit(solution)/shard_map/ppermute | solution.py:375
  138.0 10.2 %collective-permute-start.18 = (bf16[256,256]{1,0:T(8,128)(2,1)S(1)}, bf16[256,256]{1,0:T(8,128)(2,1)S(1)}, u32[]{:S(2)}, u32[]{:S(2)}) collective-permute-start(bf16[256,256]{1,0:T(8,128)(2,1)S(1)} %collective-permute-done.14.refs_2_), channel_id=1, source_target_pairs={{0,1},{1,0},{2,3},{3,2},{4,5},{5,4},{6,7},{7,6},{8,9},{9,8},{10,11... | collective-permute-start | bytes 393224 | tf_op jit(solution)/shard_map/ppermute | solution.py:375
  138.6 12.8 %collective-permute-start.19 = (bf16[256,256]{1,0:T(8,128)(2,1)S(1)}, bf16[256,256]{1,0:T(8,128)(2,1)S(1)}, u32[]{:S(2)}, u32[]{:S(2)}) collective-permute-start(bf16[256,256]{1,0:T(8,128)(2,1)S(1)} %collective-permute-done.15.refs_3_), channel_id=1, source_target_pairs={{0,1},{1,0},{2,3},{3,2},{4,5},{5,4},{6,7},{7,6},{8,9},{9,8},{10,11... | collective-permute-start | bytes 393224 | tf_op jit(solution)/shard_map/ppermute | solution.py:375
  140.9 10.5 %collective-permute-start.20 = (bf16[256,256]{1,0:T(8,128)(2,1)S(1)}, bf16[256,256]{1,0:T(8,128)(2,1)S(1)}, u32[]{:S(2)}, u32[]{:S(2)}) collective-permute-start(bf16[256,256]{1,0:T(8,128)(2,1)S(1)} %collective-permute-done.16.refs_4_), channel_id=1, source_target_pairs={{0,1},{1,0},{2,3},{3,2},{4,5},{5,4},{6,7},{7,6},{8,9},{9,8},{10,11... | collective-permute-start | bytes 393224 | tf_op jit(solution)/shard_map/ppermute | solution.py:375
  144.5 8.3 %collective-permute-start.22 = (bf16[256,256]{1,0:T(8,128)(2,1)S(1)}, bf16[256,256]{1,0:T(8,128)(2,1)S(1)}, u32[]{:S(2)}, u32[]{:S(2)}) collective-permute-start(bf16[256,256]{1,0:T(8,128)(2,1)S(1)} %get-tuple-element.36), channel_id=1, source_target_pairs={{0,2},{1,3},{2,4},{3,5},{4,6},{5,7},{6,0},{7,1},{8,10},{9,11},{10,... | collective-permute-start | bytes 393224 | tf_op jit(solution)/shard_map/ppermute | solution.py:379
  145.6 8.9 %collective-permute-start.23 = (bf16[256,256]{1,0:T(8,128)(2,1)S(1)}, bf16[256,256]{1,0:T(8,128)(2,1)S(1)}, u32[]{:S(2)}, u32[]{:S(2)}) collective-permute-start(bf16[256,256]{1,0:T(8,128)(2,1)S(1)} %get-tuple-element.37), channel_id=1, source_target_pairs={{0,4},{1,5},{2,6},{3,7},{4,0},{5,1},{6,2},{7,3},{8,12},{9,13},{10,... | collective-permute-start | bytes 393224 | tf_op jit(solution)/shard_map/ppermute | solution.py:379
  148.2 6.4 %collective-permute-start.24 = (bf16[256,256]{1,0:T(8,128)(2,1)S(1)}, bf16[256,256]{1,0:T(8,128)(2,1)S(1)}, u32[]{:S(2)}, u32[]{:S(2)}) collective-permute-start(bf16[256,256]{1,0:T(8,128)(2,1)S(1)} %get-tuple-element.38), channel_id=1, source_target_pairs={{0,6},{1,7},{2,0},{3,1},{4,2},{5,3},{6,4},{7,5},{8,14},{9,15},{10,... | collective-permute-start | bytes 393224 | tf_op jit(solution)/shard_map/ppermute | solution.py:379

commit v6 on v5

--- a/solution.py
+++ b/solution.py
@@ -120,7 +120,7 @@
 
 
 def make_requests(owners, cap):
-    def kernel(parent, place, tally, table, rank_ref, rank_t_ref, ask, table_low_ref, row_ref):
+    def kernel(parent, place, tally, rank_ref, rank_t_ref, ask):
         parent_ref, place_ref = parent.get(), place.get()
         slots, pairs = parent_ref.shape
         line = iota((LANES, pairs), 0)
@@ -133,30 +133,25 @@
             where = jnp.where(hit, place_ref[c : c + 1, :].astype(F32), where)
         before = (iota((pairs, pairs), 0) < iota((pairs, pairs), 1)).astype(F32).astype(BF16)
         rank_t = jnp.where(named > 0, mm(named.astype(BF16), before), -1.0)
-        rank = rank_t.T
+        own_rank, own_place = rank_t[0:owners], where[0:owners]
+        lane = iota((owners, LANES), 1)
+        asks = jnp.zeros((owners, LANES), F32)
+        for p in range(cap):
+            row = jnp.sum(jnp.where(own_rank == p, own_place, 0.0), axis=1, keepdims=True)
+            asks = jnp.where(lane == p, row, asks)
+        asks = asks.astype(jnp.int32)
+        for o in range(owners):
+            ask.stage[o] = jnp.broadcast_to(asks[o : o + 1, :], ask.stage.shape[1:])
+        ask.start()
         rank_t_ref[...] = rank_t.astype(BF16)
-        rank_ref[...] = rank.astype(BF16)
-        where = where.T.astype(jnp.int32)
-        high = (where // 64).astype(F32).astype(BF16)
-        low = (where % 64).astype(F32).astype(BF16)
-        rank = rank.astype(BF16)
-        total = owners * cap
-        width = 512
-        for base in range(0, total, width):
-            spread = expander(LANES, cap, base, width)
-            want = (iota((pairs, width), 1) % cap).astype(F32)
-            place = mm(high, spread) * 64.0 + mm(low, spread)
-            row_ref[:, base : base + width] = jnp.sum(
-                jnp.where(mm(rank, spread) == want, place, 0.0), axis=0, keepdims=True
-            )
-        for o in range(owners):
-            row = row_ref[:, o * cap : (o + 1) * cap].astype(jnp.int32)
-            ask.stage[o, :, 0:cap] = jnp.broadcast_to(row, (ask.stage.shape[1], cap))
-        ask.start()
-        table_low_ref[...] = table.get()[...].astype(BF16)
+        rank_ref[...] = rank_t.T.astype(BF16)
         ask.finish()
 
     return kernel
+
+
+def narrow(table, out_ref):
+    out_ref[...] = table.get()[...].astype(BF16)
 
 
 def normalize(rows):
@@ -218,20 +213,24 @@
     return kernel
 
 
-def fetch(ask_ref, table_ref, out):
+def fetch(ask_ref, table_ref, out, column_ref):
     rows = table_ref.shape[0]
-    cap = out.stage.shape[1]
+    owners, cap, _ = out.stage.shape
     group = out.width
     diagonal = iota((cap, cap), 0) == iota((cap, cap), 1)
-    lane = iota((group * cap, rows), 1)
+    for o in range(owners):
+        ask = ask_ref[o, 0:1, 0:cap].astype(F32)
+        column_ref[o * cap : (o + 1) * cap, :] = jnp.sum(
+            jnp.where(diagonal, ask, 0.0), axis=1, keepdims=True
+        ).astype(jnp.int32)
+    size = group * cap
+    lane = iota((size, rows), 1).astype(jnp.int16)
 
     def compute(i):
-        columns = []
-        for g in range(group):
-            ask = ask_ref[i * group + g, 0:1, 0:cap]
-            columns.append(jnp.sum(jnp.where(diagonal, ask, 0).astype(F32), axis=1, keepdims=True))
-        column = jnp.concatenate(columns, axis=0).astype(jnp.int32)
-        hit = (column == lane).astype(F32).astype(BF16)
+        column = column_ref[pl.ds(i * size, size), :]
+        column = jnp.broadcast_to(column, (size, LANES)).astype(jnp.int16)
+        column = jnp.tile(column, (1, rows // LANES))
+        hit = jnp.where(column == lane, jnp.ones((), BF16), jnp.zeros((), BF16))
         return mm(hit, table_ref[...]).astype(BF16).reshape(group, cap, table_ref.shape[1])
 
     out.run(compute)
@@ -396,14 +395,14 @@
     hot_rows = hot_table.shape[0]
     block = lax.axis_index("blk").astype(jnp.int32).reshape(1)
 
-    rank, rank_t, ask, table_low = call(
+    rank, rank_t, ask = call(
         make_requests(owners, cap),
-        [shape((pairs, LANES), BF16), shape((LANES, pairs), BF16), HBM((owners, 8, LANES), jnp.int32), shape((rows, width), BF16)],
-        parent.T, place.T, tally.reshape(1, pairs), cold_table,
-        kinds=["h"] * 4,
-        scratch=[pltpu.VMEM((1, total), F32)],
-        flops=2 * pairs * total * LANES * 3,
-    )
+        [shape((pairs, LANES), BF16), shape((LANES, pairs), BF16), HBM((owners, 8, LANES), jnp.int32)],
+        parent.T, place.T, tally.reshape(1, pairs),
+        kinds=["h"] * 3,
+        flops=2 * pairs * pairs * LANES,
+    )
+    (table_low,) = call(narrow, [shape((rows, width), BF16)], cold_table, kinds=["h"])
     asked = swap(ask, "shard")
 
     steps = 8
@@ -411,6 +410,7 @@
         fetch,
         [HBM((owners, cap, width), BF16)],
         asked, table_low,
+        scratch=[pltpu.VMEM((total, 1), jnp.int32)],
         steps=steps,
         flops=2 * total * rows * width,
     )

time: 156 us -> 155 us (level)
  blocking collectives: 35.4 us -> 14.2 us
  starting transfers between devices: 64.8 us -> 76.8 us
  waiting for transfers between devices: 19.1 us -> 26.6 us
    all_to_all x2 -> x1, blocking collectives: 35.4 us -> 14.2 us  [swap(): return lax.all_to_all(array, axis, split_axis=0, concat_axis=0, tiled=True)]
    all_to_all x3 -> x4, starting transfers between devices: 20.3 us -> 32.3 us  [swap(): return lax.all_to_all(array, axis, split_axis=0, concat_axis=0, tiled=True)]
    all_to_all x3 -> x4, waiting for transfers between devices: 13.7 us -> 21.1 us  [swap(): return lax.all_to_all(array, axis, split_axis=0, concat_axis=0, tiled=True)]
    pallas_call x13 -> x14, Pallas kernels: 33.8 us -> 33.9 us  [call(): pl.pallas_call(run, out_shape=list(outs), in_specs=[pl.BlockSpec(memory_s...]
  transfers between devices with their start and end apart: 28 -> 29, of which waited for: 7 -> 8; matrix products, arithmetic and copies ran while one was open for 0% -> 0% of each run, Pallas kernels for 12% -> 14%
where the time goes in v6:
time: 155 us; the launch traced here: 154 us
  starting transfers between devices  76.8 us (50%)
  Pallas kernels  33.9 us (22%)
  waiting for transfers between devices  26.6 us (17%)
  blocking collectives  14.2 us (9%)
  between operations  2.34 us (2%)
    pallas_call x14, Pallas kernels, call(): pl.pallas_call(run, out_shape=list(outs), in_specs=[pl.BlockSpec(memory_s...  33.9 us
    all_to_all x4, starting transfers between devices, swap(): return lax.all_to_all(array, axis, split_axis=0, concat_axis=0, tiled=True)  32.3 us
    ppermute x13, starting transfers between devices, cross(): return lax.ppermute(array, 'blk', [(i, i ^ 1) for i in range(blocks)])  25.8 us
    all_to_all x4, waiting for transfers between devices, swap(): return lax.all_to_all(array, axis, split_axis=0, concat_axis=0, tiled=True)  21.1 us
    ppermute x12, starting transfers between devices, shift(): lax.ppermute(array, 'blk', [(i, (i + 2 * d) % blocks) for i in range(bloc...  18.8 us
    all_to_all x1, blocking collectives, swap(): return lax.all_to_all(array, axis, split_axis=0, concat_axis=0, tiled=True)  14.2 us
    ppermute x12, waiting for transfers between devices, shift(): lax.ppermute(array, 'blk', [(i, (i + 2 * d) % blocks) for i in range(bloc...  3.9 us
  transfers between devices with their start and end apart: 29, of which 8 were waited for; matrix products, arithmetic and copies ran while one was open for 0% of the time, Pallas kernels for 14%

profile of v6, /device:TPU:1, one launch (start us, length us, event | category | flops | bytes accessed | tf_op | source)
XLA Modules:
  0.0 153.9 jit_solution(2178040309062423633)
XLA Ops:
  0.6 1.9 %shard_map.112 = (bf16[256,128]{1,0:T(8,128)(2,1)S(1)}, bf16[128,256]{1,0:T(8,128)(2,1)S(1)}, s32[32,8,128]{2,1,0:T(8,128)}) custom-call(s32[4,256]{1,0:T(4,128)} %bitcast.22, s32[4,256]{1,0:T(4,128)} %bitcast.23, s32[1,256]{1,0:T(1,128)} %bitcast.24), custom_call_target="tpu_custom_call" | custom-call | flops 16777216 | bytes 9216 | tf_op jit(solution)/shard_map/pallas_call | solution.py:100
  2.6 12.0 %all-to-all-start = ((s32[32,8,128]{2,1,0:T(8,128)}), s32[32,8,128]{2,1,0:T(8,128)S(1)}, u32[]{:S(2)}, u32[]{:S(2)}) async-start(s32[32,8,128]{2,1,0:T(8,128)} %get-tuple-element.20), calls=%async_computation | async-start | bytes 262144 | tf_op jit(solution)/shard_map/all_to_all | solution.py:370
  14.6 1.7 %shard_map.113.refs_1_ = bf16[2048,256]{1,0:T(8,128)(2,1)S(1)} custom-call(f32[2048,256]{1,0:T(8,128)} %refs_0_.3), custom_call_target="tpu_custom_call" | custom-call | bytes 2097152 | tf_op jit(solution)/shard_map/pallas_call | solution.py:100
  16.3 7.4 %all-to-all-done.refs_0_.refs_1_ = s32[32,8,128]{2,1,0:T(8,128)S(1)} async-done(((s32[32,8,128]{2,1,0:T(8,128)}), s32[32,8,128]{2,1,0:T(8,128)S(1)}, u32[]{:S(2)}, u32[]{:S(2)}) %all-to-all-start) | async-done | bytes 131104 | tf_op jit(solution)/shard_map/all_to_all | solution.py:370
  23.8 4.9 %shard_map.114 = bf16[32,64,256]{2,1,0:T(8,128)(2,1)} custom-call(s32[32,8,128]{2,1,0:T(8,128)S(1)} %all-to-all-done.refs_0_.refs_1_, bf16[2048,256]{1,0:T(8,128)(2,1)S(1)} %shard_map.113.refs_1_), custom_call_target="tpu_custom_call" | custom-call | flops 2147483648 | bytes 1179648 | tf_op jit(solution)/shard_map/pallas_call | solution.py:100
  28.7 3.9 %all-to-all-start.1 = ((bf16[32,64,256]{2,1,0:T(8,128)(2,1)}), bf16[32,64,256]{2,1,0:T(8,128)(2,1)S(1)}, u32[]{:S(2)}, u32[]{:S(2)}) async-start(bf16[32,64,256]{2,1,0:T(8,128)(2,1)} %shard_map.114), calls=%async_computation.1 | async-start | bytes 2097152 | tf_op jit(solution)/shard_map/all_to_all | solution.py:370
  32.7 1.1 shard_map.116.refs_6_
  33.8 0.0 copy-start
  33.8 1.3 collective-permute-start
  35.1 2.5 %collective-permute-start.1 = (bf16[272,256]{1,0:T(8,128)(2,1)S(1)}, bf16[272,256]{1,0:T(8,128)(2,1)S(1)}, u32[]{:S(2)}, u32[]{:S(2)}) collective-permute-start(bf16[272,256]{1,0:T(8,128)(2,1)S(1)} %shard_map.116.refs_6_), channel_id=1, source_target_pairs={{0,4},{1,5},{2,6},{3,7},{4,0},{5,1},{6,2},{7,3},{8,12},{9,13},{10,... | collective-permute-start | bytes 417800 | tf_op jit(solution)/shard_map/ppermute | solution.py:378
  37.5 1.2 collective-permute-start.2
  38.7 2.9 %collective-permute-start.3 = (bf16[272,256]{1,0:T(8,128)(2,1)S(1)}, bf16[272,256]{1,0:T(8,128)(2,1)S(1)}, u32[]{:S(2)}, u32[]{:S(2)}) collective-permute-start(bf16[272,256]{1,0:T(8,128)(2,1)S(1)} %shard_map.116.refs_6_), channel_id=1, source_target_pairs={{0,1},{1,0},{2,3},{3,2},{4,5},{5,4},{6,7},{7,6},{8,9},{9,8},{10,11... | collective-permute-start | bytes 417800 | tf_op jit(solution)/shard_map/ppermute | solution.py:374
  41.6 0.0 collective-permute-done.refs_7_
  41.6 2.0 %collective-permute-start.4 = (bf16[272,256]{1,0:T(8,128)(2,1)S(1)}, bf16[272,256]{1,0:T(8,128)(2,1)S(1)}, u32[]{:S(2)}, u32[]{:S(2)}) collective-permute-start(bf16[272,256]{1,0:T(8,128)(2,1)S(1)} %collective-permute-done.refs_7_), channel_id=1, source_target_pairs={{0,1},{1,0},{2,3},{3,2},{4,5},{5,4},{6,7},{7,6},{8,9},{9,8},{10,11... | collective-permute-start | bytes 417800 | tf_op jit(solution)/shard_map/ppermute | solution.py:374
  43.6 0.0 collective-permute-done.1.refs_8_
  43.6 1.5 collective-permute-start.5
  45.1 0.1 collective-permute-start.6
  46.5 6.2 %shard_map.115 = (bf16[256,2048]{1,0:T(8,128)(2,1)S(1)}, bf16[2048,256]{1,0:T(8,128)(2,1)}, f32[256,256]{1,0:T(8,128)}) custom-call(bf16[256,128]{1,0:T(8,128)(2,1)S(1)} %get-tuple-element.25.refs_0_, bf16[128,256]{1,0:T(8,128)(2,1)S(1)} %get-tuple-element.26.refs_1_, s32[4,256]{1,0:T(4,128)} %bitcast.21, bf16[2048,256]{1,0:T(8,128)(2,1)} %refs_3_.1), custom_call_target="tpu_custom_call" | custom-call | flops 536870912 | bytes 1183744 | tf_op jit(solution)/shard_map/pallas_call | solution.py:100
  52.7 0.0 collective-permute-done.4.refs_11_
  52.7 0.0 collective-permute-done.5.refs_12_
  52.7 4.5 %all-to-all-done.1 = bf16[32,64,256]{2,1,0:T(8,128)(2,1)S(1)} async-done(((bf16[32,64,256]{2,1,0:T(8,128)(2,1)}), bf16[32,64,256]{2,1,0:T(8,128)(2,1)S(1)}, u32[]{:S(2)}, u32[]{:S(2)}) %all-to-all-start.1) | async-done | bytes 1048608 | tf_op jit(solution)/shard_map/all_to_all | solution.py:370
  57.2 5.3 %shard_map.117 = (bf16[512,256]{1,0:T(8,128)(2,1)S(1)}, bf16[8,16,256]{2,1,0:T(8,128)(2,1)S(1)}, bf16[2048,256]{1,0:T(8,128)(2,1)}) custom-call(f32[1]{0:T(128)S(6)} %copy.12.refs_0_, f32[1]{0:T(128)S(6)} %copy.13.refs_1_, bf16[2048,256]{1,0:T(8,128)(2,1)S(1)} %bitcast.10, bf16[256,2048]{1,0:T(8,128)(2,1)S(1)} %get-tuple-element.27.refs_3_, ...), custom_call_target="tpu_custom_call" | custom-call | flops 1073741824 | bytes 4521992 | tf_op jit(solution)/shard_map/pallas_call | solution.py:100
  62.5 8.2 %all-to-all-start.4 = ((bf16[32,64,256]{2,1,0:T(8,128)(2,1)}), bf16[32,64,256]{2,1,0:T(8,128)(2,1)S(1)}, u32[]{:S(2)}, u32[]{:S(2)}) async-start(bf16[32,64,256]{2,1,0:T(8,128)(2,1)} %bitcast.18), calls=%async_computation.4 | async-start | bytes 2097152 | tf_op jit(solution)/shard_map/all_to_all | solution.py:370
  70.8 1.3 collective-permute-start.7
  72.1 2.5 %collective-permute-start.8 = (bf16[512,256]{1,0:T(8,128)(2,1)S(1)}, bf16[512,256]{1,0:T(8,128)(2,1)S(1)}, u32[]{:S(2)}, u32[]{:S(2)}) collective-permute-start(bf16[512,256]{1,0:T(8,128)(2,1)S(1)} %get-tuple-element.30.refs_3_.refs_2_), channel_id=1, source_target_pairs={{0,4},{1,5},{2,6},{3,7},{4,0},{5,1},{6,2},{7,3},{8,12},{9,13},{10,... | collective-permute-start | bytes 786440 | tf_op jit(solution)/shard_map/ppermute | solution.py:378
  74.5 1.2 collective-permute-start.9
  75.7 2.9 %collective-permute-start.10 = (bf16[512,256]{1,0:T(8,128)(2,1)S(1)}, bf16[512,256]{1,0:T(8,128)(2,1)S(1)}, u32[]{:S(2)}, u32[]{:S(2)}) collective-permute-start(bf16[512,256]{1,0:T(8,128)(2,1)S(1)} %get-tuple-element.30.refs_3_.refs_2_), channel_id=1, source_target_pairs={{0,1},{1,0},{2,3},{3,2},{4,5},{5,4},{6,7},{7,6},{8,9},{9,8},{10,11... | collective-permute-start | bytes 786440 | tf_op jit(solution)/shard_map/ppermute | solution.py:374
  78.6 3.7 %collective-permute-start.11 = (bf16[512,256]{1,0:T(8,128)(2,1)S(1)}, bf16[512,256]{1,0:T(8,128)(2,1)S(1)}, u32[]{:S(2)}, u32[]{:S(2)}) collective-permute-start(bf16[512,256]{1,0:T(8,128)(2,1)S(1)} %collective-permute-done.7.refs_4_.refs_3_), channel_id=1, source_target_pairs={{0,1},{1,0},{2,3},{3,2},{4,5},{5,4},{6,7},{7,6},{8,9},{9,8},{10,11... | collective-permute-start | bytes 786440 | tf_op jit(solution)/shard_map/ppermute | solution.py:374
  82.3 2.2 %collective-permute-done.8.refs_5_.refs_4_ = bf16[512,256]{1,0:T(8,128)(2,1)S(1)} collective-permute-done((bf16[512,256]{1,0:T(8,128)(2,1)S(1)}, bf16[512,256]{1,0:T(8,128)(2,1)S(1)}, u32[]{:S(2)}, u32[]{:S(2)}) %collective-permute-start.8) | collective-permute-done | bytes 262176 | tf_op jit(solution)/shard_map/ppermute | solution.py:378
  84.5 2.9 %collective-permute-start.12 = (bf16[512,256]{1,0:T(8,128)(2,1)S(1)}, bf16[512,256]{1,0:T(8,128)(2,1)S(1)}, u32[]{:S(2)}, u32[]{:S(2)}) collective-permute-start(bf16[512,256]{1,0:T(8,128)(2,1)S(1)} %collective-permute-done.8.refs_5_.refs_4_), channel_id=1, source_target_pairs={{0,1},{1,0},{2,3},{3,2},{4,5},{5,4},{6,7},{7,6},{8,9},{9,8},{10,11... | collective-permute-start | bytes 786440 | tf_op jit(solution)/shard_map/ppermute | solution.py:374
  87.4 0.0 collective-permute-done.9.refs_6_.refs_5_
  87.4 0.0 collective-permute-start.13
  87.4 0.0 collective-permute-done.11.refs_8_.refs_7_
  87.4 1.1 collective-permute-done.12.refs_9_.refs_8_
  88.6 0.4 collective-permute-done.13.refs_10_.refs_9_
  88.9 1.6 %shard_map.119 = bf16[256,256]{1,0:T(8,128)(2,1)} custom-call(s32[1]{0:T(128)} %bitcast.5.refs_0_, bf16[8,16,256]{2,1,0:T(8,128)(2,1)S(1)} %get-tuple-element.31.refs_1_, bf16[512,256]{1,0:T(8,128)(2,1)S(1)} %get-tuple-element.30.refs_3_.refs_2_, bf16[512,256]{1,0:T(8,128)(2,1)S(1)} %collective-permute-done.7.refs_4_.refs_3_, ...), custom_call_target="tpu_custom_call" | custom-call | flops 268435456 | bytes 2162692 | tf_op jit(solution)/shard_map/pallas_call | solution.py:100
  90.5 4.8 %all-to-all-done.4 = bf16[32,64,256]{2,1,0:T(8,128)(2,1)S(1)} async-done(((bf16[32,64,256]{2,1,0:T(8,128)(2,1)}), bf16[32,64,256]{2,1,0:T(8,128)(2,1)S(1)}, u32[]{:S(2)}, u32[]{:S(2)}) %all-to-all-start.4) | async-done | bytes 1048608 | tf_op jit(solution)/shard_map/all_to_all | solution.py:370
  95.3 8.1 %all-to-all-start.2 = ((bf16[32,8,256]{2,1,0:T(8,128)(2,1)}), bf16[32,8,256]{2,1,0:T(8,128)(2,1)S(1)}, u32[]{:S(2)}, u32[]{:S(2)}) async-start(bf16[32,8,256]{2,1,0:T(8,128)(2,1)} %bitcast.19), calls=%async_computation.2 | async-start | bytes 262144 | tf_op jit(solution)/shard_map/all_to_all | solution.py:370
  103.4 2.7 %shard_map.123 = bf16[4,256,256]{2,1,0:T(8,128)(2,1)} custom-call(s32[1]{0:T(128)} %bitcast.5.refs_0_, s32[32,8,128]{2,1,0:T(8,128)S(1)} %copy-done.2, bf16[2048,256]{1,0:T(8,128)(2,1)S(1)} %bitcast.11), custom_call_target="tpu_custom_call" | custom-call | flops 1073741824 | bytes 1179652 | tf_op jit(solution)/shard_map/pallas_call | solution.py:100
  106.1 2.1 %collective-permute-start.21 = (bf16[4,256,256]{2,1,0:T(8,128)(2,1)}, bf16[4,256,256]{2,1,0:T(8,128)(2,1)}, u32[]{:S(2)}, u32[]{:S(2)}) collective-permute-start(bf16[4,256,256]{2,1,0:T(8,128)(2,1)} %shard_map.123), channel_id=1, source_target_pairs={{0,1},{1,0},{2,3},{3,2},{4,5},{5,4},{6,7},{7,6},{8,9},{9,8},{10,11... | collective-permute-start | bytes 1572872 | tf_op jit(solution)/shard_map/ppermute | solution.py:374
  108.1 4.4 %all-to-all-done.2.refs_0_ = bf16[32,8,256]{2,1,0:T(8,128)(2,1)S(1)} async-done(((bf16[32,8,256]{2,1,0:T(8,128)(2,1)}), bf16[32,8,256]{2,1,0:T(8,128)(2,1)S(1)}, u32[]{:S(2)}, u32[]{:S(2)}) %all-to-all-start.2) | async-done | bytes 131104 | tf_op jit(solution)/shard_map/all_to_all | solution.py:370
  112.5 0.7 shard_map.120
  113.3 14.2 %all_to_all.25 = bf16[32,8,256]{2,1,0:T(8,128)(2,1)S(1)} all-to-all(bf16[32,8,256]{2,1,0:T(8,128)(2,1)} %shard_map.120), channel_id=1, replica_groups=mesh['shard'=32,'blk'=8] {'shard'}, dimensions={0} | all-to-all | bytes 262144 | tf_op jit(solution)/shard_map/all_to_all | solution.py:370
  127.5 1.2 collective-permute-start.14
  128.7 2.5 %collective-permute-start.15 = (bf16[256,256]{1,0:T(8,128)(2,1)S(1)}, bf16[256,256]{1,0:T(8,128)(2,1)S(1)}, u32[]{:S(2)}, u32[]{:S(2)}) collective-permute-start(bf16[256,256]{1,0:T(8,128)(2,1)S(1)} %bitcast.14), channel_id=1, source_target_pairs={{0,4},{1,5},{2,6},{3,7},{4,0},{5,1},{6,2},{7,3},{8,12},{9,13},{10,... | collective-permute-start | bytes 393224 | tf_op jit(solution)/shard_map/ppermute | solution.py:378
  131.2 1.2 collective-permute-start.16
  132.3 4.1 %collective-permute-start.17 = (bf16[256,256]{1,0:T(8,128)(2,1)S(1)}, bf16[256,256]{1,0:T(8,128)(2,1)S(1)}, u32[]{:S(2)}, u32[]{:S(2)}) collective-permute-start(bf16[256,256]{1,0:T(8,128)(2,1)S(1)} %bitcast.16), channel_id=1, source_target_pairs={{0,1},{1,0},{2,3},{3,2},{4,5},{5,4},{6,7},{7,6},{8,9},{9,8},{10,11... | collective-permute-start | bytes 393224 | tf_op jit(solution)/shard_map/ppermute | solution.py:374
  136.4 0.0 collective-permute-done.14.refs_2_
  136.4 0.6 collective-permute-start.18
  137.0 0.0 collective-permute-done.15.refs_3_
  137.0 2.3 %collective-permute-start.19 = (bf16[256,256]{1,0:T(8,128)(2,1)S(1)}, bf16[256,256]{1,0:T(8,128)(2,1)S(1)}, u32[]{:S(2)}, u32[]{:S(2)}) collective-permute-start(bf16[256,256]{1,0:T(8,128)(2,1)S(1)} %collective-permute-done.15.refs_3_), channel_id=1, source_target_pairs={{0,1},{1,0},{2,3},{3,2},{4,5},{5,4},{6,7},{7,6},{8,9},{9,8},{10,11... | collective-permute-start | bytes 393224 | tf_op jit(solution)/shard_map/ppermute | solution.py:374
  139.3 0.6 collective-permute-start.20
  140.0 1.9 %shard_map.122.refs_0_ = f32[4,256,256]{2,1,0:T(8,128)S(1)} custom-call(s32[1]{0:T(128)} %bitcast.5.refs_0_, s32[32,8,128]{2,1,0:T(8,128)S(1)} %copy-done.2, bf16[2048,256]{1,0:T(8,128)(2,1)S(1)} %bitcast.12), custom_call_target="tpu_custom_call" | custom-call | flops 1073741824 | bytes 1179652 | tf_op jit(solution)/shard_map/pallas_call | solution.py:100
  141.8 1.1 shard_map.124
  143.0 1.1 collective-permute-start.22
  144.0 2.5 %collective-permute-start.23 = (bf16[256,256]{1,0:T(8,128)(2,1)S(1)}, bf16[256,256]{1,0:T(8,128)(2,1)S(1)}, u32[]{:S(2)}, u32[]{:S(2)}) collective-permute-start(bf16[256,256]{1,0:T(8,128)(2,1)S(1)} %get-tuple-element.35), channel_id=1, source_target_pairs={{0,4},{1,5},{2,6},{3,7},{4,0},{5,1},{6,2},{7,3},{8,12},{9,13},{10,... | collective-permute-start | bytes 393224 | tf_op jit(solution)/shard_map/ppermute | solution.py:378
  146.6 0.0 collective-permute-done.18.refs_6_
  146.6 0.6 collective-permute-start.24
  147.2 2.7 %shard_map.118 = f32[256,256]{1,0:T(8,128)} custom-call(f32[1]{0:T(128)S(6)} %copy.12.refs_0_, f32[1]{0:T(128)S(6)} %copy.13.refs_1_, bf16[256,256]{1,0:T(8,128)(2,1)} %refs_2_, bf16[512,256]{1,0:T(8,128)(2,1)S(1)} %get-tuple-element.30.refs_3_.refs_2_, bf16[512,256]{1,0:T(8,128)(2,1)S(1)} %collective-permute-done.7.refs_4_.refs_3_, ...), custom_call_target="tpu_custom_call" | custom-call | flops 536870912 | bytes 2228232 | tf_op jit(solution)/shard_map/pallas_call | solution.py:100
  149.8 0.0 collective-permute-done.19.refs_7_
  149.8 0.0 collective-permute-done.20.refs_8_
  149.9 1.4 shard_map.121
  151.3 1.7 %collective-permute-done.23.refs_2_ = bf16[256,256]{1,0:T(8,128)(2,1)S(1)} collective-permute-done((bf16[256,256]{1,0:T(8,128)(2,1)S(1)}, bf16[256,256]{1,0:T(8,128)(2,1)S(1)}, u32[]{:S(2)}, u32[]{:S(2)}) %collective-permute-start.23) | collective-permute-done | bytes 131104 | tf_op jit(solution)/shard_map/ppermute | solution.py:378
  153.0 0.8 shard_map.125
  (15 shorter events, 0.0 us)
Async XLA Ops:
  2.6 21.2 %all-to-all-start = ((s32[32,8,128]{2,1,0:T(8,128)}), s32[32,8,128]{2,1,0:T(8,128)S(1)}, u32[]{:S(2)}, u32[]{:S(2)}) async-start(s32[32,8,128]{2,1,0:T(8,128)} %get-tuple-element.20), calls=%async_computation | async-start | bytes 262144 | tf_op jit(solution)/shard_map/all_to_all | solution.py:370
  23.8 4.9 %copy-start.1 = (s32[32,8,128]{2,1,0:T(8,128)}, s32[32,8,128]{2,1,0:T(8,128)S(1)}, u32[]{:S(2)}) copy-start(s32[32,8,128]{2,1,0:T(8,128)S(1)} %all-to-all-done.refs_0_.refs_1_) | copy-start | bytes 393220
  28.7 28.5 %all-to-all-start.1 = ((bf16[32,64,256]{2,1,0:T(8,128)(2,1)}), bf16[32,64,256]{2,1,0:T(8,128)(2,1)S(1)}, u32[]{:S(2)}, u32[]{:S(2)}) async-start(bf16[32,64,256]{2,1,0:T(8,128)(2,1)} %shard_map.114), calls=%async_computation.1 | async-start | bytes 2097152 | tf_op jit(solution)/shard_map/all_to_all | solution.py:370
  33.8 23.4 %copy-start = (bf16[272,256]{1,0:T(8,128)(2,1)}, bf16[272,256]{1,0:T(8,128)(2,1)S(1)}, u32[]{:S(2)}) copy-start(bf16[272,256]{1,0:T(8,128)(2,1)S(1)} %shard_map.116.refs_6_) | copy-start | bytes 417796
  33.8 7.8 %collective-permute-start = (bf16[272,256]{1,0:T(8,128)(2,1)S(1)}, bf16[272,256]{1,0:T(8,128)(2,1)S(1)}, u32[]{:S(2)}, u32[]{:S(2)}) collective-permute-start(bf16[272,256]{1,0:T(8,128)(2,1)S(1)} %shard_map.116.refs_6_), channel_id=1, source_target_pairs={{0,2},{1,3},{2,4},{3,5},{4,6},{5,7},{6,0},{7,1},{8,10},{9,11},{10,... | collective-permute-start | bytes 417800 | tf_op jit(solution)/shard_map/ppermute | solution.py:378
  35.1 8.6 %collective-permute-start.1 = (bf16[272,256]{1,0:T(8,128)(2,1)S(1)}, bf16[272,256]{1,0:T(8,128)(2,1)S(1)}, u32[]{:S(2)}, u32[]{:S(2)}) collective-permute-start(bf16[272,256]{1,0:T(8,128)(2,1)S(1)} %shard_map.116.refs_6_), channel_id=1, source_target_pairs={{0,4},{1,5},{2,6},{3,7},{4,0},{5,1},{6,2},{7,3},{8,12},{9,13},{10,... | collective-permute-start | bytes 417800 | tf_op jit(solution)/shard_map/ppermute | solution.py:378
  37.5 7.6 %collective-permute-start.2 = (bf16[272,256]{1,0:T(8,128)(2,1)S(1)}, bf16[272,256]{1,0:T(8,128)(2,1)S(1)}, u32[]{:S(2)}, u32[]{:S(2)}) collective-permute-start(bf16[272,256]{1,0:T(8,128)(2,1)S(1)} %shard_map.116.refs_6_), channel_id=1, source_target_pairs={{0,6},{1,7},{2,0},{3,1},{4,2},{5,3},{6,4},{7,5},{8,14},{9,15},{10,... | collective-permute-start | bytes 417800 | tf_op jit(solution)/shard_map/ppermute | solution.py:378
  38.7 14.0 %collective-permute-start.3 = (bf16[272,256]{1,0:T(8,128)(2,1)S(1)}, bf16[272,256]{1,0:T(8,128)(2,1)S(1)}, u32[]{:S(2)}, u32[]{:S(2)}) collective-permute-start(bf16[272,256]{1,0:T(8,128)(2,1)S(1)} %shard_map.116.refs_6_), channel_id=1, source_target_pairs={{0,1},{1,0},{2,3},{3,2},{4,5},{5,4},{6,7},{7,6},{8,9},{9,8},{10,11... | collective-permute-start | bytes 417800 | tf_op jit(solution)/shard_map/ppermute | solution.py:374
  41.6 11.1 %collective-permute-start.4 = (bf16[272,256]{1,0:T(8,128)(2,1)S(1)}, bf16[272,256]{1,0:T(8,128)(2,1)S(1)}, u32[]{:S(2)}, u32[]{:S(2)}) collective-permute-start(bf16[272,256]{1,0:T(8,128)(2,1)S(1)} %collective-permute-done.refs_7_), channel_id=1, source_target_pairs={{0,1},{1,0},{2,3},{3,2},{4,5},{5,4},{6,7},{7,6},{8,9},{9,8},{10,11... | collective-permute-start | bytes 417800 | tf_op jit(solution)/shard_map/ppermute | solution.py:374
  43.6 9.1 %collective-permute-start.5 = (bf16[272,256]{1,0:T(8,128)(2,1)S(1)}, bf16[272,256]{1,0:T(8,128)(2,1)S(1)}, u32[]{:S(2)}, u32[]{:S(2)}) collective-permute-start(bf16[272,256]{1,0:T(8,128)(2,1)S(1)} %collective-permute-done.1.refs_8_), channel_id=1, source_target_pairs={{0,1},{1,0},{2,3},{3,2},{4,5},{5,4},{6,7},{7,6},{8,9},{9,8},{10,11... | collective-permute-start | bytes 417800 | tf_op jit(solution)/shard_map/ppermute | solution.py:374
  45.1 7.6 %collective-permute-start.6 = (bf16[272,256]{1,0:T(8,128)(2,1)S(1)}, bf16[272,256]{1,0:T(8,128)(2,1)S(1)}, u32[]{:S(2)}, u32[]{:S(2)}) collective-permute-start(bf16[272,256]{1,0:T(8,128)(2,1)S(1)} %collective-permute-done.2.refs_9_), channel_id=1, source_target_pairs={{0,1},{1,0},{2,3},{3,2},{4,5},{5,4},{6,7},{7,6},{8,9},{9,8},{10,11... | collective-permute-start | bytes 417800 | tf_op jit(solution)/shard_map/ppermute | solution.py:374
  62.5 40.9 %copy-start.2 = (s32[32,8,128]{2,1,0:T(8,128)S(1)}, s32[32,8,128]{2,1,0:T(8,128)}, u32[]{:S(2)}) copy-start(s32[32,8,128]{2,1,0:T(8,128)} %copy-done.1) | copy-start | bytes 393220
  62.5 32.8 %all-to-all-start.4 = ((bf16[32,64,256]{2,1,0:T(8,128)(2,1)}), bf16[32,64,256]{2,1,0:T(8,128)(2,1)S(1)}, u32[]{:S(2)}, u32[]{:S(2)}) async-start(bf16[32,64,256]{2,1,0:T(8,128)(2,1)} %bitcast.18), calls=%async_computation.4 | async-start | bytes 2097152 | tf_op jit(solution)/shard_map/all_to_all | solution.py:370
  70.8 7.8 %collective-permute-start.7 = (bf16[512,256]{1,0:T(8,128)(2,1)S(1)}, bf16[512,256]{1,0:T(8,128)(2,1)S(1)}, u32[]{:S(2)}, u32[]{:S(2)}) collective-permute-start(bf16[512,256]{1,0:T(8,128)(2,1)S(1)} %get-tuple-element.30.refs_3_.refs_2_), channel_id=1, source_target_pairs={{0,2},{1,3},{2,4},{3,5},{4,6},{5,7},{6,0},{7,1},{8,10},{9,11},{10,... | collective-permute-start | bytes 786440 | tf_op jit(solution)/shard_map/ppermute | solution.py:378
  72.1 12.4 %collective-permute-start.8 = (bf16[512,256]{1,0:T(8,128)(2,1)S(1)}, bf16[512,256]{1,0:T(8,128)(2,1)S(1)}, u32[]{:S(2)}, u32[]{:S(2)}) collective-permute-start(bf16[512,256]{1,0:T(8,128)(2,1)S(1)} %get-tuple-element.30.refs_3_.refs_2_), channel_id=1, source_target_pairs={{0,4},{1,5},{2,6},{3,7},{4,0},{5,1},{6,2},{7,3},{8,12},{9,13},{10,... | collective-permute-start | bytes 786440 | tf_op jit(solution)/shard_map/ppermute | solution.py:378
  74.5 12.9 %collective-permute-start.9 = (bf16[512,256]{1,0:T(8,128)(2,1)S(1)}, bf16[512,256]{1,0:T(8,128)(2,1)S(1)}, u32[]{:S(2)}, u32[]{:S(2)}) collective-permute-start(bf16[512,256]{1,0:T(8,128)(2,1)S(1)} %get-tuple-element.30.refs_3_.refs_2_), channel_id=1, source_target_pairs={{0,6},{1,7},{2,0},{3,1},{4,2},{5,3},{6,4},{7,5},{8,14},{9,15},{10,... | collective-permute-start | bytes 786440 | tf_op jit(solution)/shard_map/ppermute | solution.py:378
  75.7 11.7 %collective-permute-start.10 = (bf16[512,256]{1,0:T(8,128)(2,1)S(1)}, bf16[512,256]{1,0:T(8,128)(2,1)S(1)}, u32[]{:S(2)}, u32[]{:S(2)}) collective-permute-start(bf16[512,256]{1,0:T(8,128)(2,1)S(1)} %get-tuple-element.30.refs_3_.refs_2_), channel_id=1, source_target_pairs={{0,1},{1,0},{2,3},{3,2},{4,5},{5,4},{6,7},{7,6},{8,9},{9,8},{10,11... | collective-permute-start | bytes 786440 | tf_op jit(solution)/shard_map/ppermute | solution.py:374
  78.6 8.8 %collective-permute-start.11 = (bf16[512,256]{1,0:T(8,128)(2,1)S(1)}, bf16[512,256]{1,0:T(8,128)(2,1)S(1)}, u32[]{:S(2)}, u32[]{:S(2)}) collective-permute-start(bf16[512,256]{1,0:T(8,128)(2,1)S(1)} %collective-permute-done.7.refs_4_.refs_3_), channel_id=1, source_target_pairs={{0,1},{1,0},{2,3},{3,2},{4,5},{5,4},{6,7},{7,6},{8,9},{9,8},{10,11... | collective-permute-start | bytes 786440 | tf_op jit(solution)/shard_map/ppermute | solution.py:374
  84.5 4.1 %collective-permute-start.12 = (bf16[512,256]{1,0:T(8,128)(2,1)S(1)}, bf16[512,256]{1,0:T(8,128)(2,1)S(1)}, u32[]{:S(2)}, u32[]{:S(2)}) collective-permute-start(bf16[512,256]{1,0:T(8,128)(2,1)S(1)} %collective-permute-done.8.refs_5_.refs_4_), channel_id=1, source_target_pairs={{0,1},{1,0},{2,3},{3,2},{4,5},{5,4},{6,7},{7,6},{8,9},{9,8},{10,11... | collective-permute-start | bytes 786440 | tf_op jit(solution)/shard_map/ppermute | solution.py:374
  87.4 1.5 collective-permute-start.13
  95.3 17.2 %all-to-all-start.2 = ((bf16[32,8,256]{2,1,0:T(8,128)(2,1)}), bf16[32,8,256]{2,1,0:T(8,128)(2,1)S(1)}, u32[]{:S(2)}, u32[]{:S(2)}) async-start(bf16[32,8,256]{2,1,0:T(8,128)(2,1)} %bitcast.19), calls=%async_computation.2 | async-start | bytes 262144 | tf_op jit(solution)/shard_map/all_to_all | solution.py:370
  106.1 35.8 %collective-permute-start.21 = (bf16[4,256,256]{2,1,0:T(8,128)(2,1)}, bf16[4,256,256]{2,1,0:T(8,128)(2,1)}, u32[]{:S(2)}, u32[]{:S(2)}) collective-permute-start(bf16[4,256,256]{2,1,0:T(8,128)(2,1)} %shard_map.123), channel_id=1, source_target_pairs={{0,1},{1,0},{2,3},{3,2},{4,5},{5,4},{6,7},{7,6},{8,9},{9,8},{10,11... | collective-permute-start | bytes 1572872 | tf_op jit(solution)/shard_map/ppermute | solution.py:374
  127.5 8.9 %collective-permute-start.14 = (bf16[256,256]{1,0:T(8,128)(2,1)S(1)}, bf16[256,256]{1,0:T(8,128)(2,1)S(1)}, u32[]{:S(2)}, u32[]{:S(2)}) collective-permute-start(bf16[256,256]{1,0:T(8,128)(2,1)S(1)} %bitcast.13), channel_id=1, source_target_pairs={{0,2},{1,3},{2,4},{3,5},{4,6},{5,7},{6,0},{7,1},{8,10},{9,11},{10,... | collective-permute-start | bytes 393224 | tf_op jit(solution)/shard_map/ppermute | solution.py:378
  128.7 8.3 %collective-permute-start.15 = (bf16[256,256]{1,0:T(8,128)(2,1)S(1)}, bf16[256,256]{1,0:T(8,128)(2,1)S(1)}, u32[]{:S(2)}, u32[]{:S(2)}) collective-permute-start(bf16[256,256]{1,0:T(8,128)(2,1)S(1)} %bitcast.14), channel_id=1, source_target_pairs={{0,4},{1,5},{2,6},{3,7},{4,0},{5,1},{6,2},{7,3},{8,12},{9,13},{10,... | collective-permute-start | bytes 393224 | tf_op jit(solution)/shard_map/ppermute | solution.py:378
  131.2 8.2 %collective-permute-start.16 = (bf16[256,256]{1,0:T(8,128)(2,1)S(1)}, bf16[256,256]{1,0:T(8,128)(2,1)S(1)}, u32[]{:S(2)}, u32[]{:S(2)}) collective-permute-start(bf16[256,256]{1,0:T(8,128)(2,1)S(1)} %bitcast.15), channel_id=1, source_target_pairs={{0,6},{1,7},{2,0},{3,1},{4,2},{5,3},{6,4},{7,5},{8,14},{9,15},{10,... | collective-permute-start | bytes 393224 | tf_op jit(solution)/shard_map/ppermute | solution.py:378
  132.3 11.7 %collective-permute-start.17 = (bf16[256,256]{1,0:T(8,128)(2,1)S(1)}, bf16[256,256]{1,0:T(8,128)(2,1)S(1)}, u32[]{:S(2)}, u32[]{:S(2)}) collective-permute-start(bf16[256,256]{1,0:T(8,128)(2,1)S(1)} %bitcast.16), channel_id=1, source_target_pairs={{0,1},{1,0},{2,3},{3,2},{4,5},{5,4},{6,7},{7,6},{8,9},{9,8},{10,11... | collective-permute-start | bytes 393224 | tf_op jit(solution)/shard_map/ppermute | solution.py:374
  136.4 10.2 %collective-permute-start.18 = (bf16[256,256]{1,0:T(8,128)(2,1)S(1)}, bf16[256,256]{1,0:T(8,128)(2,1)S(1)}, u32[]{:S(2)}, u32[]{:S(2)}) collective-permute-start(bf16[256,256]{1,0:T(8,128)(2,1)S(1)} %collective-permute-done.14.refs_2_), channel_id=1, source_target_pairs={{0,1},{1,0},{2,3},{3,2},{4,5},{5,4},{6,7},{7,6},{8,9},{9,8},{10,11... | collective-permute-start | bytes 393224 | tf_op jit(solution)/shard_map/ppermute | solution.py:374
  137.0 12.8 %collective-permute-start.19 = (bf16[256,256]{1,0:T(8,128)(2,1)S(1)}, bf16[256,256]{1,0:T(8,128)(2,1)S(1)}, u32[]{:S(2)}, u32[]{:S(2)}) collective-permute-start(bf16[256,256]{1,0:T(8,128)(2,1)S(1)} %collective-permute-done.15.refs_3_), channel_id=1, source_target_pairs={{0,1},{1,0},{2,3},{3,2},{4,5},{5,4},{6,7},{7,6},{8,9},{9,8},{10,11... | collective-permute-start | bytes 393224 | tf_op jit(solution)/shard_map/ppermute | solution.py:374
  139.3 10.5 %collective-permute-start.20 = (bf16[256,256]{1,0:T(8,128)(2,1)S(1)}, bf16[256,256]{1,0:T(8,128)(2,1)S(1)}, u32[]{:S(2)}, u32[]{:S(2)}) collective-permute-start(bf16[256,256]{1,0:T(8,128)(2,1)S(1)} %collective-permute-done.16.refs_4_), channel_id=1, source_target_pairs={{0,1},{1,0},{2,3},{3,2},{4,5},{5,4},{6,7},{7,6},{8,9},{9,8},{10,11... | collective-permute-start | bytes 393224 | tf_op jit(solution)/shard_map/ppermute | solution.py:374
  143.0 8.3 %collective-permute-start.22 = (bf16[256,256]{1,0:T(8,128)(2,1)S(1)}, bf16[256,256]{1,0:T(8,128)(2,1)S(1)}, u32[]{:S(2)}, u32[]{:S(2)}) collective-permute-start(bf16[256,256]{1,0:T(8,128)(2,1)S(1)} %get-tuple-element.34), channel_id=1, source_target_pairs={{0,2},{1,3},{2,4},{3,5},{4,6},{5,7},{6,0},{7,1},{8,10},{9,11},{10,... | collective-permute-start | bytes 393224 | tf_op jit(solution)/shard_map/ppermute | solution.py:378
  144.0 8.9 %collective-permute-start.23 = (bf16[256,256]{1,0:T(8,128)(2,1)S(1)}, bf16[256,256]{1,0:T(8,128)(2,1)S(1)}, u32[]{:S(2)}, u32[]{:S(2)}) collective-permute-start(bf16[256,256]{1,0:T(8,128)(2,1)S(1)} %get-tuple-element.35), channel_id=1, source_target_pairs={{0,4},{1,5},{2,6},{3,7},{4,0},{5,1},{6,2},{7,3},{8,12},{9,13},{10,... | collective-permute-start | bytes 393224 | tf_op jit(solution)/shard_map/ppermute | solution.py:378
  146.6 6.4 %collective-permute-start.24 = (bf16[256,256]{1,0:T(8,128)(2,1)S(1)}, bf16[256,256]{1,0:T(8,128)(2,1)S(1)}, u32[]{:S(2)}, u32[]{:S(2)}) collective-permute-start(bf16[256,256]{1,0:T(8,128)(2,1)S(1)} %get-tuple-element.36), channel_id=1, source_target_pairs={{0,6},{1,7},{2,0},{3,1},{4,2},{5,3},{6,4},{7,5},{8,14},{9,15},{10,... | collective-permute-start | bytes 393224 | tf_op jit(solution)/shard_map/ppermute | solution.py:378

commit v7 on v6

--- a/solution.py
+++ b/solution.py
@@ -176,7 +176,7 @@
 
 
 def prepare(cap):
-    def kernel(rank_ref, rank_t_ref, lines, hot, pick_ref, placed, hot_sum):
+    def kernel(rank_ref, rank_t_ref, lines, hot, pick_ref, placed, hot_sum_ref):
         lines_ref = lines.get()
         pairs = rank_ref.shape[0]
         slots = lines_ref.shape[0]
@@ -190,7 +190,6 @@
         want = (iota((pairs, width), 1) % cap).astype(F32)
         want_t = (iota((width, pairs), 0) % cap).astype(F32)
         hot_ref = hot.get()
-        hot_sum_ref = hot_sum.stage
         hot_sum_ref[...] = jnp.zeros_like(hot_sum_ref)
 
         def compute(i):
@@ -207,8 +206,6 @@
             return hit.astype(F32).astype(BF16)
 
         placed.run(compute)
-        hot_sum.start()
-        hot_sum.finish()
 
     return kernel
 
@@ -236,17 +233,16 @@
     out.run(compute)
 
 
-def loss_side(own_low, other_refs, total_ref, sharpness, additive):
+def loss_side(own_low, others, own_at, sharpness, additive):
     rows = own_low.shape[0]
-    for i, ref in enumerate(other_refs):
-        other = ref[0:rows, :]
+    others = [other[0:rows, :] for other in others]
+    grads = []
+    for i, other in enumerate(others):
         grad = jax.nn.sigmoid(sharpness * mm(own_low, other, NT) + additive)
-        if i == 0:
+        if i == own_at:
             grad = grad - (iota((rows, rows), 0) == iota((rows, rows), 1)).astype(F32)
-            total_ref[...] = mm(grad.astype(BF16), other)
-        else:
-            total_ref[...] += mm(grad.astype(BF16), other)
-    return sharpness * total_ref[...]
+        grads.append(grad.astype(BF16))
+    return sharpness * mm(jnp.concatenate(grads, axis=1), jnp.concatenate(others, axis=0))
 
 
 def project(unit, radius, direction):
@@ -254,18 +250,18 @@
     return (direction - unit * inner) / radius
 
 
-def item_side(blocks):
-    def kernel(sharp_ref, add_ref, fetched_ref, pick_ref, hot_sum, place, own, *refs):
-        query_refs, refs = refs[: blocks - 1], refs[blocks - 1 :]
-        (sides_ref, tails_ref, outgoing, total_ref) = refs
-        pairs = total_ref.shape[0]
-        unit, radius = normalize(mm(pick_ref[...], fetched_ref[...]) + hot_sum.get()[...])
+def item_side(near, far):
+    def kernel(sharp_ref, add_ref, fetched_ref, pick_ref, hot_sum_ref, *refs):
+        near_refs, far_blocks, place = refs[:near], refs[near : near + far], refs[near + far]
+        sides_ref, tails_ref, outgoing = refs[near + far + 1 :]
+        pairs = hot_sum_ref.shape[0]
+        unit, radius = normalize(mm(pick_ref[...], fetched_ref[...]) + hot_sum_ref[...])
         low = unit.astype(BF16)
         sides_ref[0:pairs, :] = low
-        query_refs = [own.get()] + list(query_refs)
-        direction = loss_side(low, query_refs, total_ref, sharp_ref[0], add_ref[0])
-        for i, ref in enumerate(query_refs):
+        queries = list(near_refs) + [block.get() for block in far_blocks]
+        for i, ref in enumerate(queries):
             tails_ref[i] = ref[pairs:, :]
+        direction = loss_side(low, queries, near + far - 1, sharp_ref[0], add_ref[0])
         grad = project(unit, radius, direction).astype(BF16)
         sides_ref[pairs:, :] = grad
         place_ref = place.get()
@@ -276,9 +272,9 @@
 
 
 def query_side(sharp_ref, add_ref, query, *refs):
-    item_refs, (out, total_ref) = refs[:-2], refs[-2:]
+    item_refs, out = refs[:-1], refs[-1]
     unit, radius = normalize(query.get()[...].astype(F32))
-    direction = loss_side(unit.astype(BF16), item_refs, total_ref, sharp_ref[0], add_ref[0])
+    direction = loss_side(unit.astype(BF16), item_refs, 0, sharp_ref[0], add_ref[0])
     out.write(project(unit, radius, direction))
     out.finish()
 
@@ -423,19 +419,20 @@
 
     pick, placed, hot_sum = call(
         prepare(cap),
-        [shape((pairs, total), BF16), HBM((total, pairs), BF16), HBM((pairs, width), F32)],
+        [shape((pairs, total), BF16), HBM((total, pairs), BF16), shape((pairs, width), F32)],
         rank, rank_t, lines_t, hot_table,
         kinds=["v", "v", "h", "h"],
         steps=steps,
         flops=2 * pairs * total * (width + 2 * LANES),
     )
 
+    far = 3
+    order = list(range(1, blocks)) + [0]
     sides, tails, outgoing = call(
-        item_side(blocks),
+        item_side(blocks - far, far),
         [shape((2 * pairs, width), BF16), shape((blocks, 16, width), BF16), HBM((total, width), BF16)],
-        sharpness, additive, fetched, pick, hot_sum, placed, *query_blocks,
-        kinds=["s", "s", "v", "v", "h", "h", "h"] + ["v"] * (blocks - 1),
-        scratch=[pltpu.VMEM((pairs, width), F32)],
+        sharpness, additive, fetched, pick, hot_sum, *[query_blocks[i] for i in order], placed,
+        kinds=["s", "s", "v", "v", "v"] + ["v"] * (blocks - far) + ["h"] * (far + 1),
         steps=steps,
         flops=2 * pairs * width * (2 * total + 2 * blocks * pairs),
     )
@@ -445,7 +442,7 @@
     (hot_block,) = call(
         hot_terms(blocks, slots),
         [HBM((hot_rows // blocks, width), BF16)],
-        block, tails, *side_blocks,
+        block, tails, *[side_blocks[i] for i in order],
         kinds=["s"] + ["v"] * (blocks + 1),
         scratch=[pltpu.VMEM((hot_rows // blocks, width), F32)],
         flops=2 * blocks * pairs * width * hot_rows // blocks,
@@ -455,7 +452,6 @@
         [HBM((pairs, width), F32)],
         sharpness, additive, queries, *side_blocks,
         kinds=["s", "s", "h"] + ["v"] * blocks,
-        scratch=[pltpu.VMEM((pairs, width), F32)],
         flops=4 * pairs * width * blocks * pairs,
     )
     hot_parts = swap(hot_block.reshape(owners, hot_rows // blocks // owners, width), "shard")

time: 155 us -> 154 us (level)
  transfers between devices with their start and end apart: 29 -> 29, of which waited for: 8 -> 8; matrix products, arithmetic and copies ran while one was open for 0% -> 0% of each run, Pallas kernels for 14% -> 13%
where the time goes in v7:
time: 154 us; the launch traced here: 153 us
  starting transfers between devices  76.8 us (50%)
  Pallas kernels  32.5 us (21%)
  waiting for transfers between devices  26.7 us (17%)
  blocking collectives  14.2 us (9%)
  between operations  2.34 us (2%)
    pallas_call x14, Pallas kernels, call(): pl.pallas_call(run, out_shape=list(outs), in_specs=[pl.BlockSpec(memory_s...  32.5 us
    all_to_all x4, starting transfers between devices, swap(): return lax.all_to_all(array, axis, split_axis=0, concat_axis=0, tiled=True)  32.3 us
    ppermute x13, starting transfers between devices, cross(): return lax.ppermute(array, 'blk', [(i, i ^ 1) for i in range(blocks)])  25.8 us
    all_to_all x4, waiting for transfers between devices, swap(): return lax.all_to_all(array, axis, split_axis=0, concat_axis=0, tiled=True)  21.2 us
    ppermute x12, starting transfers between devices, shift(): lax.ppermute(array, 'blk', [(i, (i + 2 * d) % blocks) for i in range(bloc...  18.8 us
    all_to_all x1, blocking collectives, swap(): return lax.all_to_all(array, axis, split_axis=0, concat_axis=0, tiled=True)  14.2 us
    ppermute x12, waiting for transfers between devices, shift(): lax.ppermute(array, 'blk', [(i, (i + 2 * d) % blocks) for i in range(bloc...  3.96 us
  transfers between devices with their start and end apart: 29, of which 8 were waited for; matrix products, arithmetic and copies ran while one was open for 0% of the time, Pallas kernels for 13%

profile of v7, /device:TPU:1, one launch (start us, length us, event | category | flops | bytes accessed | tf_op | source)
XLA Modules:
  0.0 153.3 jit_solution(9174317630517438001)
XLA Ops:
  0.6 1.9 %shard_map.112 = (bf16[256,128]{1,0:T(8,128)(2,1)S(1)}, bf16[128,256]{1,0:T(8,128)(2,1)S(1)}, s32[32,8,128]{2,1,0:T(8,128)}) custom-call(s32[4,256]{1,0:T(4,128)} %bitcast.22, s32[4,256]{1,0:T(4,128)} %bitcast.23, s32[1,256]{1,0:T(1,128)} %bitcast.24), custom_call_target="tpu_custom_call" | custom-call | flops 16777216 | bytes 9216 | tf_op jit(solution)/shard_map/pallas_call | solution.py:100
  2.6 12.0 %all-to-all-start = ((s32[32,8,128]{2,1,0:T(8,128)}), s32[32,8,128]{2,1,0:T(8,128)S(1)}, u32[]{:S(2)}, u32[]{:S(2)}) async-start(s32[32,8,128]{2,1,0:T(8,128)} %get-tuple-element.20), calls=%async_computation | async-start | bytes 262144 | tf_op jit(solution)/shard_map/all_to_all | solution.py:366
  14.6 1.7 %shard_map.113.refs_1_ = bf16[2048,256]{1,0:T(8,128)(2,1)S(1)} custom-call(f32[2048,256]{1,0:T(8,128)} %refs_0_.3), custom_call_target="tpu_custom_call" | custom-call | bytes 2097152 | tf_op jit(solution)/shard_map/pallas_call | solution.py:100
  16.3 7.4 %all-to-all-done.refs_0_.refs_1_ = s32[32,8,128]{2,1,0:T(8,128)S(1)} async-done(((s32[32,8,128]{2,1,0:T(8,128)}), s32[32,8,128]{2,1,0:T(8,128)S(1)}, u32[]{:S(2)}, u32[]{:S(2)}) %all-to-all-start) | async-done | bytes 131104 | tf_op jit(solution)/shard_map/all_to_all | solution.py:366
  23.8 4.9 %shard_map.114 = bf16[32,64,256]{2,1,0:T(8,128)(2,1)} custom-call(s32[32,8,128]{2,1,0:T(8,128)S(1)} %all-to-all-done.refs_0_.refs_1_, bf16[2048,256]{1,0:T(8,128)(2,1)S(1)} %shard_map.113.refs_1_), custom_call_target="tpu_custom_call" | custom-call | flops 2147483648 | bytes 1179648 | tf_op jit(solution)/shard_map/pallas_call | solution.py:100
  28.7 3.9 %all-to-all-start.1 = ((bf16[32,64,256]{2,1,0:T(8,128)(2,1)}), bf16[32,64,256]{2,1,0:T(8,128)(2,1)S(1)}, u32[]{:S(2)}, u32[]{:S(2)}) async-start(bf16[32,64,256]{2,1,0:T(8,128)(2,1)} %shard_map.114), calls=%async_computation.1 | async-start | bytes 2097152 | tf_op jit(solution)/shard_map/all_to_all | solution.py:366
  32.7 1.1 shard_map.116.refs_12_
  33.8 0.0 copy-start
  33.8 1.3 collective-permute-start
  35.1 2.5 %collective-permute-start.1 = (bf16[272,256]{1,0:T(8,128)(2,1)S(1)}, bf16[272,256]{1,0:T(8,128)(2,1)S(1)}, u32[]{:S(2)}, u32[]{:S(2)}) collective-permute-start(bf16[272,256]{1,0:T(8,128)(2,1)S(1)} %shard_map.116.refs_12_), channel_id=1, source_target_pairs={{0,4},{1,5},{2,6},{3,7},{4,0},{5,1},{6,2},{7,3},{8,12},{9,13},{10,... | collective-permute-start | bytes 417800 | tf_op jit(solution)/shard_map/ppermute | solution.py:374
  37.5 1.2 collective-permute-start.2
  38.7 2.9 %collective-permute-start.3 = (bf16[272,256]{1,0:T(8,128)(2,1)S(1)}, bf16[272,256]{1,0:T(8,128)(2,1)S(1)}, u32[]{:S(2)}, u32[]{:S(2)}) collective-permute-start(bf16[272,256]{1,0:T(8,128)(2,1)S(1)} %shard_map.116.refs_12_), channel_id=1, source_target_pairs={{0,1},{1,0},{2,3},{3,2},{4,5},{5,4},{6,7},{7,6},{8,9},{9,8},{10,11... | collective-permute-start | bytes 417800 | tf_op jit(solution)/shard_map/ppermute | solution.py:370
  41.6 0.0 collective-permute-done.refs_5_
  41.6 2.0 %collective-permute-start.4 = (bf16[272,256]{1,0:T(8,128)(2,1)S(1)}, bf16[272,256]{1,0:T(8,128)(2,1)S(1)}, u32[]{:S(2)}, u32[]{:S(2)}) collective-permute-start(bf16[272,256]{1,0:T(8,128)(2,1)S(1)} %collective-permute-done.refs_5_), channel_id=1, source_target_pairs={{0,1},{1,0},{2,3},{3,2},{4,5},{5,4},{6,7},{7,6},{8,9},{9,8},{10,11... | collective-permute-start | bytes 417800 | tf_op jit(solution)/shard_map/ppermute | solution.py:370
  43.6 0.0 collective-permute-done.1.refs_6_
  43.6 1.5 collective-permute-start.5
  45.1 0.1 collective-permute-start.6
  46.5 5.4 %shard_map.115 = (bf16[256,2048]{1,0:T(8,128)(2,1)S(1)}, bf16[2048,256]{1,0:T(8,128)(2,1)}, f32[256,256]{1,0:T(8,128)S(1)}) custom-call(bf16[256,128]{1,0:T(8,128)(2,1)S(1)} %get-tuple-element.25.refs_0_, bf16[128,256]{1,0:T(8,128)(2,1)S(1)} %get-tuple-element.26.refs_1_, s32[4,256]{1,0:T(4,128)} %bitcast.21, bf16[2048,256]{1,0:T(8,128)(2,1)} %refs_3_.1), custom_call_target="tpu_custom_call" | custom-call | flops 536870912 | bytes 1183744 | tf_op jit(solution)/shard_map/pallas_call | solution.py:100
  51.9 0.0 collective-permute-done.3.refs_8_
  51.9 0.0 collective-permute-done.5.refs_10_
  52.0 0.0 copy-start.3
  52.0 0.6 copy-done.3
  52.6 0.0 collective-permute-done.6.refs_11_
  52.6 4.6 %all-to-all-done.1 = bf16[32,64,256]{2,1,0:T(8,128)(2,1)S(1)} async-done(((bf16[32,64,256]{2,1,0:T(8,128)(2,1)}), bf16[32,64,256]{2,1,0:T(8,128)(2,1)S(1)}, u32[]{:S(2)}, u32[]{:S(2)}) %all-to-all-start.1) | async-done | bytes 1048608 | tf_op jit(solution)/shard_map/all_to_all | solution.py:366
  57.2 4.7 %shard_map.117 = (bf16[512,256]{1,0:T(8,128)(2,1)S(1)}, bf16[8,16,256]{2,1,0:T(8,128)(2,1)S(1)}, bf16[2048,256]{1,0:T(8,128)(2,1)}) custom-call(f32[1]{0:T(128)S(6)} %copy.12.refs_0_, f32[1]{0:T(128)S(6)} %copy.13.refs_1_, bf16[2048,256]{1,0:T(8,128)(2,1)S(1)} %bitcast.10, bf16[256,2048]{1,0:T(8,128)(2,1)S(1)} %get-tuple-element.27.refs_3_, ...), custom_call_target="tpu_custom_call" | custom-call | flops 1073741824 | bytes 4521992 | tf_op jit(solution)/shard_map/pallas_call | solution.py:100
  61.9 8.2 %all-to-all-start.4 = ((bf16[32,64,256]{2,1,0:T(8,128)(2,1)}), bf16[32,64,256]{2,1,0:T(8,128)(2,1)S(1)}, u32[]{:S(2)}, u32[]{:S(2)}) async-start(bf16[32,64,256]{2,1,0:T(8,128)(2,1)} %bitcast.18), calls=%async_computation.4 | async-start | bytes 2097152 | tf_op jit(solution)/shard_map/all_to_all | solution.py:366
  70.2 1.3 collective-permute-start.7
  71.5 2.5 %collective-permute-start.8 = (bf16[512,256]{1,0:T(8,128)(2,1)S(1)}, bf16[512,256]{1,0:T(8,128)(2,1)S(1)}, u32[]{:S(2)}, u32[]{:S(2)}) collective-permute-start(bf16[512,256]{1,0:T(8,128)(2,1)S(1)} %get-tuple-element.30.refs_3_.refs_9_), channel_id=1, source_target_pairs={{0,4},{1,5},{2,6},{3,7},{4,0},{5,1},{6,2},{7,3},{8,12},{9,13},{10,... | collective-permute-start | bytes 786440 | tf_op jit(solution)/shard_map/ppermute | solution.py:374
  73.9 1.2 collective-permute-start.9
  75.1 2.9 %collective-permute-start.10 = (bf16[512,256]{1,0:T(8,128)(2,1)S(1)}, bf16[512,256]{1,0:T(8,128)(2,1)S(1)}, u32[]{:S(2)}, u32[]{:S(2)}) collective-permute-start(bf16[512,256]{1,0:T(8,128)(2,1)S(1)} %get-tuple-element.30.refs_3_.refs_9_), channel_id=1, source_target_pairs={{0,1},{1,0},{2,3},{3,2},{4,5},{5,4},{6,7},{7,6},{8,9},{9,8},{10,11... | collective-permute-start | bytes 786440 | tf_op jit(solution)/shard_map/ppermute | solution.py:370
  78.0 0.0 collective-permute-done.7.refs_4_.refs_2_
  78.0 3.7 %collective-permute-start.11 = (bf16[512,256]{1,0:T(8,128)(2,1)S(1)}, bf16[512,256]{1,0:T(8,128)(2,1)S(1)}, u32[]{:S(2)}, u32[]{:S(2)}) collective-permute-start(bf16[512,256]{1,0:T(8,128)(2,1)S(1)} %collective-permute-done.7.refs_4_.refs_2_), channel_id=1, source_target_pairs={{0,1},{1,0},{2,3},{3,2},{4,5},{5,4},{6,7},{7,6},{8,9},{9,8},{10,11... | collective-permute-start | bytes 786440 | tf_op jit(solution)/shard_map/ppermute | solution.py:370
  81.7 2.2 %collective-permute-done.8.refs_5_.refs_3_ = bf16[512,256]{1,0:T(8,128)(2,1)S(1)} collective-permute-done((bf16[512,256]{1,0:T(8,128)(2,1)S(1)}, bf16[512,256]{1,0:T(8,128)(2,1)S(1)}, u32[]{:S(2)}, u32[]{:S(2)}) %collective-permute-start.8) | collective-permute-done | bytes 262176 | tf_op jit(solution)/shard_map/ppermute | solution.py:374
  83.9 2.9 %collective-permute-start.12 = (bf16[512,256]{1,0:T(8,128)(2,1)S(1)}, bf16[512,256]{1,0:T(8,128)(2,1)S(1)}, u32[]{:S(2)}, u32[]{:S(2)}) collective-permute-start(bf16[512,256]{1,0:T(8,128)(2,1)S(1)} %collective-permute-done.8.refs_5_.refs_3_), channel_id=1, source_target_pairs={{0,1},{1,0},{2,3},{3,2},{4,5},{5,4},{6,7},{7,6},{8,9},{9,8},{10,11... | collective-permute-start | bytes 786440 | tf_op jit(solution)/shard_map/ppermute | solution.py:370
  86.8 0.0 collective-permute-start.13
  86.8 0.0 collective-permute-done.10.refs_7_.refs_5_
  86.8 0.0 collective-permute-done.11.refs_8_.refs_6_
  86.8 1.1 collective-permute-done.12.refs_9_.refs_7_
  88.0 0.4 collective-permute-done.13.refs_10_.refs_8_
  88.3 1.6 %shard_map.119 = bf16[256,256]{1,0:T(8,128)(2,1)} custom-call(s32[1]{0:T(128)} %bitcast.5.refs_0_, bf16[8,16,256]{2,1,0:T(8,128)(2,1)S(1)} %get-tuple-element.31.refs_1_, bf16[512,256]{1,0:T(8,128)(2,1)S(1)} %collective-permute-done.7.refs_4_.refs_2_, bf16[512,256]{1,0:T(8,128)(2,1)S(1)} %collective-permute-done.8.refs_5_.refs_3_, ...), custom_call_target="tpu_custom_call" | custom-call | flops 268435456 | bytes 2162692 | tf_op jit(solution)/shard_map/pallas_call | solution.py:100
  89.9 4.8 %all-to-all-done.4 = bf16[32,64,256]{2,1,0:T(8,128)(2,1)S(1)} async-done(((bf16[32,64,256]{2,1,0:T(8,128)(2,1)}), bf16[32,64,256]{2,1,0:T(8,128)(2,1)S(1)}, u32[]{:S(2)}, u32[]{:S(2)}) %all-to-all-start.4) | async-done | bytes 1048608 | tf_op jit(solution)/shard_map/all_to_all | solution.py:366
  94.7 8.1 %all-to-all-start.2 = ((bf16[32,8,256]{2,1,0:T(8,128)(2,1)}), bf16[32,8,256]{2,1,0:T(8,128)(2,1)S(1)}, u32[]{:S(2)}, u32[]{:S(2)}) async-start(bf16[32,8,256]{2,1,0:T(8,128)(2,1)} %bitcast.19), calls=%async_computation.2 | async-start | bytes 262144 | tf_op jit(solution)/shard_map/all_to_all | solution.py:366
  102.8 2.7 %shard_map.123 = bf16[4,256,256]{2,1,0:T(8,128)(2,1)} custom-call(s32[1]{0:T(128)} %bitcast.5.refs_0_, s32[32,8,128]{2,1,0:T(8,128)S(1)} %copy-done.2, bf16[2048,256]{1,0:T(8,128)(2,1)S(1)} %bitcast.11), custom_call_target="tpu_custom_call" | custom-call | flops 1073741824 | bytes 1179652 | tf_op jit(solution)/shard_map/pallas_call | solution.py:100
  105.5 2.1 %collective-permute-start.21 = (bf16[4,256,256]{2,1,0:T(8,128)(2,1)}, bf16[4,256,256]{2,1,0:T(8,128)(2,1)}, u32[]{:S(2)}, u32[]{:S(2)}) collective-permute-start(bf16[4,256,256]{2,1,0:T(8,128)(2,1)} %shard_map.123), channel_id=1, source_target_pairs={{0,1},{1,0},{2,3},{3,2},{4,5},{5,4},{6,7},{7,6},{8,9},{9,8},{10,11... | collective-permute-start | bytes 1572872 | tf_op jit(solution)/shard_map/ppermute | solution.py:370
  107.5 4.4 %all-to-all-done.2.refs_0_ = bf16[32,8,256]{2,1,0:T(8,128)(2,1)S(1)} async-done(((bf16[32,8,256]{2,1,0:T(8,128)(2,1)}), bf16[32,8,256]{2,1,0:T(8,128)(2,1)S(1)}, u32[]{:S(2)}, u32[]{:S(2)}) %all-to-all-start.2) | async-done | bytes 131104 | tf_op jit(solution)/shard_map/all_to_all | solution.py:366
  111.9 0.7 shard_map.120
  112.7 14.2 %all_to_all.25 = bf16[32,8,256]{2,1,0:T(8,128)(2,1)S(1)} all-to-all(bf16[32,8,256]{2,1,0:T(8,128)(2,1)} %shard_map.120), channel_id=1, replica_groups=mesh['shard'=32,'blk'=8] {'shard'}, dimensions={0} | all-to-all | bytes 262144 | tf_op jit(solution)/shard_map/all_to_all | solution.py:366
  126.9 1.2 collective-permute-start.14
  128.1 2.4 %collective-permute-start.15 = (bf16[256,256]{1,0:T(8,128)(2,1)S(1)}, bf16[256,256]{1,0:T(8,128)(2,1)S(1)}, u32[]{:S(2)}, u32[]{:S(2)}) collective-permute-start(bf16[256,256]{1,0:T(8,128)(2,1)S(1)} %bitcast.14), channel_id=1, source_target_pairs={{0,4},{1,5},{2,6},{3,7},{4,0},{5,1},{6,2},{7,3},{8,12},{9,13},{10,... | collective-permute-start | bytes 393224 | tf_op jit(solution)/shard_map/ppermute | solution.py:374
  130.6 1.2 collective-permute-start.16
  131.7 4.1 %collective-permute-start.17 = (bf16[256,256]{1,0:T(8,128)(2,1)S(1)}, bf16[256,256]{1,0:T(8,128)(2,1)S(1)}, u32[]{:S(2)}, u32[]{:S(2)}) collective-permute-start(bf16[256,256]{1,0:T(8,128)(2,1)S(1)} %bitcast.16), channel_id=1, source_target_pairs={{0,1},{1,0},{2,3},{3,2},{4,5},{5,4},{6,7},{7,6},{8,9},{9,8},{10,11... | collective-permute-start | bytes 393224 | tf_op jit(solution)/shard_map/ppermute | solution.py:370
  135.8 0.6 collective-permute-start.18
  136.4 0.0 collective-permute-done.15.refs_3_
  136.4 2.3 %collective-permute-start.19 = (bf16[256,256]{1,0:T(8,128)(2,1)S(1)}, bf16[256,256]{1,0:T(8,128)(2,1)S(1)}, u32[]{:S(2)}, u32[]{:S(2)}) collective-permute-start(bf16[256,256]{1,0:T(8,128)(2,1)S(1)} %collective-permute-done.15.refs_3_), channel_id=1, source_target_pairs={{0,1},{1,0},{2,3},{3,2},{4,5},{5,4},{6,7},{7,6},{8,9},{9,8},{10,11... | collective-permute-start | bytes 393224 | tf_op jit(solution)/shard_map/ppermute | solution.py:370
  138.7 0.6 collective-permute-start.20
  139.4 1.9 %shard_map.122.refs_0_ = f32[4,256,256]{2,1,0:T(8,128)S(1)} custom-call(s32[1]{0:T(128)} %bitcast.5.refs_0_, s32[32,8,128]{2,1,0:T(8,128)S(1)} %copy-done.2, bf16[2048,256]{1,0:T(8,128)(2,1)S(1)} %bitcast.12), custom_call_target="tpu_custom_call" | custom-call | flops 1073741824 | bytes 1179652 | tf_op jit(solution)/shard_map/pallas_call | solution.py:100
  141.2 1.1 shard_map.124
  142.4 1.1 collective-permute-start.22
  143.4 2.6 %collective-permute-start.23 = (bf16[256,256]{1,0:T(8,128)(2,1)S(1)}, bf16[256,256]{1,0:T(8,128)(2,1)S(1)}, u32[]{:S(2)}, u32[]{:S(2)}) collective-permute-start(bf16[256,256]{1,0:T(8,128)(2,1)S(1)} %get-tuple-element.35), channel_id=1, source_target_pairs={{0,4},{1,5},{2,6},{3,7},{4,0},{5,1},{6,2},{7,3},{8,12},{9,13},{10,... | collective-permute-start | bytes 393224 | tf_op jit(solution)/shard_map/ppermute | solution.py:374
  146.0 0.6 collective-permute-start.24
  146.6 2.6 %shard_map.118 = f32[256,256]{1,0:T(8,128)} custom-call(f32[1]{0:T(128)S(6)} %copy.12.refs_0_, f32[1]{0:T(128)S(6)} %copy.13.refs_1_, bf16[256,256]{1,0:T(8,128)(2,1)} %refs_2_, bf16[512,256]{1,0:T(8,128)(2,1)S(1)} %get-tuple-element.30.refs_3_.refs_9_, bf16[512,256]{1,0:T(8,128)(2,1)S(1)} %collective-permute-done.7.refs_4_.refs_2_, ...), custom_call_target="tpu_custom_call" | custom-call | flops 536870912 | bytes 2228232 | tf_op jit(solution)/shard_map/pallas_call | solution.py:100
  149.2 1.4 shard_map.121
  150.6 1.8 %collective-permute-done.23.refs_2_ = bf16[256,256]{1,0:T(8,128)(2,1)S(1)} collective-permute-done((bf16[256,256]{1,0:T(8,128)(2,1)S(1)}, bf16[256,256]{1,0:T(8,128)(2,1)S(1)}, u32[]{:S(2)}, u32[]{:S(2)}) %collective-permute-start.23) | collective-permute-done | bytes 131104 | tf_op jit(solution)/shard_map/ppermute | solution.py:374
  152.4 0.8 shard_map.125
  (17 shorter events, 0.0 us)
Async XLA Ops:
  2.6 21.2 %all-to-all-start = ((s32[32,8,128]{2,1,0:T(8,128)}), s32[32,8,128]{2,1,0:T(8,128)S(1)}, u32[]{:S(2)}, u32[]{:S(2)}) async-start(s32[32,8,128]{2,1,0:T(8,128)} %get-tuple-element.20), calls=%async_computation | async-start | bytes 262144 | tf_op jit(solution)/shard_map/all_to_all | solution.py:366
  23.8 4.9 %copy-start.1 = (s32[32,8,128]{2,1,0:T(8,128)}, s32[32,8,128]{2,1,0:T(8,128)S(1)}, u32[]{:S(2)}) copy-start(s32[32,8,128]{2,1,0:T(8,128)S(1)} %all-to-all-done.refs_0_.refs_1_) | copy-start | bytes 393220
  28.7 28.5 %all-to-all-start.1 = ((bf16[32,64,256]{2,1,0:T(8,128)(2,1)}), bf16[32,64,256]{2,1,0:T(8,128)(2,1)S(1)}, u32[]{:S(2)}, u32[]{:S(2)}) async-start(bf16[32,64,256]{2,1,0:T(8,128)(2,1)} %shard_map.114), calls=%async_computation.1 | async-start | bytes 2097152 | tf_op jit(solution)/shard_map/all_to_all | solution.py:366
  33.8 23.4 %copy-start = (bf16[272,256]{1,0:T(8,128)(2,1)}, bf16[272,256]{1,0:T(8,128)(2,1)S(1)}, u32[]{:S(2)}) copy-start(bf16[272,256]{1,0:T(8,128)(2,1)S(1)} %shard_map.116.refs_12_) | copy-start | bytes 417796
  33.8 7.8 %collective-permute-start = (bf16[272,256]{1,0:T(8,128)(2,1)S(1)}, bf16[272,256]{1,0:T(8,128)(2,1)S(1)}, u32[]{:S(2)}, u32[]{:S(2)}) collective-permute-start(bf16[272,256]{1,0:T(8,128)(2,1)S(1)} %shard_map.116.refs_12_), channel_id=1, source_target_pairs={{0,2},{1,3},{2,4},{3,5},{4,6},{5,7},{6,0},{7,1},{8,10},{9,11},{10,... | collective-permute-start | bytes 417800 | tf_op jit(solution)/shard_map/ppermute | solution.py:374
  35.1 8.6 %collective-permute-start.1 = (bf16[272,256]{1,0:T(8,128)(2,1)S(1)}, bf16[272,256]{1,0:T(8,128)(2,1)S(1)}, u32[]{:S(2)}, u32[]{:S(2)}) collective-permute-start(bf16[272,256]{1,0:T(8,128)(2,1)S(1)} %shard_map.116.refs_12_), channel_id=1, source_target_pairs={{0,4},{1,5},{2,6},{3,7},{4,0},{5,1},{6,2},{7,3},{8,12},{9,13},{10,... | collective-permute-start | bytes 417800 | tf_op jit(solution)/shard_map/ppermute | solution.py:374
  37.5 7.6 %collective-permute-start.2 = (bf16[272,256]{1,0:T(8,128)(2,1)S(1)}, bf16[272,256]{1,0:T(8,128)(2,1)S(1)}, u32[]{:S(2)}, u32[]{:S(2)}) collective-permute-start(bf16[272,256]{1,0:T(8,128)(2,1)S(1)} %shard_map.116.refs_12_), channel_id=1, source_target_pairs={{0,6},{1,7},{2,0},{3,1},{4,2},{5,3},{6,4},{7,5},{8,14},{9,15},{10,... | collective-permute-start | bytes 417800 | tf_op jit(solution)/shard_map/ppermute | solution.py:374
  38.7 13.3 %collective-permute-start.3 = (bf16[272,256]{1,0:T(8,128)(2,1)S(1)}, bf16[272,256]{1,0:T(8,128)(2,1)S(1)}, u32[]{:S(2)}, u32[]{:S(2)}) collective-permute-start(bf16[272,256]{1,0:T(8,128)(2,1)S(1)} %shard_map.116.refs_12_), channel_id=1, source_target_pairs={{0,1},{1,0},{2,3},{3,2},{4,5},{5,4},{6,7},{7,6},{8,9},{9,8},{10,11... | collective-permute-start | bytes 417800 | tf_op jit(solution)/shard_map/ppermute | solution.py:370
  41.6 10.3 %collective-permute-start.4 = (bf16[272,256]{1,0:T(8,128)(2,1)S(1)}, bf16[272,256]{1,0:T(8,128)(2,1)S(1)}, u32[]{:S(2)}, u32[]{:S(2)}) collective-permute-start(bf16[272,256]{1,0:T(8,128)(2,1)S(1)} %collective-permute-done.refs_5_), channel_id=1, source_target_pairs={{0,1},{1,0},{2,3},{3,2},{4,5},{5,4},{6,7},{7,6},{8,9},{9,8},{10,11... | collective-permute-start | bytes 417800 | tf_op jit(solution)/shard_map/ppermute | solution.py:370
  43.6 8.3 %collective-permute-start.5 = (bf16[272,256]{1,0:T(8,128)(2,1)S(1)}, bf16[272,256]{1,0:T(8,128)(2,1)S(1)}, u32[]{:S(2)}, u32[]{:S(2)}) collective-permute-start(bf16[272,256]{1,0:T(8,128)(2,1)S(1)} %collective-permute-done.1.refs_6_), channel_id=1, source_target_pairs={{0,1},{1,0},{2,3},{3,2},{4,5},{5,4},{6,7},{7,6},{8,9},{9,8},{10,11... | collective-permute-start | bytes 417800 | tf_op jit(solution)/shard_map/ppermute | solution.py:370
  45.1 7.5 %collective-permute-start.6 = (bf16[272,256]{1,0:T(8,128)(2,1)S(1)}, bf16[272,256]{1,0:T(8,128)(2,1)}, u32[]{:S(2)}, u32[]{:S(2)}) collective-permute-start(bf16[272,256]{1,0:T(8,128)(2,1)S(1)} %collective-permute-done.2.refs_7_), channel_id=1, source_target_pairs={{0,1},{1,0},{2,3},{3,2},{4,5},{5,4},{6,7},{7,6},{8,9},{9,8},{10,11... | collective-permute-start | bytes 417800 | tf_op jit(solution)/shard_map/ppermute | solution.py:370
  52.0 0.7 copy-start.3
  61.9 40.9 %copy-start.2 = (s32[32,8,128]{2,1,0:T(8,128)S(1)}, s32[32,8,128]{2,1,0:T(8,128)}, u32[]{:S(2)}) copy-start(s32[32,8,128]{2,1,0:T(8,128)} %copy-done.1) | copy-start | bytes 393220
  61.9 32.8 %all-to-all-start.4 = ((bf16[32,64,256]{2,1,0:T(8,128)(2,1)}), bf16[32,64,256]{2,1,0:T(8,128)(2,1)S(1)}, u32[]{:S(2)}, u32[]{:S(2)}) async-start(bf16[32,64,256]{2,1,0:T(8,128)(2,1)} %bitcast.18), calls=%async_computation.4 | async-start | bytes 2097152 | tf_op jit(solution)/shard_map/all_to_all | solution.py:366
  70.2 7.8 %collective-permute-start.7 = (bf16[512,256]{1,0:T(8,128)(2,1)S(1)}, bf16[512,256]{1,0:T(8,128)(2,1)S(1)}, u32[]{:S(2)}, u32[]{:S(2)}) collective-permute-start(bf16[512,256]{1,0:T(8,128)(2,1)S(1)} %get-tuple-element.30.refs_3_.refs_9_), channel_id=1, source_target_pairs={{0,2},{1,3},{2,4},{3,5},{4,6},{5,7},{6,0},{7,1},{8,10},{9,11},{10,... | collective-permute-start | bytes 786440 | tf_op jit(solution)/shard_map/ppermute | solution.py:374
  71.5 12.4 %collective-permute-start.8 = (bf16[512,256]{1,0:T(8,128)(2,1)S(1)}, bf16[512,256]{1,0:T(8,128)(2,1)S(1)}, u32[]{:S(2)}, u32[]{:S(2)}) collective-permute-start(bf16[512,256]{1,0:T(8,128)(2,1)S(1)} %get-tuple-element.30.refs_3_.refs_9_), channel_id=1, source_target_pairs={{0,4},{1,5},{2,6},{3,7},{4,0},{5,1},{6,2},{7,3},{8,12},{9,13},{10,... | collective-permute-start | bytes 786440 | tf_op jit(solution)/shard_map/ppermute | solution.py:374
  73.9 12.9 %collective-permute-start.9 = (bf16[512,256]{1,0:T(8,128)(2,1)S(1)}, bf16[512,256]{1,0:T(8,128)(2,1)S(1)}, u32[]{:S(2)}, u32[]{:S(2)}) collective-permute-start(bf16[512,256]{1,0:T(8,128)(2,1)S(1)} %get-tuple-element.30.refs_3_.refs_9_), channel_id=1, source_target_pairs={{0,6},{1,7},{2,0},{3,1},{4,2},{5,3},{6,4},{7,5},{8,14},{9,15},{10,... | collective-permute-start | bytes 786440 | tf_op jit(solution)/shard_map/ppermute | solution.py:374
  75.1 11.7 %collective-permute-start.10 = (bf16[512,256]{1,0:T(8,128)(2,1)S(1)}, bf16[512,256]{1,0:T(8,128)(2,1)S(1)}, u32[]{:S(2)}, u32[]{:S(2)}) collective-permute-start(bf16[512,256]{1,0:T(8,128)(2,1)S(1)} %get-tuple-element.30.refs_3_.refs_9_), channel_id=1, source_target_pairs={{0,1},{1,0},{2,3},{3,2},{4,5},{5,4},{6,7},{7,6},{8,9},{9,8},{10,11... | collective-permute-start | bytes 786440 | tf_op jit(solution)/shard_map/ppermute | solution.py:370
  78.0 8.8 %collective-permute-start.11 = (bf16[512,256]{1,0:T(8,128)(2,1)S(1)}, bf16[512,256]{1,0:T(8,128)(2,1)S(1)}, u32[]{:S(2)}, u32[]{:S(2)}) collective-permute-start(bf16[512,256]{1,0:T(8,128)(2,1)S(1)} %collective-permute-done.7.refs_4_.refs_2_), channel_id=1, source_target_pairs={{0,1},{1,0},{2,3},{3,2},{4,5},{5,4},{6,7},{7,6},{8,9},{9,8},{10,11... | collective-permute-start | bytes 786440 | tf_op jit(solution)/shard_map/ppermute | solution.py:370
  83.9 4.1 %collective-permute-start.12 = (bf16[512,256]{1,0:T(8,128)(2,1)S(1)}, bf16[512,256]{1,0:T(8,128)(2,1)S(1)}, u32[]{:S(2)}, u32[]{:S(2)}) collective-permute-start(bf16[512,256]{1,0:T(8,128)(2,1)S(1)} %collective-permute-done.8.refs_5_.refs_3_), channel_id=1, source_target_pairs={{0,1},{1,0},{2,3},{3,2},{4,5},{5,4},{6,7},{7,6},{8,9},{9,8},{10,11... | collective-permute-start | bytes 786440 | tf_op jit(solution)/shard_map/ppermute | solution.py:370
  86.8 1.5 %collective-permute-start.13 = (bf16[512,256]{1,0:T(8,128)(2,1)S(1)}, bf16[512,256]{1,0:T(8,128)(2,1)S(1)}, u32[]{:S(2)}, u32[]{:S(2)}) collective-permute-start(bf16[512,256]{1,0:T(8,128)(2,1)S(1)} %collective-permute-done.9.refs_6_.refs_4_), channel_id=1, source_target_pairs={{0,1},{1,0},{2,3},{3,2},{4,5},{5,4},{6,7},{7,6},{8,9},{9,8},{10,11... | collective-permute-start | bytes 786440 | tf_op jit(solution)/shard_map/ppermute | solution.py:370
  94.7 17.2 %all-to-all-start.2 = ((bf16[32,8,256]{2,1,0:T(8,128)(2,1)}), bf16[32,8,256]{2,1,0:T(8,128)(2,1)S(1)}, u32[]{:S(2)}, u32[]{:S(2)}) async-start(bf16[32,8,256]{2,1,0:T(8,128)(2,1)} %bitcast.19), calls=%async_computation.2 | async-start | bytes 262144 | tf_op jit(solution)/shard_map/all_to_all | solution.py:366
  105.5 35.8 %collective-permute-start.21 = (bf16[4,256,256]{2,1,0:T(8,128)(2,1)}, bf16[4,256,256]{2,1,0:T(8,128)(2,1)}, u32[]{:S(2)}, u32[]{:S(2)}) collective-permute-start(bf16[4,256,256]{2,1,0:T(8,128)(2,1)} %shard_map.123), channel_id=1, source_target_pairs={{0,1},{1,0},{2,3},{3,2},{4,5},{5,4},{6,7},{7,6},{8,9},{9,8},{10,11... | collective-permute-start | bytes 1572872 | tf_op jit(solution)/shard_map/ppermute | solution.py:370
  126.9 8.9 %collective-permute-start.14 = (bf16[256,256]{1,0:T(8,128)(2,1)S(1)}, bf16[256,256]{1,0:T(8,128)(2,1)S(1)}, u32[]{:S(2)}, u32[]{:S(2)}) collective-permute-start(bf16[256,256]{1,0:T(8,128)(2,1)S(1)} %bitcast.13), channel_id=1, source_target_pairs={{0,2},{1,3},{2,4},{3,5},{4,6},{5,7},{6,0},{7,1},{8,10},{9,11},{10,... | collective-permute-start | bytes 393224 | tf_op jit(solution)/shard_map/ppermute | solution.py:374
  128.1 8.3 %collective-permute-start.15 = (bf16[256,256]{1,0:T(8,128)(2,1)S(1)}, bf16[256,256]{1,0:T(8,128)(2,1)S(1)}, u32[]{:S(2)}, u32[]{:S(2)}) collective-permute-start(bf16[256,256]{1,0:T(8,128)(2,1)S(1)} %bitcast.14), channel_id=1, source_target_pairs={{0,4},{1,5},{2,6},{3,7},{4,0},{5,1},{6,2},{7,3},{8,12},{9,13},{10,... | collective-permute-start | bytes 393224 | tf_op jit(solution)/shard_map/ppermute | solution.py:374
  130.6 8.2 %collective-permute-start.16 = (bf16[256,256]{1,0:T(8,128)(2,1)S(1)}, bf16[256,256]{1,0:T(8,128)(2,1)S(1)}, u32[]{:S(2)}, u32[]{:S(2)}) collective-permute-start(bf16[256,256]{1,0:T(8,128)(2,1)S(1)} %bitcast.15), channel_id=1, source_target_pairs={{0,6},{1,7},{2,0},{3,1},{4,2},{5,3},{6,4},{7,5},{8,14},{9,15},{10,... | collective-permute-start | bytes 393224 | tf_op jit(solution)/shard_map/ppermute | solution.py:374
  131.7 11.7 %collective-permute-start.17 = (bf16[256,256]{1,0:T(8,128)(2,1)S(1)}, bf16[256,256]{1,0:T(8,128)(2,1)S(1)}, u32[]{:S(2)}, u32[]{:S(2)}) collective-permute-start(bf16[256,256]{1,0:T(8,128)(2,1)S(1)} %bitcast.16), channel_id=1, source_target_pairs={{0,1},{1,0},{2,3},{3,2},{4,5},{5,4},{6,7},{7,6},{8,9},{9,8},{10,11... | collective-permute-start | bytes 393224 | tf_op jit(solution)/shard_map/ppermute | solution.py:370
  135.8 10.2 %collective-permute-start.18 = (bf16[256,256]{1,0:T(8,128)(2,1)S(1)}, bf16[256,256]{1,0:T(8,128)(2,1)S(1)}, u32[]{:S(2)}, u32[]{:S(2)}) collective-permute-start(bf16[256,256]{1,0:T(8,128)(2,1)S(1)} %collective-permute-done.14.refs_2_), channel_id=1, source_target_pairs={{0,1},{1,0},{2,3},{3,2},{4,5},{5,4},{6,7},{7,6},{8,9},{9,8},{10,11... | collective-permute-start | bytes 393224 | tf_op jit(solution)/shard_map/ppermute | solution.py:370
  136.4 12.7 %collective-permute-start.19 = (bf16[256,256]{1,0:T(8,128)(2,1)S(1)}, bf16[256,256]{1,0:T(8,128)(2,1)S(1)}, u32[]{:S(2)}, u32[]{:S(2)}) collective-permute-start(bf16[256,256]{1,0:T(8,128)(2,1)S(1)} %collective-permute-done.15.refs_3_), channel_id=1, source_target_pairs={{0,1},{1,0},{2,3},{3,2},{4,5},{5,4},{6,7},{7,6},{8,9},{9,8},{10,11... | collective-permute-start | bytes 393224 | tf_op jit(solution)/shard_map/ppermute | solution.py:370
  138.7 10.4 %collective-permute-start.20 = (bf16[256,256]{1,0:T(8,128)(2,1)S(1)}, bf16[256,256]{1,0:T(8,128)(2,1)S(1)}, u32[]{:S(2)}, u32[]{:S(2)}) collective-permute-start(bf16[256,256]{1,0:T(8,128)(2,1)S(1)} %collective-permute-done.16.refs_4_), channel_id=1, source_target_pairs={{0,1},{1,0},{2,3},{3,2},{4,5},{5,4},{6,7},{7,6},{8,9},{9,8},{10,11... | collective-permute-start | bytes 393224 | tf_op jit(solution)/shard_map/ppermute | solution.py:370
  142.4 8.2 %collective-permute-start.22 = (bf16[256,256]{1,0:T(8,128)(2,1)S(1)}, bf16[256,256]{1,0:T(8,128)(2,1)S(1)}, u32[]{:S(2)}, u32[]{:S(2)}) collective-permute-start(bf16[256,256]{1,0:T(8,128)(2,1)S(1)} %get-tuple-element.34), channel_id=1, source_target_pairs={{0,2},{1,3},{2,4},{3,5},{4,6},{5,7},{6,0},{7,1},{8,10},{9,11},{10,... | collective-permute-start | bytes 393224 | tf_op jit(solution)/shard_map/ppermute | solution.py:374
  143.4 8.9 %collective-permute-start.23 = (bf16[256,256]{1,0:T(8,128)(2,1)S(1)}, bf16[256,256]{1,0:T(8,128)(2,1)S(1)}, u32[]{:S(2)}, u32[]{:S(2)}) collective-permute-start(bf16[256,256]{1,0:T(8,128)(2,1)S(1)} %get-tuple-element.35), channel_id=1, source_target_pairs={{0,4},{1,5},{2,6},{3,7},{4,0},{5,1},{6,2},{7,3},{8,12},{9,13},{10,... | collective-permute-start | bytes 393224 | tf_op jit(solution)/shard_map/ppermute | solution.py:374
  146.0 6.4 %collective-permute-start.24 = (bf16[256,256]{1,0:T(8,128)(2,1)S(1)}, bf16[256,256]{1,0:T(8,128)(2,1)S(1)}, u32[]{:S(2)}, u32[]{:S(2)}) collective-permute-start(bf16[256,256]{1,0:T(8,128)(2,1)S(1)} %get-tuple-element.36), channel_id=1, source_target_pairs={{0,6},{1,7},{2,0},{3,1},{4,2},{5,3},{6,4},{7,5},{8,14},{9,15},{10,... | collective-permute-start | bytes 393224 | tf_op jit(solution)/shard_map/ppermute | solution.py:374

commit v8 on v7

--- a/solution.py
+++ b/solution.py
@@ -214,12 +214,10 @@
     rows = table_ref.shape[0]
     owners, cap, _ = out.stage.shape
     group = out.width
-    diagonal = iota((cap, cap), 0) == iota((cap, cap), 1)
+    asks = [ask_ref[o, 0:1, :].astype(F32) for o in range(owners)]
+    asks = jnp.concatenate(asks + [jnp.zeros((LANES - owners, LANES), F32)], axis=0).T.astype(jnp.int32)
     for o in range(owners):
-        ask = ask_ref[o, 0:1, 0:cap].astype(F32)
-        column_ref[o * cap : (o + 1) * cap, :] = jnp.sum(
-            jnp.where(diagonal, ask, 0.0), axis=1, keepdims=True
-        ).astype(jnp.int32)
+        column_ref[o * cap : (o + 1) * cap, :] = asks[0:cap, o : o + 1]
     size = group * cap
     lane = iota((size, rows), 1).astype(jnp.int16)
 
@@ -376,7 +374,9 @@
 
 def gather_blocks(array, blocks):
     first = cross(array, blocks)
-    mine = [shift(array, blocks, d) for d in range(1, blocks // 2)]
+    mine = []
+    for d in range(1, blocks // 2):
+        mine.append(shift(array, blocks, d))
     return [array] + mine + [first] + [cross(m, blocks) for m in mine]
 
 
@@ -407,7 +407,7 @@
         [HBM((owners, cap, width), BF16)],
         asked, table_low,
         scratch=[pltpu.VMEM((total, 1), jnp.int32)],
-        steps=steps,
+        steps=4,
         flops=2 * total * rows * width,
     )
     looked, queries, rank, rank_t = lax.optimization_barrier((looked, queries, rank, rank_t))

time: 154 us -> 153 us (level)
  no operation moved by 1% of the time
where the time goes in v8:
time: 153 us
  starting transfers between devices  76.9 us (50%)
  Pallas kernels  31.8 us (21%)
  waiting for transfers between devices  26.7 us (17%)
  blocking collectives  14.2 us (9%)
  between operations  2.34 us (2%)
    all_to_all x4, starting transfers between devices, swap(): return lax.all_to_all(array, axis, split_axis=0, concat_axis=0, tiled=True)  32.3 us
    pallas_call x14, Pallas kernels, call(): pl.pallas_call(run, out_shape=list(outs), in_specs=[pl.BlockSpec(memory_s...  31.8 us
    ppermute x13, starting transfers between devices, cross(): return lax.ppermute(array, 'blk', [(i, i ^ 1) for i in range(blocks)])  25.8 us
    all_to_all x4, waiting for transfers between devices, swap(): return lax.all_to_all(array, axis, split_axis=0, concat_axis=0, tiled=True)  21.2 us
    ppermute x12, starting transfers between devices, shift(): lax.ppermute(array, 'blk', [(i, (i + 2 * d) % blocks) for i in range(bloc...  18.8 us
    all_to_all x1, blocking collectives, swap(): return lax.all_to_all(array, axis, split_axis=0, concat_axis=0, tiled=True)  14.2 us
    ppermute x12, waiting for transfers between devices, shift(): lax.ppermute(array, 'blk', [(i, (i + 2 * d) % blocks) for i in range(bloc...  4 us
  transfers between devices with their start and end apart: 29, of which 8 were waited for; matrix products, arithmetic and copies ran while one was open for 0% of the time, Pallas kernels for 13%

profile of v8, /device:TPU:1, one launch (start us, length us, event | category | flops | bytes accessed | tf_op | source)
XLA Modules:
  0.0 152.6 jit_solution(5738804740724187485)
XLA Ops:
  0.6 1.9 %shard_map.112 = (bf16[256,128]{1,0:T(8,128)(2,1)S(1)}, bf16[128,256]{1,0:T(8,128)(2,1)S(1)}, s32[32,8,128]{2,1,0:T(8,128)}) custom-call(s32[4,256]{1,0:T(4,128)} %bitcast.22, s32[4,256]{1,0:T(4,128)} %bitcast.23, s32[1,256]{1,0:T(1,128)} %bitcast.24), custom_call_target="tpu_custom_call" | custom-call | flops 16777216 | bytes 9216 | tf_op jit(solution)/shard_map/pallas_call | solution.py:100
  2.6 12.0 %all-to-all-start = ((s32[32,8,128]{2,1,0:T(8,128)}), s32[32,8,128]{2,1,0:T(8,128)S(1)}, u32[]{:S(2)}, u32[]{:S(2)}) async-start(s32[32,8,128]{2,1,0:T(8,128)} %get-tuple-element.20), calls=%async_computation | async-start | bytes 262144 | tf_op jit(solution)/shard_map/all_to_all | solution.py:364
  14.6 1.7 %shard_map.113.refs_1_ = bf16[2048,256]{1,0:T(8,128)(2,1)S(1)} custom-call(f32[2048,256]{1,0:T(8,128)} %refs_0_.3), custom_call_target="tpu_custom_call" | custom-call | bytes 2097152 | tf_op jit(solution)/shard_map/pallas_call | solution.py:100
  16.3 7.4 %all-to-all-done.refs_0_.refs_1_ = s32[32,8,128]{2,1,0:T(8,128)S(1)} async-done(((s32[32,8,128]{2,1,0:T(8,128)}), s32[32,8,128]{2,1,0:T(8,128)S(1)}, u32[]{:S(2)}, u32[]{:S(2)}) %all-to-all-start) | async-done | bytes 131104 | tf_op jit(solution)/shard_map/all_to_all | solution.py:364
  23.8 4.2 %shard_map.114 = bf16[32,64,256]{2,1,0:T(8,128)(2,1)} custom-call(s32[32,8,128]{2,1,0:T(8,128)S(1)} %all-to-all-done.refs_0_.refs_1_, bf16[2048,256]{1,0:T(8,128)(2,1)S(1)} %shard_map.113.refs_1_), custom_call_target="tpu_custom_call" | custom-call | flops 2147483648 | bytes 1179648 | tf_op jit(solution)/shard_map/pallas_call | solution.py:100
  28.0 3.9 %all-to-all-start.1 = ((bf16[32,64,256]{2,1,0:T(8,128)(2,1)}), bf16[32,64,256]{2,1,0:T(8,128)(2,1)S(1)}, u32[]{:S(2)}, u32[]{:S(2)}) async-start(bf16[32,64,256]{2,1,0:T(8,128)(2,1)} %shard_map.114), calls=%async_computation.1 | async-start | bytes 2097152 | tf_op jit(solution)/shard_map/all_to_all | solution.py:364
  31.9 1.1 shard_map.116.refs_12_
  33.0 0.0 copy-start
  33.0 1.3 collective-permute-start
  34.3 2.4 %collective-permute-start.1 = (bf16[272,256]{1,0:T(8,128)(2,1)S(1)}, bf16[272,256]{1,0:T(8,128)(2,1)S(1)}, u32[]{:S(2)}, u32[]{:S(2)}) collective-permute-start(bf16[272,256]{1,0:T(8,128)(2,1)S(1)} %shard_map.116.refs_12_), channel_id=1, source_target_pairs={{0,4},{1,5},{2,6},{3,7},{4,0},{5,1},{6,2},{7,3},{8,12},{9,13},{10,... | collective-permute-start | bytes 417800 | tf_op jit(solution)/shard_map/ppermute | solution.py:372
  36.8 1.1 collective-permute-start.2
  37.9 2.9 %collective-permute-start.3 = (bf16[272,256]{1,0:T(8,128)(2,1)S(1)}, bf16[272,256]{1,0:T(8,128)(2,1)S(1)}, u32[]{:S(2)}, u32[]{:S(2)}) collective-permute-start(bf16[272,256]{1,0:T(8,128)(2,1)S(1)} %shard_map.116.refs_12_), channel_id=1, source_target_pairs={{0,1},{1,0},{2,3},{3,2},{4,5},{5,4},{6,7},{7,6},{8,9},{9,8},{10,11... | collective-permute-start | bytes 417800 | tf_op jit(solution)/shard_map/ppermute | solution.py:368
  40.9 2.0 %collective-permute-start.4 = (bf16[272,256]{1,0:T(8,128)(2,1)S(1)}, bf16[272,256]{1,0:T(8,128)(2,1)S(1)}, u32[]{:S(2)}, u32[]{:S(2)}) collective-permute-start(bf16[272,256]{1,0:T(8,128)(2,1)S(1)} %collective-permute-done.refs_5_), channel_id=1, source_target_pairs={{0,1},{1,0},{2,3},{3,2},{4,5},{5,4},{6,7},{7,6},{8,9},{9,8},{10,11... | collective-permute-start | bytes 417800 | tf_op jit(solution)/shard_map/ppermute | solution.py:368
  42.9 1.5 collective-permute-start.5
  44.4 0.0 collective-permute-done.2.refs_7_
  44.4 0.1 collective-permute-start.6
  45.8 5.4 %shard_map.115 = (bf16[256,2048]{1,0:T(8,128)(2,1)S(1)}, bf16[2048,256]{1,0:T(8,128)(2,1)}, f32[256,256]{1,0:T(8,128)S(1)}) custom-call(bf16[256,128]{1,0:T(8,128)(2,1)S(1)} %get-tuple-element.25.refs_0_, bf16[128,256]{1,0:T(8,128)(2,1)S(1)} %get-tuple-element.26.refs_1_, s32[4,256]{1,0:T(4,128)} %bitcast.21, bf16[2048,256]{1,0:T(8,128)(2,1)} %refs_3_.1), custom_call_target="tpu_custom_call" | custom-call | flops 536870912 | bytes 1183744 | tf_op jit(solution)/shard_map/pallas_call | solution.py:100
  51.2 0.0 collective-permute-done.3.refs_8_
  51.2 0.0 collective-permute-done.5.refs_10_
  51.2 0.0 copy-start.3
  51.2 0.6 copy-done.3
  51.9 0.0 collective-permute-done.6.refs_11_
  51.9 4.5 %all-to-all-done.1 = bf16[32,64,256]{2,1,0:T(8,128)(2,1)S(1)} async-done(((bf16[32,64,256]{2,1,0:T(8,128)(2,1)}), bf16[32,64,256]{2,1,0:T(8,128)(2,1)S(1)}, u32[]{:S(2)}, u32[]{:S(2)}) %all-to-all-start.1) | async-done | bytes 1048608 | tf_op jit(solution)/shard_map/all_to_all | solution.py:364
  56.4 4.7 %shard_map.117 = (bf16[512,256]{1,0:T(8,128)(2,1)S(1)}, bf16[8,16,256]{2,1,0:T(8,128)(2,1)S(1)}, bf16[2048,256]{1,0:T(8,128)(2,1)}) custom-call(f32[1]{0:T(128)S(6)} %copy.12.refs_0_, f32[1]{0:T(128)S(6)} %copy.13.refs_1_, bf16[2048,256]{1,0:T(8,128)(2,1)S(1)} %bitcast.10, bf16[256,2048]{1,0:T(8,128)(2,1)S(1)} %get-tuple-element.27.refs_3_, ...), custom_call_target="tpu_custom_call" | custom-call | flops 1073741824 | bytes 4521992 | tf_op jit(solution)/shard_map/pallas_call | solution.py:100
  61.2 8.3 %all-to-all-start.4 = ((bf16[32,64,256]{2,1,0:T(8,128)(2,1)}), bf16[32,64,256]{2,1,0:T(8,128)(2,1)S(1)}, u32[]{:S(2)}, u32[]{:S(2)}) async-start(bf16[32,64,256]{2,1,0:T(8,128)(2,1)} %bitcast.18), calls=%async_computation.4 | async-start | bytes 2097152 | tf_op jit(solution)/shard_map/all_to_all | solution.py:364
  69.4 1.3 collective-permute-start.7
  70.7 2.4 %collective-permute-start.8 = (bf16[512,256]{1,0:T(8,128)(2,1)S(1)}, bf16[512,256]{1,0:T(8,128)(2,1)S(1)}, u32[]{:S(2)}, u32[]{:S(2)}) collective-permute-start(bf16[512,256]{1,0:T(8,128)(2,1)S(1)} %get-tuple-element.30.refs_3_.refs_9_), channel_id=1, source_target_pairs={{0,4},{1,5},{2,6},{3,7},{4,0},{5,1},{6,2},{7,3},{8,12},{9,13},{10,... | collective-permute-start | bytes 786440 | tf_op jit(solution)/shard_map/ppermute | solution.py:372
  73.2 1.1 collective-permute-start.9
  74.3 2.9 %collective-permute-start.10 = (bf16[512,256]{1,0:T(8,128)(2,1)S(1)}, bf16[512,256]{1,0:T(8,128)(2,1)S(1)}, u32[]{:S(2)}, u32[]{:S(2)}) collective-permute-start(bf16[512,256]{1,0:T(8,128)(2,1)S(1)} %get-tuple-element.30.refs_3_.refs_9_), channel_id=1, source_target_pairs={{0,1},{1,0},{2,3},{3,2},{4,5},{5,4},{6,7},{7,6},{8,9},{9,8},{10,11... | collective-permute-start | bytes 786440 | tf_op jit(solution)/shard_map/ppermute | solution.py:368
  77.2 3.7 %collective-permute-start.11 = (bf16[512,256]{1,0:T(8,128)(2,1)S(1)}, bf16[512,256]{1,0:T(8,128)(2,1)S(1)}, u32[]{:S(2)}, u32[]{:S(2)}) collective-permute-start(bf16[512,256]{1,0:T(8,128)(2,1)S(1)} %collective-permute-done.7.refs_4_.refs_2_), channel_id=1, source_target_pairs={{0,1},{1,0},{2,3},{3,2},{4,5},{5,4},{6,7},{7,6},{8,9},{9,8},{10,11... | collective-permute-start | bytes 786440 | tf_op jit(solution)/shard_map/ppermute | solution.py:368
  81.0 2.2 %collective-permute-done.8.refs_5_.refs_3_ = bf16[512,256]{1,0:T(8,128)(2,1)S(1)} collective-permute-done((bf16[512,256]{1,0:T(8,128)(2,1)S(1)}, bf16[512,256]{1,0:T(8,128)(2,1)S(1)}, u32[]{:S(2)}, u32[]{:S(2)}) %collective-permute-start.8) | collective-permute-done | bytes 262176 | tf_op jit(solution)/shard_map/ppermute | solution.py:372
  83.1 2.9 %collective-permute-start.12 = (bf16[512,256]{1,0:T(8,128)(2,1)S(1)}, bf16[512,256]{1,0:T(8,128)(2,1)S(1)}, u32[]{:S(2)}, u32[]{:S(2)}) collective-permute-start(bf16[512,256]{1,0:T(8,128)(2,1)S(1)} %collective-permute-done.8.refs_5_.refs_3_), channel_id=1, source_target_pairs={{0,1},{1,0},{2,3},{3,2},{4,5},{5,4},{6,7},{7,6},{8,9},{9,8},{10,11... | collective-permute-start | bytes 786440 | tf_op jit(solution)/shard_map/ppermute | solution.py:368
  86.1 0.0 collective-permute-start.13
  86.1 0.0 collective-permute-done.11.refs_8_.refs_6_
  86.1 1.1 collective-permute-done.12.refs_9_.refs_7_
  87.2 0.4 collective-permute-done.13.refs_10_.refs_8_
  87.6 1.6 %shard_map.119 = bf16[256,256]{1,0:T(8,128)(2,1)} custom-call(s32[1]{0:T(128)} %bitcast.5.refs_0_, bf16[8,16,256]{2,1,0:T(8,128)(2,1)S(1)} %get-tuple-element.31.refs_1_, bf16[512,256]{1,0:T(8,128)(2,1)S(1)} %collective-permute-done.7.refs_4_.refs_2_, bf16[512,256]{1,0:T(8,128)(2,1)S(1)} %collective-permute-done.8.refs_5_.refs_3_, ...), custom_call_target="tpu_custom_call" | custom-call | flops 268435456 | bytes 2162692 | tf_op jit(solution)/shard_map/pallas_call | solution.py:100
  89.2 4.8 %all-to-all-done.4 = bf16[32,64,256]{2,1,0:T(8,128)(2,1)S(1)} async-done(((bf16[32,64,256]{2,1,0:T(8,128)(2,1)}), bf16[32,64,256]{2,1,0:T(8,128)(2,1)S(1)}, u32[]{:S(2)}, u32[]{:S(2)}) %all-to-all-start.4) | async-done | bytes 1048608 | tf_op jit(solution)/shard_map/all_to_all | solution.py:364
  94.0 8.1 %all-to-all-start.2 = ((bf16[32,8,256]{2,1,0:T(8,128)(2,1)}), bf16[32,8,256]{2,1,0:T(8,128)(2,1)S(1)}, u32[]{:S(2)}, u32[]{:S(2)}) async-start(bf16[32,8,256]{2,1,0:T(8,128)(2,1)} %bitcast.19), calls=%async_computation.2 | async-start | bytes 262144 | tf_op jit(solution)/shard_map/all_to_all | solution.py:364
  102.1 2.7 %shard_map.123 = bf16[4,256,256]{2,1,0:T(8,128)(2,1)} custom-call(s32[1]{0:T(128)} %bitcast.5.refs_0_, s32[32,8,128]{2,1,0:T(8,128)S(1)} %copy-done.2, bf16[2048,256]{1,0:T(8,128)(2,1)S(1)} %bitcast.11), custom_call_target="tpu_custom_call" | custom-call | flops 1073741824 | bytes 1179652 | tf_op jit(solution)/shard_map/pallas_call | solution.py:100
  104.7 2.1 %collective-permute-start.21 = (bf16[4,256,256]{2,1,0:T(8,128)(2,1)}, bf16[4,256,256]{2,1,0:T(8,128)(2,1)}, u32[]{:S(2)}, u32[]{:S(2)}) collective-permute-start(bf16[4,256,256]{2,1,0:T(8,128)(2,1)} %shard_map.123), channel_id=1, source_target_pairs={{0,1},{1,0},{2,3},{3,2},{4,5},{5,4},{6,7},{7,6},{8,9},{9,8},{10,11... | collective-permute-start | bytes 1572872 | tf_op jit(solution)/shard_map/ppermute | solution.py:368
  106.8 4.4 %all-to-all-done.2.refs_0_ = bf16[32,8,256]{2,1,0:T(8,128)(2,1)S(1)} async-done(((bf16[32,8,256]{2,1,0:T(8,128)(2,1)}), bf16[32,8,256]{2,1,0:T(8,128)(2,1)S(1)}, u32[]{:S(2)}, u32[]{:S(2)}) %all-to-all-start.2) | async-done | bytes 131104 | tf_op jit(solution)/shard_map/all_to_all | solution.py:364
  111.2 0.7 shard_map.120
  111.9 14.2 %all_to_all.25 = bf16[32,8,256]{2,1,0:T(8,128)(2,1)S(1)} all-to-all(bf16[32,8,256]{2,1,0:T(8,128)(2,1)} %shard_map.120), channel_id=1, replica_groups=mesh['shard'=32,'blk'=8] {'shard'}, dimensions={0} | all-to-all | bytes 262144 | tf_op jit(solution)/shard_map/all_to_all | solution.py:364
  126.2 1.2 collective-permute-start.14
  127.4 2.4 %collective-permute-start.15 = (bf16[256,256]{1,0:T(8,128)(2,1)S(1)}, bf16[256,256]{1,0:T(8,128)(2,1)S(1)}, u32[]{:S(2)}, u32[]{:S(2)}) collective-permute-start(bf16[256,256]{1,0:T(8,128)(2,1)S(1)} %bitcast.14), channel_id=1, source_target_pairs={{0,4},{1,5},{2,6},{3,7},{4,0},{5,1},{6,2},{7,3},{8,12},{9,13},{10,... | collective-permute-start | bytes 393224 | tf_op jit(solution)/shard_map/ppermute | solution.py:372
  129.8 1.1 collective-permute-start.16
  131.0 4.1 %collective-permute-start.17 = (bf16[256,256]{1,0:T(8,128)(2,1)S(1)}, bf16[256,256]{1,0:T(8,128)(2,1)S(1)}, u32[]{:S(2)}, u32[]{:S(2)}) collective-permute-start(bf16[256,256]{1,0:T(8,128)(2,1)S(1)} %bitcast.16), channel_id=1, source_target_pairs={{0,1},{1,0},{2,3},{3,2},{4,5},{5,4},{6,7},{7,6},{8,9},{9,8},{10,11... | collective-permute-start | bytes 393224 | tf_op jit(solution)/shard_map/ppermute | solution.py:368
  135.1 0.0 collective-permute-done.14.refs_2_
  135.1 0.6 collective-permute-start.18
  135.7 0.0 collective-permute-done.15.refs_3_
  135.7 2.3 %collective-permute-start.19 = (bf16[256,256]{1,0:T(8,128)(2,1)S(1)}, bf16[256,256]{1,0:T(8,128)(2,1)S(1)}, u32[]{:S(2)}, u32[]{:S(2)}) collective-permute-start(bf16[256,256]{1,0:T(8,128)(2,1)S(1)} %collective-permute-done.15.refs_3_), channel_id=1, source_target_pairs={{0,1},{1,0},{2,3},{3,2},{4,5},{5,4},{6,7},{7,6},{8,9},{9,8},{10,11... | collective-permute-start | bytes 393224 | tf_op jit(solution)/shard_map/ppermute | solution.py:368
  138.0 0.6 collective-permute-start.20
  138.6 1.9 %shard_map.122.refs_0_ = f32[4,256,256]{2,1,0:T(8,128)S(1)} custom-call(s32[1]{0:T(128)} %bitcast.5.refs_0_, s32[32,8,128]{2,1,0:T(8,128)S(1)} %copy-done.2, bf16[2048,256]{1,0:T(8,128)(2,1)S(1)} %bitcast.12), custom_call_target="tpu_custom_call" | custom-call | flops 1073741824 | bytes 1179652 | tf_op jit(solution)/shard_map/pallas_call | solution.py:100
  140.5 1.1 shard_map.124
  141.6 1.1 collective-permute-start.22
  142.7 0.0 collective-permute-done.17.refs_5_
  142.7 2.5 %collective-permute-start.23 = (bf16[256,256]{1,0:T(8,128)(2,1)S(1)}, bf16[256,256]{1,0:T(8,128)(2,1)S(1)}, u32[]{:S(2)}, u32[]{:S(2)}) collective-permute-start(bf16[256,256]{1,0:T(8,128)(2,1)S(1)} %get-tuple-element.35), channel_id=1, source_target_pairs={{0,4},{1,5},{2,6},{3,7},{4,0},{5,1},{6,2},{7,3},{8,12},{9,13},{10,... | collective-permute-start | bytes 393224 | tf_op jit(solution)/shard_map/ppermute | solution.py:372
  145.2 0.0 collective-permute-done.18.refs_6_
  145.2 0.6 collective-permute-start.24
  145.8 2.6 %shard_map.118 = f32[256,256]{1,0:T(8,128)} custom-call(f32[1]{0:T(128)S(6)} %copy.12.refs_0_, f32[1]{0:T(128)S(6)} %copy.13.refs_1_, bf16[256,256]{1,0:T(8,128)(2,1)} %refs_2_, bf16[512,256]{1,0:T(8,128)(2,1)S(1)} %get-tuple-element.30.refs_3_.refs_9_, bf16[512,256]{1,0:T(8,128)(2,1)S(1)} %collective-permute-done.7.refs_4_.refs_2_, ...), custom_call_target="tpu_custom_call" | custom-call | flops 536870912 | bytes 2228232 | tf_op jit(solution)/shard_map/pallas_call | solution.py:100
  148.4 1.4 shard_map.121
  149.8 1.8 %collective-permute-done.23.refs_2_ = bf16[256,256]{1,0:T(8,128)(2,1)S(1)} collective-permute-done((bf16[256,256]{1,0:T(8,128)(2,1)S(1)}, bf16[256,256]{1,0:T(8,128)(2,1)S(1)}, u32[]{:S(2)}, u32[]{:S(2)}) %collective-permute-start.23) | collective-permute-done | bytes 131104 | tf_op jit(solution)/shard_map/ppermute | solution.py:372
  151.6 0.8 shard_map.125
  (17 shorter events, 0.0 us)
Async XLA Ops:
  2.6 21.2 %all-to-all-start = ((s32[32,8,128]{2,1,0:T(8,128)}), s32[32,8,128]{2,1,0:T(8,128)S(1)}, u32[]{:S(2)}, u32[]{:S(2)}) async-start(s32[32,8,128]{2,1,0:T(8,128)} %get-tuple-element.20), calls=%async_computation | async-start | bytes 262144 | tf_op jit(solution)/shard_map/all_to_all | solution.py:364
  23.8 4.2 %copy-start.1 = (s32[32,8,128]{2,1,0:T(8,128)}, s32[32,8,128]{2,1,0:T(8,128)S(1)}, u32[]{:S(2)}) copy-start(s32[32,8,128]{2,1,0:T(8,128)S(1)} %all-to-all-done.refs_0_.refs_1_) | copy-start | bytes 393220
  28.0 28.5 %all-to-all-start.1 = ((bf16[32,64,256]{2,1,0:T(8,128)(2,1)}), bf16[32,64,256]{2,1,0:T(8,128)(2,1)S(1)}, u32[]{:S(2)}, u32[]{:S(2)}) async-start(bf16[32,64,256]{2,1,0:T(8,128)(2,1)} %shard_map.114), calls=%async_computation.1 | async-start | bytes 2097152 | tf_op jit(solution)/shard_map/all_to_all | solution.py:364
  33.0 23.4 %copy-start = (bf16[272,256]{1,0:T(8,128)(2,1)}, bf16[272,256]{1,0:T(8,128)(2,1)S(1)}, u32[]{:S(2)}) copy-start(bf16[272,256]{1,0:T(8,128)(2,1)S(1)} %shard_map.116.refs_12_) | copy-start | bytes 417796
  33.0 7.8 %collective-permute-start = (bf16[272,256]{1,0:T(8,128)(2,1)S(1)}, bf16[272,256]{1,0:T(8,128)(2,1)S(1)}, u32[]{:S(2)}, u32[]{:S(2)}) collective-permute-start(bf16[272,256]{1,0:T(8,128)(2,1)S(1)} %shard_map.116.refs_12_), channel_id=1, source_target_pairs={{0,2},{1,3},{2,4},{3,5},{4,6},{5,7},{6,0},{7,1},{8,10},{9,11},{10,... | collective-permute-start | bytes 417800 | tf_op jit(solution)/shard_map/ppermute | solution.py:372
  34.3 8.6 %collective-permute-start.1 = (bf16[272,256]{1,0:T(8,128)(2,1)S(1)}, bf16[272,256]{1,0:T(8,128)(2,1)S(1)}, u32[]{:S(2)}, u32[]{:S(2)}) collective-permute-start(bf16[272,256]{1,0:T(8,128)(2,1)S(1)} %shard_map.116.refs_12_), channel_id=1, source_target_pairs={{0,4},{1,5},{2,6},{3,7},{4,0},{5,1},{6,2},{7,3},{8,12},{9,13},{10,... | collective-permute-start | bytes 417800 | tf_op jit(solution)/shard_map/ppermute | solution.py:372
  36.8 7.6 %collective-permute-start.2 = (bf16[272,256]{1,0:T(8,128)(2,1)S(1)}, bf16[272,256]{1,0:T(8,128)(2,1)S(1)}, u32[]{:S(2)}, u32[]{:S(2)}) collective-permute-start(bf16[272,256]{1,0:T(8,128)(2,1)S(1)} %shard_map.116.refs_12_), channel_id=1, source_target_pairs={{0,6},{1,7},{2,0},{3,1},{4,2},{5,3},{6,4},{7,5},{8,14},{9,15},{10,... | collective-permute-start | bytes 417800 | tf_op jit(solution)/shard_map/ppermute | solution.py:372
  37.9 13.3 %collective-permute-start.3 = (bf16[272,256]{1,0:T(8,128)(2,1)S(1)}, bf16[272,256]{1,0:T(8,128)(2,1)S(1)}, u32[]{:S(2)}, u32[]{:S(2)}) collective-permute-start(bf16[272,256]{1,0:T(8,128)(2,1)S(1)} %shard_map.116.refs_12_), channel_id=1, source_target_pairs={{0,1},{1,0},{2,3},{3,2},{4,5},{5,4},{6,7},{7,6},{8,9},{9,8},{10,11... | collective-permute-start | bytes 417800 | tf_op jit(solution)/shard_map/ppermute | solution.py:368
  40.9 10.3 %collective-permute-start.4 = (bf16[272,256]{1,0:T(8,128)(2,1)S(1)}, bf16[272,256]{1,0:T(8,128)(2,1)S(1)}, u32[]{:S(2)}, u32[]{:S(2)}) collective-permute-start(bf16[272,256]{1,0:T(8,128)(2,1)S(1)} %collective-permute-done.refs_5_), channel_id=1, source_target_pairs={{0,1},{1,0},{2,3},{3,2},{4,5},{5,4},{6,7},{7,6},{8,9},{9,8},{10,11... | collective-permute-start | bytes 417800 | tf_op jit(solution)/shard_map/ppermute | solution.py:368
  42.9 8.3 %collective-permute-start.5 = (bf16[272,256]{1,0:T(8,128)(2,1)S(1)}, bf16[272,256]{1,0:T(8,128)(2,1)S(1)}, u32[]{:S(2)}, u32[]{:S(2)}) collective-permute-start(bf16[272,256]{1,0:T(8,128)(2,1)S(1)} %collective-permute-done.1.refs_6_), channel_id=1, source_target_pairs={{0,1},{1,0},{2,3},{3,2},{4,5},{5,4},{6,7},{7,6},{8,9},{9,8},{10,11... | collective-permute-start | bytes 417800 | tf_op jit(solution)/shard_map/ppermute | solution.py:368
  44.4 7.5 %collective-permute-start.6 = (bf16[272,256]{1,0:T(8,128)(2,1)S(1)}, bf16[272,256]{1,0:T(8,128)(2,1)}, u32[]{:S(2)}, u32[]{:S(2)}) collective-permute-start(bf16[272,256]{1,0:T(8,128)(2,1)S(1)} %collective-permute-done.2.refs_7_), channel_id=1, source_target_pairs={{0,1},{1,0},{2,3},{3,2},{4,5},{5,4},{6,7},{7,6},{8,9},{9,8},{10,11... | collective-permute-start | bytes 417800 | tf_op jit(solution)/shard_map/ppermute | solution.py:368
  51.2 0.7 copy-start.3
  61.2 40.9 %copy-start.2 = (s32[32,8,128]{2,1,0:T(8,128)S(1)}, s32[32,8,128]{2,1,0:T(8,128)}, u32[]{:S(2)}) copy-start(s32[32,8,128]{2,1,0:T(8,128)} %copy-done.1) | copy-start | bytes 393220
  61.2 32.8 %all-to-all-start.4 = ((bf16[32,64,256]{2,1,0:T(8,128)(2,1)}), bf16[32,64,256]{2,1,0:T(8,128)(2,1)S(1)}, u32[]{:S(2)}, u32[]{:S(2)}) async-start(bf16[32,64,256]{2,1,0:T(8,128)(2,1)} %bitcast.18), calls=%async_computation.4 | async-start | bytes 2097152 | tf_op jit(solution)/shard_map/all_to_all | solution.py:364
  69.4 7.8 %collective-permute-start.7 = (bf16[512,256]{1,0:T(8,128)(2,1)S(1)}, bf16[512,256]{1,0:T(8,128)(2,1)S(1)}, u32[]{:S(2)}, u32[]{:S(2)}) collective-permute-start(bf16[512,256]{1,0:T(8,128)(2,1)S(1)} %get-tuple-element.30.refs_3_.refs_9_), channel_id=1, source_target_pairs={{0,2},{1,3},{2,4},{3,5},{4,6},{5,7},{6,0},{7,1},{8,10},{9,11},{10,... | collective-permute-start | bytes 786440 | tf_op jit(solution)/shard_map/ppermute | solution.py:372
  70.7 12.4 %collective-permute-start.8 = (bf16[512,256]{1,0:T(8,128)(2,1)S(1)}, bf16[512,256]{1,0:T(8,128)(2,1)S(1)}, u32[]{:S(2)}, u32[]{:S(2)}) collective-permute-start(bf16[512,256]{1,0:T(8,128)(2,1)S(1)} %get-tuple-element.30.refs_3_.refs_9_), channel_id=1, source_target_pairs={{0,4},{1,5},{2,6},{3,7},{4,0},{5,1},{6,2},{7,3},{8,12},{9,13},{10,... | collective-permute-start | bytes 786440 | tf_op jit(solution)/shard_map/ppermute | solution.py:372
  73.2 12.9 %collective-permute-start.9 = (bf16[512,256]{1,0:T(8,128)(2,1)S(1)}, bf16[512,256]{1,0:T(8,128)(2,1)S(1)}, u32[]{:S(2)}, u32[]{:S(2)}) collective-permute-start(bf16[512,256]{1,0:T(8,128)(2,1)S(1)} %get-tuple-element.30.refs_3_.refs_9_), channel_id=1, source_target_pairs={{0,6},{1,7},{2,0},{3,1},{4,2},{5,3},{6,4},{7,5},{8,14},{9,15},{10,... | collective-permute-start | bytes 786440 | tf_op jit(solution)/shard_map/ppermute | solution.py:372
  74.3 11.7 %collective-permute-start.10 = (bf16[512,256]{1,0:T(8,128)(2,1)S(1)}, bf16[512,256]{1,0:T(8,128)(2,1)S(1)}, u32[]{:S(2)}, u32[]{:S(2)}) collective-permute-start(bf16[512,256]{1,0:T(8,128)(2,1)S(1)} %get-tuple-element.30.refs_3_.refs_9_), channel_id=1, source_target_pairs={{0,1},{1,0},{2,3},{3,2},{4,5},{5,4},{6,7},{7,6},{8,9},{9,8},{10,11... | collective-permute-start | bytes 786440 | tf_op jit(solution)/shard_map/ppermute | solution.py:368
  77.2 8.9 %collective-permute-start.11 = (bf16[512,256]{1,0:T(8,128)(2,1)S(1)}, bf16[512,256]{1,0:T(8,128)(2,1)S(1)}, u32[]{:S(2)}, u32[]{:S(2)}) collective-permute-start(bf16[512,256]{1,0:T(8,128)(2,1)S(1)} %collective-permute-done.7.refs_4_.refs_2_), channel_id=1, source_target_pairs={{0,1},{1,0},{2,3},{3,2},{4,5},{5,4},{6,7},{7,6},{8,9},{9,8},{10,11... | collective-permute-start | bytes 786440 | tf_op jit(solution)/shard_map/ppermute | solution.py:368
  83.1 4.1 %collective-permute-start.12 = (bf16[512,256]{1,0:T(8,128)(2,1)S(1)}, bf16[512,256]{1,0:T(8,128)(2,1)S(1)}, u32[]{:S(2)}, u32[]{:S(2)}) collective-permute-start(bf16[512,256]{1,0:T(8,128)(2,1)S(1)} %collective-permute-done.8.refs_5_.refs_3_), channel_id=1, source_target_pairs={{0,1},{1,0},{2,3},{3,2},{4,5},{5,4},{6,7},{7,6},{8,9},{9,8},{10,11... | collective-permute-start | bytes 786440 | tf_op jit(solution)/shard_map/ppermute | solution.py:368
  86.1 1.5 %collective-permute-start.13 = (bf16[512,256]{1,0:T(8,128)(2,1)S(1)}, bf16[512,256]{1,0:T(8,128)(2,1)S(1)}, u32[]{:S(2)}, u32[]{:S(2)}) collective-permute-start(bf16[512,256]{1,0:T(8,128)(2,1)S(1)} %collective-permute-done.9.refs_6_.refs_4_), channel_id=1, source_target_pairs={{0,1},{1,0},{2,3},{3,2},{4,5},{5,4},{6,7},{7,6},{8,9},{9,8},{10,11... | collective-permute-start | bytes 786440 | tf_op jit(solution)/shard_map/ppermute | solution.py:368
  94.0 17.2 %all-to-all-start.2 = ((bf16[32,8,256]{2,1,0:T(8,128)(2,1)}), bf16[32,8,256]{2,1,0:T(8,128)(2,1)S(1)}, u32[]{:S(2)}, u32[]{:S(2)}) async-start(bf16[32,8,256]{2,1,0:T(8,128)(2,1)} %bitcast.19), calls=%async_computation.2 | async-start | bytes 262144 | tf_op jit(solution)/shard_map/all_to_all | solution.py:364
  104.7 35.8 %collective-permute-start.21 = (bf16[4,256,256]{2,1,0:T(8,128)(2,1)}, bf16[4,256,256]{2,1,0:T(8,128)(2,1)}, u32[]{:S(2)}, u32[]{:S(2)}) collective-permute-start(bf16[4,256,256]{2,1,0:T(8,128)(2,1)} %shard_map.123), channel_id=1, source_target_pairs={{0,1},{1,0},{2,3},{3,2},{4,5},{5,4},{6,7},{7,6},{8,9},{9,8},{10,11... | collective-permute-start | bytes 1572872 | tf_op jit(solution)/shard_map/ppermute | solution.py:368
  126.2 8.9 %collective-permute-start.14 = (bf16[256,256]{1,0:T(8,128)(2,1)S(1)}, bf16[256,256]{1,0:T(8,128)(2,1)S(1)}, u32[]{:S(2)}, u32[]{:S(2)}) collective-permute-start(bf16[256,256]{1,0:T(8,128)(2,1)S(1)} %bitcast.13), channel_id=1, source_target_pairs={{0,2},{1,3},{2,4},{3,5},{4,6},{5,7},{6,0},{7,1},{8,10},{9,11},{10,... | collective-permute-start | bytes 393224 | tf_op jit(solution)/shard_map/ppermute | solution.py:372
  127.4 8.3 %collective-permute-start.15 = (bf16[256,256]{1,0:T(8,128)(2,1)S(1)}, bf16[256,256]{1,0:T(8,128)(2,1)S(1)}, u32[]{:S(2)}, u32[]{:S(2)}) collective-permute-start(bf16[256,256]{1,0:T(8,128)(2,1)S(1)} %bitcast.14), channel_id=1, source_target_pairs={{0,4},{1,5},{2,6},{3,7},{4,0},{5,1},{6,2},{7,3},{8,12},{9,13},{10,... | collective-permute-start | bytes 393224 | tf_op jit(solution)/shard_map/ppermute | solution.py:372
  129.8 8.2 %collective-permute-start.16 = (bf16[256,256]{1,0:T(8,128)(2,1)S(1)}, bf16[256,256]{1,0:T(8,128)(2,1)S(1)}, u32[]{:S(2)}, u32[]{:S(2)}) collective-permute-start(bf16[256,256]{1,0:T(8,128)(2,1)S(1)} %bitcast.15), channel_id=1, source_target_pairs={{0,6},{1,7},{2,0},{3,1},{4,2},{5,3},{6,4},{7,5},{8,14},{9,15},{10,... | collective-permute-start | bytes 393224 | tf_op jit(solution)/shard_map/ppermute | solution.py:372
  131.0 11.7 %collective-permute-start.17 = (bf16[256,256]{1,0:T(8,128)(2,1)S(1)}, bf16[256,256]{1,0:T(8,128)(2,1)S(1)}, u32[]{:S(2)}, u32[]{:S(2)}) collective-permute-start(bf16[256,256]{1,0:T(8,128)(2,1)S(1)} %bitcast.16), channel_id=1, source_target_pairs={{0,1},{1,0},{2,3},{3,2},{4,5},{5,4},{6,7},{7,6},{8,9},{9,8},{10,11... | collective-permute-start | bytes 393224 | tf_op jit(solution)/shard_map/ppermute | solution.py:368
  135.1 10.2 %collective-permute-start.18 = (bf16[256,256]{1,0:T(8,128)(2,1)S(1)}, bf16[256,256]{1,0:T(8,128)(2,1)S(1)}, u32[]{:S(2)}, u32[]{:S(2)}) collective-permute-start(bf16[256,256]{1,0:T(8,128)(2,1)S(1)} %collective-permute-done.14.refs_2_), channel_id=1, source_target_pairs={{0,1},{1,0},{2,3},{3,2},{4,5},{5,4},{6,7},{7,6},{8,9},{9,8},{10,11... | collective-permute-start | bytes 393224 | tf_op jit(solution)/shard_map/ppermute | solution.py:368
  135.7 12.7 %collective-permute-start.19 = (bf16[256,256]{1,0:T(8,128)(2,1)S(1)}, bf16[256,256]{1,0:T(8,128)(2,1)S(1)}, u32[]{:S(2)}, u32[]{:S(2)}) collective-permute-start(bf16[256,256]{1,0:T(8,128)(2,1)S(1)} %collective-permute-done.15.refs_3_), channel_id=1, source_target_pairs={{0,1},{1,0},{2,3},{3,2},{4,5},{5,4},{6,7},{7,6},{8,9},{9,8},{10,11... | collective-permute-start | bytes 393224 | tf_op jit(solution)/shard_map/ppermute | solution.py:368
  138.0 10.4 %collective-permute-start.20 = (bf16[256,256]{1,0:T(8,128)(2,1)S(1)}, bf16[256,256]{1,0:T(8,128)(2,1)S(1)}, u32[]{:S(2)}, u32[]{:S(2)}) collective-permute-start(bf16[256,256]{1,0:T(8,128)(2,1)S(1)} %collective-permute-done.16.refs_4_), channel_id=1, source_target_pairs={{0,1},{1,0},{2,3},{3,2},{4,5},{5,4},{6,7},{7,6},{8,9},{9,8},{10,11... | collective-permute-start | bytes 393224 | tf_op jit(solution)/shard_map/ppermute | solution.py:368
  141.6 8.2 %collective-permute-start.22 = (bf16[256,256]{1,0:T(8,128)(2,1)S(1)}, bf16[256,256]{1,0:T(8,128)(2,1)S(1)}, u32[]{:S(2)}, u32[]{:S(2)}) collective-permute-start(bf16[256,256]{1,0:T(8,128)(2,1)S(1)} %get-tuple-element.34), channel_id=1, source_target_pairs={{0,2},{1,3},{2,4},{3,5},{4,6},{5,7},{6,0},{7,1},{8,10},{9,11},{10,... | collective-permute-start | bytes 393224 | tf_op jit(solution)/shard_map/ppermute | solution.py:372
  142.7 8.9 %collective-permute-start.23 = (bf16[256,256]{1,0:T(8,128)(2,1)S(1)}, bf16[256,256]{1,0:T(8,128)(2,1)S(1)}, u32[]{:S(2)}, u32[]{:S(2)}) collective-permute-start(bf16[256,256]{1,0:T(8,128)(2,1)S(1)} %get-tuple-element.35), channel_id=1, source_target_pairs={{0,4},{1,5},{2,6},{3,7},{4,0},{5,1},{6,2},{7,3},{8,12},{9,13},{10,... | collective-permute-start | bytes 393224 | tf_op jit(solution)/shard_map/ppermute | solution.py:372
  145.2 6.4 %collective-permute-start.24 = (bf16[256,256]{1,0:T(8,128)(2,1)S(1)}, bf16[256,256]{1,0:T(8,128)(2,1)S(1)}, u32[]{:S(2)}, u32[]{:S(2)}) collective-permute-start(bf16[256,256]{1,0:T(8,128)(2,1)S(1)} %get-tuple-element.36), channel_id=1, source_target_pairs={{0,6},{1,7},{2,0},{3,1},{4,2},{5,3},{6,4},{7,5},{8,14},{9,15},{10,... | collective-permute-start | bytes 393224 | tf_op jit(solution)/shard_map/ppermute | solution.py:372

commit v9 on v8

--- a/solution.py
+++ b/solution.py
@@ -374,9 +374,7 @@
 
 def gather_blocks(array, blocks):
     first = cross(array, blocks)
-    mine = []
-    for d in range(1, blocks // 2):
-        mine.append(shift(array, blocks, d))
+    mine = [shift(array, blocks, d) for d in range(1, blocks // 2)]
     return [array] + mine + [first] + [cross(m, blocks) for m in mine]
 
 
@@ -433,7 +431,7 @@
         [shape((2 * pairs, width), BF16), shape((blocks, 16, width), BF16), HBM((total, width), BF16)],
         sharpness, additive, fetched, pick, hot_sum, *[query_blocks[i] for i in order], placed,
         kinds=["s", "s", "v", "v", "v"] + ["v"] * (blocks - far) + ["h"] * (far + 1),
-        steps=steps,
+        steps=4,
         flops=2 * pairs * width * (2 * total + 2 * blocks * pairs),
     )
     incoming = swap(outgoing.reshape(owners, cap, width), "shard").reshape(total, width)

time: 153 us -> 153 us (level)
  no operation moved by 1% of the time
where the time goes in v9:
time: 153 us; the launch traced here: 152 us
  starting transfers between devices  76.8 us (50%)
  Pallas kernels  31.2 us (20%)
  waiting for transfers between devices  26.7 us (17%)
  blocking collectives  14.2 us (9%)
  between operations  2.34 us (2%)
    all_to_all x4, starting transfers between devices, swap(): return lax.all_to_all(array, axis, split_axis=0, concat_axis=0, tiled=True)  32.3 us
    pallas_call x14, Pallas kernels, call(): pl.pallas_call(run, out_shape=list(outs), in_specs=[pl.BlockSpec(memory_s...  31.2 us
    ppermute x13, starting transfers between devices, cross(): return lax.ppermute(array, 'blk', [(i, i ^ 1) for i in range(blocks)])  25.8 us
    all_to_all x4, waiting for transfers between devices, swap(): return lax.all_to_all(array, axis, split_axis=0, concat_axis=0, tiled=True)  21.2 us
    ppermute x12, starting transfers between devices, shift(): lax.ppermute(array, 'blk', [(i, (i + 2 * d) % blocks) for i in range(bloc...  18.7 us
    all_to_all x1, blocking collectives, swap(): return lax.all_to_all(array, axis, split_axis=0, concat_axis=0, tiled=True)  14.2 us
    ppermute x12, waiting for transfers between devices, shift(): lax.ppermute(array, 'blk', [(i, (i + 2 * d) % blocks) for i in range(bloc...  3.97 us
  transfers between devices with their start and end apart: 29, of which 8 were waited for; matrix products, arithmetic and copies ran while one was open for 0% of the time, Pallas kernels for 13%

profile of v9, /device:TPU:1, one launch (start us, length us, event | category | flops | bytes accessed | tf_op | source)
XLA Modules:
  0.0 152.0 jit_solution(5156846687991347928)
XLA Ops:
  0.6 1.9 %shard_map.112 = (bf16[256,128]{1,0:T(8,128)(2,1)S(1)}, bf16[128,256]{1,0:T(8,128)(2,1)S(1)}, s32[32,8,128]{2,1,0:T(8,128)}) custom-call(s32[4,256]{1,0:T(4,128)} %bitcast.22, s32[4,256]{1,0:T(4,128)} %bitcast.23, s32[1,256]{1,0:T(1,128)} %bitcast.24), custom_call_target="tpu_custom_call" | custom-call | flops 16777216 | bytes 9216 | tf_op jit(solution)/shard_map/pallas_call | solution.py:100
  2.6 12.0 %all-to-all-start = ((s32[32,8,128]{2,1,0:T(8,128)}), s32[32,8,128]{2,1,0:T(8,128)S(1)}, u32[]{:S(2)}, u32[]{:S(2)}) async-start(s32[32,8,128]{2,1,0:T(8,128)} %get-tuple-element.20), calls=%async_computation | async-start | bytes 262144 | tf_op jit(solution)/shard_map/all_to_all | solution.py:364
  14.6 1.7 %shard_map.113.refs_1_ = bf16[2048,256]{1,0:T(8,128)(2,1)S(1)} custom-call(f32[2048,256]{1,0:T(8,128)} %refs_0_.3), custom_call_target="tpu_custom_call" | custom-call | bytes 2097152 | tf_op jit(solution)/shard_map/pallas_call | solution.py:100
  16.3 7.4 %all-to-all-done.refs_0_.refs_1_ = s32[32,8,128]{2,1,0:T(8,128)S(1)} async-done(((s32[32,8,128]{2,1,0:T(8,128)}), s32[32,8,128]{2,1,0:T(8,128)S(1)}, u32[]{:S(2)}, u32[]{:S(2)}) %all-to-all-start) | async-done | bytes 131104 | tf_op jit(solution)/shard_map/all_to_all | solution.py:364
  23.8 4.2 %shard_map.114 = bf16[32,64,256]{2,1,0:T(8,128)(2,1)} custom-call(s32[32,8,128]{2,1,0:T(8,128)S(1)} %all-to-all-done.refs_0_.refs_1_, bf16[2048,256]{1,0:T(8,128)(2,1)S(1)} %shard_map.113.refs_1_), custom_call_target="tpu_custom_call" | custom-call | flops 2147483648 | bytes 1179648 | tf_op jit(solution)/shard_map/pallas_call | solution.py:100
  28.0 3.9 %all-to-all-start.1 = ((bf16[32,64,256]{2,1,0:T(8,128)(2,1)}), bf16[32,64,256]{2,1,0:T(8,128)(2,1)S(1)}, u32[]{:S(2)}, u32[]{:S(2)}) async-start(bf16[32,64,256]{2,1,0:T(8,128)(2,1)} %shard_map.114), calls=%async_computation.1 | async-start | bytes 2097152 | tf_op jit(solution)/shard_map/all_to_all | solution.py:364
  31.9 1.1 shard_map.116.refs_12_
  33.0 0.0 copy-start
  33.0 1.3 collective-permute-start
  34.3 2.4 %collective-permute-start.1 = (bf16[272,256]{1,0:T(8,128)(2,1)S(1)}, bf16[272,256]{1,0:T(8,128)(2,1)S(1)}, u32[]{:S(2)}, u32[]{:S(2)}) collective-permute-start(bf16[272,256]{1,0:T(8,128)(2,1)S(1)} %shard_map.116.refs_12_), channel_id=1, source_target_pairs={{0,4},{1,5},{2,6},{3,7},{4,0},{5,1},{6,2},{7,3},{8,12},{9,13},{10,... | collective-permute-start | bytes 417800 | tf_op jit(solution)/shard_map/ppermute | solution.py:372
  36.8 1.1 collective-permute-start.2
  37.9 2.9 %collective-permute-start.3 = (bf16[272,256]{1,0:T(8,128)(2,1)S(1)}, bf16[272,256]{1,0:T(8,128)(2,1)S(1)}, u32[]{:S(2)}, u32[]{:S(2)}) collective-permute-start(bf16[272,256]{1,0:T(8,128)(2,1)S(1)} %shard_map.116.refs_12_), channel_id=1, source_target_pairs={{0,1},{1,0},{2,3},{3,2},{4,5},{5,4},{6,7},{7,6},{8,9},{9,8},{10,11... | collective-permute-start | bytes 417800 | tf_op jit(solution)/shard_map/ppermute | solution.py:368
  40.9 2.0 %collective-permute-start.4 = (bf16[272,256]{1,0:T(8,128)(2,1)S(1)}, bf16[272,256]{1,0:T(8,128)(2,1)S(1)}, u32[]{:S(2)}, u32[]{:S(2)}) collective-permute-start(bf16[272,256]{1,0:T(8,128)(2,1)S(1)} %collective-permute-done.refs_5_), channel_id=1, source_target_pairs={{0,1},{1,0},{2,3},{3,2},{4,5},{5,4},{6,7},{7,6},{8,9},{9,8},{10,11... | collective-permute-start | bytes 417800 | tf_op jit(solution)/shard_map/ppermute | solution.py:368
  42.9 1.5 collective-permute-start.5
  44.4 0.0 collective-permute-done.2.refs_7_
  44.4 0.1 collective-permute-start.6
  45.8 5.4 %shard_map.115 = (bf16[256,2048]{1,0:T(8,128)(2,1)S(1)}, bf16[2048,256]{1,0:T(8,128)(2,1)}, f32[256,256]{1,0:T(8,128)S(1)}) custom-call(bf16[256,128]{1,0:T(8,128)(2,1)S(1)} %get-tuple-element.25.refs_0_, bf16[128,256]{1,0:T(8,128)(2,1)S(1)} %get-tuple-element.26.refs_1_, s32[4,256]{1,0:T(4,128)} %bitcast.21, bf16[2048,256]{1,0:T(8,128)(2,1)} %refs_3_.1), custom_call_target="tpu_custom_call" | custom-call | flops 536870912 | bytes 1183744 | tf_op jit(solution)/shard_map/pallas_call | solution.py:100
  51.2 0.0 collective-permute-done.3.refs_8_
  51.2 0.0 collective-permute-done.5.refs_10_
  51.2 0.0 copy-start.3
  51.2 0.6 copy-done.3
  51.9 0.0 collective-permute-done.6.refs_11_
  51.9 4.5 %all-to-all-done.1 = bf16[32,64,256]{2,1,0:T(8,128)(2,1)S(1)} async-done(((bf16[32,64,256]{2,1,0:T(8,128)(2,1)}), bf16[32,64,256]{2,1,0:T(8,128)(2,1)S(1)}, u32[]{:S(2)}, u32[]{:S(2)}) %all-to-all-start.1) | async-done | bytes 1048608 | tf_op jit(solution)/shard_map/all_to_all | solution.py:364
  56.4 4.1 %shard_map.117 = (bf16[512,256]{1,0:T(8,128)(2,1)S(1)}, bf16[8,16,256]{2,1,0:T(8,128)(2,1)S(1)}, bf16[2048,256]{1,0:T(8,128)(2,1)}) custom-call(f32[1]{0:T(128)S(6)} %copy.12.refs_0_, f32[1]{0:T(128)S(6)} %copy.13.refs_1_, bf16[2048,256]{1,0:T(8,128)(2,1)S(1)} %bitcast.10, bf16[256,2048]{1,0:T(8,128)(2,1)S(1)} %get-tuple-element.27.refs_3_, ...), custom_call_target="tpu_custom_call" | custom-call | flops 1073741824 | bytes 4521992 | tf_op jit(solution)/shard_map/pallas_call | solution.py:100
  60.6 8.3 %all-to-all-start.4 = ((bf16[32,64,256]{2,1,0:T(8,128)(2,1)}), bf16[32,64,256]{2,1,0:T(8,128)(2,1)S(1)}, u32[]{:S(2)}, u32[]{:S(2)}) async-start(bf16[32,64,256]{2,1,0:T(8,128)(2,1)} %bitcast.18), calls=%async_computation.4 | async-start | bytes 2097152 | tf_op jit(solution)/shard_map/all_to_all | solution.py:364
  68.9 1.3 collective-permute-start.7
  70.1 2.5 %collective-permute-start.8 = (bf16[512,256]{1,0:T(8,128)(2,1)S(1)}, bf16[512,256]{1,0:T(8,128)(2,1)S(1)}, u32[]{:S(2)}, u32[]{:S(2)}) collective-permute-start(bf16[512,256]{1,0:T(8,128)(2,1)S(1)} %get-tuple-element.30.refs_3_.refs_9_), channel_id=1, source_target_pairs={{0,4},{1,5},{2,6},{3,7},{4,0},{5,1},{6,2},{7,3},{8,12},{9,13},{10,... | collective-permute-start | bytes 786440 | tf_op jit(solution)/shard_map/ppermute | solution.py:372
  72.6 1.1 collective-permute-start.9
  73.7 2.9 %collective-permute-start.10 = (bf16[512,256]{1,0:T(8,128)(2,1)S(1)}, bf16[512,256]{1,0:T(8,128)(2,1)S(1)}, u32[]{:S(2)}, u32[]{:S(2)}) collective-permute-start(bf16[512,256]{1,0:T(8,128)(2,1)S(1)} %get-tuple-element.30.refs_3_.refs_9_), channel_id=1, source_target_pairs={{0,1},{1,0},{2,3},{3,2},{4,5},{5,4},{6,7},{7,6},{8,9},{9,8},{10,11... | collective-permute-start | bytes 786440 | tf_op jit(solution)/shard_map/ppermute | solution.py:368
  76.6 0.0 collective-permute-done.7.refs_4_.refs_2_
  76.6 3.8 %collective-permute-start.11 = (bf16[512,256]{1,0:T(8,128)(2,1)S(1)}, bf16[512,256]{1,0:T(8,128)(2,1)S(1)}, u32[]{:S(2)}, u32[]{:S(2)}) collective-permute-start(bf16[512,256]{1,0:T(8,128)(2,1)S(1)} %collective-permute-done.7.refs_4_.refs_2_), channel_id=1, source_target_pairs={{0,1},{1,0},{2,3},{3,2},{4,5},{5,4},{6,7},{7,6},{8,9},{9,8},{10,11... | collective-permute-start | bytes 786440 | tf_op jit(solution)/shard_map/ppermute | solution.py:368
  80.4 2.2 %collective-permute-done.8.refs_5_.refs_3_ = bf16[512,256]{1,0:T(8,128)(2,1)S(1)} collective-permute-done((bf16[512,256]{1,0:T(8,128)(2,1)S(1)}, bf16[512,256]{1,0:T(8,128)(2,1)S(1)}, u32[]{:S(2)}, u32[]{:S(2)}) %collective-permute-start.8) | collective-permute-done | bytes 262176 | tf_op jit(solution)/shard_map/ppermute | solution.py:372
  82.6 2.9 %collective-permute-start.12 = (bf16[512,256]{1,0:T(8,128)(2,1)S(1)}, bf16[512,256]{1,0:T(8,128)(2,1)S(1)}, u32[]{:S(2)}, u32[]{:S(2)}) collective-permute-start(bf16[512,256]{1,0:T(8,128)(2,1)S(1)} %collective-permute-done.8.refs_5_.refs_3_), channel_id=1, source_target_pairs={{0,1},{1,0},{2,3},{3,2},{4,5},{5,4},{6,7},{7,6},{8,9},{9,8},{10,11... | collective-permute-start | bytes 786440 | tf_op jit(solution)/shard_map/ppermute | solution.py:368
  85.5 0.0 collective-permute-start.13
  85.5 0.0 collective-permute-done.11.refs_8_.refs_6_
  85.5 1.1 collective-permute-done.12.refs_9_.refs_7_
  86.6 0.4 collective-permute-done.13.refs_10_.refs_8_
  87.0 1.6 %shard_map.119 = bf16[256,256]{1,0:T(8,128)(2,1)} custom-call(s32[1]{0:T(128)} %bitcast.5.refs_0_, bf16[8,16,256]{2,1,0:T(8,128)(2,1)S(1)} %get-tuple-element.31.refs_1_, bf16[512,256]{1,0:T(8,128)(2,1)S(1)} %collective-permute-done.7.refs_4_.refs_2_, bf16[512,256]{1,0:T(8,128)(2,1)S(1)} %collective-permute-done.8.refs_5_.refs_3_, ...), custom_call_target="tpu_custom_call" | custom-call | flops 268435456 | bytes 2162692 | tf_op jit(solution)/shard_map/pallas_call | solution.py:100
  88.6 4.8 %all-to-all-done.4 = bf16[32,64,256]{2,1,0:T(8,128)(2,1)S(1)} async-done(((bf16[32,64,256]{2,1,0:T(8,128)(2,1)}), bf16[32,64,256]{2,1,0:T(8,128)(2,1)S(1)}, u32[]{:S(2)}, u32[]{:S(2)}) %all-to-all-start.4) | async-done | bytes 1048608 | tf_op jit(solution)/shard_map/all_to_all | solution.py:364
  93.4 8.1 %all-to-all-start.2 = ((bf16[32,8,256]{2,1,0:T(8,128)(2,1)}), bf16[32,8,256]{2,1,0:T(8,128)(2,1)S(1)}, u32[]{:S(2)}, u32[]{:S(2)}) async-start(bf16[32,8,256]{2,1,0:T(8,128)(2,1)} %bitcast.19), calls=%async_computation.2 | async-start | bytes 262144 | tf_op jit(solution)/shard_map/all_to_all | solution.py:364
  101.5 2.7 %shard_map.123 = bf16[4,256,256]{2,1,0:T(8,128)(2,1)} custom-call(s32[1]{0:T(128)} %bitcast.5.refs_0_, s32[32,8,128]{2,1,0:T(8,128)S(1)} %copy-done.2, bf16[2048,256]{1,0:T(8,128)(2,1)S(1)} %bitcast.11), custom_call_target="tpu_custom_call" | custom-call | flops 1073741824 | bytes 1179652 | tf_op jit(solution)/shard_map/pallas_call | solution.py:100
  104.1 2.1 %collective-permute-start.21 = (bf16[4,256,256]{2,1,0:T(8,128)(2,1)}, bf16[4,256,256]{2,1,0:T(8,128)(2,1)}, u32[]{:S(2)}, u32[]{:S(2)}) collective-permute-start(bf16[4,256,256]{2,1,0:T(8,128)(2,1)} %shard_map.123), channel_id=1, source_target_pairs={{0,1},{1,0},{2,3},{3,2},{4,5},{5,4},{6,7},{7,6},{8,9},{9,8},{10,11... | collective-permute-start | bytes 1572872 | tf_op jit(solution)/shard_map/ppermute | solution.py:368
  106.2 4.4 %all-to-all-done.2.refs_0_ = bf16[32,8,256]{2,1,0:T(8,128)(2,1)S(1)} async-done(((bf16[32,8,256]{2,1,0:T(8,128)(2,1)}), bf16[32,8,256]{2,1,0:T(8,128)(2,1)S(1)}, u32[]{:S(2)}, u32[]{:S(2)}) %all-to-all-start.2) | async-done | bytes 131104 | tf_op jit(solution)/shard_map/all_to_all | solution.py:364
  110.6 0.7 shard_map.120
  111.3 14.2 %all_to_all.25 = bf16[32,8,256]{2,1,0:T(8,128)(2,1)S(1)} all-to-all(bf16[32,8,256]{2,1,0:T(8,128)(2,1)} %shard_map.120), channel_id=1, replica_groups=mesh['shard'=32,'blk'=8] {'shard'}, dimensions={0} | all-to-all | bytes 262144 | tf_op jit(solution)/shard_map/all_to_all | solution.py:364
  125.6 1.2 collective-permute-start.14
  126.8 2.5 %collective-permute-start.15 = (bf16[256,256]{1,0:T(8,128)(2,1)S(1)}, bf16[256,256]{1,0:T(8,128)(2,1)S(1)}, u32[]{:S(2)}, u32[]{:S(2)}) collective-permute-start(bf16[256,256]{1,0:T(8,128)(2,1)S(1)} %bitcast.14), channel_id=1, source_target_pairs={{0,4},{1,5},{2,6},{3,7},{4,0},{5,1},{6,2},{7,3},{8,12},{9,13},{10,... | collective-permute-start | bytes 393224 | tf_op jit(solution)/shard_map/ppermute | solution.py:372
  129.3 1.1 collective-permute-start.16
  130.4 4.1 %collective-permute-start.17 = (bf16[256,256]{1,0:T(8,128)(2,1)S(1)}, bf16[256,256]{1,0:T(8,128)(2,1)S(1)}, u32[]{:S(2)}, u32[]{:S(2)}) collective-permute-start(bf16[256,256]{1,0:T(8,128)(2,1)S(1)} %bitcast.16), channel_id=1, source_target_pairs={{0,1},{1,0},{2,3},{3,2},{4,5},{5,4},{6,7},{7,6},{8,9},{9,8},{10,11... | collective-permute-start | bytes 393224 | tf_op jit(solution)/shard_map/ppermute | solution.py:368
  134.5 0.6 collective-permute-start.18
  135.1 0.0 collective-permute-done.15.refs_3_
  135.1 2.3 %collective-permute-start.19 = (bf16[256,256]{1,0:T(8,128)(2,1)S(1)}, bf16[256,256]{1,0:T(8,128)(2,1)S(1)}, u32[]{:S(2)}, u32[]{:S(2)}) collective-permute-start(bf16[256,256]{1,0:T(8,128)(2,1)S(1)} %collective-permute-done.15.refs_3_), channel_id=1, source_target_pairs={{0,1},{1,0},{2,3},{3,2},{4,5},{5,4},{6,7},{7,6},{8,9},{9,8},{10,11... | collective-permute-start | bytes 393224 | tf_op jit(solution)/shard_map/ppermute | solution.py:368
  137.4 0.0 collective-permute-done.16.refs_4_
  137.4 0.6 collective-permute-start.20
  138.0 1.9 %shard_map.122.refs_0_ = f32[4,256,256]{2,1,0:T(8,128)S(1)} custom-call(s32[1]{0:T(128)} %bitcast.5.refs_0_, s32[32,8,128]{2,1,0:T(8,128)S(1)} %copy-done.2, bf16[2048,256]{1,0:T(8,128)(2,1)S(1)} %bitcast.12), custom_call_target="tpu_custom_call" | custom-call | flops 1073741824 | bytes 1179652 | tf_op jit(solution)/shard_map/pallas_call | solution.py:100
  139.9 1.1 shard_map.124
  141.0 1.1 collective-permute-start.22
  142.1 2.5 %collective-permute-start.23 = (bf16[256,256]{1,0:T(8,128)(2,1)S(1)}, bf16[256,256]{1,0:T(8,128)(2,1)S(1)}, u32[]{:S(2)}, u32[]{:S(2)}) collective-permute-start(bf16[256,256]{1,0:T(8,128)(2,1)S(1)} %get-tuple-element.35), channel_id=1, source_target_pairs={{0,4},{1,5},{2,6},{3,7},{4,0},{5,1},{6,2},{7,3},{8,12},{9,13},{10,... | collective-permute-start | bytes 393224 | tf_op jit(solution)/shard_map/ppermute | solution.py:372
  144.7 0.6 collective-permute-start.24
  145.2 2.6 %shard_map.118 = f32[256,256]{1,0:T(8,128)} custom-call(f32[1]{0:T(128)S(6)} %copy.12.refs_0_, f32[1]{0:T(128)S(6)} %copy.13.refs_1_, bf16[256,256]{1,0:T(8,128)(2,1)} %refs_2_, bf16[512,256]{1,0:T(8,128)(2,1)S(1)} %get-tuple-element.30.refs_3_.refs_9_, bf16[512,256]{1,0:T(8,128)(2,1)S(1)} %collective-permute-done.7.refs_4_.refs_2_, ...), custom_call_target="tpu_custom_call" | custom-call | flops 536870912 | bytes 2228232 | tf_op jit(solution)/shard_map/pallas_call | solution.py:100
  147.8 0.0 collective-permute-done.19.refs_7_
  147.8 1.4 shard_map.121
  149.3 1.8 %collective-permute-done.23.refs_2_ = bf16[256,256]{1,0:T(8,128)(2,1)S(1)} collective-permute-done((bf16[256,256]{1,0:T(8,128)(2,1)S(1)}, bf16[256,256]{1,0:T(8,128)(2,1)S(1)}, u32[]{:S(2)}, u32[]{:S(2)}) %collective-permute-start.23) | collective-permute-done | bytes 131104 | tf_op jit(solution)/shard_map/ppermute | solution.py:372
  151.0 0.8 shard_map.125
  (17 shorter events, 0.0 us)
Async XLA Ops:
  2.6 21.2 %all-to-all-start = ((s32[32,8,128]{2,1,0:T(8,128)}), s32[32,8,128]{2,1,0:T(8,128)S(1)}, u32[]{:S(2)}, u32[]{:S(2)}) async-start(s32[32,8,128]{2,1,0:T(8,128)} %get-tuple-element.20), calls=%async_computation | async-start | bytes 262144 | tf_op jit(solution)/shard_map/all_to_all | solution.py:364
  23.8 4.2 %copy-start.1 = (s32[32,8,128]{2,1,0:T(8,128)}, s32[32,8,128]{2,1,0:T(8,128)S(1)}, u32[]{:S(2)}) copy-start(s32[32,8,128]{2,1,0:T(8,128)S(1)} %all-to-all-done.refs_0_.refs_1_) | copy-start | bytes 393220
  28.0 28.5 %all-to-all-start.1 = ((bf16[32,64,256]{2,1,0:T(8,128)(2,1)}), bf16[32,64,256]{2,1,0:T(8,128)(2,1)S(1)}, u32[]{:S(2)}, u32[]{:S(2)}) async-start(bf16[32,64,256]{2,1,0:T(8,128)(2,1)} %shard_map.114), calls=%async_computation.1 | async-start | bytes 2097152 | tf_op jit(solution)/shard_map/all_to_all | solution.py:364
  33.0 23.4 %copy-start = (bf16[272,256]{1,0:T(8,128)(2,1)}, bf16[272,256]{1,0:T(8,128)(2,1)S(1)}, u32[]{:S(2)}) copy-start(bf16[272,256]{1,0:T(8,128)(2,1)S(1)} %shard_map.116.refs_12_) | copy-start | bytes 417796
  33.0 7.8 %collective-permute-start = (bf16[272,256]{1,0:T(8,128)(2,1)S(1)}, bf16[272,256]{1,0:T(8,128)(2,1)S(1)}, u32[]{:S(2)}, u32[]{:S(2)}) collective-permute-start(bf16[272,256]{1,0:T(8,128)(2,1)S(1)} %shard_map.116.refs_12_), channel_id=1, source_target_pairs={{0,2},{1,3},{2,4},{3,5},{4,6},{5,7},{6,0},{7,1},{8,10},{9,11},{10,... | collective-permute-start | bytes 417800 | tf_op jit(solution)/shard_map/ppermute | solution.py:372
  34.3 8.6 %collective-permute-start.1 = (bf16[272,256]{1,0:T(8,128)(2,1)S(1)}, bf16[272,256]{1,0:T(8,128)(2,1)S(1)}, u32[]{:S(2)}, u32[]{:S(2)}) collective-permute-start(bf16[272,256]{1,0:T(8,128)(2,1)S(1)} %shard_map.116.refs_12_), channel_id=1, source_target_pairs={{0,4},{1,5},{2,6},{3,7},{4,0},{5,1},{6,2},{7,3},{8,12},{9,13},{10,... | collective-permute-start | bytes 417800 | tf_op jit(solution)/shard_map/ppermute | solution.py:372
  36.8 7.6 %collective-permute-start.2 = (bf16[272,256]{1,0:T(8,128)(2,1)S(1)}, bf16[272,256]{1,0:T(8,128)(2,1)S(1)}, u32[]{:S(2)}, u32[]{:S(2)}) collective-permute-start(bf16[272,256]{1,0:T(8,128)(2,1)S(1)} %shard_map.116.refs_12_), channel_id=1, source_target_pairs={{0,6},{1,7},{2,0},{3,1},{4,2},{5,3},{6,4},{7,5},{8,14},{9,15},{10,... | collective-permute-start | bytes 417800 | tf_op jit(solution)/shard_map/ppermute | solution.py:372
  37.9 13.3 %collective-permute-start.3 = (bf16[272,256]{1,0:T(8,128)(2,1)S(1)}, bf16[272,256]{1,0:T(8,128)(2,1)S(1)}, u32[]{:S(2)}, u32[]{:S(2)}) collective-permute-start(bf16[272,256]{1,0:T(8,128)(2,1)S(1)} %shard_map.116.refs_12_), channel_id=1, source_target_pairs={{0,1},{1,0},{2,3},{3,2},{4,5},{5,4},{6,7},{7,6},{8,9},{9,8},{10,11... | collective-permute-start | bytes 417800 | tf_op jit(solution)/shard_map/ppermute | solution.py:368
  40.9 10.3 %collective-permute-start.4 = (bf16[272,256]{1,0:T(8,128)(2,1)S(1)}, bf16[272,256]{1,0:T(8,128)(2,1)S(1)}, u32[]{:S(2)}, u32[]{:S(2)}) collective-permute-start(bf16[272,256]{1,0:T(8,128)(2,1)S(1)} %collective-permute-done.refs_5_), channel_id=1, source_target_pairs={{0,1},{1,0},{2,3},{3,2},{4,5},{5,4},{6,7},{7,6},{8,9},{9,8},{10,11... | collective-permute-start | bytes 417800 | tf_op jit(solution)/shard_map/ppermute | solution.py:368
  42.9 8.3 %collective-permute-start.5 = (bf16[272,256]{1,0:T(8,128)(2,1)S(1)}, bf16[272,256]{1,0:T(8,128)(2,1)S(1)}, u32[]{:S(2)}, u32[]{:S(2)}) collective-permute-start(bf16[272,256]{1,0:T(8,128)(2,1)S(1)} %collective-permute-done.1.refs_6_), channel_id=1, source_target_pairs={{0,1},{1,0},{2,3},{3,2},{4,5},{5,4},{6,7},{7,6},{8,9},{9,8},{10,11... | collective-permute-start | bytes 417800 | tf_op jit(solution)/shard_map/ppermute | solution.py:368
  44.4 7.5 %collective-permute-start.6 = (bf16[272,256]{1,0:T(8,128)(2,1)S(1)}, bf16[272,256]{1,0:T(8,128)(2,1)}, u32[]{:S(2)}, u32[]{:S(2)}) collective-permute-start(bf16[272,256]{1,0:T(8,128)(2,1)S(1)} %collective-permute-done.2.refs_7_), channel_id=1, source_target_pairs={{0,1},{1,0},{2,3},{3,2},{4,5},{5,4},{6,7},{7,6},{8,9},{9,8},{10,11... | collective-permute-start | bytes 417800 | tf_op jit(solution)/shard_map/ppermute | solution.py:368
  51.2 0.7 copy-start.3
  60.6 40.9 %copy-start.2 = (s32[32,8,128]{2,1,0:T(8,128)S(1)}, s32[32,8,128]{2,1,0:T(8,128)}, u32[]{:S(2)}) copy-start(s32[32,8,128]{2,1,0:T(8,128)} %copy-done.1) | copy-start | bytes 393220
  60.6 32.8 %all-to-all-start.4 = ((bf16[32,64,256]{2,1,0:T(8,128)(2,1)}), bf16[32,64,256]{2,1,0:T(8,128)(2,1)S(1)}, u32[]{:S(2)}, u32[]{:S(2)}) async-start(bf16[32,64,256]{2,1,0:T(8,128)(2,1)} %bitcast.18), calls=%async_computation.4 | async-start | bytes 2097152 | tf_op jit(solution)/shard_map/all_to_all | solution.py:364
  68.9 7.8 %collective-permute-start.7 = (bf16[512,256]{1,0:T(8,128)(2,1)S(1)}, bf16[512,256]{1,0:T(8,128)(2,1)S(1)}, u32[]{:S(2)}, u32[]{:S(2)}) collective-permute-start(bf16[512,256]{1,0:T(8,128)(2,1)S(1)} %get-tuple-element.30.refs_3_.refs_9_), channel_id=1, source_target_pairs={{0,2},{1,3},{2,4},{3,5},{4,6},{5,7},{6,0},{7,1},{8,10},{9,11},{10,... | collective-permute-start | bytes 786440 | tf_op jit(solution)/shard_map/ppermute | solution.py:372
  70.1 12.4 %collective-permute-start.8 = (bf16[512,256]{1,0:T(8,128)(2,1)S(1)}, bf16[512,256]{1,0:T(8,128)(2,1)S(1)}, u32[]{:S(2)}, u32[]{:S(2)}) collective-permute-start(bf16[512,256]{1,0:T(8,128)(2,1)S(1)} %get-tuple-element.30.refs_3_.refs_9_), channel_id=1, source_target_pairs={{0,4},{1,5},{2,6},{3,7},{4,0},{5,1},{6,2},{7,3},{8,12},{9,13},{10,... | collective-permute-start | bytes 786440 | tf_op jit(solution)/shard_map/ppermute | solution.py:372
  72.6 12.9 %collective-permute-start.9 = (bf16[512,256]{1,0:T(8,128)(2,1)S(1)}, bf16[512,256]{1,0:T(8,128)(2,1)S(1)}, u32[]{:S(2)}, u32[]{:S(2)}) collective-permute-start(bf16[512,256]{1,0:T(8,128)(2,1)S(1)} %get-tuple-element.30.refs_3_.refs_9_), channel_id=1, source_target_pairs={{0,6},{1,7},{2,0},{3,1},{4,2},{5,3},{6,4},{7,5},{8,14},{9,15},{10,... | collective-permute-start | bytes 786440 | tf_op jit(solution)/shard_map/ppermute | solution.py:372
  73.7 11.8 %collective-permute-start.10 = (bf16[512,256]{1,0:T(8,128)(2,1)S(1)}, bf16[512,256]{1,0:T(8,128)(2,1)S(1)}, u32[]{:S(2)}, u32[]{:S(2)}) collective-permute-start(bf16[512,256]{1,0:T(8,128)(2,1)S(1)} %get-tuple-element.30.refs_3_.refs_9_), channel_id=1, source_target_pairs={{0,1},{1,0},{2,3},{3,2},{4,5},{5,4},{6,7},{7,6},{8,9},{9,8},{10,11... | collective-permute-start | bytes 786440 | tf_op jit(solution)/shard_map/ppermute | solution.py:368
  76.6 8.9 %collective-permute-start.11 = (bf16[512,256]{1,0:T(8,128)(2,1)S(1)}, bf16[512,256]{1,0:T(8,128)(2,1)S(1)}, u32[]{:S(2)}, u32[]{:S(2)}) collective-permute-start(bf16[512,256]{1,0:T(8,128)(2,1)S(1)} %collective-permute-done.7.refs_4_.refs_2_), channel_id=1, source_target_pairs={{0,1},{1,0},{2,3},{3,2},{4,5},{5,4},{6,7},{7,6},{8,9},{9,8},{10,11... | collective-permute-start | bytes 786440 | tf_op jit(solution)/shard_map/ppermute | solution.py:368
  82.6 4.1 %collective-permute-start.12 = (bf16[512,256]{1,0:T(8,128)(2,1)S(1)}, bf16[512,256]{1,0:T(8,128)(2,1)S(1)}, u32[]{:S(2)}, u32[]{:S(2)}) collective-permute-start(bf16[512,256]{1,0:T(8,128)(2,1)S(1)} %collective-permute-done.8.refs_5_.refs_3_), channel_id=1, source_target_pairs={{0,1},{1,0},{2,3},{3,2},{4,5},{5,4},{6,7},{7,6},{8,9},{9,8},{10,11... | collective-permute-start | bytes 786440 | tf_op jit(solution)/shard_map/ppermute | solution.py:368
  85.5 1.5 %collective-permute-start.13 = (bf16[512,256]{1,0:T(8,128)(2,1)S(1)}, bf16[512,256]{1,0:T(8,128)(2,1)S(1)}, u32[]{:S(2)}, u32[]{:S(2)}) collective-permute-start(bf16[512,256]{1,0:T(8,128)(2,1)S(1)} %collective-permute-done.9.refs_6_.refs_4_), channel_id=1, source_target_pairs={{0,1},{1,0},{2,3},{3,2},{4,5},{5,4},{6,7},{7,6},{8,9},{9,8},{10,11... | collective-permute-start | bytes 786440 | tf_op jit(solution)/shard_map/ppermute | solution.py:368
  93.4 17.2 %all-to-all-start.2 = ((bf16[32,8,256]{2,1,0:T(8,128)(2,1)}), bf16[32,8,256]{2,1,0:T(8,128)(2,1)S(1)}, u32[]{:S(2)}, u32[]{:S(2)}) async-start(bf16[32,8,256]{2,1,0:T(8,128)(2,1)} %bitcast.19), calls=%async_computation.2 | async-start | bytes 262144 | tf_op jit(solution)/shard_map/all_to_all | solution.py:364
  104.1 35.8 %collective-permute-start.21 = (bf16[4,256,256]{2,1,0:T(8,128)(2,1)}, bf16[4,256,256]{2,1,0:T(8,128)(2,1)}, u32[]{:S(2)}, u32[]{:S(2)}) collective-permute-start(bf16[4,256,256]{2,1,0:T(8,128)(2,1)} %shard_map.123), channel_id=1, source_target_pairs={{0,1},{1,0},{2,3},{3,2},{4,5},{5,4},{6,7},{7,6},{8,9},{9,8},{10,11... | collective-permute-start | bytes 1572872 | tf_op jit(solution)/shard_map/ppermute | solution.py:368
  125.6 8.9 %collective-permute-start.14 = (bf16[256,256]{1,0:T(8,128)(2,1)S(1)}, bf16[256,256]{1,0:T(8,128)(2,1)S(1)}, u32[]{:S(2)}, u32[]{:S(2)}) collective-permute-start(bf16[256,256]{1,0:T(8,128)(2,1)S(1)} %bitcast.13), channel_id=1, source_target_pairs={{0,2},{1,3},{2,4},{3,5},{4,6},{5,7},{6,0},{7,1},{8,10},{9,11},{10,... | collective-permute-start | bytes 393224 | tf_op jit(solution)/shard_map/ppermute | solution.py:372
  126.8 8.3 %collective-permute-start.15 = (bf16[256,256]{1,0:T(8,128)(2,1)S(1)}, bf16[256,256]{1,0:T(8,128)(2,1)S(1)}, u32[]{:S(2)}, u32[]{:S(2)}) collective-permute-start(bf16[256,256]{1,0:T(8,128)(2,1)S(1)} %bitcast.14), channel_id=1, source_target_pairs={{0,4},{1,5},{2,6},{3,7},{4,0},{5,1},{6,2},{7,3},{8,12},{9,13},{10,... | collective-permute-start | bytes 393224 | tf_op jit(solution)/shard_map/ppermute | solution.py:372
  129.3 8.2 %collective-permute-start.16 = (bf16[256,256]{1,0:T(8,128)(2,1)S(1)}, bf16[256,256]{1,0:T(8,128)(2,1)S(1)}, u32[]{:S(2)}, u32[]{:S(2)}) collective-permute-start(bf16[256,256]{1,0:T(8,128)(2,1)S(1)} %bitcast.15), channel_id=1, source_target_pairs={{0,6},{1,7},{2,0},{3,1},{4,2},{5,3},{6,4},{7,5},{8,14},{9,15},{10,... | collective-permute-start | bytes 393224 | tf_op jit(solution)/shard_map/ppermute | solution.py:372
  130.4 11.7 %collective-permute-start.17 = (bf16[256,256]{1,0:T(8,128)(2,1)S(1)}, bf16[256,256]{1,0:T(8,128)(2,1)S(1)}, u32[]{:S(2)}, u32[]{:S(2)}) collective-permute-start(bf16[256,256]{1,0:T(8,128)(2,1)S(1)} %bitcast.16), channel_id=1, source_target_pairs={{0,1},{1,0},{2,3},{3,2},{4,5},{5,4},{6,7},{7,6},{8,9},{9,8},{10,11... | collective-permute-start | bytes 393224 | tf_op jit(solution)/shard_map/ppermute | solution.py:368
  134.5 10.2 %collective-permute-start.18 = (bf16[256,256]{1,0:T(8,128)(2,1)S(1)}, bf16[256,256]{1,0:T(8,128)(2,1)S(1)}, u32[]{:S(2)}, u32[]{:S(2)}) collective-permute-start(bf16[256,256]{1,0:T(8,128)(2,1)S(1)} %collective-permute-done.14.refs_2_), channel_id=1, source_target_pairs={{0,1},{1,0},{2,3},{3,2},{4,5},{5,4},{6,7},{7,6},{8,9},{9,8},{10,11... | collective-permute-start | bytes 393224 | tf_op jit(solution)/shard_map/ppermute | solution.py:368
  135.1 12.7 %collective-permute-start.19 = (bf16[256,256]{1,0:T(8,128)(2,1)S(1)}, bf16[256,256]{1,0:T(8,128)(2,1)S(1)}, u32[]{:S(2)}, u32[]{:S(2)}) collective-permute-start(bf16[256,256]{1,0:T(8,128)(2,1)S(1)} %collective-permute-done.15.refs_3_), channel_id=1, source_target_pairs={{0,1},{1,0},{2,3},{3,2},{4,5},{5,4},{6,7},{7,6},{8,9},{9,8},{10,11... | collective-permute-start | bytes 393224 | tf_op jit(solution)/shard_map/ppermute | solution.py:368
  137.4 10.4 %collective-permute-start.20 = (bf16[256,256]{1,0:T(8,128)(2,1)S(1)}, bf16[256,256]{1,0:T(8,128)(2,1)S(1)}, u32[]{:S(2)}, u32[]{:S(2)}) collective-permute-start(bf16[256,256]{1,0:T(8,128)(2,1)S(1)} %collective-permute-done.16.refs_4_), channel_id=1, source_target_pairs={{0,1},{1,0},{2,3},{3,2},{4,5},{5,4},{6,7},{7,6},{8,9},{9,8},{10,11... | collective-permute-start | bytes 393224 | tf_op jit(solution)/shard_map/ppermute | solution.py:368
  141.0 8.2 %collective-permute-start.22 = (bf16[256,256]{1,0:T(8,128)(2,1)S(1)}, bf16[256,256]{1,0:T(8,128)(2,1)S(1)}, u32[]{:S(2)}, u32[]{:S(2)}) collective-permute-start(bf16[256,256]{1,0:T(8,128)(2,1)S(1)} %get-tuple-element.34), channel_id=1, source_target_pairs={{0,2},{1,3},{2,4},{3,5},{4,6},{5,7},{6,0},{7,1},{8,10},{9,11},{10,... | collective-permute-start | bytes 393224 | tf_op jit(solution)/shard_map/ppermute | solution.py:372
  142.1 8.9 %collective-permute-start.23 = (bf16[256,256]{1,0:T(8,128)(2,1)S(1)}, bf16[256,256]{1,0:T(8,128)(2,1)S(1)}, u32[]{:S(2)}, u32[]{:S(2)}) collective-permute-start(bf16[256,256]{1,0:T(8,128)(2,1)S(1)} %get-tuple-element.35), channel_id=1, source_target_pairs={{0,4},{1,5},{2,6},{3,7},{4,0},{5,1},{6,2},{7,3},{8,12},{9,13},{10,... | collective-permute-start | bytes 393224 | tf_op jit(solution)/shard_map/ppermute | solution.py:372
  144.7 6.4 %collective-permute-start.24 = (bf16[256,256]{1,0:T(8,128)(2,1)S(1)}, bf16[256,256]{1,0:T(8,128)(2,1)S(1)}, u32[]{:S(2)}, u32[]{:S(2)}) collective-permute-start(bf16[256,256]{1,0:T(8,128)(2,1)S(1)} %get-tuple-element.36), channel_id=1, source_target_pairs={{0,6},{1,7},{2,0},{3,1},{4,2},{5,3},{6,4},{7,5},{8,14},{9,15},{10,... | collective-permute-start | bytes 393224 | tf_op jit(solution)/shard_map/ppermute | solution.py:372
